TPU v7x, 256 devices: a whole 4x4x8 slice. The times are simulated.
256 devices in a mesh: ka: 32 (over z, y_lo, core), ga: 8 (over x, y_hi).
Axes of the slice: x: 4, y: 4 (y_hi: 2, y_lo: 2; y = y_hi * 2 + y_lo), z: 8, core: 2. Of those that a mesh axis runs over, the one named last changes fastest.
Arguments:
- offsets: int32 [2], replicated, may hold values from 0 to 31
- q_slots: int32 [32], replicated, may hold values from 0 to 31, each once
- forms: bfloat16 [1024, 128, 512], P('ka', None, 'ga'), may hold values from -0.25 to 0.25
- vectors: bfloat16 [1024, 32, 128], P('ka'), may hold values from -6 to 6
- energies: float32 [1024, 128], P('ka'), may hold values from 0.5 to 2
- screened: bfloat16 [32, 512, 32, 512], P('ka', 'ga'), may hold values from -0.046875 to 0.046875
- umklapp: int32 [32, 32, 512], P('ka'), may hold values from 0 to 511, as said below
Outputs:
- applied: float32 [1024, 32, 128], P('ka')
Inputs may be any that keep to these rules, and one draw needn't show every extreme that they name: Each row umklapp[qx, s, :] holds every value of 0 to 511 once. `q_slots`: each slot's value appears once.
All inputs are finite; a program needn't handle non-finite values.
Results may differ from a plain program's by a relative error of at most 0.0025.
Values may be sent and summed in bfloat16 or wider, within the bound.
A program may use at most 128 MiB of HBM per device.

v0:
```python
import functools

import jax
import jax.numpy as jnp
from jax import lax
from jax.experimental import pallas as pl
from jax.experimental.pallas import tpu as pltpu
from jax.sharding import PartitionSpec as P


def from_behind(value, axis, by):
    count = lax.axis_size(axis)
    return lax.ppermute(value, axis, [(i, (i + by) % count) for i in range(count)])


def swap(value, axis, bit):
    count = lax.axis_size(axis)
    return lax.ppermute(value, axis, [(i, i ^ bit) for i in range(count)])


def pick_half(tree, axis_at, which):
    return jax.tree.map(lambda a: lax.dynamic_slice_in_dim(a, which, 1, axis=axis_at), tree)


def scatter_from_roots(own, roots, axis, order):
    nbits = len(order)
    me = lax.axis_index(axis)
    full = (1 << nbits) - 1
    held = [own] * len(roots)
    shared = True
    done_mask = 0
    for bit in order:
        axis_at = nbits - 1 - bit
        mine = (me >> bit) & 1
        if shared:
            sends = pick_half(own, axis_at, 1 - mine)
            got = swap(sends, axis, 1 << bit)
            got = [got] * len(roots)
        else:
            sends = [pick_half(h, axis_at, 1 - mine) for h in held]
            got = swap(sends, axis, 1 << bit)
        new_held = []
        for r, root in enumerate(roots):
            holder = ((me ^ root) & (full & ~done_mask)) == 0
            keep = pick_half(held[r], axis_at, mine)
            new_held.append(
                jax.tree.map(lambda k, g: jnp.where(holder, k, g), keep, got[r])
            )
        held = new_held
        shared = False
        done_mask |= 1 << bit
    return held


def gather_all(pieces, axis, order):
    nbits = len(order)
    me = lax.axis_index(axis)
    held = pieces
    for bit in order:
        axis_at = nbits - 1 - bit
        mine = (me >> bit) & 1
        got = swap(held, axis, 1 << bit)

        def join(h, g):
            low = jnp.where(mine == 0, h, g)
            high = jnp.where(mine == 0, g, h)
            return jnp.concatenate([low, high], axis=axis_at)

        held = jax.tree.map(join, held, got)
    return held


def sum_all(value, axis, order):
    nbits = len(order)
    me = lax.axis_index(axis)
    held = value
    for bit in order:
        axis_at = nbits - 1 - bit
        mine = (me >> bit) & 1
        sends = lax.dynamic_slice_in_dim(held, 1 - mine, 1, axis=axis_at)
        keep = lax.dynamic_slice_in_dim(held, mine, 1, axis=axis_at)
        held = keep + swap(sends, axis, 1 << bit)
    return gather_all(held, axis, order[::-1])


def contract_kernel(block, q_ref, perm_ref, mov_ref, out_ref, acc_ref):
    slots = perm_ref.shape[1]
    rows = out_ref.shape[1]
    count = rows // block
    acc_ref[...] = jnp.zeros_like(acc_ref)

    def one_slot(s, carry):
        start = pl.multiple_of((count - q_ref[s]) * block, block)
        rolled = mov_ref[0, pl.ds(start, rows), :]
        acc_ref[...] += lax.dot_general(
            rolled, perm_ref[0, s], (((1,), (1,)), ((), ())),
            preferred_element_type=jnp.float32,
        )
        return carry

    lax.fori_loop(0, slots, one_slot, 0)
    out_ref[0] = acc_ref[...].astype(out_ref.dtype)


def contract(q_slots, permuted, doubled, block):
    steps, slots, local, waves = permuted.shape
    rows = doubled.shape[1] // 2
    return pl.pallas_call(
        functools.partial(contract_kernel, block),
        out_shape=jax.ShapeDtypeStruct((steps, rows, local), jnp.bfloat16),
        grid_spec=pltpu.PrefetchScalarGridSpec(
            num_scalar_prefetch=1,
            grid=(steps,),
            in_specs=[
                pl.BlockSpec((1, slots, local, waves), lambda i, q: (i, 0, 0, 0)),
                pl.BlockSpec((1, 2 * rows, waves), lambda i, q: (i, 0, 0)),
            ],
            out_specs=pl.BlockSpec((1, rows, local), lambda i, q: (i, 0, 0)),
            scratch_shapes=[pltpu.VMEM((rows, local), jnp.float32)],
        ),
        cost_estimate=pl.CostEstimate(
            flops=2 * steps * slots * rows * local * waves,
            bytes_accessed=2 * steps * (slots * local * waves + 2 * rows * waves + rows * local),
            transcendentals=0,
        ),
    )(q_slots, permuted, doubled)


def body(offsets, q_slots, forms, vectors, energies, screened, umklapp):
    kpoint_count = vectors.shape[0]
    vector_count = vectors.shape[1]
    pair_count = vectors.shape[2]
    local_waves = forms.shape[2]
    slot_count = screened.shape[2]
    plane_waves = screened.shape[3]
    step_count = offsets.shape[0]
    ka_size = lax.axis_size("ka")
    ga_size = lax.axis_size("ga")
    ka_bits = ka_size.bit_length() - 1
    ga_bits = ga_size.bit_length() - 1
    me_ka = lax.axis_index("ka")

    projected = lax.dot_general(
        vectors, forms, (((2,), (1,)), ((0,), (0,))), preferred_element_type=jnp.float32
    ).astype(jnp.bfloat16)

    per_piece = slot_count // ka_size
    slab = jnp.transpose(screened[0], (1, 0, 2))
    slab = slab.reshape((2,) * ka_bits + (per_piece, local_waves, plane_waves))
    table = umklapp[0].reshape((2,) * ka_bits + (per_piece, plane_waves))
    roots = [offsets[i] for i in range(step_count)]
    pieces = scatter_from_roots((slab, table), roots, "ka", list(range(ka_bits)))
    waves = jnp.arange(plane_waves, dtype=jnp.int32)
    permuted_pieces = []
    for piece, rows in pieces:
        piece = piece.reshape(per_piece, local_waves, plane_waves)
        rows = rows.reshape(per_piece, plane_waves)
        onehot = (rows[:, :, None] == waves[None, None, :]).astype(jnp.bfloat16)
        moved_cols = lax.dot_general(
            piece, onehot, (((2,), (1,)), ((0,), (0,))), preferred_element_type=jnp.float32
        ).astype(jnp.bfloat16)
        permuted_pieces.append(
            moved_cols.reshape((1,) * ka_bits + (per_piece, local_waves, plane_waves))
        )
    gathered = gather_all(permuted_pieces, "ka", list(range(ka_bits))[::-1])

    moving = [projected] * step_count
    for level in range(ka_bits):
        hopped = from_behind(jnp.stack(moving), "ka", 1 << level)
        moving = [
            jnp.where(roots[i] >> level & 1 == 1, hopped[i], moving[i])
            for i in range(step_count)
        ]
    moving_all = lax.all_gather(jnp.stack(moving), "ga", axis=3, tiled=True)

    permuted_all = jnp.stack(
        [gathered[i].reshape(slot_count, local_waves, plane_waves) for i in range(step_count)]
    )
    moving_rows = moving_all.reshape(step_count, kpoint_count * vector_count, plane_waves)
    doubled = jnp.concatenate([moving_rows, moving_rows], axis=1)
    kernel_part = contract(q_slots, permuted_all, doubled, vector_count)
    kernel_part = kernel_part.reshape(step_count, kpoint_count, vector_count, local_waves)
    kernel_cat = jnp.concatenate([kernel_part[i] for i in range(step_count)], axis=1)
    action = lax.dot_general(
        kernel_cat, forms, (((2,), (2,)), ((0,), (0,))), preferred_element_type=jnp.float32
    )
    action = action.reshape(kpoint_count, step_count, vector_count, pair_count).sum(axis=1)
    ga_order = [1, 0, 2][:ga_bits] if ga_bits == 3 else list(range(ga_bits))
    action = action.reshape((2,) * ga_bits + (kpoint_count // ga_size, vector_count, pair_count))
    action = sum_all(action, "ga", ga_order).reshape(kpoint_count, vector_count, pair_count)
    return energies[:, None, :] * vectors.astype(jnp.float32) - action


def solution(mesh):
    return jax.shard_map(
        body,
        mesh=mesh,
        in_specs=(
            P(),
            P(),
            P("ka", None, "ga"),
            P("ka", None, None),
            P("ka", None),
            P("ka", "ga", None, None),
            P("ka", None, None),
        ),
        out_specs=P("ka", None, None),
        check_vma=False,
    )
```

profile of v0, /device:TPU:32, one launch (start us, length us, event | category | flops | bytes accessed | tf_op | source)
XLA Modules:
  0.0 344.6 jit_solution(7808134986049273504)
XLA Ops:
  30.7 4.3 %collective-permute-start.8 = (s32[2,1,1,1,1,1,512]{6,4,3,2,1,0,5:T(1,128)S(1)}, s32[2,1,1,1,1,1,512]{6,4,3,2,1,0,5:T(1,128)S(1)}, u32[]{:S(2)}, u32[]{:S(2)}) collective-permute-start(s32[2,1,1,1,1,1,512]{6,4,3,2,1,0,5:T(1,128)S(1)} %constant_dynamic-slice_fusion.16), channel_id=1, source_target_pairs={{0,64},{8,72},{16,80},{24,88},{32,96},{40,104},{48,112},{56,120},{... | collective-permute-start | bytes 12296 | tf_op jit(solution)/shard_map/ppermute | solution.py:18
  37.5 10.9 %collective-permute-done.29 = bf16[2,32,32,64]{3,2,1,0:T(8,128)(2,1)S(1)} collective-permute-done((bf16[2,32,32,64]{3,2,1,0:T(8,128)(2,1)S(1)}, bf16[2,32,32,64]{3,2,1,0:T(8,128)(2,1)S(1)}, u32[]{:S(2)}, u32[]{:S(2)}) %collective-permute-start.29) | collective-permute-done | bytes 262176 | tf_op jit(solution)/shard_map/ppermute | solution.py:13
  49.3 4.5 %collective-permute-start.9 = (s32[1,1,1,1,1,1,512]{6,4,3,2,1,0,5:T(1,128)S(1)}, s32[1,1,1,1,1,1,512]{6,4,3,2,1,0,5:T(1,128)S(1)}, u32[]{:S(2)}, u32[]{:S(2)}) collective-permute-start(s32[1,1,1,1,1,1,512]{6,4,3,2,1,0,5:T(1,128)S(1)} %constant_dynamic-slice_fusion.14), channel_id=1, source_target_pairs={{0,128},{8,136},{16,144},{24,152},{32,160},{40,168},{48,176},{56,1... | collective-permute-start | bytes 6152 | tf_op jit(solution)/shard_map/ppermute | solution.py:18
  53.8 6.4 %collective-permute-done.30 = bf16[2,32,32,64]{3,2,1,0:T(8,128)(2,1)S(1)} collective-permute-done((bf16[2,32,32,64]{3,2,1,0:T(8,128)(2,1)S(1)}, bf16[2,32,32,64]{3,2,1,0:T(8,128)(2,1)S(1)}, u32[]{:S(2)}, u32[]{:S(2)}) %collective-permute-start.30) | collective-permute-done | bytes 262176 | tf_op jit(solution)/shard_map/ppermute | solution.py:13
  60.4 5.0 %collective-permute-start.31 = (bf16[2,32,32,64]{3,2,1,0:T(8,128)(2,1)S(1)}, bf16[2,32,32,64]{3,2,1,0:T(8,128)(2,1)S(1)}, u32[]{:S(2)}, u32[]{:S(2)}) collective-permute-start(bf16[2,32,32,64]{3,2,1,0:T(8,128)(2,1)S(1)} %pad_maximum_fusion.11), channel_id=1, source_target_pairs={{0,64},{8,72},{16,80},{24,88},{32,96},{40,104},{48,112},{56,120},{... | collective-permute-start | bytes 786440 | tf_op jit(solution)/shard_map/ppermute | solution.py:13
  65.4 19.5 %collective-permute-done.31 = bf16[2,32,32,64]{3,2,1,0:T(8,128)(2,1)S(1)} collective-permute-done((bf16[2,32,32,64]{3,2,1,0:T(8,128)(2,1)S(1)}, bf16[2,32,32,64]{3,2,1,0:T(8,128)(2,1)S(1)}, u32[]{:S(2)}, u32[]{:S(2)}) %collective-permute-start.31) | collective-permute-done | bytes 262176 | tf_op jit(solution)/shard_map/ppermute | solution.py:13
  85.1 26.0 %collective-permute-start.32 = (bf16[2,32,32,64]{3,2,1,0:T(8,128)(2,1)S(1)}, bf16[2,32,32,64]{3,2,1,0:T(8,128)(2,1)S(1)}, u32[]{:S(2)}, u32[]{:S(2)}) collective-permute-start(bf16[2,32,32,64]{3,2,1,0:T(8,128)(2,1)S(1)} %pad_maximum_fusion.12), channel_id=1, source_target_pairs={{0,128},{8,136},{16,144},{24,152},{32,160},{40,168},{48,176},{56,1... | collective-permute-start | bytes 786440 | tf_op jit(solution)/shard_map/ppermute | solution.py:13
  116.4 9.0 %collective-permute-done.32 = bf16[2,32,32,64]{3,2,1,0:T(8,128)(2,1)S(1)} collective-permute-done((bf16[2,32,32,64]{3,2,1,0:T(8,128)(2,1)S(1)}, bf16[2,32,32,64]{3,2,1,0:T(8,128)(2,1)S(1)}, u32[]{:S(2)}, u32[]{:S(2)}) %collective-permute-start.32) | collective-permute-done | bytes 262176 | tf_op jit(solution)/shard_map/ppermute | solution.py:13
  132.5 4.4 %collective-permute-done.2 = bf16[2,2,1,1,1,1,64,512]{7,6,5,4,3,2,1,0:T(8,128)(2,1)S(1)} collective-permute-done((bf16[2,2,1,1,1,1,64,512]{7,6,5,4,3,2,1,0:T(8,128)(2,1)S(1)}, bf16[2,2,1,1,1,1,64,512]{7,6,5,4,3,2,1,0:T(8,128)(2,1)S(1)}, u32[]{:S(2)}, u32[]{:S(2)}) %collective-permute-start.2) | collective-permute-done | bytes 262176 | tf_op jit(solution)/shard_map/ppermute | solution.py:18
  137.0 6.2 %collective-permute-start.3 = (bf16[2,1,1,1,1,1,64,512]{7,6,5,4,3,2,1,0:T(8,128)(2,1)S(1)}, bf16[2,1,1,1,1,1,64,512]{7,6,5,4,3,2,1,0:T(8,128)(2,1)S(1)}, u32[]{:S(2)}, u32[]{:S(2)}) collective-permute-start(bf16[2,1,1,1,1,1,64,512]{7,6,5,4,3,2,1,0:T(8,128)(2,1)S(1)} %constant_dynamic-slice_fusion.23), channel_id=1, source_target_pairs={{0,64},{8,72},{16,80},{24,88},{32,96},{40,104},{48,112},{56,120},{... | collective-permute-start | bytes 393224 | tf_op jit(solution)/shard_map/ppermute | solution.py:18
  143.2 3.8 %collective-permute-start.17 = (bf16[2,1,1,1,1,1,64,512]{7,6,5,4,3,2,1,0:T(8,128)(2,1)S(1)}, bf16[2,1,1,1,1,1,64,512]{7,6,5,4,3,2,1,0:T(8,128)(2,1)S(1)}, u32[]{:S(2)}, u32[]{:S(2)}) collective-permute-start(bf16[2,1,1,1,1,1,64,512]{7,6,5,4,3,2,1,0:T(8,128)(2,1)S(1)} %constant_dynamic-slice_fusion.11), channel_id=1, source_target_pairs={{0,64},{8,72},{16,80},{24,88},{32,96},{40,104},{48,112},{56,120},{... | collective-permute-start | bytes 393224 | tf_op jit(solution)/shard_map/ppermute | solution.py:18
  147.0 5.1 %collective-permute-done.3 = bf16[2,1,1,1,1,1,64,512]{7,6,5,4,3,2,1,0:T(8,128)(2,1)S(1)} collective-permute-done((bf16[2,1,1,1,1,1,64,512]{7,6,5,4,3,2,1,0:T(8,128)(2,1)S(1)}, bf16[2,1,1,1,1,1,64,512]{7,6,5,4,3,2,1,0:T(8,128)(2,1)S(1)}, u32[]{:S(2)}, u32[]{:S(2)}) %collective-permute-start.3) | collective-permute-done | bytes 131104 | tf_op jit(solution)/shard_map/ppermute | solution.py:18
  177.1 4.3 %collective-permute-done.24 = bf16[2,1,1,1,1,1,64,512]{7,6,5,4,3,2,1,0:T(8,128)(2,1)S(1)} collective-permute-done((bf16[2,1,1,1,1,1,64,512]{7,6,5,4,3,2,1,0:T(8,128)(2,1)S(1)}, bf16[2,1,1,1,1,1,64,512]{7,6,5,4,3,2,1,0:T(8,128)(2,1)S(1)}, u32[]{:S(2)}, u32[]{:S(2)}) %collective-permute-start.24) | collective-permute-done | bytes 131104 | tf_op jit(solution)/shard_map/ppermute | solution.py:18
  183.7 4.3 %collective-permute-done.25 = bf16[2,2,1,1,1,1,64,512]{7,6,5,4,3,2,1,0:T(8,128)(2,1)S(1)} collective-permute-done((bf16[2,2,1,1,1,1,64,512]{7,6,5,4,3,2,1,0:T(8,128)(2,1)S(1)}, bf16[2,2,1,1,1,1,64,512]{7,6,5,4,3,2,1,0:T(8,128)(2,1)S(1)}, u32[]{:S(2)}, u32[]{:S(2)}) %collective-permute-start.25) | collective-permute-done | bytes 262176 | tf_op jit(solution)/shard_map/ppermute | solution.py:18
  188.1 16.0 %collective-permute-done.13 = bf16[2,2,2,1,1,1,64,512]{7,6,5,4,3,2,1,0:T(8,128)(2,1)} collective-permute-done((bf16[2,2,2,1,1,1,64,512]{7,6,5,4,3,2,1,0:T(8,128)(2,1)S(1)}, bf16[2,2,2,1,1,1,64,512]{7,6,5,4,3,2,1,0:T(8,128)(2,1)}, u32[]{:S(2)}, u32[]{:S(2)}) %collective-permute-start.13) | collective-permute-done | bytes 524320 | tf_op jit(solution)/shard_map/ppermute | solution.py:18
  206.3 14.7 %collective-permute-done.26 = bf16[2,2,2,1,1,1,64,512]{7,6,5,4,3,2,1,0:T(8,128)(2,1)} collective-permute-done((bf16[2,2,2,1,1,1,64,512]{7,6,5,4,3,2,1,0:T(8,128)(2,1)S(1)}, bf16[2,2,2,1,1,1,64,512]{7,6,5,4,3,2,1,0:T(8,128)(2,1)}, u32[]{:S(2)}, u32[]{:S(2)}) %collective-permute-start.26) | collective-permute-done | bytes 524320 | tf_op jit(solution)/shard_map/ppermute | solution.py:18
  230.2 24.9 %all-gather.2.cloned.1.call-done = bf16[2,32,32,512]{2,1,0,3:T(8,128)(2,1)} async-done(((bf16[2,32,32,64]{2,1,0,3:T(8,128)(2,1)}), bf16[2,32,32,512]{2,1,0,3:T(8,128)(2,1)}) %all-gather.2.cloned.1.call-update) | async-done | bytes 2097168 | tf_op jit(solution)/shard_map/all_gather | solution.py:174
  255.1 8.3 %copy.11 = bf16[2,32,32,512]{3,2,1,0:T(8,128)(2,1)S(1)} copy(bf16[2,32,32,512]{2,1,0,3:T(8,128)(2,1)} %all-gather.2.cloned.1.call-done) | data formatting | bytes 4194304 | tf_op jit(solution)/shard_map/all_gather | solution.py:174
  265.8 30.1 %shard_map.73 = bf16[2,1024,64]{2,1,0:T(8,128)(2,1)} custom-call(s32[32]{0:T(128)} %q_ref.1, bf16[2,32,64,512]{3,2,1,0:T(8,128)(2,1)} %pad_maximum_fusion.perm_ref, bf16[2,2048,512]{2,1,0:T(8,128)(2,1)} %pad_maximum_fusion.1.mov_ref), custom_call_target="tpu_custom_call" | custom-call | flops 4294967296 | bytes 8650752 | tf_op jit(solution)/shard_map/pallas_call | solution.py:108
  297.9 7.3 %collective-permute-done.33 = f32[2,1,2,4,32,128]{5,4,3,2,1,0:T(8,128)S(1)} collective-permute-done((f32[2,1,2,4,32,128]{5,4,3,2,1,0:T(8,128)S(1)}, f32[2,1,2,4,32,128]{5,4,3,2,1,0:T(8,128)S(1)}, u32[]{:S(2)}, u32[]{:S(2)}) %collective-permute-start.33) | collective-permute-done | bytes 262176 | tf_op jit(solution)/shard_map/ppermute | solution.py:18
  305.9 6.0 %collective-permute-done.34 = f32[2,1,1,4,32,128]{5,4,3,2,1,0:T(8,128)S(1)} collective-permute-done((f32[2,1,1,4,32,128]{5,4,3,2,1,0:T(8,128)S(1)}, f32[2,1,1,4,32,128]{5,4,3,2,1,0:T(8,128)S(1)}, u32[]{:S(2)}, u32[]{:S(2)}) %collective-permute-start.34) | collective-permute-done | bytes 131104 | tf_op jit(solution)/shard_map/ppermute | solution.py:18
  314.0 3.7 %collective-permute-done.35 = f32[1,1,1,4,32,128]{5,4,3,2,1,0:T(8,128)S(1)} collective-permute-done((f32[1,1,1,4,32,128]{5,4,3,2,1,0:T(8,128)S(1)}, f32[1,1,1,4,32,128]{5,4,3,2,1,0:T(8,128)S(1)}, u32[]{:S(2)}, u32[]{:S(2)}) %collective-permute-start.35) | collective-permute-done | bytes 65568 | tf_op jit(solution)/shard_map/ppermute | solution.py:18
  324.3 6.0 %collective-permute-done.37 = f32[2,1,1,4,32,128]{5,4,3,2,1,0:T(8,128)S(1)} collective-permute-done((f32[2,1,1,4,32,128]{5,4,3,2,1,0:T(8,128)S(1)}, f32[2,1,1,4,32,128]{5,4,3,2,1,0:T(8,128)S(1)}, u32[]{:S(2)}, u32[]{:S(2)}) %collective-permute-start.37) | collective-permute-done | bytes 131104 | tf_op jit(solution)/shard_map/ppermute | solution.py:18
  330.9 5.8 %collective-permute-done.38 = f32[2,1,2,4,32,128]{5,4,3,2,1,0:T(8,128)S(1)} collective-permute-done((f32[2,1,2,4,32,128]{5,4,3,2,1,0:T(8,128)S(1)}, f32[2,1,2,4,32,128]{5,4,3,2,1,0:T(8,128)S(1)}, u32[]{:S(2)}, u32[]{:S(2)}) %collective-permute-start.38) | collective-permute-done | bytes 262176 | tf_op jit(solution)/shard_map/ppermute | solution.py:18
  (167 shorter events, 87.4 us)
Async XLA Ops:
  6.5 248.5 %all-gather.2.cloned.1.call-start = ((), (), s32[]{:S(2)}) async-start(), calls=%async_computation | async-start | bytes 9437184 | tf_op jit(solution)/shard_map/all_gather | solution.py:174
  9.8 25.3 %collective-permute-start.28 = (bf16[2,32,32,64]{3,2,1,0:T(8,128)(2,1)}, bf16[2,32,32,64]{3,2,1,0:T(8,128)(2,1)S(1)}, u32[]{:S(2)}, u32[]{:S(2)}) collective-permute-start(bf16[2,32,32,64]{3,2,1,0:T(8,128)(2,1)} %pad_maximum_fusion.8), channel_id=1, source_target_pairs={{0,8},{8,16},{16,24},{24,32},{32,40},{40,48},{48,56},{56,64},{64,7... | collective-permute-start | bytes 786440 | tf_op jit(solution)/shard_map/ppermute | solution.py:13
  13.7 97.4 %collective-permute-start = (bf16[2,2,2,2,1,1,64,512]{7,6,5,4,3,2,1,0:T(8,128)(2,1)}, bf16[2,2,2,2,1,1,64,512]{7,6,5,4,3,2,1,0:T(8,128)(2,1)}, u32[]{:S(2)}, u32[]{:S(2)}) collective-permute-start(bf16[2,2,2,2,1,1,64,512]{7,6,5,4,3,2,1,0:T(8,128)(2,1)} %constant_dynamic-slice_fusion.26), channel_id=1, source_target_pairs={{0,8},{8,0},{16,24},{24,16},{32,40},{40,32},{48,56},{56,48},{64,72... | collective-permute-start | bytes 3145736 | tf_op jit(solution)/shard_map/ppermute | solution.py:18
  35.3 13.1 %collective-permute-start.29 = (bf16[2,32,32,64]{3,2,1,0:T(8,128)(2,1)S(1)}, bf16[2,32,32,64]{3,2,1,0:T(8,128)(2,1)S(1)}, u32[]{:S(2)}, u32[]{:S(2)}) collective-permute-start(bf16[2,32,32,64]{3,2,1,0:T(8,128)(2,1)S(1)} %pad_maximum_fusion.9), channel_id=1, source_target_pairs={{0,16},{8,24},{16,32},{24,40},{32,48},{40,56},{48,64},{56,72},{64,... | collective-permute-start | bytes 786440 | tf_op jit(solution)/shard_map/ppermute | solution.py:13
  37.4 16.4 %collective-permute-start.21 = (s32[2,1,1,1,1,1,512]{6,4,3,2,1,0,5:T(1,128)S(1)}, s32[2,1,1,1,1,1,512]{6,4,3,2,1,0,5:T(1,128)S(1)}, u32[]{:S(2)}, u32[]{:S(2)}) collective-permute-start(s32[2,1,1,1,1,1,512]{6,4,3,2,1,0,5:T(1,128)S(1)} %constant_dynamic-slice_fusion.5), channel_id=1, source_target_pairs={{0,64},{8,72},{16,80},{24,88},{32,96},{40,104},{48,112},{56,120},{... | collective-permute-start | bytes 12296 | tf_op jit(solution)/shard_map/ppermute | solution.py:18
  48.6 11.6 %collective-permute-start.30 = (bf16[2,32,32,64]{3,2,1,0:T(8,128)(2,1)S(1)}, bf16[2,32,32,64]{3,2,1,0:T(8,128)(2,1)S(1)}, u32[]{:S(2)}, u32[]{:S(2)}) collective-permute-start(bf16[2,32,32,64]{3,2,1,0:T(8,128)(2,1)S(1)} %pad_maximum_fusion.10), channel_id=1, source_target_pairs={{0,32},{8,40},{16,48},{24,56},{32,64},{40,72},{48,80},{56,88},{64,... | collective-permute-start | bytes 786440 | tf_op jit(solution)/shard_map/ppermute | solution.py:13
  49.3 16.1 %collective-permute-start.9 = (s32[1,1,1,1,1,1,512]{6,4,3,2,1,0,5:T(1,128)S(1)}, s32[1,1,1,1,1,1,512]{6,4,3,2,1,0,5:T(1,128)S(1)}, u32[]{:S(2)}, u32[]{:S(2)}) collective-permute-start(s32[1,1,1,1,1,1,512]{6,4,3,2,1,0,5:T(1,128)S(1)} %constant_dynamic-slice_fusion.14), channel_id=1, source_target_pairs={{0,128},{8,136},{16,144},{24,152},{32,160},{40,168},{48,176},{56,1... | collective-permute-start | bytes 6152 | tf_op jit(solution)/shard_map/ppermute | solution.py:18
  60.4 24.5 %collective-permute-start.31 = (bf16[2,32,32,64]{3,2,1,0:T(8,128)(2,1)S(1)}, bf16[2,32,32,64]{3,2,1,0:T(8,128)(2,1)S(1)}, u32[]{:S(2)}, u32[]{:S(2)}) collective-permute-start(bf16[2,32,32,64]{3,2,1,0:T(8,128)(2,1)S(1)} %pad_maximum_fusion.11), channel_id=1, source_target_pairs={{0,64},{8,72},{16,80},{24,88},{32,96},{40,104},{48,112},{56,120},{... | collective-permute-start | bytes 786440 | tf_op jit(solution)/shard_map/ppermute | solution.py:13
  65.3 48.1 %collective-permute-start.22 = (s32[1,1,1,1,1,1,512]{6,4,3,2,1,0,5:T(1,128)S(1)}, s32[1,1,1,1,1,1,512]{6,4,3,2,1,0,5:T(1,128)S(1)}, u32[]{:S(2)}, u32[]{:S(2)}) collective-permute-start(s32[1,1,1,1,1,1,512]{6,4,3,2,1,0,5:T(1,128)S(1)} %constant_dynamic-slice_fusion.3), channel_id=1, source_target_pairs={{0,128},{8,136},{16,144},{24,152},{32,160},{40,168},{48,176},{56,1... | collective-permute-start | bytes 6152 | tf_op jit(solution)/shard_map/ppermute | solution.py:18
  85.1 40.3 %collective-permute-start.32 = (bf16[2,32,32,64]{3,2,1,0:T(8,128)(2,1)S(1)}, bf16[2,32,32,64]{3,2,1,0:T(8,128)(2,1)S(1)}, u32[]{:S(2)}, u32[]{:S(2)}) collective-permute-start(bf16[2,32,32,64]{3,2,1,0:T(8,128)(2,1)S(1)} %pad_maximum_fusion.12), channel_id=1, source_target_pairs={{0,128},{8,136},{16,144},{24,152},{32,160},{40,168},{48,176},{56,1... | collective-permute-start | bytes 786440 | tf_op jit(solution)/shard_map/ppermute | solution.py:13
  113.5 14.6 %collective-permute-start.1 = (bf16[2,2,2,1,1,1,64,512]{7,6,5,4,3,2,1,0:T(8,128)(2,1)}, bf16[2,2,2,1,1,1,64,512]{7,6,5,4,3,2,1,0:T(8,128)(2,1)}, u32[]{:S(2)}, u32[]{:S(2)}) collective-permute-start(bf16[2,2,2,1,1,1,64,512]{7,6,5,4,3,2,1,0:T(8,128)(2,1)} %constant_dynamic-slice_fusion.25), channel_id=1, source_target_pairs={{0,16},{8,24},{16,0},{24,8},{32,48},{40,56},{48,32},{56,40},{64,80... | collective-permute-start | bytes 1572872 | tf_op jit(solution)/shard_map/ppermute | solution.py:18
  114.5 14.8 %collective-permute-start.15 = (bf16[2,2,2,1,1,1,64,512]{7,6,5,4,3,2,1,0:T(8,128)(2,1)}, bf16[2,2,2,1,1,1,64,512]{7,6,5,4,3,2,1,0:T(8,128)(2,1)}, u32[]{:S(2)}, u32[]{:S(2)}) collective-permute-start(bf16[2,2,2,1,1,1,64,512]{7,6,5,4,3,2,1,0:T(8,128)(2,1)} %constant_dynamic-slice_fusion.13), channel_id=1, source_target_pairs={{0,16},{8,24},{16,0},{24,8},{32,48},{40,56},{48,32},{56,40},{64,80... | collective-permute-start | bytes 1572872 | tf_op jit(solution)/shard_map/ppermute | solution.py:18
  129.2 7.7 %collective-permute-start.2 = (bf16[2,2,1,1,1,1,64,512]{7,6,5,4,3,2,1,0:T(8,128)(2,1)S(1)}, bf16[2,2,1,1,1,1,64,512]{7,6,5,4,3,2,1,0:T(8,128)(2,1)S(1)}, u32[]{:S(2)}, u32[]{:S(2)}) collective-permute-start(bf16[2,2,1,1,1,1,64,512]{7,6,5,4,3,2,1,0:T(8,128)(2,1)S(1)} %constant_dynamic-slice_fusion.24), channel_id=1, source_target_pairs={{0,32},{8,40},{16,48},{24,56},{32,0},{40,8},{48,16},{56,24},{64,96... | collective-permute-start | bytes 786440 | tf_op jit(solution)/shard_map/ppermute | solution.py:18
  130.5 12.7 %collective-permute-start.16 = (bf16[2,2,1,1,1,1,64,512]{7,6,5,4,3,2,1,0:T(8,128)(2,1)S(1)}, bf16[2,2,1,1,1,1,64,512]{7,6,5,4,3,2,1,0:T(8,128)(2,1)S(1)}, u32[]{:S(2)}, u32[]{:S(2)}) collective-permute-start(bf16[2,2,1,1,1,1,64,512]{7,6,5,4,3,2,1,0:T(8,128)(2,1)S(1)} %constant_dynamic-slice_fusion.12), channel_id=1, source_target_pairs={{0,32},{8,40},{16,48},{24,56},{32,0},{40,8},{48,16},{56,24},{64,96... | collective-permute-start | bytes 786440 | tf_op jit(solution)/shard_map/ppermute | solution.py:18
  137.0 15.1 %collective-permute-start.3 = (bf16[2,1,1,1,1,1,64,512]{7,6,5,4,3,2,1,0:T(8,128)(2,1)S(1)}, bf16[2,1,1,1,1,1,64,512]{7,6,5,4,3,2,1,0:T(8,128)(2,1)S(1)}, u32[]{:S(2)}, u32[]{:S(2)}) collective-permute-start(bf16[2,1,1,1,1,1,64,512]{7,6,5,4,3,2,1,0:T(8,128)(2,1)S(1)} %constant_dynamic-slice_fusion.23), channel_id=1, source_target_pairs={{0,64},{8,72},{16,80},{24,88},{32,96},{40,104},{48,112},{56,120},{... | collective-permute-start | bytes 393224 | tf_op jit(solution)/shard_map/ppermute | solution.py:18
  143.2 13.1 %collective-permute-start.17 = (bf16[2,1,1,1,1,1,64,512]{7,6,5,4,3,2,1,0:T(8,128)(2,1)S(1)}, bf16[2,1,1,1,1,1,64,512]{7,6,5,4,3,2,1,0:T(8,128)(2,1)S(1)}, u32[]{:S(2)}, u32[]{:S(2)}) collective-permute-start(bf16[2,1,1,1,1,1,64,512]{7,6,5,4,3,2,1,0:T(8,128)(2,1)S(1)} %constant_dynamic-slice_fusion.11), channel_id=1, source_target_pairs={{0,64},{8,72},{16,80},{24,88},{32,96},{40,104},{48,112},{56,120},{... | collective-permute-start | bytes 393224 | tf_op jit(solution)/shard_map/ppermute | solution.py:18
  152.2 9.0 %collective-permute-start.4 = (bf16[1,1,1,1,1,1,64,512]{7,6,5,4,3,2,1,0:T(8,128)(2,1)S(1)}, bf16[1,1,1,1,1,1,64,512]{7,6,5,4,3,2,1,0:T(8,128)(2,1)S(1)}, u32[]{:S(2)}, u32[]{:S(2)}) collective-permute-start(bf16[1,1,1,1,1,1,64,512]{7,6,5,4,3,2,1,0:T(8,128)(2,1)S(1)} %constant_dynamic-slice_fusion.22), channel_id=1, source_target_pairs={{0,128},{8,136},{16,144},{24,152},{32,160},{40,168},{48,176},{56,1... | collective-permute-start | bytes 196616 | tf_op jit(solution)/shard_map/ppermute | solution.py:18
  156.3 9.1 %collective-permute-start.18 = (bf16[1,1,1,1,1,1,64,512]{7,6,5,4,3,2,1,0:T(8,128)(2,1)S(1)}, bf16[1,1,1,1,1,1,64,512]{7,6,5,4,3,2,1,0:T(8,128)(2,1)S(1)}, u32[]{:S(2)}, u32[]{:S(2)}) collective-permute-start(bf16[1,1,1,1,1,1,64,512]{7,6,5,4,3,2,1,0:T(8,128)(2,1)S(1)} %constant_dynamic-slice_fusion.10), channel_id=1, source_target_pairs={{0,128},{8,136},{16,144},{24,152},{32,160},{40,168},{48,176},{56,1... | collective-permute-start | bytes 196616 | tf_op jit(solution)/shard_map/ppermute | solution.py:18
  161.5 8.3 %collective-permute-start.10 = (bf16[1,1,1,1,1,1,64,512]{7,6,5,4,3,2,1,0:T(8,128)(2,1)S(1)}, bf16[1,1,1,1,1,1,64,512]{7,6,5,4,3,2,1,0:T(8,128)(2,1)S(1)}, u32[]{:S(2)}, u32[]{:S(2)}) collective-permute-start(bf16[1,1,1,1,1,1,64,512]{7,6,5,4,3,2,1,0:T(8,128)(2,1)S(1)} %fusion), channel_id=1, source_target_pairs={{0,128},{8,136},{16,144},{24,152},{32,160},{40,168},{48,176},{56,1... | collective-permute-start | bytes 196616 | tf_op jit(solution)/shard_map/ppermute | solution.py:18
  165.8 9.6 %collective-permute-start.23 = (bf16[1,1,1,1,1,1,64,512]{7,6,5,4,3,2,1,0:T(8,128)(2,1)S(1)}, bf16[1,1,1,1,1,1,64,512]{7,6,5,4,3,2,1,0:T(8,128)(2,1)S(1)}, u32[]{:S(2)}, u32[]{:S(2)}) collective-permute-start(bf16[1,1,1,1,1,1,64,512]{7,6,5,4,3,2,1,0:T(8,128)(2,1)S(1)} %fusion.1), channel_id=1, source_target_pairs={{0,128},{8,136},{16,144},{24,152},{32,160},{40,168},{48,176},{56,1... | collective-permute-start | bytes 196616 | tf_op jit(solution)/shard_map/ppermute | solution.py:18
  183.6 20.6 %collective-permute-start.13 = (bf16[2,2,2,1,1,1,64,512]{7,6,5,4,3,2,1,0:T(8,128)(2,1)S(1)}, bf16[2,2,2,1,1,1,64,512]{7,6,5,4,3,2,1,0:T(8,128)(2,1)}, u32[]{:S(2)}, u32[]{:S(2)}) collective-permute-start(bf16[2,2,2,1,1,1,64,512]{7,6,5,4,3,2,1,0:T(8,128)(2,1)S(1)} %pad_maximum_fusion.6), channel_id=1, source_target_pairs={{0,16},{8,24},{16,0},{24,8},{32,48},{40,56},{48,32},{56,40},{64,80... | collective-permute-start | bytes 1572872 | tf_op jit(solution)/shard_map/ppermute | solution.py:18
  188.0 33.0 %collective-permute-start.26 = (bf16[2,2,2,1,1,1,64,512]{7,6,5,4,3,2,1,0:T(8,128)(2,1)S(1)}, bf16[2,2,2,1,1,1,64,512]{7,6,5,4,3,2,1,0:T(8,128)(2,1)}, u32[]{:S(2)}, u32[]{:S(2)}) collective-permute-start(bf16[2,2,2,1,1,1,64,512]{7,6,5,4,3,2,1,0:T(8,128)(2,1)S(1)} %pad_maximum_fusion.7), channel_id=1, source_target_pairs={{0,16},{8,24},{16,0},{24,8},{32,48},{40,56},{48,32},{56,40},{64,80... | collective-permute-start | bytes 1572872 | tf_op jit(solution)/shard_map/ppermute | solution.py:18
  206.3 16.9 %collective-permute-start.14 = (bf16[2,2,2,2,1,1,64,512]{7,6,5,4,3,2,1,0:T(8,128)(2,1)}, bf16[2,2,2,2,1,1,64,512]{7,6,5,4,3,2,1,0:T(8,128)(2,1)}, u32[]{:S(2)}, u32[]{:S(2)}) collective-permute-start(bf16[2,2,2,2,1,1,64,512]{7,6,5,4,3,2,1,0:T(8,128)(2,1)} %pad_maximum_fusion.4), channel_id=1, source_target_pairs={{0,8},{8,0},{16,24},{24,16},{32,40},{40,32},{48,56},{56,48},{64,72... | collective-permute-start | bytes 3145736 | tf_op jit(solution)/shard_map/ppermute | solution.py:18
  297.5 7.7 %collective-permute-start.33 = (f32[2,1,2,4,32,128]{5,4,3,2,1,0:T(8,128)S(1)}, f32[2,1,2,4,32,128]{5,4,3,2,1,0:T(8,128)S(1)}, u32[]{:S(2)}, u32[]{:S(2)}) collective-permute-start(f32[2,1,2,4,32,128]{5,4,3,2,1,0:T(8,128)S(1)} %constant_dynamic-slice_fusion.2), channel_id=1, source_target_pairs={{0,2},{1,3},{2,0},{3,1},{4,6},{5,7},{6,4},{7,5},{8,10},{9,11},{10,... | collective-permute-start | bytes 786440 | tf_op jit(solution)/shard_map/ppermute | solution.py:18
  (25 other events, 169.2 us)
Sparse Core Ops, SparseCore 0:
  128.2 126.8 all-gather.1
where the time goes:
time: 346 us; the launch traced here: 345 us
  waiting for transfers between devices  172 us (50%)
  starting transfers between devices  79.9 us (23%)
  Pallas kernels  30.1 us (9%)
  between operations  20.8 us (6%)
  local copies, waits for them, and re-layouts  19.6 us (6%)
  other arithmetic  19.6 us (6%)
    ppermute x34, waiting for transfers between devices, swap(): return lax.ppermute(value, axis, [(i, i ^ bit) for i in range(count)])  102 us
    ppermute x34, starting transfers between devices, swap(): return lax.ppermute(value, axis, [(i, i ^ bit) for i in range(count)])  46 us
    ppermute x5, waiting for transfers between devices, from_behind(): lax.ppermute(value, axis, [(i, (i + by) % count) for i in range(count)])  45.8 us
    ppermute x5, starting transfers between devices, from_behind(): lax.ppermute(value, axis, [(i, (i + by) % count) for i in range(count)])  33.8 us
    pallas_call x1, Pallas kernels, contract(): pl.pallas_call(functools.partial(contract_kernel, block), out_shape=jax.S...  30.1 us
    all_gather x1, waiting for transfers between devices, body(): moving_all = lax.all_gather(jnp.stack(moving), 'ga', axis=3, tiled=True)  24.9 us
    all_gather x1, local copies, waits for them, and re-layouts, body(): moving_all = lax.all_gather(jnp.stack(moving), 'ga', axis=3, tiled=True)  8.3 us
  transfers between devices with their start and end apart: 40, of which 27 were waited for; matrix products, arithmetic and copies ran while one was open for 7% of the time, Pallas kernels for 0%

commit v1 on v0

--- a/solution.py
+++ b/solution.py
@@ -38,7 +38,9 @@
             got = [got] * len(roots)
         else:
             sends = [pick_half(h, axis_at, 1 - mine) for h in held]
-            got = swap(sends, axis, 1 << bit)
+            stacked = jax.tree.map(lambda *xs: jnp.stack(xs), *sends)
+            stacked = swap(stacked, axis, 1 << bit)
+            got = [jax.tree.map(lambda x: x[r], stacked) for r in range(len(roots))]
         new_held = []
         for r, root in enumerate(roots):
             holder = ((me ^ root) & (full & ~done_mask)) == 0
@@ -52,12 +54,12 @@
     return held
 
 
-def gather_all(pieces, axis, order):
+def gather_all(pieces, axis, order, lead=0):
     nbits = len(order)
     me = lax.axis_index(axis)
     held = pieces
     for bit in order:
-        axis_at = nbits - 1 - bit
+        axis_at = lead + nbits - 1 - bit
         mine = (me >> bit) & 1
         got = swap(held, axis, 1 << bit)
 
@@ -86,25 +88,23 @@
 def contract_kernel(block, q_ref, perm_ref, mov_ref, out_ref, acc_ref):
     slots = perm_ref.shape[1]
     rows = out_ref.shape[1]
-    count = rows // block
     acc_ref[...] = jnp.zeros_like(acc_ref)
 
     def one_slot(s, carry):
-        start = pl.multiple_of((count - q_ref[s]) * block, block)
-        rolled = mov_ref[0, pl.ds(start, rows), :]
-        acc_ref[...] += lax.dot_general(
-            rolled, perm_ref[0, s], (((1,), (1,)), ((), ())),
+        start = pl.multiple_of(q_ref[s] * block, block)
+        acc_ref[pl.ds(start, rows), :] += lax.dot_general(
+            mov_ref[0], perm_ref[0, s], (((1,), (1,)), ((), ())),
             preferred_element_type=jnp.float32,
         )
         return carry
 
     lax.fori_loop(0, slots, one_slot, 0)
-    out_ref[0] = acc_ref[...].astype(out_ref.dtype)
-
-
-def contract(q_slots, permuted, doubled, block):
+    out_ref[0] = (acc_ref[:rows, :] + acc_ref[rows:, :]).astype(out_ref.dtype)
+
+
+def contract(q_slots, permuted, moving, block):
     steps, slots, local, waves = permuted.shape
-    rows = doubled.shape[1] // 2
+    rows = moving.shape[1]
     return pl.pallas_call(
         functools.partial(contract_kernel, block),
         out_shape=jax.ShapeDtypeStruct((steps, rows, local), jnp.bfloat16),
@@ -113,17 +113,17 @@
             grid=(steps,),
             in_specs=[
                 pl.BlockSpec((1, slots, local, waves), lambda i, q: (i, 0, 0, 0)),
-                pl.BlockSpec((1, 2 * rows, waves), lambda i, q: (i, 0, 0)),
+                pl.BlockSpec((1, rows, waves), lambda i, q: (i, 0, 0)),
             ],
             out_specs=pl.BlockSpec((1, rows, local), lambda i, q: (i, 0, 0)),
-            scratch_shapes=[pltpu.VMEM((rows, local), jnp.float32)],
+            scratch_shapes=[pltpu.VMEM((2 * rows, local), jnp.float32)],
         ),
         cost_estimate=pl.CostEstimate(
             flops=2 * steps * slots * rows * local * waves,
-            bytes_accessed=2 * steps * (slots * local * waves + 2 * rows * waves + rows * local),
+            bytes_accessed=2 * steps * (slots * local * waves + rows * waves + rows * local),
             transcendentals=0,
         ),
-    )(q_slots, permuted, doubled)
+    )(q_slots, permuted, moving)
 
 
 def body(offsets, q_slots, forms, vectors, energies, screened, umklapp):
@@ -162,7 +162,7 @@
         permuted_pieces.append(
             moved_cols.reshape((1,) * ka_bits + (per_piece, local_waves, plane_waves))
         )
-    gathered = gather_all(permuted_pieces, "ka", list(range(ka_bits))[::-1])
+    gathered = gather_all(jnp.stack(permuted_pieces), "ka", list(range(ka_bits))[::-1], lead=1)
 
     moving = [projected] * step_count
     for level in range(ka_bits):
@@ -173,12 +173,9 @@
         ]
     moving_all = lax.all_gather(jnp.stack(moving), "ga", axis=3, tiled=True)
 
-    permuted_all = jnp.stack(
-        [gathered[i].reshape(slot_count, local_waves, plane_waves) for i in range(step_count)]
-    )
+    permuted_all = gathered.reshape(step_count, slot_count, local_waves, plane_waves)
     moving_rows = moving_all.reshape(step_count, kpoint_count * vector_count, plane_waves)
-    doubled = jnp.concatenate([moving_rows, moving_rows], axis=1)
-    kernel_part = contract(q_slots, permuted_all, doubled, vector_count)
+    kernel_part = contract(q_slots, permuted_all, moving_rows, vector_count)
     kernel_part = kernel_part.reshape(step_count, kpoint_count, vector_count, local_waves)
     kernel_cat = jnp.concatenate([kernel_part[i] for i in range(step_count)], axis=1)
     action = lax.dot_general(

time: 346 us -> 396 us (1.14)
  waiting for transfers between devices: 172 us -> 237 us
  starting transfers between devices: 79.9 us -> 63.9 us
    all_gather x1, waiting for transfers between devices: 24.9 us -> 96.2 us  [body(): moving_all = lax.all_gather(jnp.stack(moving), 'ga', axis=3, tiled=True)]
    ppermute x34 -> x21, waiting for transfers between devices: 102 us -> 84.4 us  [swap(): return lax.ppermute(value, axis, [(i, i ^ bit) for i in range(count)])]
    ppermute x5, starting transfers between devices: 33.8 us -> 22.9 us  [from_behind(): lax.ppermute(value, axis, [(i, (i + by) % count) for i in range(count)])]
    ppermute x5, waiting for transfers between devices: 45.8 us -> 56.5 us  [from_behind(): lax.ppermute(value, axis, [(i, (i + by) % count) for i in range(count)])]
    ppermute x34 -> x21, starting transfers between devices: 46 us -> 40.9 us  [swap(): return lax.ppermute(value, axis, [(i, i ^ bit) for i in range(count)])]
  transfers between devices with their start and end apart: 40 -> 27, of which waited for: 27 -> 21; matrix products, arithmetic and copies ran while one was open for 7% -> 7% of each run, Pallas kernels for 0% -> 0%
where the time goes in v1:
time: 396 us; the launch traced here: 395 us
  waiting for transfers between devices  237 us (60%)
  starting transfers between devices  63.9 us (16%)
  Pallas kernels  30.4 us (8%)
  between operations  21.5 us (5%)
  other arithmetic  20.4 us (5%)
  local copies, waits for them, and re-layouts  20.2 us (5%)
    all_gather x1, waiting for transfers between devices, body(): moving_all = lax.all_gather(jnp.stack(moving), 'ga', axis=3, tiled=True)  96.2 us
    ppermute x21, waiting for transfers between devices, swap(): return lax.ppermute(value, axis, [(i, i ^ bit) for i in range(count)])  84.4 us
    ppermute x5, waiting for transfers between devices, from_behind(): lax.ppermute(value, axis, [(i, (i + by) % count) for i in range(count)])  56.5 us
    ppermute x21, starting transfers between devices, swap(): return lax.ppermute(value, axis, [(i, i ^ bit) for i in range(count)])  40.9 us
    pallas_call x1, Pallas kernels, contract(): pl.pallas_call(functools.partial(contract_kernel, block), out_shape=jax.S...  30.4 us
    ppermute x5, starting transfers between devices, from_behind(): lax.ppermute(value, axis, [(i, (i + by) % count) for i in range(count)])  22.9 us
    all_gather x1, local copies, waits for them, and re-layouts, body(): moving_all = lax.all_gather(jnp.stack(moving), 'ga', axis=3, tiled=True)  9.35 us
  transfers between devices with their start and end apart: 27, of which 21 were waited for; matrix products, arithmetic and copies ran while one was open for 7% of the time, Pallas kernels for 0%

profile of v1, /device:TPU:32, one launch (start us, length us, event | category | flops | bytes accessed | tf_op | source)
XLA Modules:
  0.0 394.9 jit_solution(14451789810204912785)
XLA Ops:
  31.7 6.4 %collective-permute-start.9 = (s32[2,1,1,1,1,1,1,512]{7,6,5,4,3,2,1,0:T(1,128)S(1)}, s32[2,1,1,1,1,1,1,512]{7,6,5,4,3,2,1,0:T(1,128)S(1)}, u32[]{:S(2)}, u32[]{:S(2)}) collective-permute-start(s32[2,1,1,1,1,1,1,512]{7,6,5,4,3,2,1,0:T(1,128)S(1)} %pad_add_fusion.3), channel_id=1, source_target_pairs={{0,128},{8,136},{16,144},{24,152},{32,160},{40,168},{48,176},{56,1... | collective-permute-start | bytes 12296 | tf_op jit(solution)/shard_map/ppermute | solution.py:18
  38.1 11.1 %collective-permute-done.1 = bf16[2,2,2,2,1,1,1,64,512]{8,7,1,3,2,6,5,4,0:T(8,128)(2,1)} collective-permute-done((bf16[2,2,2,2,1,1,1,64,512]{8,7,1,3,2,6,5,4,0:T(8,128)(2,1)}, bf16[2,2,2,2,1,1,1,64,512]{8,7,1,3,2,6,5,4,0:T(8,128)(2,1)}, u32[]{:S(2)}, u32[]{:S(2)}) %collective-permute-start.1) | collective-permute-done | bytes 1048608 | tf_op jit(solution)/shard_map/ppermute | solution.py:18
  59.4 4.5 %collective-permute-done.2 = bf16[2,2,2,1,1,1,1,64,512]{8,7,1,2,6,5,4,3,0:T(8,128)(2,1)} collective-permute-done((bf16[2,2,2,1,1,1,1,64,512]{8,7,1,2,6,5,4,3,0:T(8,128)(2,1)}, bf16[2,2,2,1,1,1,1,64,512]{8,7,1,2,6,5,4,3,0:T(8,128)(2,1)}, u32[]{:S(2)}, u32[]{:S(2)}) %collective-permute-start.2) | collective-permute-done | bytes 524320 | tf_op jit(solution)/shard_map/ppermute | solution.py:18
  70.4 4.3 %collective-permute-start.16 = (bf16[2,32,32,64]{3,2,1,0:T(8,128)(2,1)S(1)}, bf16[2,32,32,64]{3,2,1,0:T(8,128)(2,1)S(1)}, u32[]{:S(2)}, u32[]{:S(2)}) collective-permute-start(bf16[2,32,32,64]{3,2,1,0:T(8,128)(2,1)S(1)} %pad_maximum_fusion.7), channel_id=1, source_target_pairs={{0,16},{8,24},{16,32},{24,40},{32,48},{40,56},{48,64},{56,72},{64,... | collective-permute-start | bytes 786440 | tf_op jit(solution)/shard_map/ppermute | solution.py:13
  77.6 4.7 %collective-permute-start.4 = (bf16[2,1,1,1,1,1,1,64,512]{8,7,6,5,4,3,2,1,0:T(8,128)(2,1)S(1)}, bf16[2,1,1,1,1,1,1,64,512]{8,7,6,5,4,3,2,1,0:T(8,128)(2,1)S(1)}, u32[]{:S(2)}, u32[]{:S(2)}) collective-permute-start(bf16[2,1,1,1,1,1,1,64,512]{8,7,6,5,4,3,2,1,0:T(8,128)(2,1)S(1)} %pad_maximum_fusion.16), channel_id=1, source_target_pairs={{0,128},{8,136},{16,144},{24,152},{32,160},{40,168},{48,176},{56,1... | collective-permute-start | bytes 393224 | tf_op jit(solution)/shard_map/ppermute | solution.py:18
  82.2 6.3 %collective-permute-done.16 = bf16[2,32,32,64]{3,2,1,0:T(8,128)(2,1)S(1)} collective-permute-done((bf16[2,32,32,64]{3,2,1,0:T(8,128)(2,1)S(1)}, bf16[2,32,32,64]{3,2,1,0:T(8,128)(2,1)S(1)}, u32[]{:S(2)}, u32[]{:S(2)}) %collective-permute-start.16) | collective-permute-done | bytes 262176 | tf_op jit(solution)/shard_map/ppermute | solution.py:13
  88.7 13.7 %collective-permute-start.17 = (bf16[2,32,32,64]{3,2,1,0:T(8,128)(2,1)S(1)}, bf16[2,32,32,64]{3,2,1,0:T(8,128)(2,1)S(1)}, u32[]{:S(2)}, u32[]{:S(2)}) collective-permute-start(bf16[2,32,32,64]{3,2,1,0:T(8,128)(2,1)S(1)} %pad_maximum_fusion.8), channel_id=1, source_target_pairs={{0,32},{8,40},{16,48},{24,56},{32,64},{40,72},{48,80},{56,88},{64,... | collective-permute-start | bytes 786440 | tf_op jit(solution)/shard_map/ppermute | solution.py:13
  103.5 21.9 %collective-permute-done.17 = bf16[2,32,32,64]{3,2,1,0:T(8,128)(2,1)S(1)} collective-permute-done((bf16[2,32,32,64]{3,2,1,0:T(8,128)(2,1)S(1)}, bf16[2,32,32,64]{3,2,1,0:T(8,128)(2,1)S(1)}, u32[]{:S(2)}, u32[]{:S(2)}) %collective-permute-start.17) | collective-permute-done | bytes 262176 | tf_op jit(solution)/shard_map/ppermute | solution.py:13
  125.8 24.0 %collective-permute-done.18 = bf16[2,32,32,64]{3,2,1,0:T(8,128)(2,1)S(1)} collective-permute-done((bf16[2,32,32,64]{3,2,1,0:T(8,128)(2,1)S(1)}, bf16[2,32,32,64]{3,2,1,0:T(8,128)(2,1)S(1)}, u32[]{:S(2)}, u32[]{:S(2)}) %collective-permute-start.18) | collective-permute-done | bytes 262176 | tf_op jit(solution)/shard_map/ppermute | solution.py:13
  150.1 4.7 %collective-permute-start.19 = (bf16[2,32,32,64]{3,2,1,0:T(8,128)(2,1)S(1)}, bf16[2,32,32,64]{3,2,1,0:T(8,128)(2,1)}, u32[]{:S(2)}, u32[]{:S(2)}) collective-permute-start(bf16[2,32,32,64]{3,2,1,0:T(8,128)(2,1)S(1)} %pad_maximum_fusion.10), channel_id=1, source_target_pairs={{0,128},{8,136},{16,144},{24,152},{32,160},{40,168},{48,176},{56,1... | collective-permute-start | bytes 786440 | tf_op jit(solution)/shard_map/ppermute | solution.py:13
  155.6 4.3 %collective-permute-start.12 = (bf16[2,2,2,1,1,1,1,64,512]{8,7,6,5,4,3,2,1,0:T(8,128)(2,1)S(1)}, bf16[2,2,2,1,1,1,1,64,512]{8,7,6,5,4,3,2,1,0:T(8,128)(2,1)S(1)}, u32[]{:S(2)}, u32[]{:S(2)}) collective-permute-start(bf16[2,2,2,1,1,1,1,64,512]{8,7,6,5,4,3,2,1,0:T(8,128)(2,1)S(1)} %pad_maximum_fusion.5), channel_id=1, source_target_pairs={{0,32},{8,40},{16,48},{24,56},{32,0},{40,8},{48,16},{56,24},{64,96... | collective-permute-start | bytes 1572872 | tf_op jit(solution)/shard_map/ppermute | solution.py:18
  161.2 3.6 collective-permute-done.19
  168.4 9.7 %collective-permute-done.12 = bf16[2,2,2,1,1,1,1,64,512]{8,7,6,5,4,3,2,1,0:T(8,128)(2,1)S(1)} collective-permute-done((bf16[2,2,2,1,1,1,1,64,512]{8,7,6,5,4,3,2,1,0:T(8,128)(2,1)S(1)}, bf16[2,2,2,1,1,1,1,64,512]{8,7,6,5,4,3,2,1,0:T(8,128)(2,1)S(1)}, u32[]{:S(2)}, u32[]{:S(2)}) %collective-permute-start.12) | collective-permute-done | bytes 524320 | tf_op jit(solution)/shard_map/ppermute | solution.py:18
  179.1 7.2 %collective-permute-start.13 = (bf16[2,2,2,2,1,1,1,64,512]{8,7,6,5,4,3,2,1,0:T(8,128)(2,1)S(1)}, bf16[2,2,2,2,1,1,1,64,512]{8,7,6,5,4,3,2,1,0:T(8,128)(2,1)}, u32[]{:S(2)}, u32[]{:S(2)}) collective-permute-start(bf16[2,2,2,2,1,1,1,64,512]{8,7,6,5,4,3,2,1,0:T(8,128)(2,1)S(1)} %pad_maximum_fusion.3), channel_id=1, source_target_pairs={{0,16},{8,24},{16,0},{24,8},{32,48},{40,56},{48,32},{56,40},{64,80... | collective-permute-start | bytes 3145736 | tf_op jit(solution)/shard_map/ppermute | solution.py:18
  186.3 16.8 %collective-permute-done.13 = bf16[2,2,2,2,1,1,1,64,512]{8,7,6,5,4,3,2,1,0:T(8,128)(2,1)} collective-permute-done((bf16[2,2,2,2,1,1,1,64,512]{8,7,6,5,4,3,2,1,0:T(8,128)(2,1)S(1)}, bf16[2,2,2,2,1,1,1,64,512]{8,7,6,5,4,3,2,1,0:T(8,128)(2,1)}, u32[]{:S(2)}, u32[]{:S(2)}) %collective-permute-start.13) | collective-permute-done | bytes 1048608 | tf_op jit(solution)/shard_map/ppermute | solution.py:18
  206.1 96.2 %all-gather.2.cloned.1.call-done = bf16[2,32,32,512]{2,1,0,3:T(8,128)(2,1)} async-done(((bf16[2,32,32,64]{2,1,0,3:T(8,128)(2,1)}), bf16[2,32,32,512]{2,1,0,3:T(8,128)(2,1)}) %all-gather.2.cloned.1.call-update) | async-done | bytes 2097168 | tf_op jit(solution)/shard_map/all_gather | solution.py:174
  302.3 9.3 %copy.60 = bf16[2,32,32,512]{3,2,1,0:T(8,128)(2,1)} copy(bf16[2,32,32,512]{2,1,0,3:T(8,128)(2,1)} %all-gather.2.cloned.1.call-done) | data formatting | bytes 4194304 | tf_op jit(solution)/shard_map/all_gather | solution.py:174
  315.8 30.4 %shard_map.73 = bf16[2,1024,64]{2,1,0:T(8,128)(2,1)} custom-call(s32[32]{0:T(128)} %q_ref.1, bf16[2,32,64,512]{3,2,1,0:T(8,128)(2,1)} %bitcast.226, bf16[2,1024,512]{2,1,0:T(8,128)(2,1)} %bitcast.233), custom_call_target="tpu_custom_call" | custom-call | flops 4294967296 | bytes 6553600 | tf_op jit(solution)/shard_map/pallas_call | solution.py:108
  348.2 7.3 %collective-permute-done.20 = f32[2,1,2,4,32,128]{5,4,3,2,1,0:T(8,128)S(1)} collective-permute-done((f32[2,1,2,4,32,128]{5,4,3,2,1,0:T(8,128)S(1)}, f32[2,1,2,4,32,128]{5,4,3,2,1,0:T(8,128)S(1)}, u32[]{:S(2)}, u32[]{:S(2)}) %collective-permute-start.20) | collective-permute-done | bytes 262176 | tf_op jit(solution)/shard_map/ppermute | solution.py:18
  356.2 5.9 %collective-permute-done.21 = f32[2,1,1,4,32,128]{5,4,3,2,1,0:T(8,128)S(1)} collective-permute-done((f32[2,1,1,4,32,128]{5,4,3,2,1,0:T(8,128)S(1)}, f32[2,1,1,4,32,128]{5,4,3,2,1,0:T(8,128)S(1)}, u32[]{:S(2)}, u32[]{:S(2)}) %collective-permute-start.21) | collective-permute-done | bytes 131104 | tf_op jit(solution)/shard_map/ppermute | solution.py:18
  363.8 4.3 %collective-permute-done.22 = f32[1,1,1,4,32,128]{5,4,3,2,1,0:T(8,128)S(1)} collective-permute-done((f32[1,1,1,4,32,128]{5,4,3,2,1,0:T(8,128)S(1)}, f32[1,1,1,4,32,128]{5,4,3,2,1,0:T(8,128)S(1)}, u32[]{:S(2)}, u32[]{:S(2)}) %collective-permute-start.22) | collective-permute-done | bytes 65568 | tf_op jit(solution)/shard_map/ppermute | solution.py:18
  369.6 4.3 %collective-permute-done.23 = f32[1,1,1,4,32,128]{5,4,3,2,1,0:T(8,128)S(1)} collective-permute-done((f32[1,1,1,4,32,128]{5,4,3,2,1,0:T(8,128)S(1)}, f32[1,1,1,4,32,128]{5,4,3,2,1,0:T(8,128)S(1)}, u32[]{:S(2)}, u32[]{:S(2)}) %collective-permute-start.23) | collective-permute-done | bytes 65568 | tf_op jit(solution)/shard_map/ppermute | solution.py:18
  374.6 5.9 %collective-permute-done.24 = f32[2,1,1,4,32,128]{5,4,3,2,1,0:T(8,128)S(1)} collective-permute-done((f32[2,1,1,4,32,128]{5,4,3,2,1,0:T(8,128)S(1)}, f32[2,1,1,4,32,128]{5,4,3,2,1,0:T(8,128)S(1)}, u32[]{:S(2)}, u32[]{:S(2)}) %collective-permute-start.24) | collective-permute-done | bytes 131104 | tf_op jit(solution)/shard_map/ppermute | solution.py:18
  381.0 6.1 %collective-permute-done.25 = f32[2,1,2,4,32,128]{5,4,3,2,1,0:T(8,128)S(1)} collective-permute-done((f32[2,1,2,4,32,128]{5,4,3,2,1,0:T(8,128)S(1)}, f32[2,1,2,4,32,128]{5,4,3,2,1,0:T(8,128)S(1)}, u32[]{:S(2)}, u32[]{:S(2)}) %collective-permute-start.25) | collective-permute-done | bytes 262176 | tf_op jit(solution)/shard_map/ppermute | solution.py:18
  (136 shorter events, 60.4 us)
Async XLA Ops:
  6.5 295.8 %all-gather.2.cloned.1.call-start = ((), (), s32[]{:S(2)}) async-start(), calls=%async_computation | async-start | bytes 9437184 | tf_op jit(solution)/shard_map/all_gather | solution.py:174
  7.5 5.5 %collective-permute-start.5 = (s32[2,2,2,2,1,1,512]{6,4,3,2,1,0,5:T(1,128)S(1)}, s32[2,2,2,2,1,1,512]{6,4,3,2,1,0,5:T(1,128)S(1)}, u32[]{:S(2)}, u32[]{:S(2)}) collective-permute-start(s32[2,2,2,2,1,1,512]{6,4,3,2,1,0,5:T(1,128)S(1)} %constant_dynamic-slice_fusion.15), channel_id=1, source_target_pairs={{0,8},{8,0},{16,24},{24,16},{32,40},{40,32},{48,56},{56,48},{64,72... | collective-permute-start | bytes 98312 | tf_op jit(solution)/shard_map/ppermute | solution.py:18
  15.9 5.2 %collective-permute-start = (bf16[2,2,2,2,1,1,64,512]{7,6,4,3,2,1,0,5:T(8,128)(2,1)}, bf16[2,2,2,2,1,1,64,512]{7,6,4,3,2,1,0,5:T(8,128)(2,1)}, u32[]{:S(2)}, u32[]{:S(2)}) collective-permute-start(bf16[2,2,2,2,1,1,64,512]{7,6,4,3,2,1,0,5:T(8,128)(2,1)} %constant_dynamic-slice_fusion.18), channel_id=1, source_target_pairs={{0,8},{8,0},{16,24},{24,16},{32,40},{40,32},{48,56},{56,48},{64,72... | collective-permute-start | bytes 3145736 | tf_op jit(solution)/shard_map/ppermute | solution.py:18
  25.5 23.7 %collective-permute-start.1 = (bf16[2,2,2,2,1,1,1,64,512]{8,7,1,3,2,6,5,4,0:T(8,128)(2,1)}, bf16[2,2,2,2,1,1,1,64,512]{8,7,1,3,2,6,5,4,0:T(8,128)(2,1)}, u32[]{:S(2)}, u32[]{:S(2)}) collective-permute-start(bf16[2,2,2,2,1,1,1,64,512]{8,7,1,3,2,6,5,4,0:T(8,128)(2,1)} %pad_maximum_fusion.2), channel_id=1, source_target_pairs={{0,16},{8,24},{16,0},{24,8},{32,48},{40,56},{48,32},{56,40},{64,80... | collective-permute-start | bytes 3145736 | tf_op jit(solution)/shard_map/ppermute | solution.py:18
  31.7 27.6 %collective-permute-start.9 = (s32[2,1,1,1,1,1,1,512]{7,6,5,4,3,2,1,0:T(1,128)S(1)}, s32[2,1,1,1,1,1,1,512]{7,6,5,4,3,2,1,0:T(1,128)S(1)}, u32[]{:S(2)}, u32[]{:S(2)}) collective-permute-start(s32[2,1,1,1,1,1,1,512]{7,6,5,4,3,2,1,0:T(1,128)S(1)} %pad_add_fusion.3), channel_id=1, source_target_pairs={{0,128},{8,136},{16,144},{24,152},{32,160},{40,168},{48,176},{56,1... | collective-permute-start | bytes 12296 | tf_op jit(solution)/shard_map/ppermute | solution.py:18
  52.4 11.5 %collective-permute-start.2 = (bf16[2,2,2,1,1,1,1,64,512]{8,7,1,2,6,5,4,3,0:T(8,128)(2,1)}, bf16[2,2,2,1,1,1,1,64,512]{8,7,1,2,6,5,4,3,0:T(8,128)(2,1)}, u32[]{:S(2)}, u32[]{:S(2)}) collective-permute-start(bf16[2,2,2,1,1,1,1,64,512]{8,7,1,2,6,5,4,3,0:T(8,128)(2,1)} %pad_maximum_fusion.4), channel_id=1, source_target_pairs={{0,32},{8,40},{16,48},{24,56},{32,0},{40,8},{48,16},{56,24},{64,96... | collective-permute-start | bytes 1572872 | tf_op jit(solution)/shard_map/ppermute | solution.py:18
  54.2 16.0 %collective-permute-start.15 = (bf16[2,32,32,64]{3,2,1,0:T(8,128)(2,1)S(1)}, bf16[2,32,32,64]{3,2,1,0:T(8,128)(2,1)S(1)}, u32[]{:S(2)}, u32[]{:S(2)}) collective-permute-start(bf16[2,32,32,64]{3,2,1,0:T(8,128)(2,1)S(1)} %pad_maximum_fusion.6), channel_id=1, source_target_pairs={{0,8},{8,16},{16,24},{24,32},{32,40},{40,48},{48,56},{56,64},{64,7... | collective-permute-start | bytes 786440 | tf_op jit(solution)/shard_map/ppermute | solution.py:13
  66.0 11.5 %collective-permute-start.3 = (bf16[2,2,1,1,1,1,1,64,512]{8,7,1,6,5,4,3,2,0:T(8,128)(2,1)S(1)}, bf16[2,2,1,1,1,1,1,64,512]{8,7,1,6,5,4,3,2,0:T(8,128)(2,1)S(1)}, u32[]{:S(2)}, u32[]{:S(2)}) collective-permute-start(bf16[2,2,1,1,1,1,1,64,512]{8,7,1,6,5,4,3,2,0:T(8,128)(2,1)S(1)} %pad_maximum_fusion.13), channel_id=1, source_target_pairs={{0,64},{8,72},{16,80},{24,88},{32,96},{40,104},{48,112},{56,120},{... | collective-permute-start | bytes 786440 | tf_op jit(solution)/shard_map/ppermute | solution.py:18
  70.4 18.1 %collective-permute-start.16 = (bf16[2,32,32,64]{3,2,1,0:T(8,128)(2,1)S(1)}, bf16[2,32,32,64]{3,2,1,0:T(8,128)(2,1)S(1)}, u32[]{:S(2)}, u32[]{:S(2)}) collective-permute-start(bf16[2,32,32,64]{3,2,1,0:T(8,128)(2,1)S(1)} %pad_maximum_fusion.7), channel_id=1, source_target_pairs={{0,16},{8,24},{16,32},{24,40},{32,48},{40,56},{48,64},{56,72},{64,... | collective-permute-start | bytes 786440 | tf_op jit(solution)/shard_map/ppermute | solution.py:13
  77.6 24.9 %collective-permute-start.4 = (bf16[2,1,1,1,1,1,1,64,512]{8,7,6,5,4,3,2,1,0:T(8,128)(2,1)S(1)}, bf16[2,1,1,1,1,1,1,64,512]{8,7,6,5,4,3,2,1,0:T(8,128)(2,1)S(1)}, u32[]{:S(2)}, u32[]{:S(2)}) collective-permute-start(bf16[2,1,1,1,1,1,1,64,512]{8,7,6,5,4,3,2,1,0:T(8,128)(2,1)S(1)} %pad_maximum_fusion.16), channel_id=1, source_target_pairs={{0,128},{8,136},{16,144},{24,152},{32,160},{40,168},{48,176},{56,1... | collective-permute-start | bytes 393224 | tf_op jit(solution)/shard_map/ppermute | solution.py:18
  88.7 36.7 %collective-permute-start.17 = (bf16[2,32,32,64]{3,2,1,0:T(8,128)(2,1)S(1)}, bf16[2,32,32,64]{3,2,1,0:T(8,128)(2,1)S(1)}, u32[]{:S(2)}, u32[]{:S(2)}) collective-permute-start(bf16[2,32,32,64]{3,2,1,0:T(8,128)(2,1)S(1)} %pad_maximum_fusion.8), channel_id=1, source_target_pairs={{0,32},{8,40},{16,48},{24,56},{32,64},{40,72},{48,80},{56,88},{64,... | collective-permute-start | bytes 786440 | tf_op jit(solution)/shard_map/ppermute | solution.py:13
  103.2 22.4 %collective-permute-start.10 = (bf16[2,1,1,1,1,1,1,64,512]{8,7,6,5,4,3,2,1,0:T(8,128)(2,1)S(1)}, bf16[2,1,1,1,1,1,1,64,512]{8,7,6,5,4,3,2,1,0:T(8,128)(2,1)S(1)}, u32[]{:S(2)}, u32[]{:S(2)}) collective-permute-start(bf16[2,1,1,1,1,1,1,64,512]{8,7,6,5,4,3,2,1,0:T(8,128)(2,1)S(1)} %pad_maximum_fusion.17), channel_id=1, source_target_pairs={{0,128},{8,136},{16,144},{24,152},{32,160},{40,168},{48,176},{56,1... | collective-permute-start | bytes 393224 | tf_op jit(solution)/shard_map/ppermute | solution.py:18
  125.6 24.3 %collective-permute-start.18 = (bf16[2,32,32,64]{3,2,1,0:T(8,128)(2,1)S(1)}, bf16[2,32,32,64]{3,2,1,0:T(8,128)(2,1)S(1)}, u32[]{:S(2)}, u32[]{:S(2)}) collective-permute-start(bf16[2,32,32,64]{3,2,1,0:T(8,128)(2,1)S(1)} %pad_maximum_fusion.9), channel_id=1, source_target_pairs={{0,64},{8,72},{16,80},{24,88},{32,96},{40,104},{48,112},{56,120},{... | collective-permute-start | bytes 786440 | tf_op jit(solution)/shard_map/ppermute | solution.py:13
  125.7 29.8 %collective-permute-start.11 = (bf16[2,2,1,1,1,1,1,64,512]{8,7,6,5,4,3,2,1,0:T(8,128)(2,1)S(1)}, bf16[2,2,1,1,1,1,1,64,512]{8,7,6,5,4,3,2,1,0:T(8,128)(2,1)S(1)}, u32[]{:S(2)}, u32[]{:S(2)}) collective-permute-start(bf16[2,2,1,1,1,1,1,64,512]{8,7,6,5,4,3,2,1,0:T(8,128)(2,1)S(1)} %pad_maximum_fusion.14), channel_id=1, source_target_pairs={{0,64},{8,72},{16,80},{24,88},{32,96},{40,104},{48,112},{56,120},{... | collective-permute-start | bytes 786440 | tf_op jit(solution)/shard_map/ppermute | solution.py:18
  150.1 14.6 %collective-permute-start.19 = (bf16[2,32,32,64]{3,2,1,0:T(8,128)(2,1)S(1)}, bf16[2,32,32,64]{3,2,1,0:T(8,128)(2,1)}, u32[]{:S(2)}, u32[]{:S(2)}) collective-permute-start(bf16[2,32,32,64]{3,2,1,0:T(8,128)(2,1)S(1)} %pad_maximum_fusion.10), channel_id=1, source_target_pairs={{0,128},{8,136},{16,144},{24,152},{32,160},{40,168},{48,176},{56,1... | collective-permute-start | bytes 786440 | tf_op jit(solution)/shard_map/ppermute | solution.py:13
  155.6 22.5 %collective-permute-start.12 = (bf16[2,2,2,1,1,1,1,64,512]{8,7,6,5,4,3,2,1,0:T(8,128)(2,1)S(1)}, bf16[2,2,2,1,1,1,1,64,512]{8,7,6,5,4,3,2,1,0:T(8,128)(2,1)S(1)}, u32[]{:S(2)}, u32[]{:S(2)}) collective-permute-start(bf16[2,2,2,1,1,1,1,64,512]{8,7,6,5,4,3,2,1,0:T(8,128)(2,1)S(1)} %pad_maximum_fusion.5), channel_id=1, source_target_pairs={{0,32},{8,40},{16,48},{24,56},{32,0},{40,8},{48,16},{56,24},{64,96... | collective-permute-start | bytes 1572872 | tf_op jit(solution)/shard_map/ppermute | solution.py:18
  179.1 24.0 %collective-permute-start.13 = (bf16[2,2,2,2,1,1,1,64,512]{8,7,6,5,4,3,2,1,0:T(8,128)(2,1)S(1)}, bf16[2,2,2,2,1,1,1,64,512]{8,7,6,5,4,3,2,1,0:T(8,128)(2,1)}, u32[]{:S(2)}, u32[]{:S(2)}) collective-permute-start(bf16[2,2,2,2,1,1,1,64,512]{8,7,6,5,4,3,2,1,0:T(8,128)(2,1)S(1)} %pad_maximum_fusion.3), channel_id=1, source_target_pairs={{0,16},{8,24},{16,0},{24,8},{32,48},{40,56},{48,32},{56,40},{64,80... | collective-permute-start | bytes 3145736 | tf_op jit(solution)/shard_map/ppermute | solution.py:18
  206.1 105.6 %collective-permute-start.14 = (bf16[2,2,2,2,2,1,1,64,512]{8,7,6,5,4,3,2,1,0:T(8,128)(2,1)}, bf16[2,2,2,2,2,1,1,64,512]{8,7,6,5,4,3,2,1,0:T(8,128)(2,1)}, u32[]{:S(2)}, u32[]{:S(2)}) collective-permute-start(bf16[2,2,2,2,2,1,1,64,512]{8,7,6,5,4,3,2,1,0:T(8,128)(2,1)} %pad_maximum_fusion.1), channel_id=1, source_target_pairs={{0,8},{8,0},{16,24},{24,16},{32,40},{40,32},{48,56},{56,48},{64,72... | collective-permute-start | bytes 6291464 | tf_op jit(solution)/shard_map/ppermute | solution.py:18
  347.8 7.7 %collective-permute-start.20 = (f32[2,1,2,4,32,128]{5,4,3,2,1,0:T(8,128)S(1)}, f32[2,1,2,4,32,128]{5,4,3,2,1,0:T(8,128)S(1)}, u32[]{:S(2)}, u32[]{:S(2)}) collective-permute-start(f32[2,1,2,4,32,128]{5,4,3,2,1,0:T(8,128)S(1)} %constant_dynamic-slice_fusion.2), channel_id=1, source_target_pairs={{0,2},{1,3},{2,0},{3,1},{4,6},{5,7},{6,4},{7,5},{8,10},{9,11},{10,... | collective-permute-start | bytes 786440 | tf_op jit(solution)/shard_map/ppermute | solution.py:18
  355.6 6.6 %collective-permute-start.21 = (f32[2,1,1,4,32,128]{5,4,3,2,1,0:T(8,128)S(1)}, f32[2,1,1,4,32,128]{5,4,3,2,1,0:T(8,128)S(1)}, u32[]{:S(2)}, u32[]{:S(2)}) collective-permute-start(f32[2,1,1,4,32,128]{5,4,3,2,1,0:T(8,128)S(1)} %constant_dynamic-slice_fusion.1), channel_id=1, source_target_pairs={{0,1},{1,0},{2,3},{3,2},{4,5},{5,4},{6,7},{7,6},{8,9},{9,8},{10,11... | collective-permute-start | bytes 393224 | tf_op jit(solution)/shard_map/ppermute | solution.py:18
  362.2 5.9 %collective-permute-start.22 = (f32[1,1,1,4,32,128]{5,4,3,2,1,0:T(8,128)S(1)}, f32[1,1,1,4,32,128]{5,4,3,2,1,0:T(8,128)S(1)}, u32[]{:S(2)}, u32[]{:S(2)}) collective-permute-start(f32[1,1,1,4,32,128]{5,4,3,2,1,0:T(8,128)S(1)} %constant_dynamic-slice_fusion), channel_id=1, source_target_pairs={{0,4},{1,5},{2,6},{3,7},{4,0},{5,1},{6,2},{7,3},{8,12},{9,13},{10,... | collective-permute-start | bytes 196616 | tf_op jit(solution)/shard_map/ppermute | solution.py:18
  368.1 5.9 %collective-permute-start.23 = (f32[1,1,1,4,32,128]{5,4,3,2,1,0:T(8,128)S(1)}, f32[1,1,1,4,32,128]{5,4,3,2,1,0:T(8,128)S(1)}, u32[]{:S(2)}, u32[]{:S(2)}) collective-permute-start(f32[1,1,1,4,32,128]{5,4,3,2,1,0:T(8,128)S(1)} %dynamic-slice_add_fusion.2), channel_id=1, source_target_pairs={{0,4},{1,5},{2,6},{3,7},{4,0},{5,1},{6,2},{7,3},{8,12},{9,13},{10,... | collective-permute-start | bytes 196616 | tf_op jit(solution)/shard_map/ppermute | solution.py:18
  373.9 6.6 %collective-permute-start.24 = (f32[2,1,1,4,32,128]{5,4,3,2,1,0:T(8,128)S(1)}, f32[2,1,1,4,32,128]{5,4,3,2,1,0:T(8,128)S(1)}, u32[]{:S(2)}, u32[]{:S(2)}) collective-permute-start(f32[2,1,1,4,32,128]{5,4,3,2,1,0:T(8,128)S(1)} %pad_maximum_fusion.18), channel_id=1, source_target_pairs={{0,1},{1,0},{2,3},{3,2},{4,5},{5,4},{6,7},{7,6},{8,9},{9,8},{10,11... | collective-permute-start | bytes 393224 | tf_op jit(solution)/shard_map/ppermute | solution.py:18
  380.6 6.5 %collective-permute-start.25 = (f32[2,1,2,4,32,128]{5,4,3,2,1,0:T(8,128)S(1)}, f32[2,1,2,4,32,128]{5,4,3,2,1,0:T(8,128)S(1)}, u32[]{:S(2)}, u32[]{:S(2)}) collective-permute-start(f32[2,1,2,4,32,128]{5,4,3,2,1,0:T(8,128)S(1)} %pad_maximum_fusion.15), channel_id=1, source_target_pairs={{0,2},{1,3},{2,0},{3,1},{4,6},{5,7},{6,4},{7,5},{8,10},{9,11},{10,... | collective-permute-start | bytes 786440 | tf_op jit(solution)/shard_map/ppermute | solution.py:18
  (10 other events, 117.2 us)
Sparse Core Ops, SparseCore 0:
  168.5 133.7 all-gather.1

commit v2 on v1

--- a/solution.py
+++ b/solution.py
@@ -85,42 +85,35 @@
     return gather_all(held, axis, order[::-1])
 
 
-def contract_kernel(block, q_ref, perm_ref, mov_ref, out_ref, acc_ref):
+def contract_kernel(block, q_ref, perm_ref, mov_ref, out_ref):
     slots = perm_ref.shape[1]
-    rows = out_ref.shape[1]
-    acc_ref[...] = jnp.zeros_like(acc_ref)
-
-    def one_slot(s, carry):
-        start = pl.multiple_of(q_ref[s] * block, block)
-        acc_ref[pl.ds(start, rows), :] += lax.dot_general(
-            mov_ref[0], perm_ref[0, s], (((1,), (1,)), ((), ())),
-            preferred_element_type=jnp.float32,
-        )
-        return carry
-
-    lax.fori_loop(0, slots, one_slot, 0)
-    out_ref[0] = (acc_ref[:rows, :] + acc_ref[rows:, :]).astype(out_ref.dtype)
+
+    def one_slot(s, acc):
+        product = jnp.dot(perm_ref[0, s], mov_ref[0], preferred_element_type=jnp.float32)
+        return acc + pltpu.roll(product, q_ref[s] * block, 1)
+
+    acc = lax.fori_loop(0, slots, one_slot, jnp.zeros(out_ref.shape[1:], jnp.float32))
+    out_ref[0] = acc.astype(out_ref.dtype)
 
 
 def contract(q_slots, permuted, moving, block):
     steps, slots, local, waves = permuted.shape
-    rows = moving.shape[1]
+    cols = moving.shape[2]
     return pl.pallas_call(
         functools.partial(contract_kernel, block),
-        out_shape=jax.ShapeDtypeStruct((steps, rows, local), jnp.bfloat16),
+        out_shape=jax.ShapeDtypeStruct((steps, local, cols), jnp.bfloat16),
         grid_spec=pltpu.PrefetchScalarGridSpec(
             num_scalar_prefetch=1,
             grid=(steps,),
             in_specs=[
                 pl.BlockSpec((1, slots, local, waves), lambda i, q: (i, 0, 0, 0)),
-                pl.BlockSpec((1, rows, waves), lambda i, q: (i, 0, 0)),
+                pl.BlockSpec((1, waves, cols), lambda i, q: (i, 0, 0)),
             ],
-            out_specs=pl.BlockSpec((1, rows, local), lambda i, q: (i, 0, 0)),
-            scratch_shapes=[pltpu.VMEM((2 * rows, local), jnp.float32)],
+            out_specs=pl.BlockSpec((1, local, cols), lambda i, q: (i, 0, 0)),
         ),
         cost_estimate=pl.CostEstimate(
-            flops=2 * steps * slots * rows * local * waves,
-            bytes_accessed=2 * steps * (slots * local * waves + rows * waves + rows * local),
+            flops=2 * steps * slots * cols * local * waves,
+            bytes_accessed=2 * steps * (slots * local * waves + cols * waves + cols * local),
             transcendentals=0,
         ),
     )(q_slots, permuted, moving)
@@ -171,18 +164,24 @@
             jnp.where(roots[i] >> level & 1 == 1, hopped[i], moving[i])
             for i in range(step_count)
         ]
-    moving_all = lax.all_gather(jnp.stack(moving), "ga", axis=3, tiled=True)
+    moving = jnp.stack(moving).reshape(step_count, kpoint_count * vector_count, local_waves)
+    moving = jnp.transpose(moving, (0, 2, 1)).reshape(
+        (step_count,) + (1,) * ga_bits + (local_waves, kpoint_count * vector_count)
+    )
+    ga_order = [0, 2, 1] if ga_bits == 3 else list(range(ga_bits))
+    moving_all = gather_all(moving, "ga", ga_order, lead=1).reshape(
+        step_count, plane_waves, kpoint_count * vector_count
+    )
 
     permuted_all = gathered.reshape(step_count, slot_count, local_waves, plane_waves)
-    moving_rows = moving_all.reshape(step_count, kpoint_count * vector_count, plane_waves)
-    kernel_part = contract(q_slots, permuted_all, moving_rows, vector_count)
-    kernel_part = kernel_part.reshape(step_count, kpoint_count, vector_count, local_waves)
-    kernel_cat = jnp.concatenate([kernel_part[i] for i in range(step_count)], axis=1)
+    kernel_part = contract(q_slots, permuted_all, moving_all, vector_count)
+    kernel_part = kernel_part.reshape(step_count, local_waves, kpoint_count, vector_count)
+    kernel_cat = jnp.concatenate([kernel_part[i] for i in range(step_count)], axis=2)
     action = lax.dot_general(
-        kernel_cat, forms, (((2,), (2,)), ((0,), (0,))), preferred_element_type=jnp.float32
+        kernel_cat, forms, (((0,), (2,)), ((1,), (0,))), preferred_element_type=jnp.float32
     )
     action = action.reshape(kpoint_count, step_count, vector_count, pair_count).sum(axis=1)
-    ga_order = [1, 0, 2][:ga_bits] if ga_bits == 3 else list(range(ga_bits))
+    ga_order = [1, 0, 2] if ga_bits == 3 else list(range(ga_bits))
     action = action.reshape((2,) * ga_bits + (kpoint_count // ga_size, vector_count, pair_count))
     action = sum_all(action, "ga", ga_order).reshape(kpoint_count, vector_count, pair_count)
     return energies[:, None, :] * vectors.astype(jnp.float32) - action

time: 396 us -> 312 us (0.79)
  the two profiles are of different devices: /device:TPU:32 before, /device:TPU:96 now
where the time goes in v2:
time: 312 us; the launch traced here: 311 us
  waiting for transfers between devices  196 us (63%)
  starting transfers between devices  39.5 us (13%)
  Pallas kernels  29.5 us (9%)
  other arithmetic  29 us (9%)
  local copies, waits for them, and re-layouts  8.14 us (3%)
  between operations  7.81 us (3%)
    ppermute x24, waiting for transfers between devices, swap(): return lax.ppermute(value, axis, [(i, i ^ bit) for i in range(count)])  166 us
    ppermute x24, starting transfers between devices, swap(): return lax.ppermute(value, axis, [(i, i ^ bit) for i in range(count)])  33.1 us
    ppermute x5, waiting for transfers between devices, from_behind(): lax.ppermute(value, axis, [(i, (i + by) % count) for i in range(count)])  30.2 us
    pallas_call x1, Pallas kernels, contract(): pl.pallas_call(functools.partial(contract_kernel, block), out_shape=jax.S...  29.5 us
    concatenate x11, other arithmetic, join(): return jnp.concatenate([low, high], axis=axis_at)  9.5 us
    ppermute x5, starting transfers between devices, from_behind(): lax.ppermute(value, axis, [(i, (i + by) % count) for i in range(count)])  6.47 us
  transfers between devices with their start and end apart: 29, of which 21 were waited for; matrix products, arithmetic and copies ran while one was open for 10% of the time, Pallas kernels for 0%

profile of v2, /device:TPU:96, one launch (start us, length us, event | category | flops | bytes accessed | tf_op | source)
XLA Modules:
  0.0 311.4 jit_solution(17163111271985442175)
XLA Ops:
  22.3 23.5 %collective-permute-done.1 = bf16[2,2,2,2,1,1,1,64,512]{8,7,1,3,2,6,5,4,0:T(8,128)(2,1)} collective-permute-done((bf16[2,2,2,2,1,1,1,64,512]{8,7,1,3,2,6,5,4,0:T(8,128)(2,1)}, bf16[2,2,2,2,1,1,1,64,512]{8,7,1,3,2,6,5,4,0:T(8,128)(2,1)}, u32[]{:S(2)}, u32[]{:S(2)}) %collective-permute-start.1) | collective-permute-done | bytes 1048608 | tf_op jit(solution)/shard_map/ppermute | solution.py:18
  50.0 4.6 %collective-permute-start.9 = (s32[2,1,1,1,1,1,1,512]{7,6,5,4,3,2,1,0:T(1,128)S(1)}, s32[2,1,1,1,1,1,1,512]{7,6,5,4,3,2,1,0:T(1,128)S(1)}, u32[]{:S(2)}, u32[]{:S(2)}) collective-permute-start(s32[2,1,1,1,1,1,1,512]{7,6,5,4,3,2,1,0:T(1,128)S(1)} %pad_add_fusion.3), channel_id=1, source_target_pairs={{0,128},{8,136},{16,144},{24,152},{32,160},{40,168},{48,176},{56,1... | collective-permute-start | bytes 12296 | tf_op jit(solution)/shard_map/ppermute | solution.py:18
  54.6 5.4 %collective-permute-done.2 = bf16[2,2,2,1,1,1,1,64,512]{8,7,1,2,6,5,4,3,0:T(8,128)(2,1)S(1)} collective-permute-done((bf16[2,2,2,1,1,1,1,64,512]{8,7,1,2,6,5,4,3,0:T(8,128)(2,1)S(1)}, bf16[2,2,2,1,1,1,1,64,512]{8,7,1,2,6,5,4,3,0:T(8,128)(2,1)S(1)}, u32[]{:S(2)}, u32[]{:S(2)}) %collective-permute-start.2) | collective-permute-done | bytes 524320 | tf_op jit(solution)/shard_map/ppermute | solution.py:18
  64.2 7.8 %collective-permute-done.3 = bf16[2,2,1,1,1,1,1,64,512]{8,7,1,6,5,4,3,2,0:T(8,128)(2,1)S(1)} collective-permute-done((bf16[2,2,1,1,1,1,1,64,512]{8,7,1,6,5,4,3,2,0:T(8,128)(2,1)S(1)}, bf16[2,2,1,1,1,1,1,64,512]{8,7,1,6,5,4,3,2,0:T(8,128)(2,1)S(1)}, u32[]{:S(2)}, u32[]{:S(2)}) %collective-permute-start.3) | collective-permute-done | bytes 262176 | tf_op jit(solution)/shard_map/ppermute | solution.py:18
  72.1 5.0 %collective-permute-start.4 = (bf16[2,1,1,1,1,1,1,64,512]{8,7,6,5,4,3,2,1,0:T(8,128)(2,1)S(1)}, bf16[2,1,1,1,1,1,1,64,512]{8,7,6,5,4,3,2,1,0:T(8,128)(2,1)S(1)}, u32[]{:S(2)}, u32[]{:S(2)}) collective-permute-start(bf16[2,1,1,1,1,1,1,64,512]{8,7,6,5,4,3,2,1,0:T(8,128)(2,1)S(1)} %pad_maximum_fusion.18), channel_id=1, source_target_pairs={{0,128},{8,136},{16,144},{24,152},{32,160},{40,168},{48,176},{56,1... | collective-permute-start | bytes 393224 | tf_op jit(solution)/shard_map/ppermute | solution.py:18
  77.3 5.8 %collective-permute-done.4 = bf16[2,1,1,1,1,1,1,64,512]{8,7,6,5,4,3,2,1,0:T(8,128)(2,1)S(1)} collective-permute-done((bf16[2,1,1,1,1,1,1,64,512]{8,7,6,5,4,3,2,1,0:T(8,128)(2,1)S(1)}, bf16[2,1,1,1,1,1,1,64,512]{8,7,6,5,4,3,2,1,0:T(8,128)(2,1)S(1)}, u32[]{:S(2)}, u32[]{:S(2)}) %collective-permute-start.4) | collective-permute-done | bytes 131104 | tf_op jit(solution)/shard_map/ppermute | solution.py:18
  83.9 3.3 %collective-permute-start.10 = (bf16[2,1,1,1,1,1,1,64,512]{8,7,6,5,4,3,2,1,0:T(8,128)(2,1)S(1)}, bf16[2,1,1,1,1,1,1,64,512]{8,7,6,5,4,3,2,1,0:T(8,128)(2,1)S(1)}, u32[]{:S(2)}, u32[]{:S(2)}) collective-permute-start(bf16[2,1,1,1,1,1,1,64,512]{8,7,6,5,4,3,2,1,0:T(8,128)(2,1)S(1)} %pad_maximum_fusion.19), channel_id=1, source_target_pairs={{0,128},{8,136},{16,144},{24,152},{32,160},{40,168},{48,176},{56,1... | collective-permute-start | bytes 393224 | tf_op jit(solution)/shard_map/ppermute | solution.py:18
  87.2 7.3 %collective-permute-done.16 = bf16[2,32,32,64]{3,2,1,0:T(8,128)(2,1)S(1)} collective-permute-done((bf16[2,32,32,64]{3,2,1,0:T(8,128)(2,1)S(1)}, bf16[2,32,32,64]{3,2,1,0:T(8,128)(2,1)S(1)}, u32[]{:S(2)}, u32[]{:S(2)}) %collective-permute-start.16) | collective-permute-done | bytes 262176 | tf_op jit(solution)/shard_map/ppermute | solution.py:13
  98.9 9.4 %collective-permute-done.17 = bf16[2,32,32,64]{3,2,1,0:T(8,128)(2,1)S(1)} collective-permute-done((bf16[2,32,32,64]{3,2,1,0:T(8,128)(2,1)S(1)}, bf16[2,32,32,64]{3,2,1,0:T(8,128)(2,1)S(1)}, u32[]{:S(2)}, u32[]{:S(2)}) %collective-permute-start.17) | collective-permute-done | bytes 262176 | tf_op jit(solution)/shard_map/ppermute | solution.py:13
  109.2 3.6 %collective-permute-start.18 = (bf16[2,32,32,64]{3,2,1,0:T(8,128)(2,1)}, bf16[2,32,32,64]{3,2,1,0:T(8,128)(2,1)}, u32[]{:S(2)}, u32[]{:S(2)}) collective-permute-start(bf16[2,32,32,64]{3,2,1,0:T(8,128)(2,1)} %pad_maximum_fusion.11), channel_id=1, source_target_pairs={{0,64},{8,72},{16,80},{24,88},{32,96},{40,104},{48,112},{56,120},{... | collective-permute-start | bytes 786440 | tf_op jit(solution)/shard_map/ppermute | solution.py:13
  112.8 15.7 %collective-permute-done.11 = bf16[2,2,1,1,1,1,1,64,512]{8,7,6,5,4,3,2,1,0:T(8,128)(2,1)S(1)} collective-permute-done((bf16[2,2,1,1,1,1,1,64,512]{8,7,6,5,4,3,2,1,0:T(8,128)(2,1)S(1)}, bf16[2,2,1,1,1,1,1,64,512]{8,7,6,5,4,3,2,1,0:T(8,128)(2,1)S(1)}, u32[]{:S(2)}, u32[]{:S(2)}) %collective-permute-start.11) | collective-permute-done | bytes 262176 | tf_op jit(solution)/shard_map/ppermute | solution.py:18
  130.6 13.5 %collective-permute-done.18 = bf16[2,32,32,64]{3,2,1,0:T(8,128)(2,1)} collective-permute-done((bf16[2,32,32,64]{3,2,1,0:T(8,128)(2,1)}, bf16[2,32,32,64]{3,2,1,0:T(8,128)(2,1)}, u32[]{:S(2)}, u32[]{:S(2)}) %collective-permute-start.18) | collective-permute-done | bytes 262176 | tf_op jit(solution)/shard_map/ppermute | solution.py:13
  146.2 23.0 %collective-permute-done.12 = bf16[2,2,2,1,1,1,1,64,512]{8,7,6,5,4,3,2,1,0:T(8,128)(2,1)S(1)} collective-permute-done((bf16[2,2,2,1,1,1,1,64,512]{8,7,6,5,4,3,2,1,0:T(8,128)(2,1)}, bf16[2,2,2,1,1,1,1,64,512]{8,7,6,5,4,3,2,1,0:T(8,128)(2,1)S(1)}, u32[]{:S(2)}, u32[]{:S(2)}) %collective-permute-start.12) | collective-permute-done | bytes 524320 | tf_op jit(solution)/shard_map/ppermute | solution.py:18
  174.6 22.7 %collective-permute-done.20 = bf16[2,1,1,1,64,1024]{5,4,3,2,1,0:T(8,128)(2,1)S(1)} collective-permute-done((bf16[2,1,1,1,64,1024]{5,4,3,2,1,0:T(8,128)(2,1)S(1)}, bf16[2,1,1,1,64,1024]{5,4,3,2,1,0:T(8,128)(2,1)S(1)}, u32[]{:S(2)}, u32[]{:S(2)}) %collective-permute-start.20) | collective-permute-done | bytes 262176 | tf_op jit(solution)/shard_map/ppermute | solution.py:18
  198.3 3.0 collective-permute-start.21
  204.2 5.1 %collective-permute-done.21 = bf16[2,1,1,2,64,1024]{5,4,3,2,1,0:T(8,128)(2,1)} collective-permute-done((bf16[2,1,1,2,64,1024]{5,4,3,2,1,0:T(8,128)(2,1)}, bf16[2,1,1,2,64,1024]{5,4,3,2,1,0:T(8,128)(2,1)}, u32[]{:S(2)}, u32[]{:S(2)}) %collective-permute-start.21) | collective-permute-done | bytes 524320 | tf_op jit(solution)/shard_map/ppermute | solution.py:18
  213.8 19.3 %collective-permute-done.22 = bf16[2,2,1,2,64,1024]{5,4,3,2,1,0:T(8,128)(2,1)} collective-permute-done((bf16[2,2,1,2,64,1024]{5,4,3,2,1,0:T(8,128)(2,1)}, bf16[2,2,1,2,64,1024]{5,4,3,2,1,0:T(8,128)(2,1)}, u32[]{:S(2)}, u32[]{:S(2)}) %collective-permute-start.22) | collective-permute-done | bytes 1048608 | tf_op jit(solution)/shard_map/ppermute | solution.py:18
  240.4 29.5 %shard_map.73 = bf16[2,64,1024]{2,1,0:T(8,128)(2,1)} custom-call(s32[32]{0:T(128)} %q_ref.1, bf16[2,32,64,512]{3,2,1,0:T(8,128)(2,1)} %bitcast.228, bf16[2,512,1024]{2,1,0:T(8,128)(2,1)} %bitcast.235), custom_call_target="tpu_custom_call" | custom-call | flops 4294967296 | bytes 6553600 | tf_op jit(solution)/shard_map/pallas_call | solution.py:102
  272.4 5.8 %collective-permute-done.23 = f32[2,1,2,4,32,128]{5,4,3,2,1,0:T(8,128)S(1)} collective-permute-done((f32[2,1,2,4,32,128]{5,4,3,2,1,0:T(8,128)S(1)}, f32[2,1,2,4,32,128]{5,4,3,2,1,0:T(8,128)S(1)}, u32[]{:S(2)}, u32[]{:S(2)}) %collective-permute-start.23) | collective-permute-done | bytes 262176 | tf_op jit(solution)/shard_map/ppermute | solution.py:18
  278.7 6.1 %collective-permute-done.24 = f32[2,1,1,4,32,128]{5,4,3,2,1,0:T(8,128)S(1)} collective-permute-done((f32[2,1,1,4,32,128]{5,4,3,2,1,0:T(8,128)S(1)}, f32[2,1,1,4,32,128]{5,4,3,2,1,0:T(8,128)S(1)}, u32[]{:S(2)}, u32[]{:S(2)}) %collective-permute-start.24) | collective-permute-done | bytes 131104 | tf_op jit(solution)/shard_map/ppermute | solution.py:18
  286.7 4.0 %collective-permute-done.25 = f32[1,1,1,4,32,128]{5,4,3,2,1,0:T(8,128)S(1)} collective-permute-done((f32[1,1,1,4,32,128]{5,4,3,2,1,0:T(8,128)S(1)}, f32[1,1,1,4,32,128]{5,4,3,2,1,0:T(8,128)S(1)}, u32[]{:S(2)}, u32[]{:S(2)}) %collective-permute-start.25) | collective-permute-done | bytes 65568 | tf_op jit(solution)/shard_map/ppermute | solution.py:18
  292.6 4.8 %collective-permute-done.26 = f32[1,1,1,4,32,128]{5,4,3,2,1,0:T(8,128)S(1)} collective-permute-done((f32[1,1,1,4,32,128]{5,4,3,2,1,0:T(8,128)S(1)}, f32[1,1,1,4,32,128]{5,4,3,2,1,0:T(8,128)S(1)}, u32[]{:S(2)}, u32[]{:S(2)}) %collective-permute-start.26) | collective-permute-done | bytes 65568 | tf_op jit(solution)/shard_map/ppermute | solution.py:18
  297.8 6.1 %collective-permute-done.27 = f32[2,1,1,4,32,128]{5,4,3,2,1,0:T(8,128)S(1)} collective-permute-done((f32[2,1,1,4,32,128]{5,4,3,2,1,0:T(8,128)S(1)}, f32[2,1,1,4,32,128]{5,4,3,2,1,0:T(8,128)S(1)}, u32[]{:S(2)}, u32[]{:S(2)}) %collective-permute-start.27) | collective-permute-done | bytes 131104 | tf_op jit(solution)/shard_map/ppermute | solution.py:18
  304.7 5.8 %collective-permute-done.28 = f32[2,1,2,4,32,128]{5,4,3,2,1,0:T(8,128)S(1)} collective-permute-done((f32[2,1,2,4,32,128]{5,4,3,2,1,0:T(8,128)S(1)}, f32[2,1,2,4,32,128]{5,4,3,2,1,0:T(8,128)S(1)}, u32[]{:S(2)}, u32[]{:S(2)}) %collective-permute-start.28) | collective-permute-done | bytes 262176 | tf_op jit(solution)/shard_map/ppermute | solution.py:18
  (155 shorter events, 63.5 us)
Async XLA Ops:
  5.0 6.7 %collective-permute-start = (bf16[2,2,2,2,1,1,64,512]{7,6,4,3,2,1,0,5:T(8,128)(2,1)}, bf16[2,2,2,2,1,1,64,512]{7,6,4,3,2,1,0,5:T(8,128)(2,1)}, u32[]{:S(2)}, u32[]{:S(2)}) collective-permute-start(bf16[2,2,2,2,1,1,64,512]{7,6,4,3,2,1,0,5:T(8,128)(2,1)} %constant_dynamic-slice_fusion.18), channel_id=1, source_target_pairs={{0,8},{8,0},{16,24},{24,16},{32,40},{40,32},{48,56},{56,48},{64,72... | collective-permute-start | bytes 3145736 | tf_op jit(solution)/shard_map/ppermute | solution.py:18
  16.0 29.8 %collective-permute-start.1 = (bf16[2,2,2,2,1,1,1,64,512]{8,7,1,3,2,6,5,4,0:T(8,128)(2,1)}, bf16[2,2,2,2,1,1,1,64,512]{8,7,1,3,2,6,5,4,0:T(8,128)(2,1)}, u32[]{:S(2)}, u32[]{:S(2)}) collective-permute-start(bf16[2,2,2,2,1,1,1,64,512]{8,7,1,3,2,6,5,4,0:T(8,128)(2,1)} %pad_maximum_fusion.3), channel_id=1, source_target_pairs={{0,16},{8,24},{16,0},{24,8},{32,48},{40,56},{48,32},{56,40},{64,80... | collective-permute-start | bytes 3145736 | tf_op jit(solution)/shard_map/ppermute | solution.py:18
  18.6 58.4 %collective-permute-start.15 = (bf16[2,32,32,64]{3,2,1,0:T(8,128)(2,1)}, bf16[2,32,32,64]{3,2,1,0:T(8,128)(2,1)S(1)}, u32[]{:S(2)}, u32[]{:S(2)}) collective-permute-start(bf16[2,32,32,64]{3,2,1,0:T(8,128)(2,1)} %pad_maximum_fusion.8), channel_id=1, source_target_pairs={{0,8},{8,16},{16,24},{24,32},{32,40},{40,48},{48,56},{56,64},{64,7... | collective-permute-start | bytes 786440 | tf_op jit(solution)/shard_map/ppermute | solution.py:13
  48.2 11.9 %collective-permute-start.2 = (bf16[2,2,2,1,1,1,1,64,512]{8,7,1,2,6,5,4,3,0:T(8,128)(2,1)S(1)}, bf16[2,2,2,1,1,1,1,64,512]{8,7,1,2,6,5,4,3,0:T(8,128)(2,1)S(1)}, u32[]{:S(2)}, u32[]{:S(2)}) collective-permute-start(bf16[2,2,2,1,1,1,1,64,512]{8,7,1,2,6,5,4,3,0:T(8,128)(2,1)S(1)} %pad_maximum_fusion.6), channel_id=1, source_target_pairs={{0,32},{8,40},{16,48},{24,56},{32,0},{40,8},{48,16},{56,24},{64,96... | collective-permute-start | bytes 1572872 | tf_op jit(solution)/shard_map/ppermute | solution.py:18
  50.0 14.2 %collective-permute-start.9 = (s32[2,1,1,1,1,1,1,512]{7,6,5,4,3,2,1,0:T(1,128)S(1)}, s32[2,1,1,1,1,1,1,512]{7,6,5,4,3,2,1,0:T(1,128)S(1)}, u32[]{:S(2)}, u32[]{:S(2)}) collective-permute-start(s32[2,1,1,1,1,1,1,512]{7,6,5,4,3,2,1,0:T(1,128)S(1)} %pad_add_fusion.3), channel_id=1, source_target_pairs={{0,128},{8,136},{16,144},{24,152},{32,160},{40,168},{48,176},{56,1... | collective-permute-start | bytes 12296 | tf_op jit(solution)/shard_map/ppermute | solution.py:18
  60.2 11.8 %collective-permute-start.3 = (bf16[2,2,1,1,1,1,1,64,512]{8,7,1,6,5,4,3,2,0:T(8,128)(2,1)S(1)}, bf16[2,2,1,1,1,1,1,64,512]{8,7,1,6,5,4,3,2,0:T(8,128)(2,1)S(1)}, u32[]{:S(2)}, u32[]{:S(2)}) collective-permute-start(bf16[2,2,1,1,1,1,1,64,512]{8,7,1,6,5,4,3,2,0:T(8,128)(2,1)S(1)} %pad_maximum_fusion.15), channel_id=1, source_target_pairs={{0,64},{8,72},{16,80},{24,88},{32,96},{40,104},{48,112},{56,120},{... | collective-permute-start | bytes 786440 | tf_op jit(solution)/shard_map/ppermute | solution.py:18
  72.1 11.0 %collective-permute-start.4 = (bf16[2,1,1,1,1,1,1,64,512]{8,7,6,5,4,3,2,1,0:T(8,128)(2,1)S(1)}, bf16[2,1,1,1,1,1,1,64,512]{8,7,6,5,4,3,2,1,0:T(8,128)(2,1)S(1)}, u32[]{:S(2)}, u32[]{:S(2)}) collective-permute-start(bf16[2,1,1,1,1,1,1,64,512]{8,7,6,5,4,3,2,1,0:T(8,128)(2,1)S(1)} %pad_maximum_fusion.18), channel_id=1, source_target_pairs={{0,128},{8,136},{16,144},{24,152},{32,160},{40,168},{48,176},{56,1... | collective-permute-start | bytes 393224 | tf_op jit(solution)/shard_map/ppermute | solution.py:18
  77.3 17.3 %collective-permute-start.16 = (bf16[2,32,32,64]{3,2,1,0:T(8,128)(2,1)S(1)}, bf16[2,32,32,64]{3,2,1,0:T(8,128)(2,1)S(1)}, u32[]{:S(2)}, u32[]{:S(2)}) collective-permute-start(bf16[2,32,32,64]{3,2,1,0:T(8,128)(2,1)S(1)} %pad_maximum_fusion.9), channel_id=1, source_target_pairs={{0,16},{8,24},{16,32},{24,40},{32,48},{40,56},{48,64},{56,72},{64,... | collective-permute-start | bytes 786440 | tf_op jit(solution)/shard_map/ppermute | solution.py:13
  83.9 13.6 %collective-permute-start.10 = (bf16[2,1,1,1,1,1,1,64,512]{8,7,6,5,4,3,2,1,0:T(8,128)(2,1)S(1)}, bf16[2,1,1,1,1,1,1,64,512]{8,7,6,5,4,3,2,1,0:T(8,128)(2,1)S(1)}, u32[]{:S(2)}, u32[]{:S(2)}) collective-permute-start(bf16[2,1,1,1,1,1,1,64,512]{8,7,6,5,4,3,2,1,0:T(8,128)(2,1)S(1)} %pad_maximum_fusion.19), channel_id=1, source_target_pairs={{0,128},{8,136},{16,144},{24,152},{32,160},{40,168},{48,176},{56,1... | collective-permute-start | bytes 393224 | tf_op jit(solution)/shard_map/ppermute | solution.py:18
  94.7 13.5 %collective-permute-start.17 = (bf16[2,32,32,64]{3,2,1,0:T(8,128)(2,1)S(1)}, bf16[2,32,32,64]{3,2,1,0:T(8,128)(2,1)S(1)}, u32[]{:S(2)}, u32[]{:S(2)}) collective-permute-start(bf16[2,32,32,64]{3,2,1,0:T(8,128)(2,1)S(1)} %pad_maximum_fusion.10), channel_id=1, source_target_pairs={{0,32},{8,40},{16,48},{24,56},{32,64},{40,72},{48,80},{56,88},{64,... | collective-permute-start | bytes 786440 | tf_op jit(solution)/shard_map/ppermute | solution.py:13
  97.6 31.0 %collective-permute-start.11 = (bf16[2,2,1,1,1,1,1,64,512]{8,7,6,5,4,3,2,1,0:T(8,128)(2,1)S(1)}, bf16[2,2,1,1,1,1,1,64,512]{8,7,6,5,4,3,2,1,0:T(8,128)(2,1)S(1)}, u32[]{:S(2)}, u32[]{:S(2)}) collective-permute-start(bf16[2,2,1,1,1,1,1,64,512]{8,7,6,5,4,3,2,1,0:T(8,128)(2,1)S(1)} %pad_maximum_fusion.16), channel_id=1, source_target_pairs={{0,64},{8,72},{16,80},{24,88},{32,96},{40,104},{48,112},{56,120},{... | collective-permute-start | bytes 786440 | tf_op jit(solution)/shard_map/ppermute | solution.py:18
  109.2 34.9 %collective-permute-start.18 = (bf16[2,32,32,64]{3,2,1,0:T(8,128)(2,1)}, bf16[2,32,32,64]{3,2,1,0:T(8,128)(2,1)}, u32[]{:S(2)}, u32[]{:S(2)}) collective-permute-start(bf16[2,32,32,64]{3,2,1,0:T(8,128)(2,1)} %pad_maximum_fusion.11), channel_id=1, source_target_pairs={{0,64},{8,72},{16,80},{24,88},{32,96},{40,104},{48,112},{56,120},{... | collective-permute-start | bytes 786440 | tf_op jit(solution)/shard_map/ppermute | solution.py:13
  129.4 39.7 %collective-permute-start.12 = (bf16[2,2,2,1,1,1,1,64,512]{8,7,6,5,4,3,2,1,0:T(8,128)(2,1)}, bf16[2,2,2,1,1,1,1,64,512]{8,7,6,5,4,3,2,1,0:T(8,128)(2,1)S(1)}, u32[]{:S(2)}, u32[]{:S(2)}) collective-permute-start(bf16[2,2,2,1,1,1,1,64,512]{8,7,6,5,4,3,2,1,0:T(8,128)(2,1)} %pad_maximum_fusion.7), channel_id=1, source_target_pairs={{0,32},{8,40},{16,48},{24,56},{32,0},{40,8},{48,16},{56,24},{64,96... | collective-permute-start | bytes 1572872 | tf_op jit(solution)/shard_map/ppermute | solution.py:18
  146.2 25.4 %collective-permute-start.19 = (bf16[2,32,32,64]{3,2,1,0:T(8,128)(2,1)}, bf16[2,32,32,64]{3,2,1,0:T(8,128)(2,1)}, u32[]{:S(2)}, u32[]{:S(2)}) collective-permute-start(bf16[2,32,32,64]{3,2,1,0:T(8,128)(2,1)} %pad_maximum_fusion.12), channel_id=1, source_target_pairs={{0,128},{8,136},{16,144},{24,152},{32,160},{40,168},{48,176},{56,1... | collective-permute-start | bytes 786440 | tf_op jit(solution)/shard_map/ppermute | solution.py:13
  170.4 30.9 %collective-permute-start.13 = (bf16[2,2,2,2,1,1,1,64,512]{8,7,6,5,4,3,2,1,0:T(8,128)(2,1)}, bf16[2,2,2,2,1,1,1,64,512]{8,7,6,5,4,3,2,1,0:T(8,128)(2,1)}, u32[]{:S(2)}, u32[]{:S(2)}) collective-permute-start(bf16[2,2,2,2,1,1,1,64,512]{8,7,6,5,4,3,2,1,0:T(8,128)(2,1)} %pad_maximum_fusion.4), channel_id=1, source_target_pairs={{0,16},{8,24},{16,0},{24,8},{32,48},{40,56},{48,32},{56,40},{64,80... | collective-permute-start | bytes 3145736 | tf_op jit(solution)/shard_map/ppermute | solution.py:18
  173.0 24.3 %collective-permute-start.20 = (bf16[2,1,1,1,64,1024]{5,4,3,2,1,0:T(8,128)(2,1)S(1)}, bf16[2,1,1,1,64,1024]{5,4,3,2,1,0:T(8,128)(2,1)S(1)}, u32[]{:S(2)}, u32[]{:S(2)}) collective-permute-start(bf16[2,1,1,1,64,1024]{5,4,3,2,1,0:T(8,128)(2,1)S(1)} %maximum_bitcast_fusion), channel_id=1, source_target_pairs={{0,1},{1,0},{2,3},{3,2},{4,5},{5,4},{6,7},{7,6},{8,9},{9,8},{10,11... | collective-permute-start | bytes 786440 | tf_op jit(solution)/shard_map/ppermute | solution.py:18
  198.3 11.0 %collective-permute-start.21 = (bf16[2,1,1,2,64,1024]{5,4,3,2,1,0:T(8,128)(2,1)}, bf16[2,1,1,2,64,1024]{5,4,3,2,1,0:T(8,128)(2,1)}, u32[]{:S(2)}, u32[]{:S(2)}) collective-permute-start(bf16[2,1,1,2,64,1024]{5,4,3,2,1,0:T(8,128)(2,1)} %pad_maximum_fusion.13), channel_id=1, source_target_pairs={{0,4},{1,5},{2,6},{3,7},{4,0},{5,1},{6,2},{7,3},{8,12},{9,13},{10,... | collective-permute-start | bytes 1572872 | tf_op jit(solution)/shard_map/ppermute | solution.py:18
  204.2 32.0 %collective-permute-start.14 = (bf16[2,2,2,2,2,1,1,64,512]{8,7,6,5,4,3,2,1,0:T(8,128)(2,1)}, bf16[2,2,2,2,2,1,1,64,512]{8,7,6,5,4,3,2,1,0:T(8,128)(2,1)}, u32[]{:S(2)}, u32[]{:S(2)}) collective-permute-start(bf16[2,2,2,2,2,1,1,64,512]{8,7,6,5,4,3,2,1,0:T(8,128)(2,1)} %pad_maximum_fusion.1), channel_id=1, source_target_pairs={{0,8},{8,0},{16,24},{24,16},{32,40},{40,32},{48,56},{56,48},{64,72... | collective-permute-start | bytes 6291464 | tf_op jit(solution)/shard_map/ppermute | solution.py:18
  212.3 20.8 %collective-permute-start.22 = (bf16[2,2,1,2,64,1024]{5,4,3,2,1,0:T(8,128)(2,1)}, bf16[2,2,1,2,64,1024]{5,4,3,2,1,0:T(8,128)(2,1)}, u32[]{:S(2)}, u32[]{:S(2)}) collective-permute-start(bf16[2,2,1,2,64,1024]{5,4,3,2,1,0:T(8,128)(2,1)} %pad_maximum_fusion.5), channel_id=1, source_target_pairs={{0,2},{1,3},{2,0},{3,1},{4,6},{5,7},{6,4},{7,5},{8,10},{9,11},{10,... | collective-permute-start | bytes 3145736 | tf_op jit(solution)/shard_map/ppermute | solution.py:18
  271.7 6.5 %collective-permute-start.23 = (f32[2,1,2,4,32,128]{5,4,3,2,1,0:T(8,128)S(1)}, f32[2,1,2,4,32,128]{5,4,3,2,1,0:T(8,128)S(1)}, u32[]{:S(2)}, u32[]{:S(2)}) collective-permute-start(f32[2,1,2,4,32,128]{5,4,3,2,1,0:T(8,128)S(1)} %constant_dynamic-slice_fusion.2), channel_id=1, source_target_pairs={{0,2},{1,3},{2,0},{3,1},{4,6},{5,7},{6,4},{7,5},{8,10},{9,11},{10,... | collective-permute-start | bytes 786440 | tf_op jit(solution)/shard_map/ppermute | solution.py:18
  278.2 6.6 %collective-permute-start.24 = (f32[2,1,1,4,32,128]{5,4,3,2,1,0:T(8,128)S(1)}, f32[2,1,1,4,32,128]{5,4,3,2,1,0:T(8,128)S(1)}, u32[]{:S(2)}, u32[]{:S(2)}) collective-permute-start(f32[2,1,1,4,32,128]{5,4,3,2,1,0:T(8,128)S(1)} %constant_dynamic-slice_fusion.1), channel_id=1, source_target_pairs={{0,1},{1,0},{2,3},{3,2},{4,5},{5,4},{6,7},{7,6},{8,9},{9,8},{10,11... | collective-permute-start | bytes 393224 | tf_op jit(solution)/shard_map/ppermute | solution.py:18
  290.7 6.6 %collective-permute-start.26 = (f32[1,1,1,4,32,128]{5,4,3,2,1,0:T(8,128)S(1)}, f32[1,1,1,4,32,128]{5,4,3,2,1,0:T(8,128)S(1)}, u32[]{:S(2)}, u32[]{:S(2)}) collective-permute-start(f32[1,1,1,4,32,128]{5,4,3,2,1,0:T(8,128)S(1)} %dynamic-slice_add_fusion.2), channel_id=1, source_target_pairs={{0,4},{1,5},{2,6},{3,7},{4,0},{5,1},{6,2},{7,3},{8,12},{9,13},{10,... | collective-permute-start | bytes 196616 | tf_op jit(solution)/shard_map/ppermute | solution.py:18
  297.4 6.6 %collective-permute-start.27 = (f32[2,1,1,4,32,128]{5,4,3,2,1,0:T(8,128)S(1)}, f32[2,1,1,4,32,128]{5,4,3,2,1,0:T(8,128)S(1)}, u32[]{:S(2)}, u32[]{:S(2)}) collective-permute-start(f32[2,1,1,4,32,128]{5,4,3,2,1,0:T(8,128)S(1)} %pad_maximum_fusion.20), channel_id=1, source_target_pairs={{0,1},{1,0},{2,3},{3,2},{4,5},{5,4},{6,7},{7,6},{8,9},{9,8},{10,11... | collective-permute-start | bytes 393224 | tf_op jit(solution)/shard_map/ppermute | solution.py:18
  304.0 6.5 %collective-permute-start.28 = (f32[2,1,2,4,32,128]{5,4,3,2,1,0:T(8,128)S(1)}, f32[2,1,2,4,32,128]{5,4,3,2,1,0:T(8,128)S(1)}, u32[]{:S(2)}, u32[]{:S(2)}) collective-permute-start(f32[2,1,2,4,32,128]{5,4,3,2,1,0:T(8,128)S(1)} %pad_maximum_fusion.17), channel_id=1, source_target_pairs={{0,2},{1,3},{2,0},{3,1},{4,6},{5,7},{6,4},{7,5},{8,10},{9,11},{10,... | collective-permute-start | bytes 786440 | tf_op jit(solution)/shard_map/ppermute | solution.py:18
  (16 other events, 161.9 us)

commit v3 on v2

--- a/solution.py
+++ b/solution.py
@@ -72,27 +72,34 @@
     return held
 
 
-def sum_all(value, axis, order):
-    nbits = len(order)
+def sum_all(value, axis):
+    count = lax.axis_size(axis)
     me = lax.axis_index(axis)
-    held = value
-    for bit in order:
-        axis_at = nbits - 1 - bit
-        mine = (me >> bit) & 1
-        sends = lax.dynamic_slice_in_dim(held, 1 - mine, 1, axis=axis_at)
-        keep = lax.dynamic_slice_in_dim(held, mine, 1, axis=axis_at)
-        held = keep + swap(sends, axis, 1 << bit)
-    return gather_all(held, axis, order[::-1])
-
-
-def contract_kernel(block, q_ref, perm_ref, mov_ref, out_ref):
-    slots = perm_ref.shape[1]
-
-    def one_slot(s, acc):
-        product = jnp.dot(perm_ref[0, s], mov_ref[0], preferred_element_type=jnp.float32)
-        return acc + pltpu.roll(product, q_ref[s] * block, 1)
-
-    acc = lax.fori_loop(0, slots, one_slot, jnp.zeros(out_ref.shape[1:], jnp.float32))
+    total = lax.dynamic_index_in_dim(value, me, 0, keepdims=False)
+    for mask in range(1, count):
+        sent = lax.dynamic_index_in_dim(value, me ^ mask, 0, keepdims=False)
+        total = total + swap(sent, axis, mask)
+    result = jnp.zeros_like(value)
+    result = lax.dynamic_update_index_in_dim(result, total, me, 0)
+    for mask in range(1, count):
+        got = swap(total, axis, mask)
+        result = lax.dynamic_update_index_in_dim(result, got, me ^ mask, 0)
+    return result
+
+
+def contract_kernel(block, group, q_ref, perm_ref, mov_ref, out_ref):
+    slots, local, waves = perm_ref.shape[1:]
+
+    def some_slots(g, acc):
+        first = g * group
+        rows = perm_ref[0, pl.ds(first, group)].reshape(group * local, waves)
+        product = jnp.dot(rows, mov_ref[0], preferred_element_type=jnp.float32)
+        for j in range(group):
+            part = product[j * local:(j + 1) * local]
+            acc = acc + pltpu.roll(part, q_ref[first + j] * block, 1)
+        return acc
+
+    acc = lax.fori_loop(0, slots // group, some_slots, jnp.zeros(out_ref.shape[1:], jnp.float32))
     out_ref[0] = acc.astype(out_ref.dtype)
 
 
@@ -100,7 +107,7 @@
     steps, slots, local, waves = permuted.shape
     cols = moving.shape[2]
     return pl.pallas_call(
-        functools.partial(contract_kernel, block),
+        functools.partial(contract_kernel, block, 8 if slots % 8 == 0 else 1),
         out_shape=jax.ShapeDtypeStruct((steps, local, cols), jnp.bfloat16),
         grid_spec=pltpu.PrefetchScalarGridSpec(
             num_scalar_prefetch=1,
@@ -181,9 +188,8 @@
         kernel_cat, forms, (((0,), (2,)), ((1,), (0,))), preferred_element_type=jnp.float32
     )
     action = action.reshape(kpoint_count, step_count, vector_count, pair_count).sum(axis=1)
-    ga_order = [1, 0, 2] if ga_bits == 3 else list(range(ga_bits))
-    action = action.reshape((2,) * ga_bits + (kpoint_count // ga_size, vector_count, pair_count))
-    action = sum_all(action, "ga", ga_order).reshape(kpoint_count, vector_count, pair_count)
+    action = action.reshape(ga_size, kpoint_count // ga_size, vector_count, pair_count)
+    action = sum_all(action, "ga").reshape(kpoint_count, vector_count, pair_count)
     return energies[:, None, :] * vectors.astype(jnp.float32) - action
 
 

time: 312 us -> 293 us (0.939)
  starting transfers between devices: 39.5 us -> 59.6 us
  waiting for transfers between devices: 196 us -> 177 us
  Pallas kernels: 29.5 us -> 11.6 us
    ppermute x24 -> x32, waiting for transfers between devices: 166 us -> 143 us  [swap(): return lax.ppermute(value, axis, [(i, i ^ bit) for i in range(count)])]
    ppermute x24 -> x32, starting transfers between devices: 33.1 us -> 53 us  [swap(): return lax.ppermute(value, axis, [(i, i ^ bit) for i in range(count)])]
    pallas_call x1, Pallas kernels: 29.5 us -> 11.6 us  [contract(): pl.pallas_call(functools.partial(contract_kernel, block, 8 if slots % 8 =...]
    ppermute x5, waiting for transfers between devices: 30.2 us -> 34.2 us  [from_behind(): lax.ppermute(value, axis, [(i, (i + by) % count) for i in range(count)])]
    select_n x11 -> x8, other arithmetic: 6.16 us -> 7.12 us  [join(): low = jnp.where(mine == 0, h, g)]
    concatenate x11 -> x8, other arithmetic: 9.5 us -> 9.5 us  [join(): return jnp.concatenate([low, high], axis=axis_at)]
  transfers between devices with their start and end apart: 29 -> 37, of which waited for: 21 -> 18; matrix products, arithmetic and copies ran while one was open for 10% -> 9% of each run, Pallas kernels for 0% -> 0%
where the time goes in v3:
time: 293 us
  waiting for transfers between devices  177 us (60%)
  starting transfers between devices  59.6 us (20%)
  other arithmetic  26.9 us (9%)
  Pallas kernels  11.6 us (4%)
  local copies, waits for them, and re-layouts  8.3 us (3%)
  between operations  8.12 us (3%)
    ppermute x32, waiting for transfers between devices, swap(): return lax.ppermute(value, axis, [(i, i ^ bit) for i in range(count)])  143 us
    ppermute x32, starting transfers between devices, swap(): return lax.ppermute(value, axis, [(i, i ^ bit) for i in range(count)])  53 us
    ppermute x5, waiting for transfers between devices, from_behind(): lax.ppermute(value, axis, [(i, (i + by) % count) for i in range(count)])  34.2 us
    pallas_call x1, Pallas kernels, contract(): pl.pallas_call(functools.partial(contract_kernel, block, 8 if slots % 8 =...  11.6 us
    concatenate x8, other arithmetic, join(): return jnp.concatenate([low, high], axis=axis_at)  9.5 us
    select_n x8, other arithmetic, join(): low = jnp.where(mine == 0, h, g)  7.12 us
    ppermute x5, starting transfers between devices, from_behind(): lax.ppermute(value, axis, [(i, (i + by) % count) for i in range(count)])  6.57 us
  transfers between devices with their start and end apart: 37, of which 18 were waited for; matrix products, arithmetic and copies ran while one was open for 9% of the time, Pallas kernels for 0%

profile of v3, /device:TPU:96, one launch (start us, length us, event | category | flops | bytes accessed | tf_op | source)
XLA Modules:
  0.0 292.7 jit_solution(17565282296713733401)
XLA Ops:
  22.4 23.4 %collective-permute-done.1 = bf16[2,2,2,2,1,1,1,64,512]{8,7,1,3,2,6,5,4,0:T(8,128)(2,1)} collective-permute-done((bf16[2,2,2,2,1,1,1,64,512]{8,7,1,3,2,6,5,4,0:T(8,128)(2,1)}, bf16[2,2,2,2,1,1,1,64,512]{8,7,1,3,2,6,5,4,0:T(8,128)(2,1)}, u32[]{:S(2)}, u32[]{:S(2)}) %collective-permute-start.1) | collective-permute-done | bytes 1048608 | tf_op jit(solution)/shard_map/ppermute | solution.py:18
  50.1 4.6 %collective-permute-start.9 = (s32[2,1,1,1,1,1,1,512]{7,6,5,4,3,2,1,0:T(1,128)S(1)}, s32[2,1,1,1,1,1,1,512]{7,6,5,4,3,2,1,0:T(1,128)S(1)}, u32[]{:S(2)}, u32[]{:S(2)}) collective-permute-start(s32[2,1,1,1,1,1,1,512]{7,6,5,4,3,2,1,0:T(1,128)S(1)} %pad_add_fusion.3), channel_id=1, source_target_pairs={{0,128},{8,136},{16,144},{24,152},{32,160},{40,168},{48,176},{56,1... | collective-permute-start | bytes 12296 | tf_op jit(solution)/shard_map/ppermute | solution.py:18
  54.7 5.9 %collective-permute-done.2 = bf16[2,2,2,1,1,1,1,64,512]{8,7,1,2,6,5,4,3,0:T(8,128)(2,1)S(1)} collective-permute-done((bf16[2,2,2,1,1,1,1,64,512]{8,7,1,2,6,5,4,3,0:T(8,128)(2,1)S(1)}, bf16[2,2,2,1,1,1,1,64,512]{8,7,1,2,6,5,4,3,0:T(8,128)(2,1)S(1)}, u32[]{:S(2)}, u32[]{:S(2)}) %collective-permute-start.2) | collective-permute-done | bytes 524320 | tf_op jit(solution)/shard_map/ppermute | solution.py:18
  61.4 3.0 %collective-permute-done.9 = s32[2,1,1,1,1,1,1,512]{7,6,5,4,3,2,1,0:T(1,128)S(1)} collective-permute-done((s32[2,1,1,1,1,1,1,512]{7,6,5,4,3,2,1,0:T(1,128)S(1)}, s32[2,1,1,1,1,1,1,512]{7,6,5,4,3,2,1,0:T(1,128)S(1)}, u32[]{:S(2)}, u32[]{:S(2)}) %collective-permute-start.9) | collective-permute-done | bytes 4128 | tf_op jit(solution)/shard_map/ppermute | solution.py:18
  64.3 8.5 %collective-permute-done.3 = bf16[2,2,1,1,1,1,1,64,512]{8,7,1,6,5,4,3,2,0:T(8,128)(2,1)S(1)} collective-permute-done((bf16[2,2,1,1,1,1,1,64,512]{8,7,1,6,5,4,3,2,0:T(8,128)(2,1)S(1)}, bf16[2,2,1,1,1,1,1,64,512]{8,7,1,6,5,4,3,2,0:T(8,128)(2,1)S(1)}, u32[]{:S(2)}, u32[]{:S(2)}) %collective-permute-start.3) | collective-permute-done | bytes 262176 | tf_op jit(solution)/shard_map/ppermute | solution.py:18
  72.9 4.3 %collective-permute-start.4 = (bf16[2,1,1,1,1,1,1,64,512]{8,7,6,5,4,3,2,1,0:T(8,128)(2,1)S(1)}, bf16[2,1,1,1,1,1,1,64,512]{8,7,6,5,4,3,2,1,0:T(8,128)(2,1)S(1)}, u32[]{:S(2)}, u32[]{:S(2)}) collective-permute-start(bf16[2,1,1,1,1,1,1,64,512]{8,7,6,5,4,3,2,1,0:T(8,128)(2,1)S(1)} %pad_maximum_fusion.16), channel_id=1, source_target_pairs={{0,128},{8,136},{16,144},{24,152},{32,160},{40,168},{48,176},{56,1... | collective-permute-start | bytes 393224 | tf_op jit(solution)/shard_map/ppermute | solution.py:18
  77.5 6.7 %collective-permute-done.4 = bf16[2,1,1,1,1,1,1,64,512]{8,7,6,5,4,3,2,1,0:T(8,128)(2,1)S(1)} collective-permute-done((bf16[2,1,1,1,1,1,1,64,512]{8,7,6,5,4,3,2,1,0:T(8,128)(2,1)S(1)}, bf16[2,1,1,1,1,1,1,64,512]{8,7,6,5,4,3,2,1,0:T(8,128)(2,1)S(1)}, u32[]{:S(2)}, u32[]{:S(2)}) %collective-permute-start.4) | collective-permute-done | bytes 131104 | tf_op jit(solution)/shard_map/ppermute | solution.py:18
  87.6 7.3 %collective-permute-done.16 = bf16[2,32,32,64]{3,2,1,0:T(8,128)(2,1)S(1)} collective-permute-done((bf16[2,32,32,64]{3,2,1,0:T(8,128)(2,1)S(1)}, bf16[2,32,32,64]{3,2,1,0:T(8,128)(2,1)S(1)}, u32[]{:S(2)}, u32[]{:S(2)}) %collective-permute-start.16) | collective-permute-done | bytes 262176 | tf_op jit(solution)/shard_map/ppermute | solution.py:13
  95.1 2.9 collective-permute-start.17
  98.3 10.4 %collective-permute-done.17 = bf16[2,32,32,64]{3,2,1,0:T(8,128)(2,1)S(1)} collective-permute-done((bf16[2,32,32,64]{3,2,1,0:T(8,128)(2,1)S(1)}, bf16[2,32,32,64]{3,2,1,0:T(8,128)(2,1)S(1)}, u32[]{:S(2)}, u32[]{:S(2)}) %collective-permute-start.17) | collective-permute-done | bytes 262176 | tf_op jit(solution)/shard_map/ppermute | solution.py:13
  109.7 3.5 %collective-permute-start.18 = (bf16[2,32,32,64]{3,2,1,0:T(8,128)(2,1)}, bf16[2,32,32,64]{3,2,1,0:T(8,128)(2,1)S(1)}, u32[]{:S(2)}, u32[]{:S(2)}) collective-permute-start(bf16[2,32,32,64]{3,2,1,0:T(8,128)(2,1)} %pad_maximum_fusion.11), channel_id=1, source_target_pairs={{0,64},{8,72},{16,80},{24,88},{32,96},{40,104},{48,112},{56,120},{... | collective-permute-start | bytes 786440 | tf_op jit(solution)/shard_map/ppermute | solution.py:13
  113.2 14.7 %collective-permute-done.11 = bf16[2,2,1,1,1,1,1,64,512]{8,7,6,5,4,3,2,1,0:T(8,128)(2,1)S(1)} collective-permute-done((bf16[2,2,1,1,1,1,1,64,512]{8,7,6,5,4,3,2,1,0:T(8,128)(2,1)S(1)}, bf16[2,2,1,1,1,1,1,64,512]{8,7,6,5,4,3,2,1,0:T(8,128)(2,1)S(1)}, u32[]{:S(2)}, u32[]{:S(2)}) %collective-permute-start.11) | collective-permute-done | bytes 262176 | tf_op jit(solution)/shard_map/ppermute | solution.py:18
  130.1 16.5 %collective-permute-done.18 = bf16[2,32,32,64]{3,2,1,0:T(8,128)(2,1)S(1)} collective-permute-done((bf16[2,32,32,64]{3,2,1,0:T(8,128)(2,1)}, bf16[2,32,32,64]{3,2,1,0:T(8,128)(2,1)S(1)}, u32[]{:S(2)}, u32[]{:S(2)}) %collective-permute-start.18) | collective-permute-done | bytes 262176 | tf_op jit(solution)/shard_map/ppermute | solution.py:13
  146.9 23.2 %collective-permute-done.12 = bf16[2,2,2,1,1,1,1,64,512]{8,7,6,5,4,3,2,1,0:T(8,128)(2,1)} collective-permute-done((bf16[2,2,2,1,1,1,1,64,512]{8,7,6,5,4,3,2,1,0:T(8,128)(2,1)}, bf16[2,2,2,1,1,1,1,64,512]{8,7,6,5,4,3,2,1,0:T(8,128)(2,1)}, u32[]{:S(2)}, u32[]{:S(2)}) %collective-permute-start.12) | collective-permute-done | bytes 524320 | tf_op jit(solution)/shard_map/ppermute | solution.py:18
  175.5 22.3 %collective-permute-done.20 = bf16[2,1,1,1,64,1024]{5,4,3,2,1,0:T(8,128)(2,1)S(1)} collective-permute-done((bf16[2,1,1,1,64,1024]{5,4,3,2,1,0:T(8,128)(2,1)S(1)}, bf16[2,1,1,1,64,1024]{5,4,3,2,1,0:T(8,128)(2,1)S(1)}, u32[]{:S(2)}, u32[]{:S(2)}) %collective-permute-start.20) | collective-permute-done | bytes 262176 | tf_op jit(solution)/shard_map/ppermute | solution.py:18
  198.8 3.0 %collective-permute-start.21 = (bf16[2,1,1,2,64,1024]{5,4,3,2,1,0:T(8,128)(2,1)}, bf16[2,1,1,2,64,1024]{5,4,3,2,1,0:T(8,128)(2,1)}, u32[]{:S(2)}, u32[]{:S(2)}) collective-permute-start(bf16[2,1,1,2,64,1024]{5,4,3,2,1,0:T(8,128)(2,1)} %pad_maximum_fusion.13), channel_id=1, source_target_pairs={{0,4},{1,5},{2,6},{3,7},{4,0},{5,1},{6,2},{7,3},{8,12},{9,13},{10,... | collective-permute-start | bytes 1572872 | tf_op jit(solution)/shard_map/ppermute | solution.py:18
  204.7 5.1 %collective-permute-done.21 = bf16[2,1,1,2,64,1024]{5,4,3,2,1,0:T(8,128)(2,1)} collective-permute-done((bf16[2,1,1,2,64,1024]{5,4,3,2,1,0:T(8,128)(2,1)}, bf16[2,1,1,2,64,1024]{5,4,3,2,1,0:T(8,128)(2,1)}, u32[]{:S(2)}, u32[]{:S(2)}) %collective-permute-start.21) | collective-permute-done | bytes 524320 | tf_op jit(solution)/shard_map/ppermute | solution.py:18
  214.4 19.3 %collective-permute-done.22 = bf16[2,2,1,2,64,1024]{5,4,3,2,1,0:T(8,128)(2,1)} collective-permute-done((bf16[2,2,1,2,64,1024]{5,4,3,2,1,0:T(8,128)(2,1)}, bf16[2,2,1,2,64,1024]{5,4,3,2,1,0:T(8,128)(2,1)}, u32[]{:S(2)}, u32[]{:S(2)}) %collective-permute-start.22) | collective-permute-done | bytes 1048608 | tf_op jit(solution)/shard_map/ppermute | solution.py:18
  241.0 11.6 %shard_map.73 = bf16[2,64,1024]{2,1,0:T(8,128)(2,1)} custom-call(s32[32]{0:T(128)} %q_ref.1, bf16[2,32,64,512]{3,2,1,0:T(8,128)(2,1)} %bitcast.273, bf16[2,512,1024]{2,1,0:T(8,128)(2,1)} %bitcast.280), custom_call_target="tpu_custom_call" | custom-call | flops 4294967296 | bytes 6553600 | tf_op jit(solution)/shard_map/pallas_call | solution.py:109
  260.4 3.3 %collective-permute-start.26 = (f32[4,32,128]{2,1,0:T(8,128)S(1)}, f32[4,32,128]{2,1,0:T(8,128)S(1)}, u32[]{:S(2)}, u32[]{:S(2)}) collective-permute-start(f32[4,32,128]{2,1,0:T(8,128)S(1)} %get-tuple-element.29), channel_id=1, source_target_pairs={{0,4},{1,5},{2,6},{3,7},{4,0},{5,1},{6,2},{7,3},{8,12},{9,13},{10,... | collective-permute-start | bytes 196616 | tf_op jit(solution)/shard_map/ppermute | solution.py:18
  265.8 2.9 collective-permute-start.23
  277.8 4.8 %collective-permute-start.34 = (f32[4,32,128]{2,1,0:T(8,128)S(1)}, f32[4,32,128]{2,1,0:T(8,128)S(1)}, u32[]{:S(2)}, u32[]{:S(2)}) collective-permute-start(f32[4,32,128]{2,1,0:T(8,128)S(1)} %get-tuple-element.6), channel_id=1, source_target_pairs={{0,5},{1,4},{2,7},{3,6},{4,1},{5,0},{6,3},{7,2},{8,13},{9,12},{10,... | collective-permute-start | bytes 196616 | tf_op jit(solution)/shard_map/ppermute | solution.py:18
  283.8 3.0 %collective-permute-start.36 = (f32[4,32,128]{2,1,0:T(8,128)S(1)}, f32[4,32,128]{2,1,0:T(8,128)S(1)}, u32[]{:S(2)}, u32[]{:S(2)}) collective-permute-start(f32[4,32,128]{2,1,0:T(8,128)S(1)} %get-tuple-element.6), channel_id=1, source_target_pairs={{0,7},{1,6},{2,5},{3,4},{4,3},{5,2},{6,1},{7,0},{8,15},{9,14},{10,... | collective-permute-start | bytes 196616 | tf_op jit(solution)/shard_map/ppermute | solution.py:18
  288.1 3.7 %collective-permute-done.36 = f32[4,32,128]{2,1,0:T(8,128)S(1)} collective-permute-done((f32[4,32,128]{2,1,0:T(8,128)S(1)}, f32[4,32,128]{2,1,0:T(8,128)S(1)}, u32[]{:S(2)}, u32[]{:S(2)}) %collective-permute-start.36) | collective-permute-done | bytes 65568 | tf_op jit(solution)/shard_map/ppermute | solution.py:18
  (169 shorter events, 70.8 us)
Async XLA Ops:
  14.8 31.0 %collective-permute-start.1 = (bf16[2,2,2,2,1,1,1,64,512]{8,7,1,3,2,6,5,4,0:T(8,128)(2,1)}, bf16[2,2,2,2,1,1,1,64,512]{8,7,1,3,2,6,5,4,0:T(8,128)(2,1)}, u32[]{:S(2)}, u32[]{:S(2)}) collective-permute-start(bf16[2,2,2,2,1,1,1,64,512]{8,7,1,3,2,6,5,4,0:T(8,128)(2,1)} %pad_maximum_fusion.3), channel_id=1, source_target_pairs={{0,16},{8,24},{16,0},{24,8},{32,48},{40,56},{48,32},{56,40},{64,80... | collective-permute-start | bytes 3145736 | tf_op jit(solution)/shard_map/ppermute | solution.py:18
  18.7 58.5 %collective-permute-start.15 = (bf16[2,32,32,64]{3,2,1,0:T(8,128)(2,1)}, bf16[2,32,32,64]{3,2,1,0:T(8,128)(2,1)S(1)}, u32[]{:S(2)}, u32[]{:S(2)}) collective-permute-start(bf16[2,32,32,64]{3,2,1,0:T(8,128)(2,1)} %pad_maximum_fusion.8), channel_id=1, source_target_pairs={{0,8},{8,16},{16,24},{24,32},{32,40},{40,48},{48,56},{56,64},{64,7... | collective-permute-start | bytes 786440 | tf_op jit(solution)/shard_map/ppermute | solution.py:13
  48.3 12.3 %collective-permute-start.2 = (bf16[2,2,2,1,1,1,1,64,512]{8,7,1,2,6,5,4,3,0:T(8,128)(2,1)S(1)}, bf16[2,2,2,1,1,1,1,64,512]{8,7,1,2,6,5,4,3,0:T(8,128)(2,1)S(1)}, u32[]{:S(2)}, u32[]{:S(2)}) collective-permute-start(bf16[2,2,2,1,1,1,1,64,512]{8,7,1,2,6,5,4,3,0:T(8,128)(2,1)S(1)} %pad_maximum_fusion.6), channel_id=1, source_target_pairs={{0,32},{8,40},{16,48},{24,56},{32,0},{40,8},{48,16},{56,24},{64,96... | collective-permute-start | bytes 1572872 | tf_op jit(solution)/shard_map/ppermute | solution.py:18
  50.1 14.2 %collective-permute-start.9 = (s32[2,1,1,1,1,1,1,512]{7,6,5,4,3,2,1,0:T(1,128)S(1)}, s32[2,1,1,1,1,1,1,512]{7,6,5,4,3,2,1,0:T(1,128)S(1)}, u32[]{:S(2)}, u32[]{:S(2)}) collective-permute-start(s32[2,1,1,1,1,1,1,512]{7,6,5,4,3,2,1,0:T(1,128)S(1)} %pad_add_fusion.3), channel_id=1, source_target_pairs={{0,128},{8,136},{16,144},{24,152},{32,160},{40,168},{48,176},{56,1... | collective-permute-start | bytes 12296 | tf_op jit(solution)/shard_map/ppermute | solution.py:18
  60.8 12.0 %collective-permute-start.3 = (bf16[2,2,1,1,1,1,1,64,512]{8,7,1,6,5,4,3,2,0:T(8,128)(2,1)S(1)}, bf16[2,2,1,1,1,1,1,64,512]{8,7,1,6,5,4,3,2,0:T(8,128)(2,1)S(1)}, u32[]{:S(2)}, u32[]{:S(2)}) collective-permute-start(bf16[2,2,1,1,1,1,1,64,512]{8,7,1,6,5,4,3,2,0:T(8,128)(2,1)S(1)} %pad_maximum_fusion.14), channel_id=1, source_target_pairs={{0,64},{8,72},{16,80},{24,88},{32,96},{40,104},{48,112},{56,120},{... | collective-permute-start | bytes 786440 | tf_op jit(solution)/shard_map/ppermute | solution.py:18
  72.9 11.3 %collective-permute-start.4 = (bf16[2,1,1,1,1,1,1,64,512]{8,7,6,5,4,3,2,1,0:T(8,128)(2,1)S(1)}, bf16[2,1,1,1,1,1,1,64,512]{8,7,6,5,4,3,2,1,0:T(8,128)(2,1)S(1)}, u32[]{:S(2)}, u32[]{:S(2)}) collective-permute-start(bf16[2,1,1,1,1,1,1,64,512]{8,7,6,5,4,3,2,1,0:T(8,128)(2,1)S(1)} %pad_maximum_fusion.16), channel_id=1, source_target_pairs={{0,128},{8,136},{16,144},{24,152},{32,160},{40,168},{48,176},{56,1... | collective-permute-start | bytes 393224 | tf_op jit(solution)/shard_map/ppermute | solution.py:18
  77.4 17.6 %collective-permute-start.16 = (bf16[2,32,32,64]{3,2,1,0:T(8,128)(2,1)S(1)}, bf16[2,32,32,64]{3,2,1,0:T(8,128)(2,1)S(1)}, u32[]{:S(2)}, u32[]{:S(2)}) collective-permute-start(bf16[2,32,32,64]{3,2,1,0:T(8,128)(2,1)S(1)} %pad_maximum_fusion.9), channel_id=1, source_target_pairs={{0,16},{8,24},{16,32},{24,40},{32,48},{40,56},{48,64},{56,72},{64,... | collective-permute-start | bytes 786440 | tf_op jit(solution)/shard_map/ppermute | solution.py:13
  85.0 13.0 %collective-permute-start.10 = (bf16[2,1,1,1,1,1,1,64,512]{8,7,6,5,4,3,2,1,0:T(8,128)(2,1)S(1)}, bf16[2,1,1,1,1,1,1,64,512]{8,7,6,5,4,3,2,1,0:T(8,128)(2,1)S(1)}, u32[]{:S(2)}, u32[]{:S(2)}) collective-permute-start(bf16[2,1,1,1,1,1,1,64,512]{8,7,6,5,4,3,2,1,0:T(8,128)(2,1)S(1)} %pad_maximum_fusion.17), channel_id=1, source_target_pairs={{0,128},{8,136},{16,144},{24,152},{32,160},{40,168},{48,176},{56,1... | collective-permute-start | bytes 393224 | tf_op jit(solution)/shard_map/ppermute | solution.py:18
  95.1 13.6 %collective-permute-start.17 = (bf16[2,32,32,64]{3,2,1,0:T(8,128)(2,1)S(1)}, bf16[2,32,32,64]{3,2,1,0:T(8,128)(2,1)S(1)}, u32[]{:S(2)}, u32[]{:S(2)}) collective-permute-start(bf16[2,32,32,64]{3,2,1,0:T(8,128)(2,1)S(1)} %pad_maximum_fusion.10), channel_id=1, source_target_pairs={{0,32},{8,40},{16,48},{24,56},{32,64},{40,72},{48,80},{56,88},{64,... | collective-permute-start | bytes 786440 | tf_op jit(solution)/shard_map/ppermute | solution.py:13
  98.0 29.9 %collective-permute-start.11 = (bf16[2,2,1,1,1,1,1,64,512]{8,7,6,5,4,3,2,1,0:T(8,128)(2,1)S(1)}, bf16[2,2,1,1,1,1,1,64,512]{8,7,6,5,4,3,2,1,0:T(8,128)(2,1)S(1)}, u32[]{:S(2)}, u32[]{:S(2)}) collective-permute-start(bf16[2,2,1,1,1,1,1,64,512]{8,7,6,5,4,3,2,1,0:T(8,128)(2,1)S(1)} %pad_maximum_fusion.15), channel_id=1, source_target_pairs={{0,64},{8,72},{16,80},{24,88},{32,96},{40,104},{48,112},{56,120},{... | collective-permute-start | bytes 786440 | tf_op jit(solution)/shard_map/ppermute | solution.py:18
  109.7 36.9 %collective-permute-start.18 = (bf16[2,32,32,64]{3,2,1,0:T(8,128)(2,1)}, bf16[2,32,32,64]{3,2,1,0:T(8,128)(2,1)S(1)}, u32[]{:S(2)}, u32[]{:S(2)}) collective-permute-start(bf16[2,32,32,64]{3,2,1,0:T(8,128)(2,1)} %pad_maximum_fusion.11), channel_id=1, source_target_pairs={{0,64},{8,72},{16,80},{24,88},{32,96},{40,104},{48,112},{56,120},{... | collective-permute-start | bytes 786440 | tf_op jit(solution)/shard_map/ppermute | solution.py:13
  128.9 41.2 %collective-permute-start.12 = (bf16[2,2,2,1,1,1,1,64,512]{8,7,6,5,4,3,2,1,0:T(8,128)(2,1)}, bf16[2,2,2,1,1,1,1,64,512]{8,7,6,5,4,3,2,1,0:T(8,128)(2,1)}, u32[]{:S(2)}, u32[]{:S(2)}) collective-permute-start(bf16[2,2,2,1,1,1,1,64,512]{8,7,6,5,4,3,2,1,0:T(8,128)(2,1)} %pad_maximum_fusion.7), channel_id=1, source_target_pairs={{0,32},{8,40},{16,48},{24,56},{32,0},{40,8},{48,16},{56,24},{64,96... | collective-permute-start | bytes 1572872 | tf_op jit(solution)/shard_map/ppermute | solution.py:18
  146.8 26.8 %collective-permute-start.19 = (bf16[2,32,32,64]{3,2,1,0:T(8,128)(2,1)S(1)}, bf16[2,32,32,64]{3,2,1,0:T(8,128)(2,1)}, u32[]{:S(2)}, u32[]{:S(2)}) collective-permute-start(bf16[2,32,32,64]{3,2,1,0:T(8,128)(2,1)S(1)} %pad_maximum_fusion.12), channel_id=1, source_target_pairs={{0,128},{8,136},{16,144},{24,152},{32,160},{40,168},{48,176},{56,1... | collective-permute-start | bytes 786440 | tf_op jit(solution)/shard_map/ppermute | solution.py:13
  172.4 29.4 %collective-permute-start.13 = (bf16[2,2,2,2,1,1,1,64,512]{8,7,6,5,4,3,2,1,0:T(8,128)(2,1)}, bf16[2,2,2,2,1,1,1,64,512]{8,7,6,5,4,3,2,1,0:T(8,128)(2,1)}, u32[]{:S(2)}, u32[]{:S(2)}) collective-permute-start(bf16[2,2,2,2,1,1,1,64,512]{8,7,6,5,4,3,2,1,0:T(8,128)(2,1)} %pad_maximum_fusion.4), channel_id=1, source_target_pairs={{0,16},{8,24},{16,0},{24,8},{32,48},{40,56},{48,32},{56,40},{64,80... | collective-permute-start | bytes 3145736 | tf_op jit(solution)/shard_map/ppermute | solution.py:18
  175.1 22.8 %collective-permute-start.20 = (bf16[2,1,1,1,64,1024]{5,4,3,2,1,0:T(8,128)(2,1)S(1)}, bf16[2,1,1,1,64,1024]{5,4,3,2,1,0:T(8,128)(2,1)S(1)}, u32[]{:S(2)}, u32[]{:S(2)}) collective-permute-start(bf16[2,1,1,1,64,1024]{5,4,3,2,1,0:T(8,128)(2,1)S(1)} %maximum_bitcast_fusion), channel_id=1, source_target_pairs={{0,1},{1,0},{2,3},{3,2},{4,5},{5,4},{6,7},{7,6},{8,9},{9,8},{10,11... | collective-permute-start | bytes 786440 | tf_op jit(solution)/shard_map/ppermute | solution.py:18
  198.8 11.0 %collective-permute-start.21 = (bf16[2,1,1,2,64,1024]{5,4,3,2,1,0:T(8,128)(2,1)}, bf16[2,1,1,2,64,1024]{5,4,3,2,1,0:T(8,128)(2,1)}, u32[]{:S(2)}, u32[]{:S(2)}) collective-permute-start(bf16[2,1,1,2,64,1024]{5,4,3,2,1,0:T(8,128)(2,1)} %pad_maximum_fusion.13), channel_id=1, source_target_pairs={{0,4},{1,5},{2,6},{3,7},{4,0},{5,1},{6,2},{7,3},{8,12},{9,13},{10,... | collective-permute-start | bytes 1572872 | tf_op jit(solution)/shard_map/ppermute | solution.py:18
  204.7 32.0 %collective-permute-start.14 = (bf16[2,2,2,2,2,1,1,64,512]{8,7,6,5,4,3,2,1,0:T(8,128)(2,1)}, bf16[2,2,2,2,2,1,1,64,512]{8,7,6,5,4,3,2,1,0:T(8,128)(2,1)}, u32[]{:S(2)}, u32[]{:S(2)}) collective-permute-start(bf16[2,2,2,2,2,1,1,64,512]{8,7,6,5,4,3,2,1,0:T(8,128)(2,1)} %pad_maximum_fusion.1), channel_id=1, source_target_pairs={{0,8},{8,0},{16,24},{24,16},{32,40},{40,32},{48,56},{56,48},{64,72... | collective-permute-start | bytes 6291464 | tf_op jit(solution)/shard_map/ppermute | solution.py:18
  212.9 20.8 %collective-permute-start.22 = (bf16[2,2,1,2,64,1024]{5,4,3,2,1,0:T(8,128)(2,1)}, bf16[2,2,1,2,64,1024]{5,4,3,2,1,0:T(8,128)(2,1)}, u32[]{:S(2)}, u32[]{:S(2)}) collective-permute-start(bf16[2,2,1,2,64,1024]{5,4,3,2,1,0:T(8,128)(2,1)} %pad_maximum_fusion.5), channel_id=1, source_target_pairs={{0,2},{1,3},{2,0},{3,1},{4,6},{5,7},{6,4},{7,5},{8,10},{9,11},{10,... | collective-permute-start | bytes 3145736 | tf_op jit(solution)/shard_map/ppermute | solution.py:18
  254.4 9.3 %collective-permute-start.29 = (f32[4,32,128]{2,1,0:T(8,128)S(1)}, f32[4,32,128]{2,1,0:T(8,128)S(1)}, u32[]{:S(2)}, u32[]{:S(2)}) collective-permute-start(f32[4,32,128]{2,1,0:T(8,128)S(1)} %get-tuple-element.26), channel_id=1, source_target_pairs={{0,7},{1,6},{2,5},{3,4},{4,3},{5,2},{6,1},{7,0},{8,15},{9,14},{10,... | collective-permute-start | bytes 196616 | tf_op jit(solution)/shard_map/ppermute | solution.py:18
  255.7 10.1 %collective-permute-start.28 = (f32[4,32,128]{2,1,0:T(8,128)S(1)}, f32[4,32,128]{2,1,0:T(8,128)S(1)}, u32[]{:S(2)}, u32[]{:S(2)}) collective-permute-start(f32[4,32,128]{2,1,0:T(8,128)S(1)} %get-tuple-element.27), channel_id=1, source_target_pairs={{0,6},{1,7},{2,4},{3,5},{4,2},{5,3},{6,0},{7,1},{8,14},{9,15},{10,... | collective-permute-start | bytes 196616 | tf_op jit(solution)/shard_map/ppermute | solution.py:18
  257.8 10.9 %collective-permute-start.27 = (f32[4,32,128]{2,1,0:T(8,128)S(1)}, f32[4,32,128]{2,1,0:T(8,128)S(1)}, u32[]{:S(2)}, u32[]{:S(2)}) collective-permute-start(f32[4,32,128]{2,1,0:T(8,128)S(1)} %get-tuple-element.28), channel_id=1, source_target_pairs={{0,5},{1,4},{2,7},{3,6},{4,1},{5,0},{6,3},{7,2},{8,13},{9,12},{10,... | collective-permute-start | bytes 196616 | tf_op jit(solution)/shard_map/ppermute | solution.py:18
  272.4 10.2 %collective-permute-start.30 = (f32[4,32,128]{2,1,0:T(8,128)S(1)}, f32[4,32,128]{2,1,0:T(8,128)S(1)}, u32[]{:S(2)}, u32[]{:S(2)}) collective-permute-start(f32[4,32,128]{2,1,0:T(8,128)S(1)} %get-tuple-element.6), channel_id=1, source_target_pairs={{0,1},{1,0},{2,3},{3,2},{4,5},{5,4},{6,7},{7,6},{8,9},{9,8},{10,11... | collective-permute-start | bytes 196616 | tf_op jit(solution)/shard_map/ppermute | solution.py:18
  275.4 11.4 %collective-permute-start.32 = (f32[4,32,128]{2,1,0:T(8,128)S(1)}, f32[4,32,128]{2,1,0:T(8,128)S(1)}, u32[]{:S(2)}, u32[]{:S(2)}) collective-permute-start(f32[4,32,128]{2,1,0:T(8,128)S(1)} %get-tuple-element.6), channel_id=1, source_target_pairs={{0,3},{1,2},{2,1},{3,0},{4,7},{5,6},{6,5},{7,4},{8,11},{9,10},{10,... | collective-permute-start | bytes 196616 | tf_op jit(solution)/shard_map/ppermute | solution.py:18
  277.5 9.3 %collective-permute-start.33 = (f32[4,32,128]{2,1,0:T(8,128)S(1)}, f32[4,32,128]{2,1,0:T(8,128)S(1)}, u32[]{:S(2)}, u32[]{:S(2)}) collective-permute-start(f32[4,32,128]{2,1,0:T(8,128)S(1)} %get-tuple-element.6), channel_id=1, source_target_pairs={{0,4},{1,5},{2,6},{3,7},{4,0},{5,1},{6,2},{7,3},{8,12},{9,13},{10,... | collective-permute-start | bytes 196616 | tf_op jit(solution)/shard_map/ppermute | solution.py:18
  (24 other events, 247.7 us)

commit v4 on v3

--- a/solution.py
+++ b/solution.py
@@ -18,13 +18,35 @@
     return lax.ppermute(value, axis, [(i, i ^ bit) for i in range(count)])
 
 
+def relabel(index, size):
+    if size < 8:
+        return index
+    one = (index >> 1) & 1
+    two = (index >> 2) & 1
+    swapped = index + (two - one) * 2 + (one - two) * 4
+    if isinstance(index, int):
+        return swapped if index & 1 else index
+    return jnp.where(index & 1 == 1, swapped, index)
+
+
+def swap_relabelled(value, axis, bit):
+    count = lax.axis_size(axis)
+    pairs = []
+    for i in range(count):
+        v = relabel(i, count) ^ (1 << bit)
+        pairs.append((i, [j for j in range(count) if relabel(j, count) == v][0]))
+    return lax.ppermute(value, axis, pairs)
+
+
 def pick_half(tree, axis_at, which):
     return jax.tree.map(lambda a: lax.dynamic_slice_in_dim(a, which, 1, axis=axis_at), tree)
 
 
 def scatter_from_roots(own, roots, axis, order):
     nbits = len(order)
-    me = lax.axis_index(axis)
+    count = lax.axis_size(axis)
+    me = relabel(lax.axis_index(axis), count)
+    roots = [relabel(root, count) for root in roots]
     full = (1 << nbits) - 1
     held = [own] * len(roots)
     shared = True
@@ -34,12 +56,12 @@
         mine = (me >> bit) & 1
         if shared:
             sends = pick_half(own, axis_at, 1 - mine)
-            got = swap(sends, axis, 1 << bit)
+            got = swap_relabelled(sends, axis, bit)
             got = [got] * len(roots)
         else:
             sends = [pick_half(h, axis_at, 1 - mine) for h in held]
             stacked = jax.tree.map(lambda *xs: jnp.stack(xs), *sends)
-            stacked = swap(stacked, axis, 1 << bit)
+            stacked = swap_relabelled(stacked, axis, bit)
             got = [jax.tree.map(lambda x: x[r], stacked) for r in range(len(roots))]
         new_held = []
         for r, root in enumerate(roots):
@@ -54,14 +76,20 @@
     return held
 
 
-def gather_all(pieces, axis, order, lead=0):
+def gather_all(pieces, axis, order, lead=0, relabelled=False):
     nbits = len(order)
+    count = lax.axis_size(axis)
     me = lax.axis_index(axis)
+    if relabelled:
+        me = relabel(me, count)
     held = pieces
     for bit in order:
         axis_at = lead + nbits - 1 - bit
         mine = (me >> bit) & 1
-        got = swap(held, axis, 1 << bit)
+        if relabelled:
+            got = swap_relabelled(held, axis, bit)
+        else:
+            got = swap(held, axis, 1 << bit)
 
         def join(h, g):
             low = jnp.where(mine == 0, h, g)
@@ -162,13 +190,26 @@
         permuted_pieces.append(
             moved_cols.reshape((1,) * ka_bits + (per_piece, local_waves, plane_waves))
         )
-    gathered = gather_all(jnp.stack(permuted_pieces), "ka", list(range(ka_bits))[::-1], lead=1)
-
-    moving = [projected] * step_count
-    for level in range(ka_bits):
-        hopped = from_behind(jnp.stack(moving), "ka", 1 << level)
+    gathered = gather_all(
+        jnp.stack(permuted_pieces), "ka", list(range(ka_bits))[::-1], lead=1, relabelled=True
+    )
+
+    odd = [roots[i] & 1 for i in range(step_count)]
+    hopped = from_behind(projected, "ka", 1)
+    moving = [jnp.where(odd[i] == 1, hopped, projected) for i in range(step_count)]
+    even_part = [roots[i] - odd[i] for i in range(step_count)]
+    amounts = [
+        jnp.where(me_ka & 1 == 0, even_part[i], (ka_size - even_part[i]) % ka_size)
+        for i in range(step_count)
+    ]
+    for level in range(1, ka_bits):
+        by = 1 << level
+        pairs = [
+            (j, (j + by) % ka_size if j % 2 == 0 else (j - by) % ka_size) for j in range(ka_size)
+        ]
+        hopped = lax.ppermute(jnp.stack(moving), "ka", pairs)
         moving = [
-            jnp.where(roots[i] >> level & 1 == 1, hopped[i], moving[i])
+            jnp.where(amounts[i] >> level & 1 == 1, hopped[i], moving[i])
             for i in range(step_count)
         ]
     moving = jnp.stack(moving).reshape(step_count, kpoint_count * vector_count, local_waves)

time: 293 us -> 288 us (0.983)
  the two profiles are of different devices: /device:TPU:96 before, /device:TPU:32 now
where the time goes in v4:
time: 288 us; the launch traced here: 286 us
  waiting for transfers between devices  149 us (52%)
  starting transfers between devices  80.3 us (28%)
  other arithmetic  27.2 us (9%)
  Pallas kernels  11.6 us (4%)
  between operations  8.43 us (3%)
  local copies, waits for them, and re-layouts  8.32 us (3%)
    ppermute x15, waiting for transfers between devices, swap_relabelled(): return lax.ppermute(value, axis, pairs)  72.9 us
    ppermute x17, waiting for transfers between devices, swap(): return lax.ppermute(value, axis, [(i, i ^ bit) for i in range(count)])  43.5 us
    ppermute x17, starting transfers between devices, swap(): return lax.ppermute(value, axis, [(i, i ^ bit) for i in range(count)])  36 us
    ppermute x15, starting transfers between devices, swap_relabelled(): return lax.ppermute(value, axis, pairs)  35 us
    ppermute x4, waiting for transfers between devices, body(): hopped = lax.ppermute(jnp.stack(moving), 'ka', pairs)  32.2 us
    pallas_call x1, Pallas kernels, contract(): pl.pallas_call(functools.partial(contract_kernel, block, 8 if slots % 8 =...  11.6 us
    concatenate x8, other arithmetic, join(): return jnp.concatenate([low, high], axis=axis_at)  9.5 us
    ppermute x4, starting transfers between devices, body(): hopped = lax.ppermute(jnp.stack(moving), 'ka', pairs)  9.11 us
  transfers between devices with their start and end apart: 37, of which 21 were waited for; matrix products, arithmetic and copies ran while one was open for 10% of the time, Pallas kernels for 0%

profile of v4, /device:TPU:32, one launch (start us, length us, event | category | flops | bytes accessed | tf_op | source)
XLA Modules:
  0.0 285.9 jit_solution(12360754565986907040)
XLA Ops:
  14.9 17.1 %collective-permute-done.6 = s32[2,2,2,2,1,1,1,512]{7,5,6,4,3,2,1,0:T(1,128)S(1)} collective-permute-done((s32[2,2,2,2,1,1,1,512]{7,5,6,4,3,2,1,0:T(1,128)S(1)}, s32[2,2,2,2,1,1,1,512]{7,5,6,4,3,2,1,0:T(1,128)S(1)}, u32[]{:S(2)}, u32[]{:S(2)}) %collective-permute-start.6) | collective-permute-done | bytes 32800 | tf_op jit(solution)/shard_map/ppermute | solution.py:38
  38.9 3.4 %collective-permute-start.8 = (s32[2,2,1,1,1,1,1,512]{7,5,6,4,3,2,1,0:T(1,128)S(1)}, s32[2,2,1,1,1,1,1,512]{7,5,6,4,3,2,1,0:T(1,128)S(1)}, u32[]{:S(2)}, u32[]{:S(2)}) collective-permute-start(s32[2,2,1,1,1,1,1,512]{7,5,6,4,3,2,1,0:T(1,128)S(1)} %pad_add_fusion.2), channel_id=1, source_target_pairs={{0,64},{8,72},{16,80},{24,88},{32,96},{40,104},{48,112},{56,120},{... | collective-permute-start | bytes 24584 | tf_op jit(solution)/shard_map/ppermute | solution.py:38
  44.1 10.6 %collective-permute-done.1 = bf16[2,2,2,2,1,1,1,64,512]{8,7,1,3,2,6,5,4,0:T(8,128)(2,1)} collective-permute-done((bf16[2,2,2,2,1,1,1,64,512]{8,7,1,3,2,6,5,4,0:T(8,128)(2,1)}, bf16[2,2,2,2,1,1,1,64,512]{8,7,1,3,2,6,5,4,0:T(8,128)(2,1)}, u32[]{:S(2)}, u32[]{:S(2)}) %collective-permute-start.1) | collective-permute-done | bytes 1048608 | tf_op jit(solution)/shard_map/ppermute | solution.py:38
  58.9 7.3 %collective-permute-start.9 = (s32[2,1,1,1,1,1,1,512]{7,6,5,4,3,2,1,0:T(1,128)S(1)}, s32[2,1,1,1,1,1,1,512]{7,6,5,4,3,2,1,0:T(1,128)S(1)}, u32[]{:S(2)}, u32[]{:S(2)}) collective-permute-start(s32[2,1,1,1,1,1,1,512]{7,6,5,4,3,2,1,0:T(1,128)S(1)} %pad_add_fusion.3), channel_id=1, source_target_pairs={{0,128},{8,136},{16,144},{24,152},{32,160},{40,168},{48,176},{56,1... | collective-permute-start | bytes 12296 | tf_op jit(solution)/shard_map/ppermute | solution.py:38
  70.9 5.3 %collective-permute-done.9 = s32[2,1,1,1,1,1,1,512]{7,6,5,4,3,2,1,0:T(1,128)S(1)} collective-permute-done((s32[2,1,1,1,1,1,1,512]{7,6,5,4,3,2,1,0:T(1,128)S(1)}, s32[2,1,1,1,1,1,1,512]{7,6,5,4,3,2,1,0:T(1,128)S(1)}, u32[]{:S(2)}, u32[]{:S(2)}) %collective-permute-start.9) | collective-permute-done | bytes 4128 | tf_op jit(solution)/shard_map/ppermute | solution.py:38
  76.2 4.3 %collective-permute-done.3 = bf16[2,2,1,1,1,1,1,64,512]{8,7,1,6,5,4,3,2,0:T(8,128)(2,1)S(1)} collective-permute-done((bf16[2,2,1,1,1,1,1,64,512]{8,7,1,6,5,4,3,2,0:T(8,128)(2,1)S(1)}, bf16[2,2,1,1,1,1,1,64,512]{8,7,1,6,5,4,3,2,0:T(8,128)(2,1)S(1)}, u32[]{:S(2)}, u32[]{:S(2)}) %collective-permute-start.3) | collective-permute-done | bytes 262176 | tf_op jit(solution)/shard_map/ppermute | solution.py:38
  80.6 6.6 %collective-permute-start.4 = (bf16[2,1,1,1,1,1,1,64,512]{8,7,6,5,4,3,2,1,0:T(8,128)(2,1)S(1)}, bf16[2,1,1,1,1,1,1,64,512]{8,7,6,5,4,3,2,1,0:T(8,128)(2,1)S(1)}, u32[]{:S(2)}, u32[]{:S(2)}) collective-permute-start(bf16[2,1,1,1,1,1,1,64,512]{8,7,6,5,4,3,2,1,0:T(8,128)(2,1)S(1)} %pad_maximum_fusion.15), channel_id=1, source_target_pairs={{0,128},{8,136},{16,144},{24,152},{32,160},{40,168},{48,176},{56,1... | collective-permute-start | bytes 393224 | tf_op jit(solution)/shard_map/ppermute | solution.py:38
  87.6 7.4 %collective-permute-done.4 = bf16[2,1,1,1,1,1,1,64,512]{8,7,6,5,4,3,2,1,0:T(8,128)(2,1)S(1)} collective-permute-done((bf16[2,1,1,1,1,1,1,64,512]{8,7,6,5,4,3,2,1,0:T(8,128)(2,1)S(1)}, bf16[2,1,1,1,1,1,1,64,512]{8,7,6,5,4,3,2,1,0:T(8,128)(2,1)S(1)}, u32[]{:S(2)}, u32[]{:S(2)}) %collective-permute-start.4) | collective-permute-done | bytes 131104 | tf_op jit(solution)/shard_map/ppermute | solution.py:38
  95.8 4.9 %collective-permute-start.10 = (bf16[2,1,1,1,1,1,1,64,512]{8,7,6,5,4,3,2,1,0:T(8,128)(2,1)S(1)}, bf16[2,1,1,1,1,1,1,64,512]{8,7,6,5,4,3,2,1,0:T(8,128)(2,1)S(1)}, u32[]{:S(2)}, u32[]{:S(2)}) collective-permute-start(bf16[2,1,1,1,1,1,1,64,512]{8,7,6,5,4,3,2,1,0:T(8,128)(2,1)S(1)} %pad_maximum_fusion.16), channel_id=1, source_target_pairs={{0,128},{8,136},{16,144},{24,152},{32,160},{40,168},{48,176},{56,1... | collective-permute-start | bytes 393224 | tf_op jit(solution)/shard_map/ppermute | solution.py:38
  100.8 8.8 %collective-permute-start.17 = (bf16[2,32,32,64]{3,2,1,0:T(8,128)(2,1)S(1)}, bf16[2,32,32,64]{3,2,1,0:T(8,128)(2,1)S(1)}, u32[]{:S(2)}, u32[]{:S(2)}) collective-permute-start(bf16[2,32,32,64]{3,2,1,0:T(8,128)(2,1)S(1)} %pad_maximum_fusion.9), channel_id=1, source_target_pairs={{0,32},{8,232},{16,48},{24,248},{32,64},{40,8},{48,80},{56,24},{64... | collective-permute-start | bytes 786440 | tf_op jit(solution)/shard_map/ppermute | solution.py:210
  109.7 9.3 %collective-permute-done.17 = bf16[2,32,32,64]{3,2,1,0:T(8,128)(2,1)S(1)} collective-permute-done((bf16[2,32,32,64]{3,2,1,0:T(8,128)(2,1)S(1)}, bf16[2,32,32,64]{3,2,1,0:T(8,128)(2,1)S(1)}, u32[]{:S(2)}, u32[]{:S(2)}) %collective-permute-start.17) | collective-permute-done | bytes 262176 | tf_op jit(solution)/shard_map/ppermute | solution.py:210
  122.8 3.6 %collective-permute-start.12 = (bf16[2,2,2,1,1,1,1,64,512]{8,7,6,5,4,3,2,1,0:T(8,128)(2,1)}, bf16[2,2,2,1,1,1,1,64,512]{8,7,6,5,4,3,2,1,0:T(8,128)(2,1)}, u32[]{:S(2)}, u32[]{:S(2)}) collective-permute-start(bf16[2,2,2,1,1,1,1,64,512]{8,7,6,5,4,3,2,1,0:T(8,128)(2,1)} %pad_maximum_fusion.7), channel_id=1, source_target_pairs={{0,32},{8,24},{16,48},{24,8},{32,0},{40,56},{48,16},{56,40},{64,96... | collective-permute-start | bytes 1572872 | tf_op jit(solution)/shard_map/ppermute | solution.py:38
  126.4 10.8 %collective-permute-done.18 = bf16[2,32,32,64]{3,2,1,0:T(8,128)(2,1)S(1)} collective-permute-done((bf16[2,32,32,64]{3,2,1,0:T(8,128)(2,1)}, bf16[2,32,32,64]{3,2,1,0:T(8,128)(2,1)S(1)}, u32[]{:S(2)}, u32[]{:S(2)}) %collective-permute-start.18) | collective-permute-done | bytes 262176 | tf_op jit(solution)/shard_map/ppermute | solution.py:210
  137.5 14.1 %collective-permute-done.12 = bf16[2,2,2,1,1,1,1,64,512]{8,7,6,5,4,3,2,1,0:T(8,128)(2,1)} collective-permute-done((bf16[2,2,2,1,1,1,1,64,512]{8,7,6,5,4,3,2,1,0:T(8,128)(2,1)}, bf16[2,2,2,1,1,1,1,64,512]{8,7,6,5,4,3,2,1,0:T(8,128)(2,1)}, u32[]{:S(2)}, u32[]{:S(2)}) %collective-permute-start.12) | collective-permute-done | bytes 524320 | tf_op jit(solution)/shard_map/ppermute | solution.py:38
  153.9 12.1 %collective-permute-done.19 = bf16[2,32,32,64]{3,2,1,0:T(8,128)(2,1)} collective-permute-done((bf16[2,32,32,64]{3,2,1,0:T(8,128)(2,1)S(1)}, bf16[2,32,32,64]{3,2,1,0:T(8,128)(2,1)}, u32[]{:S(2)}, u32[]{:S(2)}) %collective-permute-start.19) | collective-permute-done | bytes 262176 | tf_op jit(solution)/shard_map/ppermute | solution.py:210
  170.3 5.0 %collective-permute-done.20 = bf16[2,1,1,1,64,1024]{5,4,3,2,1,0:T(8,128)(2,1)S(1)} collective-permute-done((bf16[2,1,1,1,64,1024]{5,4,3,2,1,0:T(8,128)(2,1)S(1)}, bf16[2,1,1,1,64,1024]{5,4,3,2,1,0:T(8,128)(2,1)S(1)}, u32[]{:S(2)}, u32[]{:S(2)}) %collective-permute-start.20) | collective-permute-done | bytes 262176 | tf_op jit(solution)/shard_map/ppermute | solution.py:18
  182.2 5.1 %collective-permute-done.21 = bf16[2,1,1,2,64,1024]{5,4,3,2,1,0:T(8,128)(2,1)} collective-permute-done((bf16[2,1,1,2,64,1024]{5,4,3,2,1,0:T(8,128)(2,1)}, bf16[2,1,1,2,64,1024]{5,4,3,2,1,0:T(8,128)(2,1)}, u32[]{:S(2)}, u32[]{:S(2)}) %collective-permute-start.21) | collective-permute-done | bytes 524320 | tf_op jit(solution)/shard_map/ppermute | solution.py:18
  191.9 23.8 %collective-permute-done.22 = bf16[2,2,1,2,64,1024]{5,4,3,2,1,0:T(8,128)(2,1)} collective-permute-done((bf16[2,2,1,2,64,1024]{5,4,3,2,1,0:T(8,128)(2,1)}, bf16[2,2,1,2,64,1024]{5,4,3,2,1,0:T(8,128)(2,1)}, u32[]{:S(2)}, u32[]{:S(2)}) %collective-permute-start.22) | collective-permute-done | bytes 1048608 | tf_op jit(solution)/shard_map/ppermute | solution.py:18
  218.7 10.1 %collective-permute-done.14 = bf16[2,2,2,2,2,1,1,64,512]{8,7,6,5,4,3,2,1,0:T(8,128)(2,1)} collective-permute-done((bf16[2,2,2,2,2,1,1,64,512]{8,7,6,5,4,3,2,1,0:T(8,128)(2,1)}, bf16[2,2,2,2,2,1,1,64,512]{8,7,6,5,4,3,2,1,0:T(8,128)(2,1)}, u32[]{:S(2)}, u32[]{:S(2)}) %collective-permute-start.14) | collective-permute-done | bytes 2097184 | tf_op jit(solution)/shard_map/ppermute | solution.py:38
  233.0 11.6 %shard_map.73 = bf16[2,64,1024]{2,1,0:T(8,128)(2,1)} custom-call(s32[32]{0:T(128)} %q_ref.1, bf16[2,32,64,512]{3,2,1,0:T(8,128)(2,1)} %bitcast.256, bf16[2,512,1024]{2,1,0:T(8,128)(2,1)} %bitcast.262), custom_call_target="tpu_custom_call" | custom-call | flops 4294967296 | bytes 6553600 | tf_op jit(solution)/shard_map/pallas_call | solution.py:137
  246.5 3.9 %collective-permute-start.29 = (f32[4,32,128]{2,1,0:T(8,128)S(1)}, f32[4,32,128]{2,1,0:T(8,128)S(1)}, u32[]{:S(2)}, u32[]{:S(2)}) collective-permute-start(f32[4,32,128]{2,1,0:T(8,128)S(1)} %get-tuple-element.24), channel_id=1, source_target_pairs={{0,7},{1,6},{2,5},{3,4},{4,3},{5,2},{6,1},{7,0},{8,15},{9,14},{10,... | collective-permute-start | bytes 196616 | tf_op jit(solution)/shard_map/ppermute | solution.py:18
  267.8 3.6 %collective-permute-start.32 = (f32[4,32,128]{2,1,0:T(8,128)S(1)}, f32[4,32,128]{2,1,0:T(8,128)S(1)}, u32[]{:S(2)}, u32[]{:S(2)}) collective-permute-start(f32[4,32,128]{2,1,0:T(8,128)S(1)} %get-tuple-element.6), channel_id=1, source_target_pairs={{0,3},{1,2},{2,1},{3,0},{4,7},{5,6},{6,5},{7,4},{8,11},{9,10},{10,... | collective-permute-start | bytes 196616 | tf_op jit(solution)/shard_map/ppermute | solution.py:18
  272.4 3.4 %collective-permute-start.34 = (f32[4,32,128]{2,1,0:T(8,128)S(1)}, f32[4,32,128]{2,1,0:T(8,128)S(1)}, u32[]{:S(2)}, u32[]{:S(2)}) collective-permute-start(f32[4,32,128]{2,1,0:T(8,128)S(1)} %get-tuple-element.6), channel_id=1, source_target_pairs={{0,5},{1,4},{2,7},{3,6},{4,1},{5,0},{6,3},{7,2},{8,13},{9,12},{10,... | collective-permute-start | bytes 196616 | tf_op jit(solution)/shard_map/ppermute | solution.py:18
  277.0 3.7 %collective-permute-start.36 = (f32[4,32,128]{2,1,0:T(8,128)S(1)}, f32[4,32,128]{2,1,0:T(8,128)S(1)}, u32[]{:S(2)}, u32[]{:S(2)}) collective-permute-start(f32[4,32,128]{2,1,0:T(8,128)S(1)} %get-tuple-element.6), channel_id=1, source_target_pairs={{0,7},{1,6},{2,5},{3,4},{4,3},{5,2},{6,1},{7,0},{8,15},{9,14},{10,... | collective-permute-start | bytes 196616 | tf_op jit(solution)/shard_map/ppermute | solution.py:18
  (168 shorter events, 81.8 us)
Async XLA Ops:
  1.0 13.6 %collective-permute-start.5 = (s32[2,2,2,2,1,1,512]{6,4,3,2,1,0,5:T(1,128)S(1)}, s32[2,2,2,2,1,1,512]{6,4,3,2,1,0,5:T(1,128)S(1)}, u32[]{:S(2)}, u32[]{:S(2)}) collective-permute-start(s32[2,2,2,2,1,1,512]{6,4,3,2,1,0,5:T(1,128)S(1)} %constant_dynamic-slice_fusion.12), channel_id=1, source_target_pairs={{0,8},{8,0},{16,40},{24,32},{32,24},{40,16},{48,56},{56,48},{64,72... | collective-permute-start | bytes 98312 | tf_op jit(solution)/shard_map/ppermute | solution.py:38
  5.6 26.6 %collective-permute-start = (bf16[2,2,2,2,1,1,64,512]{7,6,4,3,2,1,0,5:T(8,128)(2,1)}, bf16[2,2,2,2,1,1,64,512]{7,6,4,3,2,1,0,5:T(8,128)(2,1)}, u32[]{:S(2)}, u32[]{:S(2)}) collective-permute-start(bf16[2,2,2,2,1,1,64,512]{7,6,4,3,2,1,0,5:T(8,128)(2,1)} %constant_dynamic-slice_fusion.15), channel_id=1, source_target_pairs={{0,8},{8,0},{16,40},{24,32},{32,24},{40,16},{48,56},{56,48},{64,72... | collective-permute-start | bytes 3145736 | tf_op jit(solution)/shard_map/ppermute | solution.py:38
  14.7 17.2 %collective-permute-start.6 = (s32[2,2,2,2,1,1,1,512]{7,5,6,4,3,2,1,0:T(1,128)S(1)}, s32[2,2,2,2,1,1,1,512]{7,5,6,4,3,2,1,0:T(1,128)S(1)}, u32[]{:S(2)}, u32[]{:S(2)}) collective-permute-start(s32[2,2,2,2,1,1,1,512]{7,5,6,4,3,2,1,0:T(1,128)S(1)} %pad_add_fusion), channel_id=1, source_target_pairs={{0,16},{8,40},{16,0},{24,56},{32,48},{40,8},{48,32},{56,24},{64,80... | collective-permute-start | bytes 98312 | tf_op jit(solution)/shard_map/ppermute | solution.py:38
  36.5 18.2 %collective-permute-start.1 = (bf16[2,2,2,2,1,1,1,64,512]{8,7,1,3,2,6,5,4,0:T(8,128)(2,1)}, bf16[2,2,2,2,1,1,1,64,512]{8,7,1,3,2,6,5,4,0:T(8,128)(2,1)}, u32[]{:S(2)}, u32[]{:S(2)}) collective-permute-start(bf16[2,2,2,2,1,1,1,64,512]{8,7,1,3,2,6,5,4,0:T(8,128)(2,1)} %pad_maximum_fusion.3), channel_id=1, source_target_pairs={{0,16},{8,40},{16,0},{24,56},{32,48},{40,8},{48,32},{56,24},{64,80... | collective-permute-start | bytes 3145736 | tf_op jit(solution)/shard_map/ppermute | solution.py:38
  42.6 44.6 %collective-permute-start.15 = (bf16[32,32,64]{2,1,0:T(8,128)(2,1)S(1)}, bf16[32,32,64]{2,1,0:T(8,128)(2,1)S(1)}, u32[]{:S(2)}, u32[]{:S(2)}) collective-permute-start(bf16[32,32,64]{2,1,0:T(8,128)(2,1)S(1)} %convolution_convert_fusion), channel_id=1, source_target_pairs={{0,8},{8,16},{16,24},{24,32},{32,40},{40,48},{48,56},{56,64},{64,7... | collective-permute-start | bytes 393224 | tf_op jit(solution)/shard_map/ppermute | solution.py:13
  57.1 11.4 %collective-permute-start.2 = (bf16[2,2,2,1,1,1,1,64,512]{8,7,1,2,6,5,4,3,0:T(8,128)(2,1)S(1)}, bf16[2,2,2,1,1,1,1,64,512]{8,7,1,2,6,5,4,3,0:T(8,128)(2,1)S(1)}, u32[]{:S(2)}, u32[]{:S(2)}) collective-permute-start(bf16[2,2,2,1,1,1,1,64,512]{8,7,1,2,6,5,4,3,0:T(8,128)(2,1)S(1)} %pad_maximum_fusion.6), channel_id=1, source_target_pairs={{0,32},{8,24},{16,48},{24,8},{32,0},{40,56},{48,16},{56,40},{64,96... | collective-permute-start | bytes 1572872 | tf_op jit(solution)/shard_map/ppermute | solution.py:38
  58.9 17.3 %collective-permute-start.9 = (s32[2,1,1,1,1,1,1,512]{7,6,5,4,3,2,1,0:T(1,128)S(1)}, s32[2,1,1,1,1,1,1,512]{7,6,5,4,3,2,1,0:T(1,128)S(1)}, u32[]{:S(2)}, u32[]{:S(2)}) collective-permute-start(s32[2,1,1,1,1,1,1,512]{7,6,5,4,3,2,1,0:T(1,128)S(1)} %pad_add_fusion.3), channel_id=1, source_target_pairs={{0,128},{8,136},{16,144},{24,152},{32,160},{40,168},{48,176},{56,1... | collective-permute-start | bytes 12296 | tf_op jit(solution)/shard_map/ppermute | solution.py:38
  68.7 11.8 %collective-permute-start.3 = (bf16[2,2,1,1,1,1,1,64,512]{8,7,1,6,5,4,3,2,0:T(8,128)(2,1)S(1)}, bf16[2,2,1,1,1,1,1,64,512]{8,7,1,6,5,4,3,2,0:T(8,128)(2,1)S(1)}, u32[]{:S(2)}, u32[]{:S(2)}) collective-permute-start(bf16[2,2,1,1,1,1,1,64,512]{8,7,1,6,5,4,3,2,0:T(8,128)(2,1)S(1)} %pad_maximum_fusion.13), channel_id=1, source_target_pairs={{0,64},{8,72},{16,80},{24,88},{32,96},{40,104},{48,112},{56,120},{... | collective-permute-start | bytes 786440 | tf_op jit(solution)/shard_map/ppermute | solution.py:38
  80.6 14.4 %collective-permute-start.4 = (bf16[2,1,1,1,1,1,1,64,512]{8,7,6,5,4,3,2,1,0:T(8,128)(2,1)S(1)}, bf16[2,1,1,1,1,1,1,64,512]{8,7,6,5,4,3,2,1,0:T(8,128)(2,1)S(1)}, u32[]{:S(2)}, u32[]{:S(2)}) collective-permute-start(bf16[2,1,1,1,1,1,1,64,512]{8,7,6,5,4,3,2,1,0:T(8,128)(2,1)S(1)} %pad_maximum_fusion.15), channel_id=1, source_target_pairs={{0,128},{8,136},{16,144},{24,152},{32,160},{40,168},{48,176},{56,1... | collective-permute-start | bytes 393224 | tf_op jit(solution)/shard_map/ppermute | solution.py:38
  87.3 13.3 %collective-permute-start.16 = (bf16[2,32,32,64]{3,2,1,0:T(8,128)(2,1)S(1)}, bf16[2,32,32,64]{3,2,1,0:T(8,128)(2,1)S(1)}, u32[]{:S(2)}, u32[]{:S(2)}) collective-permute-start(bf16[2,32,32,64]{3,2,1,0:T(8,128)(2,1)S(1)} %pad_maximum_fusion.8), channel_id=1, source_target_pairs={{0,16},{8,248},{16,32},{24,8},{32,48},{40,24},{48,64},{56,40},{64,... | collective-permute-start | bytes 786440 | tf_op jit(solution)/shard_map/ppermute | solution.py:210
  95.8 13.8 %collective-permute-start.10 = (bf16[2,1,1,1,1,1,1,64,512]{8,7,6,5,4,3,2,1,0:T(8,128)(2,1)S(1)}, bf16[2,1,1,1,1,1,1,64,512]{8,7,6,5,4,3,2,1,0:T(8,128)(2,1)S(1)}, u32[]{:S(2)}, u32[]{:S(2)}) collective-permute-start(bf16[2,1,1,1,1,1,1,64,512]{8,7,6,5,4,3,2,1,0:T(8,128)(2,1)S(1)} %pad_maximum_fusion.16), channel_id=1, source_target_pairs={{0,128},{8,136},{16,144},{24,152},{32,160},{40,168},{48,176},{56,1... | collective-permute-start | bytes 393224 | tf_op jit(solution)/shard_map/ppermute | solution.py:38
  100.8 18.3 %collective-permute-start.17 = (bf16[2,32,32,64]{3,2,1,0:T(8,128)(2,1)S(1)}, bf16[2,32,32,64]{3,2,1,0:T(8,128)(2,1)S(1)}, u32[]{:S(2)}, u32[]{:S(2)}) collective-permute-start(bf16[2,32,32,64]{3,2,1,0:T(8,128)(2,1)S(1)} %pad_maximum_fusion.9), channel_id=1, source_target_pairs={{0,32},{8,232},{16,48},{24,248},{32,64},{40,8},{48,80},{56,24},{64... | collective-permute-start | bytes 786440 | tf_op jit(solution)/shard_map/ppermute | solution.py:210
  109.6 12.3 %collective-permute-start.11 = (bf16[2,2,1,1,1,1,1,64,512]{8,7,6,5,4,3,2,1,0:T(8,128)(2,1)S(1)}, bf16[2,2,1,1,1,1,1,64,512]{8,7,6,5,4,3,2,1,0:T(8,128)(2,1)S(1)}, u32[]{:S(2)}, u32[]{:S(2)}) collective-permute-start(bf16[2,2,1,1,1,1,1,64,512]{8,7,6,5,4,3,2,1,0:T(8,128)(2,1)S(1)} %pad_maximum_fusion.14), channel_id=1, source_target_pairs={{0,64},{8,72},{16,80},{24,88},{32,96},{40,104},{48,112},{56,120},{... | collective-permute-start | bytes 786440 | tf_op jit(solution)/shard_map/ppermute | solution.py:38
  120.1 17.2 %collective-permute-start.18 = (bf16[2,32,32,64]{3,2,1,0:T(8,128)(2,1)}, bf16[2,32,32,64]{3,2,1,0:T(8,128)(2,1)S(1)}, u32[]{:S(2)}, u32[]{:S(2)}) collective-permute-start(bf16[2,32,32,64]{3,2,1,0:T(8,128)(2,1)} %pad_maximum_fusion.10), channel_id=1, source_target_pairs={{0,64},{8,200},{16,80},{24,216},{32,96},{40,232},{48,112},{56,248}... | collective-permute-start | bytes 786440 | tf_op jit(solution)/shard_map/ppermute | solution.py:210
  122.8 28.8 %collective-permute-start.12 = (bf16[2,2,2,1,1,1,1,64,512]{8,7,6,5,4,3,2,1,0:T(8,128)(2,1)}, bf16[2,2,2,1,1,1,1,64,512]{8,7,6,5,4,3,2,1,0:T(8,128)(2,1)}, u32[]{:S(2)}, u32[]{:S(2)}) collective-permute-start(bf16[2,2,2,1,1,1,1,64,512]{8,7,6,5,4,3,2,1,0:T(8,128)(2,1)} %pad_maximum_fusion.7), channel_id=1, source_target_pairs={{0,32},{8,24},{16,48},{24,8},{32,0},{40,56},{48,16},{56,40},{64,96... | collective-permute-start | bytes 1572872 | tf_op jit(solution)/shard_map/ppermute | solution.py:38
  137.4 28.5 %collective-permute-start.19 = (bf16[2,32,32,64]{3,2,1,0:T(8,128)(2,1)S(1)}, bf16[2,32,32,64]{3,2,1,0:T(8,128)(2,1)}, u32[]{:S(2)}, u32[]{:S(2)}) collective-permute-start(bf16[2,32,32,64]{3,2,1,0:T(8,128)(2,1)S(1)} %pad_maximum_fusion.11), channel_id=1, source_target_pairs={{0,128},{8,136},{16,144},{24,152},{32,160},{40,168},{48,176},{56,1... | collective-permute-start | bytes 786440 | tf_op jit(solution)/shard_map/ppermute | solution.py:210
  153.9 25.4 %collective-permute-start.13 = (bf16[2,2,2,2,1,1,1,64,512]{8,7,6,5,4,3,2,1,0:T(8,128)(2,1)}, bf16[2,2,2,2,1,1,1,64,512]{8,7,6,5,4,3,2,1,0:T(8,128)(2,1)}, u32[]{:S(2)}, u32[]{:S(2)}) collective-permute-start(bf16[2,2,2,2,1,1,1,64,512]{8,7,6,5,4,3,2,1,0:T(8,128)(2,1)} %pad_maximum_fusion.4), channel_id=1, source_target_pairs={{0,16},{8,40},{16,0},{24,56},{32,48},{40,8},{48,32},{56,24},{64,80... | collective-permute-start | bytes 3145736 | tf_op jit(solution)/shard_map/ppermute | solution.py:38
  176.3 11.0 %collective-permute-start.21 = (bf16[2,1,1,2,64,1024]{5,4,3,2,1,0:T(8,128)(2,1)}, bf16[2,1,1,2,64,1024]{5,4,3,2,1,0:T(8,128)(2,1)}, u32[]{:S(2)}, u32[]{:S(2)}) collective-permute-start(bf16[2,1,1,2,64,1024]{5,4,3,2,1,0:T(8,128)(2,1)} %pad_maximum_fusion.12), channel_id=1, source_target_pairs={{0,4},{1,5},{2,6},{3,7},{4,0},{5,1},{6,2},{7,3},{8,12},{9,13},{10,... | collective-permute-start | bytes 1572872 | tf_op jit(solution)/shard_map/ppermute | solution.py:18
  182.2 46.6 %collective-permute-start.14 = (bf16[2,2,2,2,2,1,1,64,512]{8,7,6,5,4,3,2,1,0:T(8,128)(2,1)}, bf16[2,2,2,2,2,1,1,64,512]{8,7,6,5,4,3,2,1,0:T(8,128)(2,1)}, u32[]{:S(2)}, u32[]{:S(2)}) collective-permute-start(bf16[2,2,2,2,2,1,1,64,512]{8,7,6,5,4,3,2,1,0:T(8,128)(2,1)} %pad_maximum_fusion.1), channel_id=1, source_target_pairs={{0,8},{8,0},{16,40},{24,32},{32,24},{40,16},{48,56},{56,48},{64,72... | collective-permute-start | bytes 6291464 | tf_op jit(solution)/shard_map/ppermute | solution.py:38
  190.4 25.3 %collective-permute-start.22 = (bf16[2,2,1,2,64,1024]{5,4,3,2,1,0:T(8,128)(2,1)}, bf16[2,2,1,2,64,1024]{5,4,3,2,1,0:T(8,128)(2,1)}, u32[]{:S(2)}, u32[]{:S(2)}) collective-permute-start(bf16[2,2,1,2,64,1024]{5,4,3,2,1,0:T(8,128)(2,1)} %pad_maximum_fusion.5), channel_id=1, source_target_pairs={{0,2},{1,3},{2,0},{3,1},{4,6},{5,7},{6,4},{7,5},{8,10},{9,11},{10,... | collective-permute-start | bytes 3145736 | tf_op jit(solution)/shard_map/ppermute | solution.py:18
  246.5 11.3 %collective-permute-start.29 = (f32[4,32,128]{2,1,0:T(8,128)S(1)}, f32[4,32,128]{2,1,0:T(8,128)S(1)}, u32[]{:S(2)}, u32[]{:S(2)}) collective-permute-start(f32[4,32,128]{2,1,0:T(8,128)S(1)} %get-tuple-element.24), channel_id=1, source_target_pairs={{0,7},{1,6},{2,5},{3,4},{4,3},{5,2},{6,1},{7,0},{8,15},{9,14},{10,... | collective-permute-start | bytes 196616 | tf_op jit(solution)/shard_map/ppermute | solution.py:18
  250.4 10.0 %collective-permute-start.28 = (f32[4,32,128]{2,1,0:T(8,128)S(1)}, f32[4,32,128]{2,1,0:T(8,128)S(1)}, u32[]{:S(2)}, u32[]{:S(2)}) collective-permute-start(f32[4,32,128]{2,1,0:T(8,128)S(1)} %get-tuple-element.25), channel_id=1, source_target_pairs={{0,6},{1,7},{2,4},{3,5},{4,2},{5,3},{6,0},{7,1},{8,14},{9,15},{10,... | collective-permute-start | bytes 196616 | tf_op jit(solution)/shard_map/ppermute | solution.py:18
  266.4 9.4 %collective-permute-start.30 = (f32[4,32,128]{2,1,0:T(8,128)S(1)}, f32[4,32,128]{2,1,0:T(8,128)S(1)}, u32[]{:S(2)}, u32[]{:S(2)}) collective-permute-start(f32[4,32,128]{2,1,0:T(8,128)S(1)} %get-tuple-element.6), channel_id=1, source_target_pairs={{0,1},{1,0},{2,3},{3,2},{4,5},{5,4},{6,7},{7,6},{8,9},{9,8},{10,11... | collective-permute-start | bytes 196616 | tf_op jit(solution)/shard_map/ppermute | solution.py:18
  267.8 12.9 %collective-permute-start.32 = (f32[4,32,128]{2,1,0:T(8,128)S(1)}, f32[4,32,128]{2,1,0:T(8,128)S(1)}, u32[]{:S(2)}, u32[]{:S(2)}) collective-permute-start(f32[4,32,128]{2,1,0:T(8,128)S(1)} %get-tuple-element.6), channel_id=1, source_target_pairs={{0,3},{1,2},{2,1},{3,0},{4,7},{5,6},{6,5},{7,4},{8,11},{9,10},{10,... | collective-permute-start | bytes 196616 | tf_op jit(solution)/shard_map/ppermute | solution.py:18
  (24 other events, 276.5 us)

commit v5 on v4

--- a/solution.py
+++ b/solution.py
@@ -115,6 +115,17 @@
     return result
 
 
+def gather_flat(value, axis, at):
+    count = lax.axis_size(axis)
+    me = lax.axis_index(axis)
+    shape = value.shape[:at] + (count,) + value.shape[at:]
+    result = jnp.zeros(shape, value.dtype)
+    result = lax.dynamic_update_index_in_dim(result, value, me, at)
+    for mask in range(1, count):
+        result = lax.dynamic_update_index_in_dim(result, swap(value, axis, mask), me ^ mask, at)
+    return result
+
+
 def contract_kernel(block, group, q_ref, perm_ref, mov_ref, out_ref):
     slots, local, waves = perm_ref.shape[1:]
 
@@ -213,11 +224,8 @@
             for i in range(step_count)
         ]
     moving = jnp.stack(moving).reshape(step_count, kpoint_count * vector_count, local_waves)
-    moving = jnp.transpose(moving, (0, 2, 1)).reshape(
-        (step_count,) + (1,) * ga_bits + (local_waves, kpoint_count * vector_count)
-    )
-    ga_order = [0, 2, 1] if ga_bits == 3 else list(range(ga_bits))
-    moving_all = gather_all(moving, "ga", ga_order, lead=1).reshape(
+    moving = jnp.transpose(moving, (0, 2, 1))
+    moving_all = gather_flat(moving, "ga", 1).reshape(
         step_count, plane_waves, kpoint_count * vector_count
     )
 

time: 288 us -> 318 us (1.10)
  the two profiles are of different devices: /device:TPU:32 before, /device:TPU:0 now
where the time goes in v5:
time: 318 us
  waiting for transfers between devices  184 us (58%)
  starting transfers between devices  81.8 us (26%)
  other arithmetic  22.8 us (7%)
  Pallas kernels  11.6 us (4%)
  between operations  8.43 us (3%)
  local copies, waits for them, and re-layouts  7.92 us (2%)
    ppermute x21, waiting for transfers between devices, swap(): return lax.ppermute(value, axis, [(i, i ^ bit) for i in range(count)])  73.2 us
    ppermute x15, waiting for transfers between devices, swap_relabelled(): return lax.ppermute(value, axis, pairs)  67 us
    ppermute x21, starting transfers between devices, swap(): return lax.ppermute(value, axis, [(i, i ^ bit) for i in range(count)])  45.3 us
    ppermute x4, waiting for transfers between devices, body(): hopped = lax.ppermute(jnp.stack(moving), 'ka', pairs)  40.4 us
    ppermute x15, starting transfers between devices, swap_relabelled(): return lax.ppermute(value, axis, pairs)  28.4 us
    pallas_call x1, Pallas kernels, contract(): pl.pallas_call(functools.partial(contract_kernel, block, 8 if slots % 8 =...  11.6 us
    ppermute x4, starting transfers between devices, body(): hopped = lax.ppermute(jnp.stack(moving), 'ka', pairs)  8 us
  transfers between devices with their start and end apart: 41, of which 24 were waited for; matrix products, arithmetic and copies ran while one was open for 6% of the time, Pallas kernels for 0%

profile of v5, /device:TPU:0, one launch (start us, length us, event | category | flops | bytes accessed | tf_op | source)
XLA Modules:
  0.0 317.5 jit_solution(13523886927462780881)
XLA Ops:
  14.7 15.2 %collective-permute-done.6 = s32[2,2,2,2,1,1,1,512]{7,5,6,4,3,2,1,0:T(1,128)S(1)} collective-permute-done((s32[2,2,2,2,1,1,1,512]{7,5,6,4,3,2,1,0:T(1,128)S(1)}, s32[2,2,2,2,1,1,1,512]{7,5,6,4,3,2,1,0:T(1,128)S(1)}, u32[]{:S(2)}, u32[]{:S(2)}) %collective-permute-start.6) | collective-permute-done | bytes 32800 | tf_op jit(solution)/shard_map/ppermute | solution.py:38
  37.0 3.9 %collective-permute-done.7 = s32[2,2,2,1,1,1,1,512]{7,5,6,4,3,2,1,0:T(1,128)S(1)} collective-permute-done((s32[2,2,2,1,1,1,1,512]{7,5,6,4,3,2,1,0:T(1,128)S(1)}, s32[2,2,2,1,1,1,1,512]{7,5,6,4,3,2,1,0:T(1,128)S(1)}, u32[]{:S(2)}, u32[]{:S(2)}) %collective-permute-start.7) | collective-permute-done | bytes 16416 | tf_op jit(solution)/shard_map/ppermute | solution.py:38
  44.3 5.8 %collective-permute-done.1 = bf16[2,2,2,2,1,1,1,64,512]{8,7,1,3,2,6,5,4,0:T(8,128)(2,1)} collective-permute-done((bf16[2,2,2,2,1,1,1,64,512]{8,7,1,3,2,6,5,4,0:T(8,128)(2,1)}, bf16[2,2,2,2,1,1,1,64,512]{8,7,1,3,2,6,5,4,0:T(8,128)(2,1)}, u32[]{:S(2)}, u32[]{:S(2)}) %collective-permute-start.1) | collective-permute-done | bytes 1048608 | tf_op jit(solution)/shard_map/ppermute | solution.py:38
  54.2 7.6 %collective-permute-done.2 = bf16[2,2,2,1,1,1,1,64,512]{8,7,1,2,6,5,4,3,0:T(8,128)(2,1)S(1)} collective-permute-done((bf16[2,2,2,1,1,1,1,64,512]{8,7,1,2,6,5,4,3,0:T(8,128)(2,1)S(1)}, bf16[2,2,2,1,1,1,1,64,512]{8,7,1,2,6,5,4,3,0:T(8,128)(2,1)S(1)}, u32[]{:S(2)}, u32[]{:S(2)}) %collective-permute-start.2) | collective-permute-done | bytes 524320 | tf_op jit(solution)/shard_map/ppermute | solution.py:38
  65.2 5.1 %collective-permute-start.9 = (s32[2,1,1,1,1,1,1,512]{7,6,5,4,3,2,1,0:T(1,128)S(1)}, s32[2,1,1,1,1,1,1,512]{7,6,5,4,3,2,1,0:T(1,128)S(1)}, u32[]{:S(2)}, u32[]{:S(2)}) collective-permute-start(s32[2,1,1,1,1,1,1,512]{7,6,5,4,3,2,1,0:T(1,128)S(1)} %pad_add_fusion.3), channel_id=1, source_target_pairs={{0,128},{8,136},{16,144},{24,152},{32,160},{40,168},{48,176},{56,1... | collective-permute-start | bytes 12296 | tf_op jit(solution)/shard_map/ppermute | solution.py:38
  70.2 5.4 %collective-permute-done.9 = s32[2,1,1,1,1,1,1,512]{7,6,5,4,3,2,1,0:T(1,128)S(1)} collective-permute-done((s32[2,1,1,1,1,1,1,512]{7,6,5,4,3,2,1,0:T(1,128)S(1)}, s32[2,1,1,1,1,1,1,512]{7,6,5,4,3,2,1,0:T(1,128)S(1)}, u32[]{:S(2)}, u32[]{:S(2)}) %collective-permute-start.9) | collective-permute-done | bytes 4128 | tf_op jit(solution)/shard_map/ppermute | solution.py:38
  76.8 6.1 %collective-permute-start.4 = (bf16[2,1,1,1,1,1,1,64,512]{8,7,6,5,4,3,2,1,0:T(8,128)(2,1)S(1)}, bf16[2,1,1,1,1,1,1,64,512]{8,7,6,5,4,3,2,1,0:T(8,128)(2,1)S(1)}, u32[]{:S(2)}, u32[]{:S(2)}) collective-permute-start(bf16[2,1,1,1,1,1,1,64,512]{8,7,6,5,4,3,2,1,0:T(8,128)(2,1)S(1)} %pad_maximum_fusion.13), channel_id=1, source_target_pairs={{0,128},{8,136},{16,144},{24,152},{32,160},{40,168},{48,176},{56,1... | collective-permute-start | bytes 393224 | tf_op jit(solution)/shard_map/ppermute | solution.py:38
  82.9 5.8 %collective-permute-done.4 = bf16[2,1,1,1,1,1,1,64,512]{8,7,6,5,4,3,2,1,0:T(8,128)(2,1)S(1)} collective-permute-done((bf16[2,1,1,1,1,1,1,64,512]{8,7,6,5,4,3,2,1,0:T(8,128)(2,1)S(1)}, bf16[2,1,1,1,1,1,1,64,512]{8,7,6,5,4,3,2,1,0:T(8,128)(2,1)S(1)}, u32[]{:S(2)}, u32[]{:S(2)}) %collective-permute-start.4) | collective-permute-done | bytes 131104 | tf_op jit(solution)/shard_map/ppermute | solution.py:38
  89.4 3.6 %collective-permute-start.10 = (bf16[2,1,1,1,1,1,1,64,512]{8,7,6,5,4,3,2,1,0:T(8,128)(2,1)S(1)}, bf16[2,1,1,1,1,1,1,64,512]{8,7,6,5,4,3,2,1,0:T(8,128)(2,1)S(1)}, u32[]{:S(2)}, u32[]{:S(2)}) collective-permute-start(bf16[2,1,1,1,1,1,1,64,512]{8,7,6,5,4,3,2,1,0:T(8,128)(2,1)S(1)} %pad_maximum_fusion.14), channel_id=1, source_target_pairs={{0,128},{8,136},{16,144},{24,152},{32,160},{40,168},{48,176},{56,1... | collective-permute-start | bytes 393224 | tf_op jit(solution)/shard_map/ppermute | solution.py:38
  93.6 6.3 %collective-permute-done.10 = bf16[2,1,1,1,1,1,1,64,512]{8,7,6,5,4,3,2,1,0:T(8,128)(2,1)S(1)} collective-permute-done((bf16[2,1,1,1,1,1,1,64,512]{8,7,6,5,4,3,2,1,0:T(8,128)(2,1)S(1)}, bf16[2,1,1,1,1,1,1,64,512]{8,7,6,5,4,3,2,1,0:T(8,128)(2,1)S(1)}, u32[]{:S(2)}, u32[]{:S(2)}) %collective-permute-start.10) | collective-permute-done | bytes 131104 | tf_op jit(solution)/shard_map/ppermute | solution.py:38
  103.6 8.7 %collective-permute-done.11 = bf16[2,2,1,1,1,1,1,64,512]{8,7,6,5,4,3,2,1,0:T(8,128)(2,1)S(1)} collective-permute-done((bf16[2,2,1,1,1,1,1,64,512]{8,7,6,5,4,3,2,1,0:T(8,128)(2,1)S(1)}, bf16[2,2,1,1,1,1,1,64,512]{8,7,6,5,4,3,2,1,0:T(8,128)(2,1)S(1)}, u32[]{:S(2)}, u32[]{:S(2)}) %collective-permute-start.11) | collective-permute-done | bytes 262176 | tf_op jit(solution)/shard_map/ppermute | solution.py:38
  113.7 4.8 %collective-permute-done.16 = bf16[2,32,32,64]{3,2,1,0:T(8,128)(2,1)S(1)} collective-permute-done((bf16[2,32,32,64]{3,2,1,0:T(8,128)(2,1)S(1)}, bf16[2,32,32,64]{3,2,1,0:T(8,128)(2,1)S(1)}, u32[]{:S(2)}, u32[]{:S(2)}) %collective-permute-start.16) | collective-permute-done | bytes 262176 | tf_op jit(solution)/shard_map/ppermute | solution.py:221
  119.5 7.4 %collective-permute-done.12 = bf16[2,2,2,1,1,1,1,64,512]{8,7,6,5,4,3,2,1,0:T(8,128)(2,1)} collective-permute-done((bf16[2,2,2,1,1,1,1,64,512]{8,7,6,5,4,3,2,1,0:T(8,128)(2,1)S(1)}, bf16[2,2,2,1,1,1,1,64,512]{8,7,6,5,4,3,2,1,0:T(8,128)(2,1)}, u32[]{:S(2)}, u32[]{:S(2)}) %collective-permute-start.12) | collective-permute-done | bytes 524320 | tf_op jit(solution)/shard_map/ppermute | solution.py:38
  135.6 23.7 %collective-permute-done.18 = bf16[2,32,32,64]{3,2,1,0:T(8,128)(2,1)S(1)} collective-permute-done((bf16[2,32,32,64]{3,2,1,0:T(8,128)(2,1)}, bf16[2,32,32,64]{3,2,1,0:T(8,128)(2,1)S(1)}, u32[]{:S(2)}, u32[]{:S(2)}) %collective-permute-start.18) | collective-permute-done | bytes 262176 | tf_op jit(solution)/shard_map/ppermute | solution.py:221
  160.5 4.3 %collective-permute-start.19 = (bf16[2,32,32,64]{3,2,1,0:T(8,128)(2,1)S(1)}, bf16[2,32,32,64]{3,2,1,0:T(8,128)(2,1)S(1)}, u32[]{:S(2)}, u32[]{:S(2)}) collective-permute-start(bf16[2,32,32,64]{3,2,1,0:T(8,128)(2,1)S(1)} %pad_maximum_fusion.9), channel_id=1, source_target_pairs={{0,128},{8,136},{16,144},{24,152},{32,160},{40,168},{48,176},{56,1... | collective-permute-start | bytes 786440 | tf_op jit(solution)/shard_map/ppermute | solution.py:221
  167.6 10.9 %collective-permute-done.19 = bf16[2,32,32,64]{3,2,1,0:T(8,128)(2,1)S(1)} collective-permute-done((bf16[2,32,32,64]{3,2,1,0:T(8,128)(2,1)S(1)}, bf16[2,32,32,64]{3,2,1,0:T(8,128)(2,1)S(1)}, u32[]{:S(2)}, u32[]{:S(2)}) %collective-permute-start.19) | collective-permute-done | bytes 262176 | tf_op jit(solution)/shard_map/ppermute | solution.py:221
  178.9 3.5 %collective-permute-start.20 = (bf16[2,64,1024]{2,1,0:T(8,128)(2,1)S(1)}, bf16[2,64,1024]{2,1,0:T(8,128)(2,1)S(1)}, u32[]{:S(2)}, u32[]{:S(2)}) collective-permute-start(bf16[2,64,1024]{2,1,0:T(8,128)(2,1)S(1)} %fusion.22), channel_id=1, source_target_pairs={{0,1},{1,0},{2,3},{3,2},{4,5},{5,4},{6,7},{7,6},{8,9},{9,8},{10,11... | collective-permute-start | bytes 786440 | tf_op jit(solution)/shard_map/ppermute | solution.py:18
  187.4 53.8 %collective-permute-done.20 = bf16[2,64,1024]{2,1,0:T(8,128)(2,1)S(1)} collective-permute-done((bf16[2,64,1024]{2,1,0:T(8,128)(2,1)S(1)}, bf16[2,64,1024]{2,1,0:T(8,128)(2,1)S(1)}, u32[]{:S(2)}, u32[]{:S(2)}) %collective-permute-start.20) | collective-permute-done | bytes 262176 | tf_op jit(solution)/shard_map/ppermute | solution.py:18
  244.5 5.0 %collective-permute-start.26 = (bf16[2,64,1024]{2,1,0:T(8,128)(2,1)S(1)}, bf16[2,64,1024]{2,1,0:T(8,128)(2,1)S(1)}, u32[]{:S(2)}, u32[]{:S(2)}) collective-permute-start(bf16[2,64,1024]{2,1,0:T(8,128)(2,1)S(1)} %fusion.22), channel_id=1, source_target_pairs={{0,7},{1,6},{2,5},{3,4},{4,3},{5,2},{6,1},{7,0},{8,15},{9,14},{10,... | collective-permute-start | bytes 786440 | tf_op jit(solution)/shard_map/ppermute | solution.py:18
  253.2 6.2 %collective-permute-done.26 = bf16[2,64,1024]{2,1,0:T(8,128)(2,1)S(1)} collective-permute-done((bf16[2,64,1024]{2,1,0:T(8,128)(2,1)S(1)}, bf16[2,64,1024]{2,1,0:T(8,128)(2,1)S(1)}, u32[]{:S(2)}, u32[]{:S(2)}) %collective-permute-start.26) | collective-permute-done | bytes 262176 | tf_op jit(solution)/shard_map/ppermute | solution.py:18
  264.4 11.6 %shard_map.73 = bf16[2,64,1024]{2,1,0:T(8,128)(2,1)} custom-call(s32[32]{0:T(128)} %q_ref.1, bf16[2,32,64,512]{3,2,1,0:T(8,128)(2,1)} %bitcast.281, bf16[2,512,1024]{2,1,0:T(8,128)(2,1)} %bitcast.287), custom_call_target="tpu_custom_call" | custom-call | flops 4294967296 | bytes 6553600 | tf_op jit(solution)/shard_map/pallas_call | solution.py:148
  281.1 3.4 %collective-permute-start.31 = (f32[4,32,128]{2,1,0:T(8,128)S(1)}, f32[4,32,128]{2,1,0:T(8,128)S(1)}, u32[]{:S(2)}, u32[]{:S(2)}) collective-permute-start(f32[4,32,128]{2,1,0:T(8,128)S(1)} %get-tuple-element.22), channel_id=1, source_target_pairs={{0,5},{1,4},{2,7},{3,6},{4,1},{5,0},{6,3},{7,2},{8,13},{9,12},{10,... | collective-permute-start | bytes 196616 | tf_op jit(solution)/shard_map/ppermute | solution.py:18
  302.1 4.1 %collective-permute-start.38 = (f32[4,32,128]{2,1,0:T(8,128)S(1)}, f32[4,32,128]{2,1,0:T(8,128)S(1)}, u32[]{:S(2)}, u32[]{:S(2)}) collective-permute-start(f32[4,32,128]{2,1,0:T(8,128)S(1)} %get-tuple-element.6), channel_id=1, source_target_pairs={{0,5},{1,4},{2,7},{3,6},{4,1},{5,0},{6,3},{7,2},{8,13},{9,12},{10,... | collective-permute-start | bytes 196616 | tf_op jit(solution)/shard_map/ppermute | solution.py:18
  311.8 4.9 %collective-permute-done.40 = f32[4,32,128]{2,1,0:T(8,128)S(1)} collective-permute-done((f32[4,32,128]{2,1,0:T(8,128)S(1)}, f32[4,32,128]{2,1,0:T(8,128)S(1)}, u32[]{:S(2)}, u32[]{:S(2)}) %collective-permute-start.40) | collective-permute-done | bytes 65568 | tf_op jit(solution)/shard_map/ppermute | solution.py:18
  (177 shorter events, 92.3 us)
Async XLA Ops:
  1.0 11.4 %collective-permute-start.5 = (s32[2,2,2,2,1,1,512]{6,4,3,2,1,0,5:T(1,128)S(1)}, s32[2,2,2,2,1,1,512]{6,4,3,2,1,0,5:T(1,128)S(1)}, u32[]{:S(2)}, u32[]{:S(2)}) collective-permute-start(s32[2,2,2,2,1,1,512]{6,4,3,2,1,0,5:T(1,128)S(1)} %constant_dynamic-slice_fusion.12), channel_id=1, source_target_pairs={{0,8},{8,0},{16,40},{24,32},{32,24},{40,16},{48,56},{56,48},{64,72... | collective-permute-start | bytes 98312 | tf_op jit(solution)/shard_map/ppermute | solution.py:38
  5.0 24.9 %collective-permute-start = (bf16[2,2,2,2,1,1,64,512]{7,6,4,3,2,1,0,5:T(8,128)(2,1)}, bf16[2,2,2,2,1,1,64,512]{7,6,4,3,2,1,0,5:T(8,128)(2,1)}, u32[]{:S(2)}, u32[]{:S(2)}) collective-permute-start(bf16[2,2,2,2,1,1,64,512]{7,6,4,3,2,1,0,5:T(8,128)(2,1)} %constant_dynamic-slice_fusion.15), channel_id=1, source_target_pairs={{0,8},{8,0},{16,40},{24,32},{32,24},{40,16},{48,56},{56,48},{64,72... | collective-permute-start | bytes 3145736 | tf_op jit(solution)/shard_map/ppermute | solution.py:38
  12.6 17.2 %collective-permute-start.6 = (s32[2,2,2,2,1,1,1,512]{7,5,6,4,3,2,1,0:T(1,128)S(1)}, s32[2,2,2,2,1,1,1,512]{7,5,6,4,3,2,1,0:T(1,128)S(1)}, u32[]{:S(2)}, u32[]{:S(2)}) collective-permute-start(s32[2,2,2,2,1,1,1,512]{7,5,6,4,3,2,1,0:T(1,128)S(1)} %pad_add_fusion), channel_id=1, source_target_pairs={{0,16},{8,40},{16,0},{24,56},{32,48},{40,8},{48,32},{56,24},{64,80... | collective-permute-start | bytes 98312 | tf_op jit(solution)/shard_map/ppermute | solution.py:38
  34.2 15.9 %collective-permute-start.1 = (bf16[2,2,2,2,1,1,1,64,512]{8,7,1,3,2,6,5,4,0:T(8,128)(2,1)}, bf16[2,2,2,2,1,1,1,64,512]{8,7,1,3,2,6,5,4,0:T(8,128)(2,1)}, u32[]{:S(2)}, u32[]{:S(2)}) collective-permute-start(bf16[2,2,2,2,1,1,1,64,512]{8,7,1,3,2,6,5,4,0:T(8,128)(2,1)} %pad_maximum_fusion.2), channel_id=1, source_target_pairs={{0,16},{8,40},{16,0},{24,56},{32,48},{40,8},{48,32},{56,24},{64,80... | collective-permute-start | bytes 3145736 | tf_op jit(solution)/shard_map/ppermute | solution.py:38
  41.0 13.1 %collective-permute-start.8 = (s32[2,2,1,1,1,1,1,512]{7,5,6,4,3,2,1,0:T(1,128)S(1)}, s32[2,2,1,1,1,1,1,512]{7,5,6,4,3,2,1,0:T(1,128)S(1)}, u32[]{:S(2)}, u32[]{:S(2)}) collective-permute-start(s32[2,2,1,1,1,1,1,512]{7,5,6,4,3,2,1,0:T(1,128)S(1)} %pad_add_fusion.2), channel_id=1, source_target_pairs={{0,64},{8,72},{16,80},{24,88},{32,96},{40,104},{48,112},{56,120},{... | collective-permute-start | bytes 24584 | tf_op jit(solution)/shard_map/ppermute | solution.py:38
  62.0 14.7 %collective-permute-start.3 = (bf16[2,2,1,1,1,1,1,64,512]{8,7,1,6,5,4,3,2,0:T(8,128)(2,1)S(1)}, bf16[2,2,1,1,1,1,1,64,512]{8,7,1,6,5,4,3,2,0:T(8,128)(2,1)S(1)}, u32[]{:S(2)}, u32[]{:S(2)}) collective-permute-start(bf16[2,2,1,1,1,1,1,64,512]{8,7,1,6,5,4,3,2,0:T(8,128)(2,1)S(1)} %pad_maximum_fusion.10), channel_id=1, source_target_pairs={{0,64},{8,72},{16,80},{24,88},{32,96},{40,104},{48,112},{56,120},{... | collective-permute-start | bytes 786440 | tf_op jit(solution)/shard_map/ppermute | solution.py:38
  76.8 11.8 %collective-permute-start.4 = (bf16[2,1,1,1,1,1,1,64,512]{8,7,6,5,4,3,2,1,0:T(8,128)(2,1)S(1)}, bf16[2,1,1,1,1,1,1,64,512]{8,7,6,5,4,3,2,1,0:T(8,128)(2,1)S(1)}, u32[]{:S(2)}, u32[]{:S(2)}) collective-permute-start(bf16[2,1,1,1,1,1,1,64,512]{8,7,6,5,4,3,2,1,0:T(8,128)(2,1)S(1)} %pad_maximum_fusion.13), channel_id=1, source_target_pairs={{0,128},{8,136},{16,144},{24,152},{32,160},{40,168},{48,176},{56,1... | collective-permute-start | bytes 393224 | tf_op jit(solution)/shard_map/ppermute | solution.py:38
  99.9 12.3 %collective-permute-start.11 = (bf16[2,2,1,1,1,1,1,64,512]{8,7,6,5,4,3,2,1,0:T(8,128)(2,1)S(1)}, bf16[2,2,1,1,1,1,1,64,512]{8,7,6,5,4,3,2,1,0:T(8,128)(2,1)S(1)}, u32[]{:S(2)}, u32[]{:S(2)}) collective-permute-start(bf16[2,2,1,1,1,1,1,64,512]{8,7,6,5,4,3,2,1,0:T(8,128)(2,1)S(1)} %pad_maximum_fusion.11), channel_id=1, source_target_pairs={{0,64},{8,72},{16,80},{24,88},{32,96},{40,104},{48,112},{56,120},{... | collective-permute-start | bytes 786440 | tf_op jit(solution)/shard_map/ppermute | solution.py:38
  103.1 15.4 %collective-permute-start.16 = (bf16[2,32,32,64]{3,2,1,0:T(8,128)(2,1)S(1)}, bf16[2,32,32,64]{3,2,1,0:T(8,128)(2,1)S(1)}, u32[]{:S(2)}, u32[]{:S(2)}) collective-permute-start(bf16[2,32,32,64]{3,2,1,0:T(8,128)(2,1)S(1)} %pad_maximum_fusion.6), channel_id=1, source_target_pairs={{0,16},{8,248},{16,32},{24,8},{32,48},{40,24},{48,64},{56,40},{64,... | collective-permute-start | bytes 786440 | tf_op jit(solution)/shard_map/ppermute | solution.py:221
  112.3 14.6 %collective-permute-start.12 = (bf16[2,2,2,1,1,1,1,64,512]{8,7,6,5,4,3,2,1,0:T(8,128)(2,1)S(1)}, bf16[2,2,2,1,1,1,1,64,512]{8,7,6,5,4,3,2,1,0:T(8,128)(2,1)}, u32[]{:S(2)}, u32[]{:S(2)}) collective-permute-start(bf16[2,2,2,1,1,1,1,64,512]{8,7,6,5,4,3,2,1,0:T(8,128)(2,1)S(1)} %pad_maximum_fusion.5), channel_id=1, source_target_pairs={{0,32},{8,24},{16,48},{24,8},{32,0},{40,56},{48,16},{56,40},{64,96... | collective-permute-start | bytes 1572872 | tf_op jit(solution)/shard_map/ppermute | solution.py:38
  119.5 10.7 %collective-permute-start.17 = (bf16[2,32,32,64]{3,2,1,0:T(8,128)(2,1)}, bf16[2,32,32,64]{3,2,1,0:T(8,128)(2,1)}, u32[]{:S(2)}, u32[]{:S(2)}) collective-permute-start(bf16[2,32,32,64]{3,2,1,0:T(8,128)(2,1)} %pad_maximum_fusion.7), channel_id=1, source_target_pairs={{0,32},{8,232},{16,48},{24,248},{32,64},{40,8},{48,80},{56,24},{64... | collective-permute-start | bytes 786440 | tf_op jit(solution)/shard_map/ppermute | solution.py:221
  129.2 35.5 %collective-permute-start.13 = (bf16[2,2,2,2,1,1,1,64,512]{8,7,6,5,4,3,2,1,0:T(8,128)(2,1)}, bf16[2,2,2,2,1,1,1,64,512]{8,7,6,5,4,3,2,1,0:T(8,128)(2,1)}, u32[]{:S(2)}, u32[]{:S(2)}) collective-permute-start(bf16[2,2,2,2,1,1,1,64,512]{8,7,6,5,4,3,2,1,0:T(8,128)(2,1)} %pad_maximum_fusion.3), channel_id=1, source_target_pairs={{0,16},{8,40},{16,0},{24,56},{32,48},{40,8},{48,32},{56,24},{64,80... | collective-permute-start | bytes 3145736 | tf_op jit(solution)/shard_map/ppermute | solution.py:38
  132.3 27.0 %collective-permute-start.18 = (bf16[2,32,32,64]{3,2,1,0:T(8,128)(2,1)}, bf16[2,32,32,64]{3,2,1,0:T(8,128)(2,1)S(1)}, u32[]{:S(2)}, u32[]{:S(2)}) collective-permute-start(bf16[2,32,32,64]{3,2,1,0:T(8,128)(2,1)} %pad_maximum_fusion.8), channel_id=1, source_target_pairs={{0,64},{8,200},{16,80},{24,216},{32,96},{40,232},{48,112},{56,248}... | collective-permute-start | bytes 786440 | tf_op jit(solution)/shard_map/ppermute | solution.py:221
  160.5 18.1 %collective-permute-start.19 = (bf16[2,32,32,64]{3,2,1,0:T(8,128)(2,1)S(1)}, bf16[2,32,32,64]{3,2,1,0:T(8,128)(2,1)S(1)}, u32[]{:S(2)}, u32[]{:S(2)}) collective-permute-start(bf16[2,32,32,64]{3,2,1,0:T(8,128)(2,1)S(1)} %pad_maximum_fusion.9), channel_id=1, source_target_pairs={{0,128},{8,136},{16,144},{24,152},{32,160},{40,168},{48,176},{56,1... | collective-permute-start | bytes 786440 | tf_op jit(solution)/shard_map/ppermute | solution.py:221
  167.6 91.8 %collective-permute-start.14 = (bf16[2,2,2,2,2,1,1,64,512]{8,7,6,5,4,3,2,1,0:T(8,128)(2,1)}, bf16[2,2,2,2,2,1,1,64,512]{8,7,6,5,4,3,2,1,0:T(8,128)(2,1)}, u32[]{:S(2)}, u32[]{:S(2)}) collective-permute-start(bf16[2,2,2,2,2,1,1,64,512]{8,7,6,5,4,3,2,1,0:T(8,128)(2,1)} %pad_maximum_fusion.1), channel_id=1, source_target_pairs={{0,8},{8,0},{16,40},{24,32},{32,24},{40,16},{48,56},{56,48},{64,72... | collective-permute-start | bytes 6291464 | tf_op jit(solution)/shard_map/ppermute | solution.py:38
  178.9 62.2 %collective-permute-start.20 = (bf16[2,64,1024]{2,1,0:T(8,128)(2,1)S(1)}, bf16[2,64,1024]{2,1,0:T(8,128)(2,1)S(1)}, u32[]{:S(2)}, u32[]{:S(2)}) collective-permute-start(bf16[2,64,1024]{2,1,0:T(8,128)(2,1)S(1)} %fusion.22), channel_id=1, source_target_pairs={{0,1},{1,0},{2,3},{3,2},{4,5},{5,4},{6,7},{7,6},{8,9},{9,8},{10,11... | collective-permute-start | bytes 786440 | tf_op jit(solution)/shard_map/ppermute | solution.py:18
  182.5 60.2 %collective-permute-start.21 = (bf16[2,64,1024]{2,1,0:T(8,128)(2,1)S(1)}, bf16[2,64,1024]{2,1,0:T(8,128)(2,1)S(1)}, u32[]{:S(2)}, u32[]{:S(2)}) collective-permute-start(bf16[2,64,1024]{2,1,0:T(8,128)(2,1)S(1)} %fusion.22), channel_id=1, source_target_pairs={{0,2},{1,3},{2,0},{3,1},{4,6},{5,7},{6,4},{7,5},{8,10},{9,11},{10,... | collective-permute-start | bytes 786440 | tf_op jit(solution)/shard_map/ppermute | solution.py:18
  184.0 60.6 %collective-permute-start.22 = (bf16[2,64,1024]{2,1,0:T(8,128)(2,1)S(1)}, bf16[2,64,1024]{2,1,0:T(8,128)(2,1)S(1)}, u32[]{:S(2)}, u32[]{:S(2)}) collective-permute-start(bf16[2,64,1024]{2,1,0:T(8,128)(2,1)S(1)} %fusion.22), channel_id=1, source_target_pairs={{0,3},{1,2},{2,1},{3,0},{4,7},{5,6},{6,5},{7,4},{8,11},{9,10},{10,... | collective-permute-start | bytes 786440 | tf_op jit(solution)/shard_map/ppermute | solution.py:18
  184.1 65.5 %collective-permute-start.23 = (bf16[2,64,1024]{2,1,0:T(8,128)(2,1)S(1)}, bf16[2,64,1024]{2,1,0:T(8,128)(2,1)S(1)}, u32[]{:S(2)}, u32[]{:S(2)}) collective-permute-start(bf16[2,64,1024]{2,1,0:T(8,128)(2,1)S(1)} %fusion.22), channel_id=1, source_target_pairs={{0,4},{1,5},{2,6},{3,7},{4,0},{5,1},{6,2},{7,3},{8,12},{9,13},{10,... | collective-permute-start | bytes 786440 | tf_op jit(solution)/shard_map/ppermute | solution.py:18
  241.2 10.6 %collective-permute-start.24 = (bf16[2,64,1024]{2,1,0:T(8,128)(2,1)S(1)}, bf16[2,64,1024]{2,1,0:T(8,128)(2,1)S(1)}, u32[]{:S(2)}, u32[]{:S(2)}) collective-permute-start(bf16[2,64,1024]{2,1,0:T(8,128)(2,1)S(1)} %fusion.22), channel_id=1, source_target_pairs={{0,5},{1,4},{2,7},{3,6},{4,1},{5,0},{6,3},{7,2},{8,13},{9,12},{10,... | collective-permute-start | bytes 786440 | tf_op jit(solution)/shard_map/ppermute | solution.py:18
  244.5 14.9 %collective-permute-start.26 = (bf16[2,64,1024]{2,1,0:T(8,128)(2,1)S(1)}, bf16[2,64,1024]{2,1,0:T(8,128)(2,1)S(1)}, u32[]{:S(2)}, u32[]{:S(2)}) collective-permute-start(bf16[2,64,1024]{2,1,0:T(8,128)(2,1)S(1)} %fusion.22), channel_id=1, source_target_pairs={{0,7},{1,6},{2,5},{3,4},{4,3},{5,2},{6,1},{7,0},{8,15},{9,14},{10,... | collective-permute-start | bytes 786440 | tf_op jit(solution)/shard_map/ppermute | solution.py:18
  281.1 11.2 %collective-permute-start.31 = (f32[4,32,128]{2,1,0:T(8,128)S(1)}, f32[4,32,128]{2,1,0:T(8,128)S(1)}, u32[]{:S(2)}, u32[]{:S(2)}) collective-permute-start(f32[4,32,128]{2,1,0:T(8,128)S(1)} %get-tuple-element.22), channel_id=1, source_target_pairs={{0,5},{1,4},{2,7},{3,6},{4,1},{5,0},{6,3},{7,2},{8,13},{9,12},{10,... | collective-permute-start | bytes 196616 | tf_op jit(solution)/shard_map/ppermute | solution.py:18
  295.0 11.3 %collective-permute-start.34 = (f32[4,32,128]{2,1,0:T(8,128)S(1)}, f32[4,32,128]{2,1,0:T(8,128)S(1)}, u32[]{:S(2)}, u32[]{:S(2)}) collective-permute-start(f32[4,32,128]{2,1,0:T(8,128)S(1)} %get-tuple-element.6), channel_id=1, source_target_pairs={{0,1},{1,0},{2,3},{3,2},{4,5},{5,4},{6,7},{7,6},{8,9},{9,8},{10,11... | collective-permute-start | bytes 196616 | tf_op jit(solution)/shard_map/ppermute | solution.py:18
  298.4 10.9 %collective-permute-start.36 = (f32[4,32,128]{2,1,0:T(8,128)S(1)}, f32[4,32,128]{2,1,0:T(8,128)S(1)}, u32[]{:S(2)}, u32[]{:S(2)}) collective-permute-start(f32[4,32,128]{2,1,0:T(8,128)S(1)} %get-tuple-element.6), channel_id=1, source_target_pairs={{0,3},{1,2},{2,1},{3,0},{4,7},{5,6},{6,5},{7,4},{8,11},{9,10},{10,... | collective-permute-start | bytes 196616 | tf_op jit(solution)/shard_map/ppermute | solution.py:18
  (27 other events, 399.2 us)

commit v6 on v4

--- a/solution.py
+++ b/solution.py
@@ -38,11 +38,28 @@
     return lax.ppermute(value, axis, pairs)
 
 
+def lockstep(chains):
+    states = [next(chain) for chain in chains]
+    results = [None] * len(chains)
+    live = list(range(len(chains)))
+    while live:
+        tied = lax.optimization_barrier([states[i] for i in live])
+        still = []
+        for i, state in zip(live, tied):
+            try:
+                states[i] = chains[i].send(state)
+                still.append(i)
+            except StopIteration as stop:
+                results[i] = stop.value
+        live = still
+    return results
+
+
 def pick_half(tree, axis_at, which):
     return jax.tree.map(lambda a: lax.dynamic_slice_in_dim(a, which, 1, axis=axis_at), tree)
 
 
-def scatter_from_roots(own, roots, axis, order):
+def scatter_rounds(own, roots, axis, order):
     nbits = len(order)
     count = lax.axis_size(axis)
     me = relabel(lax.axis_index(axis), count)
@@ -70,13 +87,13 @@
             new_held.append(
                 jax.tree.map(lambda k, g: jnp.where(holder, k, g), keep, got[r])
             )
-        held = new_held
+        held = yield new_held
         shared = False
         done_mask |= 1 << bit
     return held
 
 
-def gather_all(pieces, axis, order, lead=0, relabelled=False):
+def gather_rounds(pieces, axis, order, lead=0, relabelled=False):
     nbits = len(order)
     count = lax.axis_size(axis)
     me = lax.axis_index(axis)
@@ -96,7 +113,7 @@
             high = jnp.where(mine == 0, g, h)
             return jnp.concatenate([low, high], axis=axis_at)
 
-        held = jax.tree.map(join, held, got)
+        held = yield jax.tree.map(join, held, got)
     return held
 
 
@@ -177,49 +194,57 @@
     slab = slab.reshape((2,) * ka_bits + (per_piece, local_waves, plane_waves))
     table = umklapp[0].reshape((2,) * ka_bits + (per_piece, plane_waves))
     roots = [offsets[i] for i in range(step_count)]
-    pieces = scatter_from_roots((slab, table), roots, "ka", list(range(ka_bits)))
     waves = jnp.arange(plane_waves, dtype=jnp.int32)
-    permuted_pieces = []
-    for piece, rows in pieces:
-        piece = piece.reshape(per_piece, local_waves, plane_waves)
-        rows = rows.reshape(per_piece, plane_waves)
-        onehot = (rows[:, :, None] == waves[None, None, :]).astype(jnp.bfloat16)
-        moved_cols = lax.dot_general(
-            piece, onehot, (((2,), (1,)), ((0,), (0,))), preferred_element_type=jnp.float32
-        ).astype(jnp.bfloat16)
-        permuted_pieces.append(
-            moved_cols.reshape((1,) * ka_bits + (per_piece, local_waves, plane_waves))
+
+    def broadcast_chain():
+        pieces = yield from scatter_rounds((slab, table), roots, "ka", list(range(ka_bits)))
+        permuted_pieces = []
+        for piece, rows in pieces:
+            piece = piece.reshape(per_piece, local_waves, plane_waves)
+            rows = rows.reshape(per_piece, plane_waves)
+            onehot = (rows[:, :, None] == waves[None, None, :]).astype(jnp.bfloat16)
+            moved_cols = lax.dot_general(
+                piece, onehot, (((2,), (1,)), ((0,), (0,))), preferred_element_type=jnp.float32
+            ).astype(jnp.bfloat16)
+            permuted_pieces.append(
+                moved_cols.reshape((1,) * ka_bits + (per_piece, local_waves, plane_waves))
+            )
+        gathered = yield from gather_rounds(
+            jnp.stack(permuted_pieces), "ka", list(range(ka_bits))[::-1], lead=1, relabelled=True
         )
-    gathered = gather_all(
-        jnp.stack(permuted_pieces), "ka", list(range(ka_bits))[::-1], lead=1, relabelled=True
-    )
-
-    odd = [roots[i] & 1 for i in range(step_count)]
-    hopped = from_behind(projected, "ka", 1)
-    moving = [jnp.where(odd[i] == 1, hopped, projected) for i in range(step_count)]
-    even_part = [roots[i] - odd[i] for i in range(step_count)]
-    amounts = [
-        jnp.where(me_ka & 1 == 0, even_part[i], (ka_size - even_part[i]) % ka_size)
-        for i in range(step_count)
-    ]
-    for level in range(1, ka_bits):
-        by = 1 << level
-        pairs = [
-            (j, (j + by) % ka_size if j % 2 == 0 else (j - by) % ka_size) for j in range(ka_size)
-        ]
-        hopped = lax.ppermute(jnp.stack(moving), "ka", pairs)
-        moving = [
-            jnp.where(amounts[i] >> level & 1 == 1, hopped[i], moving[i])
+        return gathered
+
+    def roll_chain():
+        odd = [roots[i] & 1 for i in range(step_count)]
+        hopped = from_behind(projected, "ka", 1)
+        moving = [jnp.where(odd[i] == 1, hopped, projected) for i in range(step_count)]
+        moving = yield moving
+        even_part = [roots[i] - odd[i] for i in range(step_count)]
+        amounts = [
+            jnp.where(me_ka & 1 == 0, even_part[i], (ka_size - even_part[i]) % ka_size)
             for i in range(step_count)
         ]
-    moving = jnp.stack(moving).reshape(step_count, kpoint_count * vector_count, local_waves)
-    moving = jnp.transpose(moving, (0, 2, 1)).reshape(
-        (step_count,) + (1,) * ga_bits + (local_waves, kpoint_count * vector_count)
-    )
-    ga_order = [0, 2, 1] if ga_bits == 3 else list(range(ga_bits))
-    moving_all = gather_all(moving, "ga", ga_order, lead=1).reshape(
-        step_count, plane_waves, kpoint_count * vector_count
-    )
+        for level in range(1, ka_bits):
+            by = 1 << level
+            pairs = [
+                (j, (j + by) % ka_size if j % 2 == 0 else (j - by) % ka_size)
+                for j in range(ka_size)
+            ]
+            hopped = lax.ppermute(jnp.stack(moving), "ka", pairs)
+            moving = [
+                jnp.where(amounts[i] >> level & 1 == 1, hopped[i], moving[i])
+                for i in range(step_count)
+            ]
+            moving = yield moving
+        moving = jnp.stack(moving).reshape(step_count, kpoint_count * vector_count, local_waves)
+        moving = jnp.transpose(moving, (0, 2, 1)).reshape(
+            (step_count,) + (1,) * ga_bits + (local_waves, kpoint_count * vector_count)
+        )
+        ga_order = [0, 2, 1] if ga_bits == 3 else list(range(ga_bits))
+        moving_all = yield from gather_rounds(moving, "ga", ga_order, lead=1)
+        return moving_all.reshape(step_count, plane_waves, kpoint_count * vector_count)
+
+    gathered, moving_all = lockstep([broadcast_chain(), roll_chain()])
 
     permuted_all = gathered.reshape(step_count, slot_count, local_waves, plane_waves)
     kernel_part = contract(q_slots, permuted_all, moving_all, vector_count)

time: 288 us -> 316 us (1.097)
  waiting for transfers between devices: 149 us -> 193 us
  other arithmetic: 27.2 us -> 13.4 us
    ppermute x15, waiting for transfers between devices: 72.9 us -> 170 us  [swap_relabelled(): return lax.ppermute(value, axis, pairs)]
    ppermute x4, waiting for transfers between devices: 32.2 us -> 1.31 us  [roll_chain(): hopped = lax.ppermute(jnp.stack(moving), 'ka', pairs)]
    ppermute x17, waiting for transfers between devices: 43.5 us -> 19.7 us  [swap(): return lax.ppermute(value, axis, [(i, i ^ bit) for i in range(count)])]
    concatenate x8, other arithmetic: 9.5 us -> 4.43 us  [join(): return jnp.concatenate([low, high], axis=axis_at)]
    select_n x8, other arithmetic: 7.12 us -> 3.62 us  [join(): low = jnp.where(mine == 0, h, g)]
    select_n x21 -> x25, other arithmetic: 6.91 us -> 3.59 us  [the longest x20 3.31 us: scatter_rounds(): jnp.where(holder, k, g)]
  transfers between devices with their start and end apart: 37 -> 37, of which waited for: 21 -> 21; matrix products, arithmetic and copies ran while one was open for 10% -> 1% of each run, Pallas kernels for 0% -> 0%
where the time goes in v6:
time: 316 us; the launch traced here: 315 us
  waiting for transfers between devices  193 us (61%)
  starting transfers between devices  80.3 us (25%)
  other arithmetic  13.4 us (4%)
  Pallas kernels  11.6 us (4%)
  between operations  8.04 us (3%)
  local copies, waits for them, and re-layouts  6.58 us (2%)
    ppermute x15, waiting for transfers between devices, swap_relabelled(): return lax.ppermute(value, axis, pairs)  170 us
    ppermute x17, starting transfers between devices, swap(): return lax.ppermute(value, axis, [(i, i ^ bit) for i in range(count)])  36 us
    ppermute x15, starting transfers between devices, swap_relabelled(): return lax.ppermute(value, axis, pairs)  33 us
    ppermute x17, waiting for transfers between devices, swap(): return lax.ppermute(value, axis, [(i, i ^ bit) for i in range(count)])  19.7 us
    pallas_call x1, Pallas kernels, contract(): pl.pallas_call(functools.partial(contract_kernel, block, 8 if slots % 8 =...  11.6 us
    ppermute x4, starting transfers between devices, roll_chain(): hopped = lax.ppermute(jnp.stack(moving), 'ka', pairs)  11.2 us
  transfers between devices with their start and end apart: 37, of which 21 were waited for; matrix products, arithmetic and copies ran while one was open for 1% of the time, Pallas kernels for 0%

profile of v6, /device:TPU:32, one launch (start us, length us, event | category | flops | bytes accessed | tf_op | source)
XLA Modules:
  0.0 314.8 jit_solution(9197700349764983649)
XLA Ops:
  15.2 16.1 %collective-permute-done.1 = s32[2,2,2,2,1,1,512]{6,4,3,2,1,0,5:T(1,128)S(1)} collective-permute-done((s32[2,2,2,2,1,1,512]{6,4,3,2,1,0,5:T(1,128)S(1)}, s32[2,2,2,2,1,1,512]{6,4,3,2,1,0,5:T(1,128)S(1)}, u32[]{:S(2)}, u32[]{:S(2)}) %collective-permute-start.1) | collective-permute-done | bytes 32800 | tf_op jit(solution)/shard_map/ppermute | solution.py:38
  39.5 23.7 %collective-permute-done.4 = s32[2,2,2,2,1,1,1,512]{7,5,6,4,3,2,1,0:T(1,128)S(1)} collective-permute-done((s32[2,2,2,2,1,1,1,512]{7,5,6,4,3,2,1,0:T(1,128)S(1)}, s32[2,2,2,2,1,1,1,512]{7,5,6,4,3,2,1,0:T(1,128)S(1)}, u32[]{:S(2)}, u32[]{:S(2)}) %collective-permute-start.4) | collective-permute-done | bytes 32800 | tf_op jit(solution)/shard_map/ppermute | solution.py:38
  63.7 4.1 %collective-permute-start.8 = (bf16[2,32,32,64]{3,2,1,0:T(8,128)(2,1)S(1)}, bf16[2,32,32,64]{3,2,1,0:T(8,128)(2,1)S(1)}, u32[]{:S(2)}, u32[]{:S(2)}) collective-permute-start(bf16[2,32,32,64]{3,2,1,0:T(8,128)(2,1)S(1)} %pad_maximum_fusion.8), channel_id=1, source_target_pairs={{0,32},{8,232},{16,48},{24,248},{32,64},{40,8},{48,80},{56,24},{64... | collective-permute-start | bytes 786440 | tf_op jit(solution)/shard_map/ppermute | solution.py:233
  70.1 3.0 collective-permute-done.7
  74.5 13.1 %collective-permute-done.6 = bf16[2,2,2,1,1,1,1,64,512]{8,7,1,2,6,5,4,3,0:T(8,128)(2,1)S(1)} collective-permute-done((bf16[2,2,2,1,1,1,1,64,512]{8,7,1,2,6,5,4,3,0:T(8,128)(2,1)S(1)}, bf16[2,2,2,1,1,1,1,64,512]{8,7,1,2,6,5,4,3,0:T(8,128)(2,1)S(1)}, u32[]{:S(2)}, u32[]{:S(2)}) %collective-permute-start.6) | collective-permute-done | bytes 524320 | tf_op jit(solution)/shard_map/ppermute | solution.py:38
  87.9 4.2 %collective-permute-start.11 = (bf16[2,32,32,64]{3,2,1,0:T(8,128)(2,1)S(1)}, bf16[2,32,32,64]{3,2,1,0:T(8,128)(2,1)S(1)}, u32[]{:S(2)}, u32[]{:S(2)}) collective-permute-start(bf16[2,32,32,64]{3,2,1,0:T(8,128)(2,1)S(1)} %pad_maximum_fusion.9), channel_id=1, source_target_pairs={{0,64},{8,200},{16,80},{24,216},{32,96},{40,232},{48,112},{56,248}... | collective-permute-start | bytes 786440 | tf_op jit(solution)/shard_map/ppermute | solution.py:233
  92.1 4.3 %collective-permute-start.10 = (s32[2,2,1,1,1,1,1,512]{7,5,6,4,3,2,1,0:T(1,128)S(1)}, s32[2,2,1,1,1,1,1,512]{7,5,6,4,3,2,1,0:T(1,128)S(1)}, u32[]{:S(2)}, u32[]{:S(2)}) collective-permute-start(s32[2,2,1,1,1,1,1,512]{7,5,6,4,3,2,1,0:T(1,128)S(1)} %pad_add_fusion.2), channel_id=1, source_target_pairs={{0,64},{8,72},{16,80},{24,88},{32,96},{40,104},{48,112},{56,120},{... | collective-permute-start | bytes 24584 | tf_op jit(solution)/shard_map/ppermute | solution.py:38
  96.6 20.4 %collective-permute-done.10 = s32[2,2,1,1,1,1,1,512]{7,5,6,4,3,2,1,0:T(1,128)S(1)} collective-permute-done((s32[2,2,1,1,1,1,1,512]{7,5,6,4,3,2,1,0:T(1,128)S(1)}, s32[2,2,1,1,1,1,1,512]{7,5,6,4,3,2,1,0:T(1,128)S(1)}, u32[]{:S(2)}, u32[]{:S(2)}) %collective-permute-start.10) | collective-permute-done | bytes 8224 | tf_op jit(solution)/shard_map/ppermute | solution.py:38
  117.1 5.9 %collective-permute-done.9 = bf16[2,2,1,1,1,1,1,64,512]{8,7,1,6,5,4,3,2,0:T(8,128)(2,1)S(1)} collective-permute-done((bf16[2,2,1,1,1,1,1,64,512]{8,7,1,6,5,4,3,2,0:T(8,128)(2,1)S(1)}, bf16[2,2,1,1,1,1,1,64,512]{8,7,1,6,5,4,3,2,0:T(8,128)(2,1)S(1)}, u32[]{:S(2)}, u32[]{:S(2)}) %collective-permute-start.9) | collective-permute-done | bytes 262176 | tf_op jit(solution)/shard_map/ppermute | solution.py:38
  126.0 3.3 %collective-permute-start.13 = (s32[2,1,1,1,1,1,1,512]{7,6,5,4,3,2,1,0:T(1,128)S(1)}, s32[2,1,1,1,1,1,1,512]{7,6,5,4,3,2,1,0:T(1,128)S(1)}, u32[]{:S(2)}, u32[]{:S(2)}) collective-permute-start(s32[2,1,1,1,1,1,1,512]{7,6,5,4,3,2,1,0:T(1,128)S(1)} %pad_add_fusion.3), channel_id=1, source_target_pairs={{0,128},{8,136},{16,144},{24,152},{32,160},{40,168},{48,176},{56,1... | collective-permute-start | bytes 12296 | tf_op jit(solution)/shard_map/ppermute | solution.py:38
  132.1 4.6 %collective-permute-done.13 = s32[2,1,1,1,1,1,1,512]{7,6,5,4,3,2,1,0:T(1,128)S(1)} collective-permute-done((s32[2,1,1,1,1,1,1,512]{7,6,5,4,3,2,1,0:T(1,128)S(1)}, s32[2,1,1,1,1,1,1,512]{7,6,5,4,3,2,1,0:T(1,128)S(1)}, u32[]{:S(2)}, u32[]{:S(2)}) %collective-permute-start.13) | collective-permute-done | bytes 4128 | tf_op jit(solution)/shard_map/ppermute | solution.py:38
  145.3 7.6 %collective-permute-done.15 = bf16[2,1,1,1,1,1,1,64,512]{8,7,6,5,4,3,2,1,0:T(8,128)(2,1)S(1)} collective-permute-done((bf16[2,1,1,1,1,1,1,64,512]{8,7,6,5,4,3,2,1,0:T(8,128)(2,1)S(1)}, bf16[2,1,1,1,1,1,1,64,512]{8,7,6,5,4,3,2,1,0:T(8,128)(2,1)S(1)}, u32[]{:S(2)}, u32[]{:S(2)}) %collective-permute-start.15) | collective-permute-done | bytes 131104 | tf_op jit(solution)/shard_map/ppermute | solution.py:38
  153.2 12.3 %collective-permute-start.17 = (bf16[2,2,1,1,1,1,1,64,512]{8,7,6,5,4,3,2,1,0:T(8,128)(2,1)S(1)}, bf16[2,2,1,1,1,1,1,64,512]{8,7,6,5,4,3,2,1,0:T(8,128)(2,1)S(1)}, u32[]{:S(2)}, u32[]{:S(2)}) collective-permute-start(bf16[2,2,1,1,1,1,1,64,512]{8,7,6,5,4,3,2,1,0:T(8,128)(2,1)S(1)} %pad_maximum_fusion.14), channel_id=1, source_target_pairs={{0,64},{8,72},{16,80},{24,88},{32,96},{40,104},{48,112},{56,120},{... | collective-permute-start | bytes 786440 | tf_op jit(solution)/shard_map/ppermute | solution.py:38
  170.8 5.4 %collective-permute-done.18 = bf16[2,1,1,2,64,1024]{5,4,3,2,1,0:T(8,128)(2,1)S(1)} collective-permute-done((bf16[2,1,1,2,64,1024]{5,4,3,2,1,0:T(8,128)(2,1)S(1)}, bf16[2,1,1,2,64,1024]{5,4,3,2,1,0:T(8,128)(2,1)S(1)}, u32[]{:S(2)}, u32[]{:S(2)}) %collective-permute-start.18) | collective-permute-done | bytes 524320 | tf_op jit(solution)/shard_map/ppermute | solution.py:18
  177.8 9.2 %collective-permute-done.19 = bf16[2,2,2,1,1,1,1,64,512]{8,7,6,5,4,3,2,1,0:T(8,128)(2,1)S(1)} collective-permute-done((bf16[2,2,2,1,1,1,1,64,512]{8,7,6,5,4,3,2,1,0:T(8,128)(2,1)S(1)}, bf16[2,2,2,1,1,1,1,64,512]{8,7,6,5,4,3,2,1,0:T(8,128)(2,1)S(1)}, u32[]{:S(2)}, u32[]{:S(2)}) %collective-permute-start.19) | collective-permute-done | bytes 524320 | tf_op jit(solution)/shard_map/ppermute | solution.py:38
  187.1 4.2 %collective-permute-done.20 = bf16[2,2,1,2,64,1024]{5,4,3,2,1,0:T(8,128)(2,1)} collective-permute-done((bf16[2,2,1,2,64,1024]{5,4,3,2,1,0:T(8,128)(2,1)S(1)}, bf16[2,2,1,2,64,1024]{5,4,3,2,1,0:T(8,128)(2,1)}, u32[]{:S(2)}, u32[]{:S(2)}) %collective-permute-start.20) | collective-permute-done | bytes 1048608 | tf_op jit(solution)/shard_map/ppermute | solution.py:18
  194.7 14.4 %collective-permute-done.21 = bf16[2,2,2,2,1,1,1,64,512]{8,7,6,5,4,3,2,1,0:T(8,128)(2,1)S(1)} collective-permute-done((bf16[2,2,2,2,1,1,1,64,512]{8,7,6,5,4,3,2,1,0:T(8,128)(2,1)S(1)}, bf16[2,2,2,2,1,1,1,64,512]{8,7,6,5,4,3,2,1,0:T(8,128)(2,1)S(1)}, u32[]{:S(2)}, u32[]{:S(2)}) %collective-permute-start.21) | collective-permute-done | bytes 1048608 | tf_op jit(solution)/shard_map/ppermute | solution.py:38
  209.6 47.8 %collective-permute-done.22 = bf16[2,2,2,2,2,1,1,64,512]{8,7,6,5,4,3,2,1,0:T(8,128)(2,1)} collective-permute-done((bf16[2,2,2,2,2,1,1,64,512]{8,7,6,5,4,3,2,1,0:T(8,128)(2,1)S(1)}, bf16[2,2,2,2,2,1,1,64,512]{8,7,6,5,4,3,2,1,0:T(8,128)(2,1)}, u32[]{:S(2)}, u32[]{:S(2)}) %collective-permute-start.22) | collective-permute-done | bytes 2097184 | tf_op jit(solution)/shard_map/ppermute | solution.py:38
  261.6 11.6 %shard_map.73 = bf16[2,64,1024]{2,1,0:T(8,128)(2,1)} custom-call(s32[32]{0:T(128)} %q_ref.1, bf16[2,32,64,512]{3,2,1,0:T(8,128)(2,1)} %bitcast.238, bf16[2,512,1024]{2,1,0:T(8,128)(2,1)} %bitcast.248), custom_call_target="tpu_custom_call" | custom-call | flops 4294967296 | bytes 6553600 | tf_op jit(solution)/shard_map/pallas_call | solution.py:154
  282.8 3.2 %collective-permute-start.27 = (f32[4,32,128]{2,1,0:T(8,128)S(1)}, f32[4,32,128]{2,1,0:T(8,128)S(1)}, u32[]{:S(2)}, u32[]{:S(2)}) collective-permute-start(f32[4,32,128]{2,1,0:T(8,128)S(1)} %get-tuple-element.94), channel_id=1, source_target_pairs={{0,5},{1,4},{2,7},{3,6},{4,1},{5,0},{6,3},{7,2},{8,13},{9,12},{10,... | collective-permute-start | bytes 196616 | tf_op jit(solution)/shard_map/ppermute | solution.py:18
  291.7 4.7 %collective-permute-done.29 = f32[4,32,128]{2,1,0:T(8,128)S(1)} collective-permute-done((f32[4,32,128]{2,1,0:T(8,128)S(1)}, f32[4,32,128]{2,1,0:T(8,128)S(1)}, u32[]{:S(2)}, u32[]{:S(2)}) %collective-permute-start.29) | collective-permute-done | bytes 65568 | tf_op jit(solution)/shard_map/ppermute | solution.py:18
  297.5 4.1 %collective-permute-start.32 = (f32[4,32,128]{2,1,0:T(8,128)S(1)}, f32[4,32,128]{2,1,0:T(8,128)S(1)}, u32[]{:S(2)}, u32[]{:S(2)}) collective-permute-start(f32[4,32,128]{2,1,0:T(8,128)S(1)} %get-tuple-element.78), channel_id=1, source_target_pairs={{0,3},{1,2},{2,1},{3,0},{4,7},{5,6},{6,5},{7,4},{8,11},{9,10},{10,... | collective-permute-start | bytes 196616 | tf_op jit(solution)/shard_map/ppermute | solution.py:18
  301.8 3.7 %collective-permute-start.34 = (f32[4,32,128]{2,1,0:T(8,128)S(1)}, f32[4,32,128]{2,1,0:T(8,128)S(1)}, u32[]{:S(2)}, u32[]{:S(2)}) collective-permute-start(f32[4,32,128]{2,1,0:T(8,128)S(1)} %get-tuple-element.78), channel_id=1, source_target_pairs={{0,5},{1,4},{2,7},{3,6},{4,1},{5,0},{6,3},{7,2},{8,13},{9,12},{10,... | collective-permute-start | bytes 196616 | tf_op jit(solution)/shard_map/ppermute | solution.py:18
  305.9 5.0 %collective-permute-start.36 = (f32[4,32,128]{2,1,0:T(8,128)S(1)}, f32[4,32,128]{2,1,0:T(8,128)S(1)}, u32[]{:S(2)}, u32[]{:S(2)}) collective-permute-start(f32[4,32,128]{2,1,0:T(8,128)S(1)} %get-tuple-element.78), channel_id=1, source_target_pairs={{0,7},{1,6},{2,5},{3,4},{4,3},{5,2},{6,1},{7,0},{8,15},{9,14},{10,... | collective-permute-start | bytes 196616 | tf_op jit(solution)/shard_map/ppermute | solution.py:18
  (158 shorter events, 70.6 us)
Async XLA Ops:
  4.0 30.1 %collective-permute-start = (bf16[2,2,2,2,1,1,64,512]{7,6,4,3,2,1,0,5:T(8,128)(2,1)}, bf16[2,2,2,2,1,1,64,512]{7,6,4,3,2,1,0,5:T(8,128)(2,1)}, u32[]{:S(2)}, u32[]{:S(2)}) collective-permute-start(bf16[2,2,2,2,1,1,64,512]{7,6,4,3,2,1,0,5:T(8,128)(2,1)} %constant_dynamic-slice_fusion.15), channel_id=1, source_target_pairs={{0,8},{8,0},{16,40},{24,32},{32,24},{40,16},{48,56},{56,48},{64,72... | collective-permute-start | bytes 3145736 | tf_op jit(solution)/shard_map/ppermute | solution.py:38
  4.6 26.6 %collective-permute-start.1 = (s32[2,2,2,2,1,1,512]{6,4,3,2,1,0,5:T(1,128)S(1)}, s32[2,2,2,2,1,1,512]{6,4,3,2,1,0,5:T(1,128)S(1)}, u32[]{:S(2)}, u32[]{:S(2)}) collective-permute-start(s32[2,2,2,2,1,1,512]{6,4,3,2,1,0,5:T(1,128)S(1)} %constant_dynamic-slice_fusion.14), channel_id=1, source_target_pairs={{0,8},{8,0},{16,40},{24,32},{32,24},{40,16},{48,56},{56,48},{64,72... | collective-permute-start | bytes 98312 | tf_op jit(solution)/shard_map/ppermute | solution.py:38
  7.2 26.9 %collective-permute-start.2 = (bf16[32,32,64]{2,1,0:T(8,128)(2,1)S(1)}, bf16[32,32,64]{2,1,0:T(8,128)(2,1)S(1)}, u32[]{:S(2)}, u32[]{:S(2)}) collective-permute-start(bf16[32,32,64]{2,1,0:T(8,128)(2,1)S(1)} %convolution_convert_fusion), channel_id=1, source_target_pairs={{0,8},{8,16},{16,24},{24,32},{32,40},{40,48},{48,56},{56,64},{64,7... | collective-permute-start | bytes 393224 | tf_op jit(solution)/shard_map/ppermute | solution.py:13
  37.1 26.3 %collective-permute-start.3 = (bf16[2,2,2,2,1,1,1,64,512]{8,7,1,3,2,6,5,4,0:T(8,128)(2,1)S(1)}, bf16[2,2,2,2,1,1,1,64,512]{8,7,1,3,2,6,5,4,0:T(8,128)(2,1)S(1)}, u32[]{:S(2)}, u32[]{:S(2)}) collective-permute-start(bf16[2,2,2,2,1,1,1,64,512]{8,7,1,3,2,6,5,4,0:T(8,128)(2,1)S(1)} %pad_maximum_fusion.3), channel_id=1, source_target_pairs={{0,16},{8,40},{16,0},{24,56},{32,48},{40,8},{48,32},{56,24},{64,80... | collective-permute-start | bytes 3145736 | tf_op jit(solution)/shard_map/ppermute | solution.py:38
  37.2 26.0 %collective-permute-start.4 = (s32[2,2,2,2,1,1,1,512]{7,5,6,4,3,2,1,0:T(1,128)S(1)}, s32[2,2,2,2,1,1,1,512]{7,5,6,4,3,2,1,0:T(1,128)S(1)}, u32[]{:S(2)}, u32[]{:S(2)}) collective-permute-start(s32[2,2,2,2,1,1,1,512]{7,5,6,4,3,2,1,0:T(1,128)S(1)} %pad_add_fusion), channel_id=1, source_target_pairs={{0,16},{8,40},{16,0},{24,56},{32,48},{40,8},{48,32},{56,24},{64,80... | collective-permute-start | bytes 98312 | tf_op jit(solution)/shard_map/ppermute | solution.py:38
  39.4 23.9 %collective-permute-start.5 = (bf16[2,32,32,64]{3,2,1,0:T(8,128)(2,1)S(1)}, bf16[2,32,32,64]{3,2,1,0:T(8,128)(2,1)S(1)}, u32[]{:S(2)}, u32[]{:S(2)}) collective-permute-start(bf16[2,32,32,64]{3,2,1,0:T(8,128)(2,1)S(1)} %pad_maximum_fusion.6), channel_id=1, source_target_pairs={{0,16},{8,248},{16,32},{24,8},{32,48},{40,24},{48,64},{56,40},{64,... | collective-permute-start | bytes 786440 | tf_op jit(solution)/shard_map/ppermute | solution.py:233
  63.7 10.8 %collective-permute-start.8 = (bf16[2,32,32,64]{3,2,1,0:T(8,128)(2,1)S(1)}, bf16[2,32,32,64]{3,2,1,0:T(8,128)(2,1)S(1)}, u32[]{:S(2)}, u32[]{:S(2)}) collective-permute-start(bf16[2,32,32,64]{3,2,1,0:T(8,128)(2,1)S(1)} %pad_maximum_fusion.8), channel_id=1, source_target_pairs={{0,32},{8,232},{16,48},{24,248},{32,64},{40,8},{48,80},{56,24},{64... | collective-permute-start | bytes 786440 | tf_op jit(solution)/shard_map/ppermute | solution.py:233
  68.0 19.6 %collective-permute-start.6 = (bf16[2,2,2,1,1,1,1,64,512]{8,7,1,2,6,5,4,3,0:T(8,128)(2,1)S(1)}, bf16[2,2,2,1,1,1,1,64,512]{8,7,1,2,6,5,4,3,0:T(8,128)(2,1)S(1)}, u32[]{:S(2)}, u32[]{:S(2)}) collective-permute-start(bf16[2,2,2,1,1,1,1,64,512]{8,7,1,2,6,5,4,3,0:T(8,128)(2,1)S(1)} %pad_maximum_fusion.7), channel_id=1, source_target_pairs={{0,32},{8,24},{16,48},{24,8},{32,0},{40,56},{48,16},{56,40},{64,96... | collective-permute-start | bytes 1572872 | tf_op jit(solution)/shard_map/ppermute | solution.py:38
  87.9 35.2 %collective-permute-start.11 = (bf16[2,32,32,64]{3,2,1,0:T(8,128)(2,1)S(1)}, bf16[2,32,32,64]{3,2,1,0:T(8,128)(2,1)S(1)}, u32[]{:S(2)}, u32[]{:S(2)}) collective-permute-start(bf16[2,32,32,64]{3,2,1,0:T(8,128)(2,1)S(1)} %pad_maximum_fusion.9), channel_id=1, source_target_pairs={{0,64},{8,200},{16,80},{24,216},{32,96},{40,232},{48,112},{56,248}... | collective-permute-start | bytes 786440 | tf_op jit(solution)/shard_map/ppermute | solution.py:233
  92.1 24.9 %collective-permute-start.10 = (s32[2,2,1,1,1,1,1,512]{7,5,6,4,3,2,1,0:T(1,128)S(1)}, s32[2,2,1,1,1,1,1,512]{7,5,6,4,3,2,1,0:T(1,128)S(1)}, u32[]{:S(2)}, u32[]{:S(2)}) collective-permute-start(s32[2,2,1,1,1,1,1,512]{7,5,6,4,3,2,1,0:T(1,128)S(1)} %pad_add_fusion.2), channel_id=1, source_target_pairs={{0,64},{8,72},{16,80},{24,88},{32,96},{40,104},{48,112},{56,120},{... | collective-permute-start | bytes 24584 | tf_op jit(solution)/shard_map/ppermute | solution.py:38
  96.5 26.5 %collective-permute-start.9 = (bf16[2,2,1,1,1,1,1,64,512]{8,7,1,6,5,4,3,2,0:T(8,128)(2,1)S(1)}, bf16[2,2,1,1,1,1,1,64,512]{8,7,1,6,5,4,3,2,0:T(8,128)(2,1)S(1)}, u32[]{:S(2)}, u32[]{:S(2)}) collective-permute-start(bf16[2,2,1,1,1,1,1,64,512]{8,7,1,6,5,4,3,2,0:T(8,128)(2,1)S(1)} %pad_maximum_fusion.13), channel_id=1, source_target_pairs={{0,64},{8,72},{16,80},{24,88},{32,96},{40,104},{48,112},{56,120},{... | collective-permute-start | bytes 786440 | tf_op jit(solution)/shard_map/ppermute | solution.py:38
  123.3 15.3 %collective-permute-start.14 = (bf16[2,32,32,64]{3,2,1,0:T(8,128)(2,1)S(1)}, bf16[2,32,32,64]{3,2,1,0:T(8,128)(2,1)S(1)}, u32[]{:S(2)}, u32[]{:S(2)}) collective-permute-start(bf16[2,32,32,64]{3,2,1,0:T(8,128)(2,1)S(1)} %pad_maximum_fusion.10), channel_id=1, source_target_pairs={{0,128},{8,136},{16,144},{24,152},{32,160},{40,168},{48,176},{56,1... | collective-permute-start | bytes 786440 | tf_op jit(solution)/shard_map/ppermute | solution.py:233
  126.0 10.7 %collective-permute-start.13 = (s32[2,1,1,1,1,1,1,512]{7,6,5,4,3,2,1,0:T(1,128)S(1)}, s32[2,1,1,1,1,1,1,512]{7,6,5,4,3,2,1,0:T(1,128)S(1)}, u32[]{:S(2)}, u32[]{:S(2)}) collective-permute-start(s32[2,1,1,1,1,1,1,512]{7,6,5,4,3,2,1,0:T(1,128)S(1)} %pad_add_fusion.3), channel_id=1, source_target_pairs={{0,128},{8,136},{16,144},{24,152},{32,160},{40,168},{48,176},{56,1... | collective-permute-start | bytes 12296 | tf_op jit(solution)/shard_map/ppermute | solution.py:38
  139.4 13.6 %collective-permute-start.15 = (bf16[2,1,1,1,1,1,1,64,512]{8,7,6,5,4,3,2,1,0:T(8,128)(2,1)S(1)}, bf16[2,1,1,1,1,1,1,64,512]{8,7,6,5,4,3,2,1,0:T(8,128)(2,1)S(1)}, u32[]{:S(2)}, u32[]{:S(2)}) collective-permute-start(bf16[2,1,1,1,1,1,1,64,512]{8,7,6,5,4,3,2,1,0:T(8,128)(2,1)S(1)} %pad_maximum_fusion.16), channel_id=1, source_target_pairs={{0,128},{8,136},{16,144},{24,152},{32,160},{40,168},{48,176},{56,1... | collective-permute-start | bytes 393224 | tf_op jit(solution)/shard_map/ppermute | solution.py:38
  142.3 10.7 %collective-permute-start.16 = (bf16[2,1,1,1,64,1024]{5,4,3,2,1,0:T(8,128)(2,1)S(1)}, bf16[2,1,1,1,64,1024]{5,4,3,2,1,0:T(8,128)(2,1)S(1)}, u32[]{:S(2)}, u32[]{:S(2)}) collective-permute-start(bf16[2,1,1,1,64,1024]{5,4,3,2,1,0:T(8,128)(2,1)S(1)} %maximum_bitcast_fusion), channel_id=1, source_target_pairs={{0,1},{1,0},{2,3},{3,2},{4,5},{5,4},{6,7},{7,6},{8,9},{9,8},{10,11... | collective-permute-start | bytes 786440 | tf_op jit(solution)/shard_map/ppermute | solution.py:18
  153.2 17.5 %collective-permute-start.17 = (bf16[2,2,1,1,1,1,1,64,512]{8,7,6,5,4,3,2,1,0:T(8,128)(2,1)S(1)}, bf16[2,2,1,1,1,1,1,64,512]{8,7,6,5,4,3,2,1,0:T(8,128)(2,1)S(1)}, u32[]{:S(2)}, u32[]{:S(2)}) collective-permute-start(bf16[2,2,1,1,1,1,1,64,512]{8,7,6,5,4,3,2,1,0:T(8,128)(2,1)S(1)} %pad_maximum_fusion.14), channel_id=1, source_target_pairs={{0,64},{8,72},{16,80},{24,88},{32,96},{40,104},{48,112},{56,120},{... | collective-permute-start | bytes 786440 | tf_op jit(solution)/shard_map/ppermute | solution.py:38
  165.5 10.7 %collective-permute-start.18 = (bf16[2,1,1,2,64,1024]{5,4,3,2,1,0:T(8,128)(2,1)S(1)}, bf16[2,1,1,2,64,1024]{5,4,3,2,1,0:T(8,128)(2,1)S(1)}, u32[]{:S(2)}, u32[]{:S(2)}) collective-permute-start(bf16[2,1,1,2,64,1024]{5,4,3,2,1,0:T(8,128)(2,1)S(1)} %pad_maximum_fusion.11), channel_id=1, source_target_pairs={{0,4},{1,5},{2,6},{3,7},{4,0},{5,1},{6,2},{7,3},{8,12},{9,13},{10,... | collective-permute-start | bytes 1572872 | tf_op jit(solution)/shard_map/ppermute | solution.py:18
  176.4 15.0 %collective-permute-start.20 = (bf16[2,2,1,2,64,1024]{5,4,3,2,1,0:T(8,128)(2,1)S(1)}, bf16[2,2,1,2,64,1024]{5,4,3,2,1,0:T(8,128)(2,1)}, u32[]{:S(2)}, u32[]{:S(2)}) collective-permute-start(bf16[2,2,1,2,64,1024]{5,4,3,2,1,0:T(8,128)(2,1)S(1)} %pad_maximum_fusion.4), channel_id=1, source_target_pairs={{0,2},{1,3},{2,0},{3,1},{4,6},{5,7},{6,4},{7,5},{8,10},{9,11},{10,... | collective-permute-start | bytes 3145736 | tf_op jit(solution)/shard_map/ppermute | solution.py:18
  194.3 14.8 %collective-permute-start.21 = (bf16[2,2,2,2,1,1,1,64,512]{8,7,6,5,4,3,2,1,0:T(8,128)(2,1)S(1)}, bf16[2,2,2,2,1,1,1,64,512]{8,7,6,5,4,3,2,1,0:T(8,128)(2,1)S(1)}, u32[]{:S(2)}, u32[]{:S(2)}) collective-permute-start(bf16[2,2,2,2,1,1,1,64,512]{8,7,6,5,4,3,2,1,0:T(8,128)(2,1)S(1)} %pad_maximum_fusion.5), channel_id=1, source_target_pairs={{0,16},{8,40},{16,0},{24,56},{32,48},{40,8},{48,32},{56,24},{64,80... | collective-permute-start | bytes 3145736 | tf_op jit(solution)/shard_map/ppermute | solution.py:38
  209.4 47.9 %collective-permute-start.22 = (bf16[2,2,2,2,2,1,1,64,512]{8,7,6,5,4,3,2,1,0:T(8,128)(2,1)S(1)}, bf16[2,2,2,2,2,1,1,64,512]{8,7,6,5,4,3,2,1,0:T(8,128)(2,1)}, u32[]{:S(2)}, u32[]{:S(2)}) collective-permute-start(bf16[2,2,2,2,2,1,1,64,512]{8,7,6,5,4,3,2,1,0:T(8,128)(2,1)S(1)} %pad_maximum_fusion.2), channel_id=1, source_target_pairs={{0,8},{8,0},{16,40},{24,32},{32,24},{40,16},{48,56},{56,48},{64,72... | collective-permute-start | bytes 6291464 | tf_op jit(solution)/shard_map/ppermute | solution.py:38
  275.0 11.0 %collective-permute-start.23 = (f32[4,32,128]{2,1,0:T(8,128)S(1)}, f32[4,32,128]{2,1,0:T(8,128)S(1)}, u32[]{:S(2)}, u32[]{:S(2)}) collective-permute-start(f32[4,32,128]{2,1,0:T(8,128)S(1)} %get-tuple-element.91), channel_id=1, source_target_pairs={{0,1},{1,0},{2,3},{3,2},{4,5},{5,4},{6,7},{7,6},{8,9},{9,8},{10,11... | collective-permute-start | bytes 196616 | tf_op jit(solution)/shard_map/ppermute | solution.py:18
  278.0 10.6 %collective-permute-start.24 = (f32[4,32,128]{2,1,0:T(8,128)S(1)}, f32[4,32,128]{2,1,0:T(8,128)S(1)}, u32[]{:S(2)}, u32[]{:S(2)}) collective-permute-start(f32[4,32,128]{2,1,0:T(8,128)S(1)} %get-tuple-element.97), channel_id=1, source_target_pairs={{0,2},{1,3},{2,0},{3,1},{4,6},{5,7},{6,4},{7,5},{8,10},{9,11},{10,... | collective-permute-start | bytes 196616 | tf_op jit(solution)/shard_map/ppermute | solution.py:18
  279.3 10.0 %collective-permute-start.25 = (f32[4,32,128]{2,1,0:T(8,128)S(1)}, f32[4,32,128]{2,1,0:T(8,128)S(1)}, u32[]{:S(2)}, u32[]{:S(2)}) collective-permute-start(f32[4,32,128]{2,1,0:T(8,128)S(1)} %get-tuple-element.96), channel_id=1, source_target_pairs={{0,3},{1,2},{2,1},{3,0},{4,7},{5,6},{6,5},{7,4},{8,11},{9,10},{10,... | collective-permute-start | bytes 196616 | tf_op jit(solution)/shard_map/ppermute | solution.py:18
  297.5 13.4 %collective-permute-start.32 = (f32[4,32,128]{2,1,0:T(8,128)S(1)}, f32[4,32,128]{2,1,0:T(8,128)S(1)}, u32[]{:S(2)}, u32[]{:S(2)}) collective-permute-start(f32[4,32,128]{2,1,0:T(8,128)S(1)} %get-tuple-element.78), channel_id=1, source_target_pairs={{0,3},{1,2},{2,1},{3,0},{4,7},{5,6},{6,5},{7,4},{8,11},{9,10},{10,... | collective-permute-start | bytes 196616 | tf_op jit(solution)/shard_map/ppermute | solution.py:18
  (18 other events, 160.1 us)

commit v7 on v4

--- a/solution.py
+++ b/solution.py
@@ -174,15 +174,17 @@
 
     per_piece = slot_count // ka_size
     slab = jnp.transpose(screened[0], (1, 0, 2))
-    slab = slab.reshape((2,) * ka_bits + (per_piece, local_waves, plane_waves))
-    table = umklapp[0].reshape((2,) * ka_bits + (per_piece, plane_waves))
+    table = (umklapp[0] - plane_waves // 2).astype(jnp.bfloat16)[:, None, :]
+    slab = jnp.concatenate([slab, table], axis=1)
+    slab = slab.reshape((2,) * ka_bits + (per_piece, local_waves + 1, plane_waves))
     roots = [offsets[i] for i in range(step_count)]
-    pieces = scatter_from_roots((slab, table), roots, "ka", list(range(ka_bits)))
+    pieces = scatter_from_roots(slab, roots, "ka", list(range(ka_bits)))
     waves = jnp.arange(plane_waves, dtype=jnp.int32)
     permuted_pieces = []
-    for piece, rows in pieces:
-        piece = piece.reshape(per_piece, local_waves, plane_waves)
-        rows = rows.reshape(per_piece, plane_waves)
+    for piece in pieces:
+        piece = piece.reshape(per_piece, local_waves + 1, plane_waves)
+        rows = piece[:, local_waves, :].astype(jnp.int32) + plane_waves // 2
+        piece = piece[:, :local_waves, :]
         onehot = (rows[:, :, None] == waves[None, None, :]).astype(jnp.bfloat16)
         moved_cols = lax.dot_general(
             piece, onehot, (((2,), (1,)), ((0,), (0,))), preferred_element_type=jnp.float32

time: 288 us -> 293 us (1.017)
  local copies, waits for them, and re-layouts: 8.32 us -> 12.6 us
    ppermute x4, waiting for transfers between devices: 32.2 us -> 17.8 us  [body(): hopped = lax.ppermute(jnp.stack(moving), 'ka', pairs)]
    ppermute x15 -> x10, waiting for transfers between devices: 72.9 us -> 80.8 us  [swap_relabelled(): return lax.ppermute(value, axis, pairs)]
    ppermute x17, waiting for transfers between devices: 43.5 us -> 50.7 us  [swap(): return lax.ppermute(value, axis, [(i, i ^ bit) for i in range(count)])]
    ppermute x15 -> x10, starting transfers between devices: 35 us -> 34.7 us  [swap_relabelled(): return lax.ppermute(value, axis, pairs)]
  transfers between devices with their start and end apart: 37 -> 32, of which waited for: 21 -> 20; matrix products, arithmetic and copies ran while one was open for 10% -> 6% of each run, Pallas kernels for 0% -> 0%
where the time goes in v7:
time: 293 us; the launch traced here: 292 us
  waiting for transfers between devices  149 us (51%)
  starting transfers between devices  80.8 us (28%)
  other arithmetic  27.3 us (9%)
  local copies, waits for them, and re-layouts  12.6 us (4%)
  Pallas kernels  11.6 us (4%)
  between operations  8.77 us (3%)
    ppermute x10, waiting for transfers between devices, swap_relabelled(): return lax.ppermute(value, axis, pairs)  80.8 us
    ppermute x17, waiting for transfers between devices, swap(): return lax.ppermute(value, axis, [(i, i ^ bit) for i in range(count)])  50.7 us
    ppermute x17, starting transfers between devices, swap(): return lax.ppermute(value, axis, [(i, i ^ bit) for i in range(count)])  35.6 us
    ppermute x10, starting transfers between devices, swap_relabelled(): return lax.ppermute(value, axis, pairs)  34.7 us
    ppermute x4, waiting for transfers between devices, body(): hopped = lax.ppermute(jnp.stack(moving), 'ka', pairs)  17.8 us
    pallas_call x1, Pallas kernels, contract(): pl.pallas_call(functools.partial(contract_kernel, block, 8 if slots % 8 =...  11.6 us
    ppermute x4, starting transfers between devices, body(): hopped = lax.ppermute(jnp.stack(moving), 'ka', pairs)  10.2 us
    concatenate x8, other arithmetic, join(): return jnp.concatenate([low, high], axis=axis_at)  9.5 us
  transfers between devices with their start and end apart: 32, of which 20 were waited for; matrix products, arithmetic and copies ran while one was open for 6% of the time, Pallas kernels for 0%

profile of v7, /device:TPU:32, one launch (start us, length us, event | category | flops | bytes accessed | tf_op | source)
XLA Modules:
  0.0 291.7 jit_solution(11826677545451952346)
XLA Ops:
  12.8 19.1 %collective-permute-done = bf16[2,2,2,2,1,1,65,512]{7,3,6,5,4,2,1,0:T(2,128)(2,1)} collective-permute-done((bf16[2,2,2,2,1,1,65,512]{7,3,6,5,4,2,1,0:T(2,128)(2,1)}, bf16[2,2,2,2,1,1,65,512]{7,3,6,5,4,2,1,0:T(2,128)(2,1)}, u32[]{:S(2)}, u32[]{:S(2)}) %collective-permute-start) | collective-permute-done | bytes 1064992 | tf_op jit(solution)/shard_map/ppermute | solution.py:38
  40.7 15.2 %collective-permute-done.1 = bf16[2,2,2,2,1,1,1,65,512]{8,3,7,6,5,4,2,1,0:T(2,128)(2,1)S(1)} collective-permute-done((bf16[2,2,2,2,1,1,1,65,512]{8,3,7,6,5,4,2,1,0:T(2,128)(2,1)}, bf16[2,2,2,2,1,1,1,65,512]{8,3,7,6,5,4,2,1,0:T(2,128)(2,1)S(1)}, u32[]{:S(2)}, u32[]{:S(2)}) %collective-permute-start.1) | collective-permute-done | bytes 1064992 | tf_op jit(solution)/shard_map/ppermute | solution.py:38
  58.2 9.2 %collective-permute-done.2 = bf16[2,2,2,1,1,1,1,65,512]{8,2,7,6,5,4,3,1,0:T(2,128)(2,1)S(1)} collective-permute-done((bf16[2,2,2,1,1,1,1,65,512]{8,2,7,6,5,4,3,1,0:T(2,128)(2,1)S(1)}, bf16[2,2,2,1,1,1,1,65,512]{8,2,7,6,5,4,3,1,0:T(2,128)(2,1)S(1)}, u32[]{:S(2)}, u32[]{:S(2)}) %collective-permute-start.2) | collective-permute-done | bytes 532512 | tf_op jit(solution)/shard_map/ppermute | solution.py:38
  68.0 3.4 %collective-permute-start.3 = (bf16[2,2,1,1,1,1,1,65,512]{8,7,1,6,5,4,3,2,0:T(8,128)(2,1)S(1)}, bf16[2,2,1,1,1,1,1,65,512]{8,7,1,6,5,4,3,2,0:T(8,128)(2,1)S(1)}, u32[]{:S(2)}, u32[]{:S(2)}) collective-permute-start(bf16[2,2,1,1,1,1,1,65,512]{8,7,1,6,5,4,3,2,0:T(8,128)(2,1)S(1)} %pad_maximum_fusion.11), channel_id=1, source_target_pairs={{0,64},{8,72},{16,80},{24,88},{32,96},{40,104},{48,112},{56,120},{... | collective-permute-start | bytes 798728 | tf_op jit(solution)/shard_map/ppermute | solution.py:38
  73.4 8.8 %collective-permute-done.3 = bf16[2,2,1,1,1,1,1,65,512]{8,7,1,6,5,4,3,2,0:T(8,128)(2,1)S(1)} collective-permute-done((bf16[2,2,1,1,1,1,1,65,512]{8,7,1,6,5,4,3,2,0:T(8,128)(2,1)S(1)}, bf16[2,2,1,1,1,1,1,65,512]{8,7,1,6,5,4,3,2,0:T(8,128)(2,1)S(1)}, u32[]{:S(2)}, u32[]{:S(2)}) %collective-permute-start.3) | collective-permute-done | bytes 266272 | tf_op jit(solution)/shard_map/ppermute | solution.py:38
  82.4 4.9 %collective-permute-start.4 = (bf16[2,1,1,1,1,1,1,65,512]{8,7,6,5,4,3,2,1,0:T(8,128)(2,1)S(1)}, bf16[2,1,1,1,1,1,1,65,512]{8,7,6,5,4,3,2,1,0:T(8,128)(2,1)S(1)}, u32[]{:S(2)}, u32[]{:S(2)}) collective-permute-start(bf16[2,1,1,1,1,1,1,65,512]{8,7,6,5,4,3,2,1,0:T(8,128)(2,1)S(1)} %pad_maximum_fusion.13), channel_id=1, source_target_pairs={{0,128},{8,136},{16,144},{24,152},{32,160},{40,168},{48,176},{56,1... | collective-permute-start | bytes 399368 | tf_op jit(solution)/shard_map/ppermute | solution.py:38
  89.7 4.1 %collective-permute-done.4 = bf16[2,1,1,1,1,1,1,65,512]{8,7,6,5,4,3,2,1,0:T(8,128)(2,1)S(1)} collective-permute-done((bf16[2,1,1,1,1,1,1,65,512]{8,7,6,5,4,3,2,1,0:T(8,128)(2,1)S(1)}, bf16[2,1,1,1,1,1,1,65,512]{8,7,6,5,4,3,2,1,0:T(8,128)(2,1)S(1)}, u32[]{:S(2)}, u32[]{:S(2)}) %collective-permute-start.4) | collective-permute-done | bytes 133152 | tf_op jit(solution)/shard_map/ppermute | solution.py:38
  97.7 4.0 %collective-permute-done.11 = bf16[2,32,32,64]{3,2,1,0:T(8,128)(2,1)S(1)} collective-permute-done((bf16[2,32,32,64]{3,2,1,0:T(8,128)(2,1)S(1)}, bf16[2,32,32,64]{3,2,1,0:T(8,128)(2,1)S(1)}, u32[]{:S(2)}, u32[]{:S(2)}) %collective-permute-start.11) | collective-permute-done | bytes 262176 | tf_op jit(solution)/shard_map/ppermute | solution.py:212
  104.9 7.0 %collective-permute-start.6 = (bf16[2,2,1,1,1,1,1,64,512]{8,7,6,5,4,3,2,1,0:T(8,128)(2,1)S(1)}, bf16[2,2,1,1,1,1,1,64,512]{8,7,6,5,4,3,2,1,0:T(8,128)(2,1)S(1)}, u32[]{:S(2)}, u32[]{:S(2)}) collective-permute-start(bf16[2,2,1,1,1,1,1,64,512]{8,7,6,5,4,3,2,1,0:T(8,128)(2,1)S(1)} %pad_maximum_fusion.12), channel_id=1, source_target_pairs={{0,64},{8,72},{16,80},{24,88},{32,96},{40,104},{48,112},{56,120},{... | collective-permute-start | bytes 786440 | tf_op jit(solution)/shard_map/ppermute | solution.py:38
  115.5 4.8 %collective-permute-done.6 = bf16[2,2,1,1,1,1,1,64,512]{8,7,6,5,4,3,2,1,0:T(8,128)(2,1)S(1)} collective-permute-done((bf16[2,2,1,1,1,1,1,64,512]{8,7,6,5,4,3,2,1,0:T(8,128)(2,1)S(1)}, bf16[2,2,1,1,1,1,1,64,512]{8,7,6,5,4,3,2,1,0:T(8,128)(2,1)S(1)}, u32[]{:S(2)}, u32[]{:S(2)}) %collective-permute-start.6) | collective-permute-done | bytes 262176 | tf_op jit(solution)/shard_map/ppermute | solution.py:38
  122.8 9.0 %collective-permute-done.13 = bf16[2,32,32,64]{3,2,1,0:T(8,128)(2,1)S(1)} collective-permute-done((bf16[2,32,32,64]{3,2,1,0:T(8,128)(2,1)}, bf16[2,32,32,64]{3,2,1,0:T(8,128)(2,1)S(1)}, u32[]{:S(2)}, u32[]{:S(2)}) %collective-permute-start.13) | collective-permute-done | bytes 262176 | tf_op jit(solution)/shard_map/ppermute | solution.py:212
  132.0 6.9 %collective-permute-start.14 = (bf16[2,32,32,64]{3,2,1,0:T(8,128)(2,1)S(1)}, bf16[2,32,32,64]{3,2,1,0:T(8,128)(2,1)}, u32[]{:S(2)}, u32[]{:S(2)}) collective-permute-start(bf16[2,32,32,64]{3,2,1,0:T(8,128)(2,1)S(1)} %pad_maximum_fusion.9), channel_id=1, source_target_pairs={{0,128},{8,136},{16,144},{24,152},{32,160},{40,168},{48,176},{56,1... | collective-permute-start | bytes 786440 | tf_op jit(solution)/shard_map/ppermute | solution.py:212
  142.5 14.1 %collective-permute-start.8 = (bf16[2,2,2,2,1,1,1,64,512]{8,7,6,5,4,3,2,1,0:T(8,128)(2,1)}, bf16[2,2,2,2,1,1,1,64,512]{8,7,6,5,4,3,2,1,0:T(8,128)(2,1)}, u32[]{:S(2)}, u32[]{:S(2)}) collective-permute-start(bf16[2,2,2,2,1,1,1,64,512]{8,7,6,5,4,3,2,1,0:T(8,128)(2,1)} %pad_maximum_fusion.3), channel_id=1, source_target_pairs={{0,16},{8,40},{16,0},{24,56},{32,48},{40,8},{48,32},{56,24},{64,80... | collective-permute-start | bytes 3145736 | tf_op jit(solution)/shard_map/ppermute | solution.py:38
  163.2 17.1 %collective-permute-done.15 = bf16[2,1,1,1,64,1024]{5,4,3,2,1,0:T(8,128)(2,1)S(1)} collective-permute-done((bf16[2,1,1,1,64,1024]{5,4,3,2,1,0:T(8,128)(2,1)S(1)}, bf16[2,1,1,1,64,1024]{5,4,3,2,1,0:T(8,128)(2,1)S(1)}, u32[]{:S(2)}, u32[]{:S(2)}) %collective-permute-start.15) | collective-permute-done | bytes 262176 | tf_op jit(solution)/shard_map/ppermute | solution.py:18
  187.2 5.0 %collective-permute-done.16 = bf16[2,1,1,2,64,1024]{5,4,3,2,1,0:T(8,128)(2,1)} collective-permute-done((bf16[2,1,1,2,64,1024]{5,4,3,2,1,0:T(8,128)(2,1)}, bf16[2,1,1,2,64,1024]{5,4,3,2,1,0:T(8,128)(2,1)}, u32[]{:S(2)}, u32[]{:S(2)}) %collective-permute-start.16) | collective-permute-done | bytes 524320 | tf_op jit(solution)/shard_map/ppermute | solution.py:18
  196.8 20.3 %collective-permute-done.17 = bf16[2,2,1,2,64,1024]{5,4,3,2,1,0:T(8,128)(2,1)} collective-permute-done((bf16[2,2,1,2,64,1024]{5,4,3,2,1,0:T(8,128)(2,1)}, bf16[2,2,1,2,64,1024]{5,4,3,2,1,0:T(8,128)(2,1)}, u32[]{:S(2)}, u32[]{:S(2)}) %collective-permute-start.17) | collective-permute-done | bytes 1048608 | tf_op jit(solution)/shard_map/ppermute | solution.py:18
  220.2 15.9 %collective-permute-done.9 = bf16[2,2,2,2,2,1,1,64,512]{8,7,6,5,4,3,2,1,0:T(8,128)(2,1)} collective-permute-done((bf16[2,2,2,2,2,1,1,64,512]{8,7,6,5,4,3,2,1,0:T(8,128)(2,1)}, bf16[2,2,2,2,2,1,1,64,512]{8,7,6,5,4,3,2,1,0:T(8,128)(2,1)}, u32[]{:S(2)}, u32[]{:S(2)}) %collective-permute-start.9) | collective-permute-done | bytes 2097184 | tf_op jit(solution)/shard_map/ppermute | solution.py:38
  240.3 11.6 %shard_map.73 = bf16[2,64,1024]{2,1,0:T(8,128)(2,1)} custom-call(s32[32]{0:T(128)} %q_ref.1, bf16[2,32,64,512]{3,2,1,0:T(8,128)(2,1)} %bitcast.212, bf16[2,512,1024]{2,1,0:T(8,128)(2,1)} %bitcast.218), custom_call_target="tpu_custom_call" | custom-call | flops 4294967296 | bytes 6553600 | tf_op jit(solution)/shard_map/pallas_call | solution.py:137
  254.8 4.1 %collective-permute-start.22 = (f32[4,32,128]{2,1,0:T(8,128)S(1)}, f32[4,32,128]{2,1,0:T(8,128)S(1)}, u32[]{:S(2)}, u32[]{:S(2)}) collective-permute-start(f32[4,32,128]{2,1,0:T(8,128)S(1)} %get-tuple-element.28), channel_id=1, source_target_pairs={{0,5},{1,4},{2,7},{3,6},{4,1},{5,0},{6,3},{7,2},{8,13},{9,12},{10,... | collective-permute-start | bytes 196616 | tf_op jit(solution)/shard_map/ppermute | solution.py:18
  258.9 4.1 %collective-permute-start.21 = (f32[4,32,128]{2,1,0:T(8,128)S(1)}, f32[4,32,128]{2,1,0:T(8,128)S(1)}, u32[]{:S(2)}, u32[]{:S(2)}) collective-permute-start(f32[4,32,128]{2,1,0:T(8,128)S(1)} %get-tuple-element.29), channel_id=1, source_target_pairs={{0,4},{1,5},{2,6},{3,7},{4,0},{5,1},{6,2},{7,3},{8,12},{9,13},{10,... | collective-permute-start | bytes 196616 | tf_op jit(solution)/shard_map/ppermute | solution.py:18
  263.0 5.0 %collective-permute-start.18 = (f32[4,32,128]{2,1,0:T(8,128)S(1)}, f32[4,32,128]{2,1,0:T(8,128)S(1)}, u32[]{:S(2)}, u32[]{:S(2)}) collective-permute-start(f32[4,32,128]{2,1,0:T(8,128)S(1)} %get-tuple-element.25), channel_id=1, source_target_pairs={{0,1},{1,0},{2,3},{3,2},{4,5},{5,4},{6,7},{7,6},{8,9},{9,8},{10,11... | collective-permute-start | bytes 196616 | tf_op jit(solution)/shard_map/ppermute | solution.py:18
  270.4 3.5 %collective-permute-start.25 = (f32[4,32,128]{2,1,0:T(8,128)S(1)}, f32[4,32,128]{2,1,0:T(8,128)S(1)}, u32[]{:S(2)}, u32[]{:S(2)}) collective-permute-start(f32[4,32,128]{2,1,0:T(8,128)S(1)} %get-tuple-element.6), channel_id=1, source_target_pairs={{0,1},{1,0},{2,3},{3,2},{4,5},{5,4},{6,7},{7,6},{8,9},{9,8},{10,11... | collective-permute-start | bytes 196616 | tf_op jit(solution)/shard_map/ppermute | solution.py:18
  276.3 5.6 %collective-permute-start.29 = (f32[4,32,128]{2,1,0:T(8,128)S(1)}, f32[4,32,128]{2,1,0:T(8,128)S(1)}, u32[]{:S(2)}, u32[]{:S(2)}) collective-permute-start(f32[4,32,128]{2,1,0:T(8,128)S(1)} %get-tuple-element.6), channel_id=1, source_target_pairs={{0,5},{1,4},{2,7},{3,6},{4,1},{5,0},{6,3},{7,2},{8,13},{9,12},{10,... | collective-permute-start | bytes 196616 | tf_op jit(solution)/shard_map/ppermute | solution.py:18
  287.4 3.4 %collective-permute-done.31 = f32[4,32,128]{2,1,0:T(8,128)S(1)} collective-permute-done((f32[4,32,128]{2,1,0:T(8,128)S(1)}, f32[4,32,128]{2,1,0:T(8,128)S(1)}, u32[]{:S(2)}, u32[]{:S(2)}) %collective-permute-start.31) | collective-permute-done | bytes 65568 | tf_op jit(solution)/shard_map/ppermute | solution.py:18
  (152 shorter events, 76.9 us)
Async XLA Ops:
  4.9 27.0 %collective-permute-start = (bf16[2,2,2,2,1,1,65,512]{7,3,6,5,4,2,1,0:T(2,128)(2,1)}, bf16[2,2,2,2,1,1,65,512]{7,3,6,5,4,2,1,0:T(2,128)(2,1)}, u32[]{:S(2)}, u32[]{:S(2)}) collective-permute-start(bf16[2,2,2,2,1,1,65,512]{7,3,6,5,4,2,1,0:T(2,128)(2,1)} %copy.58), channel_id=1, source_target_pairs={{0,8},{8,0},{16,40},{24,32},{32,24},{40,16},{48,56},{56,48},{64,72... | collective-permute-start | bytes 3194888 | tf_op jit(solution)/shard_map/ppermute | solution.py:38
  40.7 15.2 %collective-permute-start.1 = (bf16[2,2,2,2,1,1,1,65,512]{8,3,7,6,5,4,2,1,0:T(2,128)(2,1)}, bf16[2,2,2,2,1,1,1,65,512]{8,3,7,6,5,4,2,1,0:T(2,128)(2,1)S(1)}, u32[]{:S(2)}, u32[]{:S(2)}) collective-permute-start(bf16[2,2,2,2,1,1,1,65,512]{8,3,7,6,5,4,2,1,0:T(2,128)(2,1)} %maximum_bitcast_fusion), channel_id=1, source_target_pairs={{0,16},{8,40},{16,0},{24,56},{32,48},{40,8},{48,32},{56,24},{64,80... | collective-permute-start | bytes 3194888 | tf_op jit(solution)/shard_map/ppermute | solution.py:38
  58.1 9.4 %collective-permute-start.2 = (bf16[2,2,2,1,1,1,1,65,512]{8,2,7,6,5,4,3,1,0:T(2,128)(2,1)S(1)}, bf16[2,2,2,1,1,1,1,65,512]{8,2,7,6,5,4,3,1,0:T(2,128)(2,1)S(1)}, u32[]{:S(2)}, u32[]{:S(2)}) collective-permute-start(bf16[2,2,2,1,1,1,1,65,512]{8,2,7,6,5,4,3,1,0:T(2,128)(2,1)S(1)} %maximum_bitcast_fusion.1), channel_id=1, source_target_pairs={{0,32},{8,24},{16,48},{24,8},{32,0},{40,56},{48,16},{56,40},{64,96... | collective-permute-start | bytes 1597448 | tf_op jit(solution)/shard_map/ppermute | solution.py:38
  68.0 14.3 %collective-permute-start.3 = (bf16[2,2,1,1,1,1,1,65,512]{8,7,1,6,5,4,3,2,0:T(8,128)(2,1)S(1)}, bf16[2,2,1,1,1,1,1,65,512]{8,7,1,6,5,4,3,2,0:T(8,128)(2,1)S(1)}, u32[]{:S(2)}, u32[]{:S(2)}) collective-permute-start(bf16[2,2,1,1,1,1,1,65,512]{8,7,1,6,5,4,3,2,0:T(8,128)(2,1)S(1)} %pad_maximum_fusion.11), channel_id=1, source_target_pairs={{0,64},{8,72},{16,80},{24,88},{32,96},{40,104},{48,112},{56,120},{... | collective-permute-start | bytes 798728 | tf_op jit(solution)/shard_map/ppermute | solution.py:38
  71.7 15.5 %collective-permute-start.10 = (bf16[32,32,64]{2,1,0:T(8,128)(2,1)S(1)}, bf16[32,32,64]{2,1,0:T(8,128)(2,1)S(1)}, u32[]{:S(2)}, u32[]{:S(2)}) collective-permute-start(bf16[32,32,64]{2,1,0:T(8,128)(2,1)S(1)} %convolution_convert_fusion), channel_id=1, source_target_pairs={{0,8},{8,16},{16,24},{24,32},{32,40},{40,48},{48,56},{56,64},{64,7... | collective-permute-start | bytes 393224 | tf_op jit(solution)/shard_map/ppermute | solution.py:13
  82.4 11.4 %collective-permute-start.4 = (bf16[2,1,1,1,1,1,1,65,512]{8,7,6,5,4,3,2,1,0:T(8,128)(2,1)S(1)}, bf16[2,1,1,1,1,1,1,65,512]{8,7,6,5,4,3,2,1,0:T(8,128)(2,1)S(1)}, u32[]{:S(2)}, u32[]{:S(2)}) collective-permute-start(bf16[2,1,1,1,1,1,1,65,512]{8,7,6,5,4,3,2,1,0:T(8,128)(2,1)S(1)} %pad_maximum_fusion.13), channel_id=1, source_target_pairs={{0,128},{8,136},{16,144},{24,152},{32,160},{40,168},{48,176},{56,1... | collective-permute-start | bytes 399368 | tf_op jit(solution)/shard_map/ppermute | solution.py:38
  87.4 14.3 %collective-permute-start.11 = (bf16[2,32,32,64]{3,2,1,0:T(8,128)(2,1)S(1)}, bf16[2,32,32,64]{3,2,1,0:T(8,128)(2,1)S(1)}, u32[]{:S(2)}, u32[]{:S(2)}) collective-permute-start(bf16[2,32,32,64]{3,2,1,0:T(8,128)(2,1)S(1)} %pad_maximum_fusion.6), channel_id=1, source_target_pairs={{0,16},{8,248},{16,32},{24,8},{32,48},{40,24},{48,64},{56,40},{64,... | collective-permute-start | bytes 786440 | tf_op jit(solution)/shard_map/ppermute | solution.py:212
  94.6 10.3 %collective-permute-start.5 = (bf16[2,1,1,1,1,1,1,64,512]{8,7,6,5,4,3,2,1,0:T(8,128)(2,1)S(1)}, bf16[2,1,1,1,1,1,1,64,512]{8,7,6,5,4,3,2,1,0:T(8,128)(2,1)S(1)}, u32[]{:S(2)}, u32[]{:S(2)}) collective-permute-start(bf16[2,1,1,1,1,1,1,64,512]{8,7,6,5,4,3,2,1,0:T(8,128)(2,1)S(1)} %pad_maximum_fusion.14), channel_id=1, source_target_pairs={{0,128},{8,136},{16,144},{24,152},{32,160},{40,168},{48,176},{56,1... | collective-permute-start | bytes 393224 | tf_op jit(solution)/shard_map/ppermute | solution.py:38
  101.9 12.1 %collective-permute-start.12 = (bf16[2,32,32,64]{3,2,1,0:T(8,128)(2,1)S(1)}, bf16[2,32,32,64]{3,2,1,0:T(8,128)(2,1)S(1)}, u32[]{:S(2)}, u32[]{:S(2)}) collective-permute-start(bf16[2,32,32,64]{3,2,1,0:T(8,128)(2,1)S(1)} %pad_maximum_fusion.7), channel_id=1, source_target_pairs={{0,32},{8,232},{16,48},{24,248},{32,64},{40,8},{48,80},{56,24},{64... | collective-permute-start | bytes 786440 | tf_op jit(solution)/shard_map/ppermute | solution.py:212
  104.9 15.5 %collective-permute-start.6 = (bf16[2,2,1,1,1,1,1,64,512]{8,7,6,5,4,3,2,1,0:T(8,128)(2,1)S(1)}, bf16[2,2,1,1,1,1,1,64,512]{8,7,6,5,4,3,2,1,0:T(8,128)(2,1)S(1)}, u32[]{:S(2)}, u32[]{:S(2)}) collective-permute-start(bf16[2,2,1,1,1,1,1,64,512]{8,7,6,5,4,3,2,1,0:T(8,128)(2,1)S(1)} %pad_maximum_fusion.12), channel_id=1, source_target_pairs={{0,64},{8,72},{16,80},{24,88},{32,96},{40,104},{48,112},{56,120},{... | collective-permute-start | bytes 786440 | tf_op jit(solution)/shard_map/ppermute | solution.py:38
  115.0 16.7 %collective-permute-start.13 = (bf16[2,32,32,64]{3,2,1,0:T(8,128)(2,1)}, bf16[2,32,32,64]{3,2,1,0:T(8,128)(2,1)S(1)}, u32[]{:S(2)}, u32[]{:S(2)}) collective-permute-start(bf16[2,32,32,64]{3,2,1,0:T(8,128)(2,1)} %pad_maximum_fusion.8), channel_id=1, source_target_pairs={{0,64},{8,200},{16,80},{24,216},{32,96},{40,232},{48,112},{56,248}... | collective-permute-start | bytes 786440 | tf_op jit(solution)/shard_map/ppermute | solution.py:212
  121.3 18.9 %collective-permute-start.7 = (bf16[2,2,2,1,1,1,1,64,512]{8,7,6,5,4,3,2,1,0:T(8,128)(2,1)}, bf16[2,2,2,1,1,1,1,64,512]{8,7,6,5,4,3,2,1,0:T(8,128)(2,1)}, u32[]{:S(2)}, u32[]{:S(2)}) collective-permute-start(bf16[2,2,2,1,1,1,1,64,512]{8,7,6,5,4,3,2,1,0:T(8,128)(2,1)} %pad_maximum_fusion.5), channel_id=1, source_target_pairs={{0,32},{8,24},{16,48},{24,8},{32,0},{40,56},{48,16},{56,40},{64,96... | collective-permute-start | bytes 1572872 | tf_op jit(solution)/shard_map/ppermute | solution.py:38
  132.0 27.3 %collective-permute-start.14 = (bf16[2,32,32,64]{3,2,1,0:T(8,128)(2,1)S(1)}, bf16[2,32,32,64]{3,2,1,0:T(8,128)(2,1)}, u32[]{:S(2)}, u32[]{:S(2)}) collective-permute-start(bf16[2,32,32,64]{3,2,1,0:T(8,128)(2,1)S(1)} %pad_maximum_fusion.9), channel_id=1, source_target_pairs={{0,128},{8,136},{16,144},{24,152},{32,160},{40,168},{48,176},{56,1... | collective-permute-start | bytes 786440 | tf_op jit(solution)/shard_map/ppermute | solution.py:212
  142.5 41.8 %collective-permute-start.8 = (bf16[2,2,2,2,1,1,1,64,512]{8,7,6,5,4,3,2,1,0:T(8,128)(2,1)}, bf16[2,2,2,2,1,1,1,64,512]{8,7,6,5,4,3,2,1,0:T(8,128)(2,1)}, u32[]{:S(2)}, u32[]{:S(2)}) collective-permute-start(bf16[2,2,2,2,1,1,1,64,512]{8,7,6,5,4,3,2,1,0:T(8,128)(2,1)} %pad_maximum_fusion.3), channel_id=1, source_target_pairs={{0,16},{8,40},{16,0},{24,56},{32,48},{40,8},{48,32},{56,24},{64,80... | collective-permute-start | bytes 3145736 | tf_op jit(solution)/shard_map/ppermute | solution.py:38
  160.7 19.6 %collective-permute-start.15 = (bf16[2,1,1,1,64,1024]{5,4,3,2,1,0:T(8,128)(2,1)S(1)}, bf16[2,1,1,1,64,1024]{5,4,3,2,1,0:T(8,128)(2,1)S(1)}, u32[]{:S(2)}, u32[]{:S(2)}) collective-permute-start(bf16[2,1,1,1,64,1024]{5,4,3,2,1,0:T(8,128)(2,1)S(1)} %maximum_bitcast_fusion.2), channel_id=1, source_target_pairs={{0,1},{1,0},{2,3},{3,2},{4,5},{5,4},{6,7},{7,6},{8,9},{9,8},{10,11... | collective-permute-start | bytes 786440 | tf_op jit(solution)/shard_map/ppermute | solution.py:18
  181.2 11.0 %collective-permute-start.16 = (bf16[2,1,1,2,64,1024]{5,4,3,2,1,0:T(8,128)(2,1)}, bf16[2,1,1,2,64,1024]{5,4,3,2,1,0:T(8,128)(2,1)}, u32[]{:S(2)}, u32[]{:S(2)}) collective-permute-start(bf16[2,1,1,2,64,1024]{5,4,3,2,1,0:T(8,128)(2,1)} %pad_maximum_fusion.10), channel_id=1, source_target_pairs={{0,4},{1,5},{2,6},{3,7},{4,0},{5,1},{6,2},{7,3},{8,12},{9,13},{10,... | collective-permute-start | bytes 1572872 | tf_op jit(solution)/shard_map/ppermute | solution.py:18
  187.2 48.8 %collective-permute-start.9 = (bf16[2,2,2,2,2,1,1,64,512]{8,7,6,5,4,3,2,1,0:T(8,128)(2,1)}, bf16[2,2,2,2,2,1,1,64,512]{8,7,6,5,4,3,2,1,0:T(8,128)(2,1)}, u32[]{:S(2)}, u32[]{:S(2)}) collective-permute-start(bf16[2,2,2,2,2,1,1,64,512]{8,7,6,5,4,3,2,1,0:T(8,128)(2,1)} %pad_maximum_fusion.1), channel_id=1, source_target_pairs={{0,8},{8,0},{16,40},{24,32},{32,24},{40,16},{48,56},{56,48},{64,72... | collective-permute-start | bytes 6291464 | tf_op jit(solution)/shard_map/ppermute | solution.py:38
  195.3 21.8 %collective-permute-start.17 = (bf16[2,2,1,2,64,1024]{5,4,3,2,1,0:T(8,128)(2,1)}, bf16[2,2,1,2,64,1024]{5,4,3,2,1,0:T(8,128)(2,1)}, u32[]{:S(2)}, u32[]{:S(2)}) collective-permute-start(bf16[2,2,1,2,64,1024]{5,4,3,2,1,0:T(8,128)(2,1)} %pad_maximum_fusion.4), channel_id=1, source_target_pairs={{0,2},{1,3},{2,0},{3,1},{4,6},{5,7},{6,4},{7,5},{8,10},{9,11},{10,... | collective-permute-start | bytes 3145736 | tf_op jit(solution)/shard_map/ppermute | solution.py:18
  253.7 9.3 %collective-permute-start.24 = (f32[4,32,128]{2,1,0:T(8,128)S(1)}, f32[4,32,128]{2,1,0:T(8,128)S(1)}, u32[]{:S(2)}, u32[]{:S(2)}) collective-permute-start(f32[4,32,128]{2,1,0:T(8,128)S(1)} %get-tuple-element.26), channel_id=1, source_target_pairs={{0,7},{1,6},{2,5},{3,4},{4,3},{5,2},{6,1},{7,0},{8,15},{9,14},{10,... | collective-permute-start | bytes 196616 | tf_op jit(solution)/shard_map/ppermute | solution.py:18
  253.8 9.2 %collective-permute-start.23 = (f32[4,32,128]{2,1,0:T(8,128)S(1)}, f32[4,32,128]{2,1,0:T(8,128)S(1)}, u32[]{:S(2)}, u32[]{:S(2)}) collective-permute-start(f32[4,32,128]{2,1,0:T(8,128)S(1)} %get-tuple-element.27), channel_id=1, source_target_pairs={{0,6},{1,7},{2,4},{3,5},{4,2},{5,3},{6,0},{7,1},{8,14},{9,15},{10,... | collective-permute-start | bytes 196616 | tf_op jit(solution)/shard_map/ppermute | solution.py:18
  254.8 13.2 %collective-permute-start.22 = (f32[4,32,128]{2,1,0:T(8,128)S(1)}, f32[4,32,128]{2,1,0:T(8,128)S(1)}, u32[]{:S(2)}, u32[]{:S(2)}) collective-permute-start(f32[4,32,128]{2,1,0:T(8,128)S(1)} %get-tuple-element.28), channel_id=1, source_target_pairs={{0,5},{1,4},{2,7},{3,6},{4,1},{5,0},{6,3},{7,2},{8,13},{9,12},{10,... | collective-permute-start | bytes 196616 | tf_op jit(solution)/shard_map/ppermute | solution.py:18
  270.4 11.5 %collective-permute-start.25 = (f32[4,32,128]{2,1,0:T(8,128)S(1)}, f32[4,32,128]{2,1,0:T(8,128)S(1)}, u32[]{:S(2)}, u32[]{:S(2)}) collective-permute-start(f32[4,32,128]{2,1,0:T(8,128)S(1)} %get-tuple-element.6), channel_id=1, source_target_pairs={{0,1},{1,0},{2,3},{3,2},{4,5},{5,4},{6,7},{7,6},{8,9},{9,8},{10,11... | collective-permute-start | bytes 196616 | tf_op jit(solution)/shard_map/ppermute | solution.py:18
  274.0 10.8 %collective-permute-start.27 = (f32[4,32,128]{2,1,0:T(8,128)S(1)}, f32[4,32,128]{2,1,0:T(8,128)S(1)}, u32[]{:S(2)}, u32[]{:S(2)}) collective-permute-start(f32[4,32,128]{2,1,0:T(8,128)S(1)} %get-tuple-element.6), channel_id=1, source_target_pairs={{0,3},{1,2},{2,1},{3,0},{4,7},{5,6},{6,5},{7,4},{8,11},{9,10},{10,... | collective-permute-start | bytes 196616 | tf_op jit(solution)/shard_map/ppermute | solution.py:18
  275.5 9.3 %collective-permute-start.28 = (f32[4,32,128]{2,1,0:T(8,128)S(1)}, f32[4,32,128]{2,1,0:T(8,128)S(1)}, u32[]{:S(2)}, u32[]{:S(2)}) collective-permute-start(f32[4,32,128]{2,1,0:T(8,128)S(1)} %get-tuple-element.6), channel_id=1, source_target_pairs={{0,4},{1,5},{2,6},{3,7},{4,0},{5,1},{6,2},{7,3},{8,12},{9,13},{10,... | collective-permute-start | bytes 196616 | tf_op jit(solution)/shard_map/ppermute | solution.py:18
  (22 other events, 307.4 us)

commit v8 on v4

--- a/solution.py
+++ b/solution.py
@@ -100,19 +100,17 @@
     return held
 
 
-def sum_all(value, axis):
-    count = lax.axis_size(axis)
+def sum_all(value, axis, order):
+    nbits = len(order)
     me = lax.axis_index(axis)
-    total = lax.dynamic_index_in_dim(value, me, 0, keepdims=False)
-    for mask in range(1, count):
-        sent = lax.dynamic_index_in_dim(value, me ^ mask, 0, keepdims=False)
-        total = total + swap(sent, axis, mask)
-    result = jnp.zeros_like(value)
-    result = lax.dynamic_update_index_in_dim(result, total, me, 0)
-    for mask in range(1, count):
-        got = swap(total, axis, mask)
-        result = lax.dynamic_update_index_in_dim(result, got, me ^ mask, 0)
-    return result
+    held = value
+    for bit in order:
+        axis_at = nbits - 1 - bit
+        mine = (me >> bit) & 1
+        sends = lax.dynamic_slice_in_dim(held, 1 - mine, 1, axis=axis_at)
+        keep = lax.dynamic_slice_in_dim(held, mine, 1, axis=axis_at)
+        held = keep + swap(sends, axis, 1 << bit)
+    return gather_all(held, axis, order[::-1])
 
 
 def contract_kernel(block, group, q_ref, perm_ref, mov_ref, out_ref):
@@ -229,8 +227,9 @@
         kernel_cat, forms, (((0,), (2,)), ((1,), (0,))), preferred_element_type=jnp.float32
     )
     action = action.reshape(kpoint_count, step_count, vector_count, pair_count).sum(axis=1)
-    action = action.reshape(ga_size, kpoint_count // ga_size, vector_count, pair_count)
-    action = sum_all(action, "ga").reshape(kpoint_count, vector_count, pair_count)
+    sum_order = [1, 0, 2] if ga_bits == 3 else list(range(ga_bits))
+    action = action.reshape((2,) * ga_bits + (kpoint_count // ga_size, vector_count, pair_count))
+    action = sum_all(action, "ga", sum_order).reshape(kpoint_count, vector_count, pair_count)
     return energies[:, None, :] * vectors.astype(jnp.float32) - action
 
 

time: 288 us -> 292 us (1.014)
  waiting for transfers between devices: 149 us -> 171 us
  starting transfers between devices: 80.3 us -> 63 us
    ppermute x17 -> x9, starting transfers between devices: 36 us -> 16.2 us  [swap(): return lax.ppermute(value, axis, [(i, i ^ bit) for i in range(count)])]
    ppermute x17 -> x9, waiting for transfers between devices: 43.5 us -> 62.1 us  [swap(): return lax.ppermute(value, axis, [(i, i ^ bit) for i in range(count)])]
    ppermute x4, waiting for transfers between devices: 32.2 us -> 41.3 us  [body(): hopped = lax.ppermute(jnp.stack(moving), 'ka', pairs)]
    ppermute x15, waiting for transfers between devices: 72.9 us -> 67.1 us  [swap_relabelled(): return lax.ppermute(value, axis, pairs)]
    select_n x8 -> x11, other arithmetic: 7.12 us -> 6.16 us  [join(): low = jnp.where(mine == 0, h, g)]
    concatenate x8 -> x11, other arithmetic: 9.5 us -> 9.5 us  [join(): return jnp.concatenate([low, high], axis=axis_at)]
  transfers between devices with their start and end apart: 37 -> 29, of which waited for: 21 -> 21; matrix products, arithmetic and copies ran while one was open for 10% -> 10% of each run, Pallas kernels for 0% -> 0%
where the time goes in v8:
time: 292 us; the launch traced here: 291 us
  waiting for transfers between devices  171 us (59%)
  starting transfers between devices  63 us (22%)
  other arithmetic  28.1 us (10%)
  Pallas kernels  11.6 us (4%)
  between operations  8.49 us (3%)
  local copies, waits for them, and re-layouts  8.2 us (3%)
    ppermute x15, waiting for transfers between devices, swap_relabelled(): return lax.ppermute(value, axis, pairs)  67.1 us
    ppermute x9, waiting for transfers between devices, swap(): return lax.ppermute(value, axis, [(i, i ^ bit) for i in range(count)])  62.1 us
    ppermute x4, waiting for transfers between devices, body(): hopped = lax.ppermute(jnp.stack(moving), 'ka', pairs)  41.3 us
    ppermute x15, starting transfers between devices, swap_relabelled(): return lax.ppermute(value, axis, pairs)  37.7 us
    ppermute x9, starting transfers between devices, swap(): return lax.ppermute(value, axis, [(i, i ^ bit) for i in range(count)])  16.2 us
    pallas_call x1, Pallas kernels, contract(): pl.pallas_call(functools.partial(contract_kernel, block, 8 if slots % 8 =...  11.6 us
    concatenate x11, other arithmetic, join(): return jnp.concatenate([low, high], axis=axis_at)  9.5 us
    ppermute x4, starting transfers between devices, body(): hopped = lax.ppermute(jnp.stack(moving), 'ka', pairs)  9.02 us
  transfers between devices with their start and end apart: 29, of which 21 were waited for; matrix products, arithmetic and copies ran while one was open for 10% of the time, Pallas kernels for 0%

profile of v8, /device:TPU:32, one launch (start us, length us, event | category | flops | bytes accessed | tf_op | source)
XLA Modules:
  0.0 291.4 jit_solution(13579050029290904105)
XLA Ops:
  14.9 17.0 %collective-permute-done.6 = s32[2,2,2,2,1,1,1,512]{7,5,6,4,3,2,1,0:T(1,128)S(1)} collective-permute-done((s32[2,2,2,2,1,1,1,512]{7,5,6,4,3,2,1,0:T(1,128)S(1)}, s32[2,2,2,2,1,1,1,512]{7,5,6,4,3,2,1,0:T(1,128)S(1)}, u32[]{:S(2)}, u32[]{:S(2)}) %collective-permute-start.6) | collective-permute-done | bytes 32800 | tf_op jit(solution)/shard_map/ppermute | solution.py:38
  44.1 10.6 %collective-permute-done.1 = bf16[2,2,2,2,1,1,1,64,512]{8,7,1,3,2,6,5,4,0:T(8,128)(2,1)} collective-permute-done((bf16[2,2,2,2,1,1,1,64,512]{8,7,1,3,2,6,5,4,0:T(8,128)(2,1)}, bf16[2,2,2,2,1,1,1,64,512]{8,7,1,3,2,6,5,4,0:T(8,128)(2,1)}, u32[]{:S(2)}, u32[]{:S(2)}) %collective-permute-start.1) | collective-permute-done | bytes 1048608 | tf_op jit(solution)/shard_map/ppermute | solution.py:38
  58.9 7.3 %collective-permute-start.9 = (s32[2,1,1,1,1,1,1,512]{7,6,5,4,3,2,1,0:T(1,128)S(1)}, s32[2,1,1,1,1,1,1,512]{7,6,5,4,3,2,1,0:T(1,128)S(1)}, u32[]{:S(2)}, u32[]{:S(2)}) collective-permute-start(s32[2,1,1,1,1,1,1,512]{7,6,5,4,3,2,1,0:T(1,128)S(1)} %pad_add_fusion.3), channel_id=1, source_target_pairs={{0,128},{8,136},{16,144},{24,152},{32,160},{40,168},{48,176},{56,1... | collective-permute-start | bytes 12296 | tf_op jit(solution)/shard_map/ppermute | solution.py:38
  70.9 5.3 %collective-permute-done.9 = s32[2,1,1,1,1,1,1,512]{7,6,5,4,3,2,1,0:T(1,128)S(1)} collective-permute-done((s32[2,1,1,1,1,1,1,512]{7,6,5,4,3,2,1,0:T(1,128)S(1)}, s32[2,1,1,1,1,1,1,512]{7,6,5,4,3,2,1,0:T(1,128)S(1)}, u32[]{:S(2)}, u32[]{:S(2)}) %collective-permute-start.9) | collective-permute-done | bytes 4128 | tf_op jit(solution)/shard_map/ppermute | solution.py:38
  76.2 4.3 %collective-permute-done.3 = bf16[2,2,1,1,1,1,1,64,512]{8,7,1,6,5,4,3,2,0:T(8,128)(2,1)S(1)} collective-permute-done((bf16[2,2,1,1,1,1,1,64,512]{8,7,1,6,5,4,3,2,0:T(8,128)(2,1)S(1)}, bf16[2,2,1,1,1,1,1,64,512]{8,7,1,6,5,4,3,2,0:T(8,128)(2,1)S(1)}, u32[]{:S(2)}, u32[]{:S(2)}) %collective-permute-start.3) | collective-permute-done | bytes 262176 | tf_op jit(solution)/shard_map/ppermute | solution.py:38
  80.6 6.6 %collective-permute-start.4 = (bf16[2,1,1,1,1,1,1,64,512]{8,7,6,5,4,3,2,1,0:T(8,128)(2,1)S(1)}, bf16[2,1,1,1,1,1,1,64,512]{8,7,6,5,4,3,2,1,0:T(8,128)(2,1)S(1)}, u32[]{:S(2)}, u32[]{:S(2)}) collective-permute-start(bf16[2,1,1,1,1,1,1,64,512]{8,7,6,5,4,3,2,1,0:T(8,128)(2,1)S(1)} %pad_maximum_fusion.17), channel_id=1, source_target_pairs={{0,128},{8,136},{16,144},{24,152},{32,160},{40,168},{48,176},{56,1... | collective-permute-start | bytes 393224 | tf_op jit(solution)/shard_map/ppermute | solution.py:38
  87.6 7.4 %collective-permute-done.4 = bf16[2,1,1,1,1,1,1,64,512]{8,7,6,5,4,3,2,1,0:T(8,128)(2,1)S(1)} collective-permute-done((bf16[2,1,1,1,1,1,1,64,512]{8,7,6,5,4,3,2,1,0:T(8,128)(2,1)S(1)}, bf16[2,1,1,1,1,1,1,64,512]{8,7,6,5,4,3,2,1,0:T(8,128)(2,1)S(1)}, u32[]{:S(2)}, u32[]{:S(2)}) %collective-permute-start.4) | collective-permute-done | bytes 131104 | tf_op jit(solution)/shard_map/ppermute | solution.py:38
  95.8 4.9 %collective-permute-start.10 = (bf16[2,1,1,1,1,1,1,64,512]{8,7,6,5,4,3,2,1,0:T(8,128)(2,1)S(1)}, bf16[2,1,1,1,1,1,1,64,512]{8,7,6,5,4,3,2,1,0:T(8,128)(2,1)S(1)}, u32[]{:S(2)}, u32[]{:S(2)}) collective-permute-start(bf16[2,1,1,1,1,1,1,64,512]{8,7,6,5,4,3,2,1,0:T(8,128)(2,1)S(1)} %pad_maximum_fusion.18), channel_id=1, source_target_pairs={{0,128},{8,136},{16,144},{24,152},{32,160},{40,168},{48,176},{56,1... | collective-permute-start | bytes 393224 | tf_op jit(solution)/shard_map/ppermute | solution.py:38
  100.8 8.8 %collective-permute-start.17 = (bf16[2,32,32,64]{3,2,1,0:T(8,128)(2,1)S(1)}, bf16[2,32,32,64]{3,2,1,0:T(8,128)(2,1)S(1)}, u32[]{:S(2)}, u32[]{:S(2)}) collective-permute-start(bf16[2,32,32,64]{3,2,1,0:T(8,128)(2,1)S(1)} %pad_maximum_fusion.9), channel_id=1, source_target_pairs={{0,32},{8,232},{16,48},{24,248},{32,64},{40,8},{48,80},{56,24},{64... | collective-permute-start | bytes 786440 | tf_op jit(solution)/shard_map/ppermute | solution.py:208
  109.7 9.3 %collective-permute-done.17 = bf16[2,32,32,64]{3,2,1,0:T(8,128)(2,1)S(1)} collective-permute-done((bf16[2,32,32,64]{3,2,1,0:T(8,128)(2,1)S(1)}, bf16[2,32,32,64]{3,2,1,0:T(8,128)(2,1)S(1)}, u32[]{:S(2)}, u32[]{:S(2)}) %collective-permute-start.17) | collective-permute-done | bytes 262176 | tf_op jit(solution)/shard_map/ppermute | solution.py:208
  122.8 3.5 %collective-permute-start.12 = (bf16[2,2,2,1,1,1,1,64,512]{8,7,6,5,4,3,2,1,0:T(8,128)(2,1)}, bf16[2,2,2,1,1,1,1,64,512]{8,7,6,5,4,3,2,1,0:T(8,128)(2,1)S(1)}, u32[]{:S(2)}, u32[]{:S(2)}) collective-permute-start(bf16[2,2,2,1,1,1,1,64,512]{8,7,6,5,4,3,2,1,0:T(8,128)(2,1)} %pad_maximum_fusion.7), channel_id=1, source_target_pairs={{0,32},{8,24},{16,48},{24,8},{32,0},{40,56},{48,16},{56,40},{64,96... | collective-permute-start | bytes 1572872 | tf_op jit(solution)/shard_map/ppermute | solution.py:38
  126.3 11.0 %collective-permute-done.18 = bf16[2,32,32,64]{3,2,1,0:T(8,128)(2,1)} collective-permute-done((bf16[2,32,32,64]{3,2,1,0:T(8,128)(2,1)}, bf16[2,32,32,64]{3,2,1,0:T(8,128)(2,1)}, u32[]{:S(2)}, u32[]{:S(2)}) %collective-permute-start.18) | collective-permute-done | bytes 262176 | tf_op jit(solution)/shard_map/ppermute | solution.py:208
  146.6 21.0 %collective-permute-done.19 = bf16[2,32,32,64]{3,2,1,0:T(8,128)(2,1)} collective-permute-done((bf16[2,32,32,64]{3,2,1,0:T(8,128)(2,1)}, bf16[2,32,32,64]{3,2,1,0:T(8,128)(2,1)}, u32[]{:S(2)}, u32[]{:S(2)}) %collective-permute-start.19) | collective-permute-done | bytes 262176 | tf_op jit(solution)/shard_map/ppermute | solution.py:208
  171.9 5.1 %collective-permute-done.20 = bf16[2,1,1,1,64,1024]{5,4,3,2,1,0:T(8,128)(2,1)S(1)} collective-permute-done((bf16[2,1,1,1,64,1024]{5,4,3,2,1,0:T(8,128)(2,1)S(1)}, bf16[2,1,1,1,64,1024]{5,4,3,2,1,0:T(8,128)(2,1)S(1)}, u32[]{:S(2)}, u32[]{:S(2)}) %collective-permute-start.20) | collective-permute-done | bytes 262176 | tf_op jit(solution)/shard_map/ppermute | solution.py:18
  183.9 5.1 %collective-permute-done.21 = bf16[2,1,1,2,64,1024]{5,4,3,2,1,0:T(8,128)(2,1)} collective-permute-done((bf16[2,1,1,2,64,1024]{5,4,3,2,1,0:T(8,128)(2,1)}, bf16[2,1,1,2,64,1024]{5,4,3,2,1,0:T(8,128)(2,1)}, u32[]{:S(2)}, u32[]{:S(2)}) %collective-permute-start.21) | collective-permute-done | bytes 524320 | tf_op jit(solution)/shard_map/ppermute | solution.py:18
  193.5 21.2 %collective-permute-done.22 = bf16[2,2,1,2,64,1024]{5,4,3,2,1,0:T(8,128)(2,1)} collective-permute-done((bf16[2,2,1,2,64,1024]{5,4,3,2,1,0:T(8,128)(2,1)}, bf16[2,2,1,2,64,1024]{5,4,3,2,1,0:T(8,128)(2,1)}, u32[]{:S(2)}, u32[]{:S(2)}) %collective-permute-start.22) | collective-permute-done | bytes 1048608 | tf_op jit(solution)/shard_map/ppermute | solution.py:18
  217.7 15.2 %collective-permute-done.14 = bf16[2,2,2,2,2,1,1,64,512]{8,7,6,5,4,3,2,1,0:T(8,128)(2,1)} collective-permute-done((bf16[2,2,2,2,2,1,1,64,512]{8,7,6,5,4,3,2,1,0:T(8,128)(2,1)}, bf16[2,2,2,2,2,1,1,64,512]{8,7,6,5,4,3,2,1,0:T(8,128)(2,1)}, u32[]{:S(2)}, u32[]{:S(2)}) %collective-permute-start.14) | collective-permute-done | bytes 2097184 | tf_op jit(solution)/shard_map/ppermute | solution.py:38
  237.1 11.6 %shard_map.73 = bf16[2,64,1024]{2,1,0:T(8,128)(2,1)} custom-call(s32[32]{0:T(128)} %q_ref.1, bf16[2,32,64,512]{3,2,1,0:T(8,128)(2,1)} %bitcast.211, bf16[2,512,1024]{2,1,0:T(8,128)(2,1)} %bitcast.217), custom_call_target="tpu_custom_call" | custom-call | flops 4294967296 | bytes 6553600 | tf_op jit(solution)/shard_map/pallas_call | solution.py:135
  251.2 7.6 %collective-permute-done.23 = f32[2,1,2,4,32,128]{5,4,3,2,1,0:T(8,128)S(1)} collective-permute-done((f32[2,1,2,4,32,128]{5,4,3,2,1,0:T(8,128)S(1)}, f32[2,1,2,4,32,128]{5,4,3,2,1,0:T(8,128)S(1)}, u32[]{:S(2)}, u32[]{:S(2)}) %collective-permute-start.23) | collective-permute-done | bytes 262176 | tf_op jit(solution)/shard_map/ppermute | solution.py:18
  261.7 3.8 %collective-permute-done.24 = f32[2,1,1,4,32,128]{5,4,3,2,1,0:T(8,128)S(1)} collective-permute-done((f32[2,1,1,4,32,128]{5,4,3,2,1,0:T(8,128)S(1)}, f32[2,1,1,4,32,128]{5,4,3,2,1,0:T(8,128)S(1)}, u32[]{:S(2)}, u32[]{:S(2)}) %collective-permute-start.24) | collective-permute-done | bytes 131104 | tf_op jit(solution)/shard_map/ppermute | solution.py:18
  266.5 4.9 %collective-permute-done.25 = f32[1,1,1,4,32,128]{5,4,3,2,1,0:T(8,128)S(1)} collective-permute-done((f32[1,1,1,4,32,128]{5,4,3,2,1,0:T(8,128)S(1)}, f32[1,1,1,4,32,128]{5,4,3,2,1,0:T(8,128)S(1)}, u32[]{:S(2)}, u32[]{:S(2)}) %collective-permute-start.25) | collective-permute-done | bytes 65568 | tf_op jit(solution)/shard_map/ppermute | solution.py:18
  272.3 4.9 %collective-permute-done.26 = f32[1,1,1,4,32,128]{5,4,3,2,1,0:T(8,128)S(1)} collective-permute-done((f32[1,1,1,4,32,128]{5,4,3,2,1,0:T(8,128)S(1)}, f32[1,1,1,4,32,128]{5,4,3,2,1,0:T(8,128)S(1)}, u32[]{:S(2)}, u32[]{:S(2)}) %collective-permute-start.26) | collective-permute-done | bytes 65568 | tf_op jit(solution)/shard_map/ppermute | solution.py:18
  280.1 3.8 %collective-permute-done.27 = f32[2,1,1,4,32,128]{5,4,3,2,1,0:T(8,128)S(1)} collective-permute-done((f32[2,1,1,4,32,128]{5,4,3,2,1,0:T(8,128)S(1)}, f32[2,1,1,4,32,128]{5,4,3,2,1,0:T(8,128)S(1)}, u32[]{:S(2)}, u32[]{:S(2)}) %collective-permute-start.27) | collective-permute-done | bytes 131104 | tf_op jit(solution)/shard_map/ppermute | solution.py:18
  284.6 5.8 %collective-permute-done.28 = f32[2,1,2,4,32,128]{5,4,3,2,1,0:T(8,128)S(1)} collective-permute-done((f32[2,1,2,4,32,128]{5,4,3,2,1,0:T(8,128)S(1)}, f32[2,1,2,4,32,128]{5,4,3,2,1,0:T(8,128)S(1)}, u32[]{:S(2)}, u32[]{:S(2)}) %collective-permute-start.28) | collective-permute-done | bytes 262176 | tf_op jit(solution)/shard_map/ppermute | solution.py:18
  (154 shorter events, 77.1 us)
Async XLA Ops:
  1.0 13.6 %collective-permute-start.5 = (s32[2,2,2,2,1,1,512]{6,4,3,2,1,0,5:T(1,128)S(1)}, s32[2,2,2,2,1,1,512]{6,4,3,2,1,0,5:T(1,128)S(1)}, u32[]{:S(2)}, u32[]{:S(2)}) collective-permute-start(s32[2,2,2,2,1,1,512]{6,4,3,2,1,0,5:T(1,128)S(1)} %constant_dynamic-slice_fusion.15), channel_id=1, source_target_pairs={{0,8},{8,0},{16,40},{24,32},{32,24},{40,16},{48,56},{56,48},{64,72... | collective-permute-start | bytes 98312 | tf_op jit(solution)/shard_map/ppermute | solution.py:38
  5.5 26.6 %collective-permute-start = (bf16[2,2,2,2,1,1,64,512]{7,6,4,3,2,1,0,5:T(8,128)(2,1)}, bf16[2,2,2,2,1,1,64,512]{7,6,4,3,2,1,0,5:T(8,128)(2,1)}, u32[]{:S(2)}, u32[]{:S(2)}) collective-permute-start(bf16[2,2,2,2,1,1,64,512]{7,6,4,3,2,1,0,5:T(8,128)(2,1)} %constant_dynamic-slice_fusion.18), channel_id=1, source_target_pairs={{0,8},{8,0},{16,40},{24,32},{32,24},{40,16},{48,56},{56,48},{64,72... | collective-permute-start | bytes 3145736 | tf_op jit(solution)/shard_map/ppermute | solution.py:38
  14.8 17.1 %collective-permute-start.6 = (s32[2,2,2,2,1,1,1,512]{7,5,6,4,3,2,1,0:T(1,128)S(1)}, s32[2,2,2,2,1,1,1,512]{7,5,6,4,3,2,1,0:T(1,128)S(1)}, u32[]{:S(2)}, u32[]{:S(2)}) collective-permute-start(s32[2,2,2,2,1,1,1,512]{7,5,6,4,3,2,1,0:T(1,128)S(1)} %pad_add_fusion), channel_id=1, source_target_pairs={{0,16},{8,40},{16,0},{24,56},{32,48},{40,8},{48,32},{56,24},{64,80... | collective-permute-start | bytes 98312 | tf_op jit(solution)/shard_map/ppermute | solution.py:38
  32.0 6.8 %collective-permute-start.7 = (s32[2,2,2,1,1,1,1,512]{7,5,6,4,3,2,1,0:T(1,128)S(1)}, s32[2,2,2,1,1,1,1,512]{7,5,6,4,3,2,1,0:T(1,128)S(1)}, u32[]{:S(2)}, u32[]{:S(2)}) collective-permute-start(s32[2,2,2,1,1,1,1,512]{7,5,6,4,3,2,1,0:T(1,128)S(1)} %pad_add_fusion.1), channel_id=1, source_target_pairs={{0,32},{8,24},{16,48},{24,8},{32,0},{40,56},{48,16},{56,40},{64,96... | collective-permute-start | bytes 49160 | tf_op jit(solution)/shard_map/ppermute | solution.py:38
  36.4 18.2 %collective-permute-start.1 = (bf16[2,2,2,2,1,1,1,64,512]{8,7,1,3,2,6,5,4,0:T(8,128)(2,1)}, bf16[2,2,2,2,1,1,1,64,512]{8,7,1,3,2,6,5,4,0:T(8,128)(2,1)}, u32[]{:S(2)}, u32[]{:S(2)}) collective-permute-start(bf16[2,2,2,2,1,1,1,64,512]{8,7,1,3,2,6,5,4,0:T(8,128)(2,1)} %pad_maximum_fusion.3), channel_id=1, source_target_pairs={{0,16},{8,40},{16,0},{24,56},{32,48},{40,8},{48,32},{56,24},{64,80... | collective-permute-start | bytes 3145736 | tf_op jit(solution)/shard_map/ppermute | solution.py:38
  42.6 44.6 %collective-permute-start.15 = (bf16[32,32,64]{2,1,0:T(8,128)(2,1)S(1)}, bf16[32,32,64]{2,1,0:T(8,128)(2,1)S(1)}, u32[]{:S(2)}, u32[]{:S(2)}) collective-permute-start(bf16[32,32,64]{2,1,0:T(8,128)(2,1)S(1)} %convolution_convert_fusion), channel_id=1, source_target_pairs={{0,8},{8,16},{16,24},{24,32},{32,40},{40,48},{48,56},{56,64},{64,7... | collective-permute-start | bytes 393224 | tf_op jit(solution)/shard_map/ppermute | solution.py:13
  57.1 11.4 %collective-permute-start.2 = (bf16[2,2,2,1,1,1,1,64,512]{8,7,1,2,6,5,4,3,0:T(8,128)(2,1)S(1)}, bf16[2,2,2,1,1,1,1,64,512]{8,7,1,2,6,5,4,3,0:T(8,128)(2,1)S(1)}, u32[]{:S(2)}, u32[]{:S(2)}) collective-permute-start(bf16[2,2,2,1,1,1,1,64,512]{8,7,1,2,6,5,4,3,0:T(8,128)(2,1)S(1)} %pad_maximum_fusion.6), channel_id=1, source_target_pairs={{0,32},{8,24},{16,48},{24,8},{32,0},{40,56},{48,16},{56,40},{64,96... | collective-permute-start | bytes 1572872 | tf_op jit(solution)/shard_map/ppermute | solution.py:38
  58.9 17.3 %collective-permute-start.9 = (s32[2,1,1,1,1,1,1,512]{7,6,5,4,3,2,1,0:T(1,128)S(1)}, s32[2,1,1,1,1,1,1,512]{7,6,5,4,3,2,1,0:T(1,128)S(1)}, u32[]{:S(2)}, u32[]{:S(2)}) collective-permute-start(s32[2,1,1,1,1,1,1,512]{7,6,5,4,3,2,1,0:T(1,128)S(1)} %pad_add_fusion.3), channel_id=1, source_target_pairs={{0,128},{8,136},{16,144},{24,152},{32,160},{40,168},{48,176},{56,1... | collective-permute-start | bytes 12296 | tf_op jit(solution)/shard_map/ppermute | solution.py:38
  68.7 11.8 %collective-permute-start.3 = (bf16[2,2,1,1,1,1,1,64,512]{8,7,1,6,5,4,3,2,0:T(8,128)(2,1)S(1)}, bf16[2,2,1,1,1,1,1,64,512]{8,7,1,6,5,4,3,2,0:T(8,128)(2,1)S(1)}, u32[]{:S(2)}, u32[]{:S(2)}) collective-permute-start(bf16[2,2,1,1,1,1,1,64,512]{8,7,1,6,5,4,3,2,0:T(8,128)(2,1)S(1)} %pad_maximum_fusion.14), channel_id=1, source_target_pairs={{0,64},{8,72},{16,80},{24,88},{32,96},{40,104},{48,112},{56,120},{... | collective-permute-start | bytes 786440 | tf_op jit(solution)/shard_map/ppermute | solution.py:38
  80.6 14.4 %collective-permute-start.4 = (bf16[2,1,1,1,1,1,1,64,512]{8,7,6,5,4,3,2,1,0:T(8,128)(2,1)S(1)}, bf16[2,1,1,1,1,1,1,64,512]{8,7,6,5,4,3,2,1,0:T(8,128)(2,1)S(1)}, u32[]{:S(2)}, u32[]{:S(2)}) collective-permute-start(bf16[2,1,1,1,1,1,1,64,512]{8,7,6,5,4,3,2,1,0:T(8,128)(2,1)S(1)} %pad_maximum_fusion.17), channel_id=1, source_target_pairs={{0,128},{8,136},{16,144},{24,152},{32,160},{40,168},{48,176},{56,1... | collective-permute-start | bytes 393224 | tf_op jit(solution)/shard_map/ppermute | solution.py:38
  87.3 13.3 %collective-permute-start.16 = (bf16[2,32,32,64]{3,2,1,0:T(8,128)(2,1)S(1)}, bf16[2,32,32,64]{3,2,1,0:T(8,128)(2,1)S(1)}, u32[]{:S(2)}, u32[]{:S(2)}) collective-permute-start(bf16[2,32,32,64]{3,2,1,0:T(8,128)(2,1)S(1)} %pad_maximum_fusion.8), channel_id=1, source_target_pairs={{0,16},{8,248},{16,32},{24,8},{32,48},{40,24},{48,64},{56,40},{64,... | collective-permute-start | bytes 786440 | tf_op jit(solution)/shard_map/ppermute | solution.py:208
  95.8 13.8 %collective-permute-start.10 = (bf16[2,1,1,1,1,1,1,64,512]{8,7,6,5,4,3,2,1,0:T(8,128)(2,1)S(1)}, bf16[2,1,1,1,1,1,1,64,512]{8,7,6,5,4,3,2,1,0:T(8,128)(2,1)S(1)}, u32[]{:S(2)}, u32[]{:S(2)}) collective-permute-start(bf16[2,1,1,1,1,1,1,64,512]{8,7,6,5,4,3,2,1,0:T(8,128)(2,1)S(1)} %pad_maximum_fusion.18), channel_id=1, source_target_pairs={{0,128},{8,136},{16,144},{24,152},{32,160},{40,168},{48,176},{56,1... | collective-permute-start | bytes 393224 | tf_op jit(solution)/shard_map/ppermute | solution.py:38
  100.8 18.3 %collective-permute-start.17 = (bf16[2,32,32,64]{3,2,1,0:T(8,128)(2,1)S(1)}, bf16[2,32,32,64]{3,2,1,0:T(8,128)(2,1)S(1)}, u32[]{:S(2)}, u32[]{:S(2)}) collective-permute-start(bf16[2,32,32,64]{3,2,1,0:T(8,128)(2,1)S(1)} %pad_maximum_fusion.9), channel_id=1, source_target_pairs={{0,32},{8,232},{16,48},{24,248},{32,64},{40,8},{48,80},{56,24},{64... | collective-permute-start | bytes 786440 | tf_op jit(solution)/shard_map/ppermute | solution.py:208
  109.6 12.3 %collective-permute-start.11 = (bf16[2,2,1,1,1,1,1,64,512]{8,7,6,5,4,3,2,1,0:T(8,128)(2,1)S(1)}, bf16[2,2,1,1,1,1,1,64,512]{8,7,6,5,4,3,2,1,0:T(8,128)(2,1)S(1)}, u32[]{:S(2)}, u32[]{:S(2)}) collective-permute-start(bf16[2,2,1,1,1,1,1,64,512]{8,7,6,5,4,3,2,1,0:T(8,128)(2,1)S(1)} %pad_maximum_fusion.15), channel_id=1, source_target_pairs={{0,64},{8,72},{16,80},{24,88},{32,96},{40,104},{48,112},{56,120},{... | collective-permute-start | bytes 786440 | tf_op jit(solution)/shard_map/ppermute | solution.py:38
  120.0 17.3 %collective-permute-start.18 = (bf16[2,32,32,64]{3,2,1,0:T(8,128)(2,1)}, bf16[2,32,32,64]{3,2,1,0:T(8,128)(2,1)}, u32[]{:S(2)}, u32[]{:S(2)}) collective-permute-start(bf16[2,32,32,64]{3,2,1,0:T(8,128)(2,1)} %pad_maximum_fusion.10), channel_id=1, source_target_pairs={{0,64},{8,200},{16,80},{24,216},{32,96},{40,232},{48,112},{56,248}... | collective-permute-start | bytes 786440 | tf_op jit(solution)/shard_map/ppermute | solution.py:208
  122.8 19.8 %collective-permute-start.12 = (bf16[2,2,2,1,1,1,1,64,512]{8,7,6,5,4,3,2,1,0:T(8,128)(2,1)}, bf16[2,2,2,1,1,1,1,64,512]{8,7,6,5,4,3,2,1,0:T(8,128)(2,1)S(1)}, u32[]{:S(2)}, u32[]{:S(2)}) collective-permute-start(bf16[2,2,2,1,1,1,1,64,512]{8,7,6,5,4,3,2,1,0:T(8,128)(2,1)} %pad_maximum_fusion.7), channel_id=1, source_target_pairs={{0,32},{8,24},{16,48},{24,8},{32,0},{40,56},{48,16},{56,40},{64,96... | collective-permute-start | bytes 1572872 | tf_op jit(solution)/shard_map/ppermute | solution.py:38
  139.3 28.3 %collective-permute-start.19 = (bf16[2,32,32,64]{3,2,1,0:T(8,128)(2,1)}, bf16[2,32,32,64]{3,2,1,0:T(8,128)(2,1)}, u32[]{:S(2)}, u32[]{:S(2)}) collective-permute-start(bf16[2,32,32,64]{3,2,1,0:T(8,128)(2,1)} %pad_maximum_fusion.11), channel_id=1, source_target_pairs={{0,128},{8,136},{16,144},{24,152},{32,160},{40,168},{48,176},{56,1... | collective-permute-start | bytes 786440 | tf_op jit(solution)/shard_map/ppermute | solution.py:208
  143.9 37.1 %collective-permute-start.13 = (bf16[2,2,2,2,1,1,1,64,512]{8,7,6,5,4,3,2,1,0:T(8,128)(2,1)}, bf16[2,2,2,2,1,1,1,64,512]{8,7,6,5,4,3,2,1,0:T(8,128)(2,1)}, u32[]{:S(2)}, u32[]{:S(2)}) collective-permute-start(bf16[2,2,2,2,1,1,1,64,512]{8,7,6,5,4,3,2,1,0:T(8,128)(2,1)} %pad_maximum_fusion.4), channel_id=1, source_target_pairs={{0,16},{8,40},{16,0},{24,56},{32,48},{40,8},{48,32},{56,24},{64,80... | collective-permute-start | bytes 3145736 | tf_op jit(solution)/shard_map/ppermute | solution.py:38
  169.0 8.0 %collective-permute-start.20 = (bf16[2,1,1,1,64,1024]{5,4,3,2,1,0:T(8,128)(2,1)S(1)}, bf16[2,1,1,1,64,1024]{5,4,3,2,1,0:T(8,128)(2,1)S(1)}, u32[]{:S(2)}, u32[]{:S(2)}) collective-permute-start(bf16[2,1,1,1,64,1024]{5,4,3,2,1,0:T(8,128)(2,1)S(1)} %maximum_bitcast_fusion), channel_id=1, source_target_pairs={{0,1},{1,0},{2,3},{3,2},{4,5},{5,4},{6,7},{7,6},{8,9},{9,8},{10,11... | collective-permute-start | bytes 786440 | tf_op jit(solution)/shard_map/ppermute | solution.py:18
  177.9 11.0 %collective-permute-start.21 = (bf16[2,1,1,2,64,1024]{5,4,3,2,1,0:T(8,128)(2,1)}, bf16[2,1,1,2,64,1024]{5,4,3,2,1,0:T(8,128)(2,1)}, u32[]{:S(2)}, u32[]{:S(2)}) collective-permute-start(bf16[2,1,1,2,64,1024]{5,4,3,2,1,0:T(8,128)(2,1)} %pad_maximum_fusion.12), channel_id=1, source_target_pairs={{0,4},{1,5},{2,6},{3,7},{4,0},{5,1},{6,2},{7,3},{8,12},{9,13},{10,... | collective-permute-start | bytes 1572872 | tf_op jit(solution)/shard_map/ppermute | solution.py:18
  183.9 49.1 %collective-permute-start.14 = (bf16[2,2,2,2,2,1,1,64,512]{8,7,6,5,4,3,2,1,0:T(8,128)(2,1)}, bf16[2,2,2,2,2,1,1,64,512]{8,7,6,5,4,3,2,1,0:T(8,128)(2,1)}, u32[]{:S(2)}, u32[]{:S(2)}) collective-permute-start(bf16[2,2,2,2,2,1,1,64,512]{8,7,6,5,4,3,2,1,0:T(8,128)(2,1)} %pad_maximum_fusion.1), channel_id=1, source_target_pairs={{0,8},{8,0},{16,40},{24,32},{32,24},{40,16},{48,56},{56,48},{64,72... | collective-permute-start | bytes 6291464 | tf_op jit(solution)/shard_map/ppermute | solution.py:38
  192.0 22.7 %collective-permute-start.22 = (bf16[2,2,1,2,64,1024]{5,4,3,2,1,0:T(8,128)(2,1)}, bf16[2,2,1,2,64,1024]{5,4,3,2,1,0:T(8,128)(2,1)}, u32[]{:S(2)}, u32[]{:S(2)}) collective-permute-start(bf16[2,2,1,2,64,1024]{5,4,3,2,1,0:T(8,128)(2,1)} %pad_maximum_fusion.5), channel_id=1, source_target_pairs={{0,2},{1,3},{2,0},{3,1},{4,6},{5,7},{6,4},{7,5},{8,10},{9,11},{10,... | collective-permute-start | bytes 3145736 | tf_op jit(solution)/shard_map/ppermute | solution.py:18
  250.5 8.3 %collective-permute-start.23 = (f32[2,1,2,4,32,128]{5,4,3,2,1,0:T(8,128)S(1)}, f32[2,1,2,4,32,128]{5,4,3,2,1,0:T(8,128)S(1)}, u32[]{:S(2)}, u32[]{:S(2)}) collective-permute-start(f32[2,1,2,4,32,128]{5,4,3,2,1,0:T(8,128)S(1)} %constant_dynamic-slice_fusion.2), channel_id=1, source_target_pairs={{0,2},{1,3},{2,0},{3,1},{4,6},{5,7},{6,4},{7,5},{8,10},{9,11},{10,... | collective-permute-start | bytes 786440 | tf_op jit(solution)/shard_map/ppermute | solution.py:18
  258.9 6.6 %collective-permute-start.24 = (f32[2,1,1,4,32,128]{5,4,3,2,1,0:T(8,128)S(1)}, f32[2,1,1,4,32,128]{5,4,3,2,1,0:T(8,128)S(1)}, u32[]{:S(2)}, u32[]{:S(2)}) collective-permute-start(f32[2,1,1,4,32,128]{5,4,3,2,1,0:T(8,128)S(1)} %constant_dynamic-slice_fusion.1), channel_id=1, source_target_pairs={{0,1},{1,0},{2,3},{3,2},{4,5},{5,4},{6,7},{7,6},{8,9},{9,8},{10,11... | collective-permute-start | bytes 393224 | tf_op jit(solution)/shard_map/ppermute | solution.py:18
  (16 other events, 193.4 us)

commit v9 on v4

--- a/solution.py
+++ b/solution.py
@@ -92,9 +92,8 @@
             got = swap(held, axis, 1 << bit)
 
         def join(h, g):
-            low = jnp.where(mine == 0, h, g)
-            high = jnp.where(mine == 0, g, h)
-            return jnp.concatenate([low, high], axis=axis_at)
+            both = jnp.concatenate([h, h], axis=axis_at)
+            return lax.dynamic_update_slice_in_dim(both, g, (1 - mine) * h.shape[axis_at], axis_at)
 
         held = jax.tree.map(join, held, got)
     return held

time: 288 us -> 339 us (1.18)
  the two profiles are of different devices: /device:TPU:32 before, /device:TPU:64 now
where the time goes in v9:
time: 339 us; the launch traced here: 338 us
  waiting for transfers between devices  199 us (59%)
  starting transfers between devices  80.3 us (24%)
  other arithmetic  19.4 us (6%)
  local copies, waits for them, and re-layouts  18.8 us (6%)
  Pallas kernels  11.6 us (3%)
  between operations  7.78 us (2%)
    ppermute x17, waiting for transfers between devices, swap(): return lax.ppermute(value, axis, [(i, i ^ bit) for i in range(count)])  93.8 us
    ppermute x15, waiting for transfers between devices, swap_relabelled(): return lax.ppermute(value, axis, pairs)  58.1 us
    ppermute x4, waiting for transfers between devices, body(): hopped = lax.ppermute(jnp.stack(moving), 'ka', pairs)  47.2 us
    ppermute x17, starting transfers between devices, swap(): return lax.ppermute(value, axis, [(i, i ^ bit) for i in range(count)])  34.7 us
    ppermute x15, starting transfers between devices, swap_relabelled(): return lax.ppermute(value, axis, pairs)  34.2 us
    pallas_call x1, Pallas kernels, contract(): pl.pallas_call(functools.partial(contract_kernel, block, 8 if slots % 8 =...  11.6 us
    dynamic_update_slice x8, local copies, waits for them, and re-layouts, join(): lax.dynamic_update_slice_in_dim(both, g, (1 - mine) * h.shape[axis_at], a...  9.66 us
    ppermute x4, starting transfers between devices, body(): hopped = lax.ppermute(jnp.stack(moving), 'ka', pairs)  8.54 us
  transfers between devices with their start and end apart: 37, of which 22 were waited for; matrix products, arithmetic and copies ran while one was open for 8% of the time, Pallas kernels for 0%

profile of v9, /device:TPU:64, one launch (start us, length us, event | category | flops | bytes accessed | tf_op | source)
XLA Modules:
  0.0 338.3 jit_solution(15269876568340568496)
XLA Ops:
  18.0 22.7 %collective-permute-done.7 = s32[2,2,2,1,1,1,1,512]{7,5,6,4,3,2,1,0:T(1,128)S(1)} collective-permute-done((s32[2,2,2,1,1,1,1,512]{7,5,6,4,3,2,1,0:T(1,128)S(1)}, s32[2,2,2,1,1,1,1,512]{7,5,6,4,3,2,1,0:T(1,128)S(1)}, u32[]{:S(2)}, u32[]{:S(2)}) %collective-permute-start.7) | collective-permute-done | bytes 16416 | tf_op jit(solution)/shard_map/ppermute | solution.py:38
  46.8 3.2 collective-permute-done.8
  50.0 4.7 %collective-permute-start.9 = (s32[2,1,1,1,1,1,1,512]{7,6,5,4,3,2,1,0:T(1,128)S(1)}, s32[2,1,1,1,1,1,1,512]{7,6,5,4,3,2,1,0:T(1,128)S(1)}, u32[]{:S(2)}, u32[]{:S(2)}) collective-permute-start(s32[2,1,1,1,1,1,1,512]{7,6,5,4,3,2,1,0:T(1,128)S(1)} %pad_add_fusion.3), channel_id=1, source_target_pairs={{0,128},{8,136},{16,144},{24,152},{32,160},{40,168},{48,176},{56,1... | collective-permute-start | bytes 12296 | tf_op jit(solution)/shard_map/ppermute | solution.py:38
  54.7 5.3 %collective-permute-done.1 = bf16[2,2,2,2,1,1,1,64,512]{8,7,1,3,2,6,5,4,0:T(8,128)(2,1)} collective-permute-done((bf16[2,2,2,2,1,1,1,64,512]{8,7,1,3,2,6,5,4,0:T(8,128)(2,1)}, bf16[2,2,2,2,1,1,1,64,512]{8,7,1,3,2,6,5,4,0:T(8,128)(2,1)}, u32[]{:S(2)}, u32[]{:S(2)}) %collective-permute-start.1) | collective-permute-done | bytes 1048608 | tf_op jit(solution)/shard_map/ppermute | solution.py:38
  75.4 4.4 %collective-permute-start.16 = (bf16[2,32,32,64]{3,2,1,0:T(8,128)(2,1)S(1)}, bf16[2,32,32,64]{3,2,1,0:T(8,128)(2,1)S(1)}, u32[]{:S(2)}, u32[]{:S(2)}) collective-permute-start(bf16[2,32,32,64]{3,2,1,0:T(8,128)(2,1)S(1)} %pad_maximum_fusion.8), channel_id=1, source_target_pairs={{0,16},{8,248},{16,32},{24,8},{32,48},{40,24},{48,64},{56,40},{64,... | collective-permute-start | bytes 786440 | tf_op jit(solution)/shard_map/ppermute | solution.py:209
  82.2 10.9 %collective-permute-start.4 = (bf16[2,1,1,1,1,1,1,64,512]{8,7,6,5,4,3,2,1,0:T(8,128)(2,1)S(1)}, bf16[2,1,1,1,1,1,1,64,512]{8,7,6,5,4,3,2,1,0:T(8,128)(2,1)S(1)}, u32[]{:S(2)}, u32[]{:S(2)}) collective-permute-start(bf16[2,1,1,1,1,1,1,64,512]{8,7,6,5,4,3,2,1,0:T(8,128)(2,1)S(1)} %pad_maximum_fusion.14), channel_id=1, source_target_pairs={{0,128},{8,136},{16,144},{24,152},{32,160},{40,168},{48,176},{56,1... | collective-permute-start | bytes 393224 | tf_op jit(solution)/shard_map/ppermute | solution.py:38
  93.1 10.2 %collective-permute-done.16 = bf16[2,32,32,64]{3,2,1,0:T(8,128)(2,1)S(1)} collective-permute-done((bf16[2,32,32,64]{3,2,1,0:T(8,128)(2,1)S(1)}, bf16[2,32,32,64]{3,2,1,0:T(8,128)(2,1)S(1)}, u32[]{:S(2)}, u32[]{:S(2)}) %collective-permute-start.16) | collective-permute-done | bytes 262176 | tf_op jit(solution)/shard_map/ppermute | solution.py:209
  104.3 3.1 collective-permute-start.10
  107.4 10.6 %collective-permute-done.10 = bf16[2,1,1,1,1,1,1,64,512]{8,7,6,5,4,3,2,1,0:T(8,128)(2,1)S(1)} collective-permute-done((bf16[2,1,1,1,1,1,1,64,512]{8,7,6,5,4,3,2,1,0:T(8,128)(2,1)S(1)}, bf16[2,1,1,1,1,1,1,64,512]{8,7,6,5,4,3,2,1,0:T(8,128)(2,1)S(1)}, u32[]{:S(2)}, u32[]{:S(2)}) %collective-permute-start.10) | collective-permute-done | bytes 131104 | tf_op jit(solution)/shard_map/ppermute | solution.py:38
  125.5 5.7 %collective-permute-start.12 = (bf16[2,2,2,1,1,1,1,64,512]{8,7,6,5,4,3,2,1,0:T(8,128)(2,1)S(1)}, bf16[2,2,2,1,1,1,1,64,512]{8,7,6,5,4,3,2,1,0:T(8,128)(2,1)}, u32[]{:S(2)}, u32[]{:S(2)}) collective-permute-start(bf16[2,2,2,1,1,1,1,64,512]{8,7,6,5,4,3,2,1,0:T(8,128)(2,1)S(1)} %constant_dynamic-update-slice_fus, ...), channel_id=1, source_target_pairs={{0,32},{8,24},{16,48},{24,8},{32,0},{40,56},{48,16},{56,40},{64,96... | collective-permute-start | bytes 1572872 | tf_op jit(solution)/shard_map/ppermute | solution.py:38
  131.2 6.1 %collective-permute-done.18 = bf16[2,32,32,64]{3,2,1,0:T(8,128)(2,1)S(1)} collective-permute-done((bf16[2,32,32,64]{3,2,1,0:T(8,128)(2,1)}, bf16[2,32,32,64]{3,2,1,0:T(8,128)(2,1)S(1)}, u32[]{:S(2)}, u32[]{:S(2)}) %collective-permute-start.18) | collective-permute-done | bytes 262176 | tf_op jit(solution)/shard_map/ppermute | solution.py:209
  138.4 8.9 %collective-permute-done.12 = bf16[2,2,2,1,1,1,1,64,512]{8,7,6,5,4,3,2,1,0:T(8,128)(2,1)} collective-permute-done((bf16[2,2,2,1,1,1,1,64,512]{8,7,6,5,4,3,2,1,0:T(8,128)(2,1)S(1)}, bf16[2,2,2,1,1,1,1,64,512]{8,7,6,5,4,3,2,1,0:T(8,128)(2,1)}, u32[]{:S(2)}, u32[]{:S(2)}) %collective-permute-start.12) | collective-permute-done | bytes 524320 | tf_op jit(solution)/shard_map/ppermute | solution.py:38
  151.6 28.2 %collective-permute-done.19 = bf16[2,32,32,64]{3,2,1,0:T(8,128)(2,1)S(1)} collective-permute-done((bf16[2,32,32,64]{3,2,1,0:T(8,128)(2,1)S(1)}, bf16[2,32,32,64]{3,2,1,0:T(8,128)(2,1)S(1)}, u32[]{:S(2)}, u32[]{:S(2)}) %collective-permute-start.19) | collective-permute-done | bytes 262176 | tf_op jit(solution)/shard_map/ppermute | solution.py:209
  185.7 50.0 %collective-permute-done.20 = bf16[2,1,1,1,64,1024]{5,4,3,2,1,0:T(8,128)(2,1)S(1)} collective-permute-done((bf16[2,1,1,1,64,1024]{5,4,3,2,1,0:T(8,128)(2,1)S(1)}, bf16[2,1,1,1,64,1024]{5,4,3,2,1,0:T(8,128)(2,1)S(1)}, u32[]{:S(2)}, u32[]{:S(2)}) %collective-permute-start.20) | collective-permute-done | bytes 262176 | tf_op jit(solution)/shard_map/ppermute | solution.py:18
  235.7 3.0 collective-permute-start.21
  239.8 11.6 %collective-permute-done.21 = bf16[2,1,1,2,64,1024]{5,4,3,2,1,0:T(8,128)(2,1)} collective-permute-done((bf16[2,1,1,2,64,1024]{5,4,3,2,1,0:T(8,128)(2,1)S(1)}, bf16[2,1,1,2,64,1024]{5,4,3,2,1,0:T(8,128)(2,1)}, u32[]{:S(2)}, u32[]{:S(2)}) %collective-permute-start.21) | collective-permute-done | bytes 524320 | tf_op jit(solution)/shard_map/ppermute | solution.py:18
  256.4 21.5 %collective-permute-done.22 = bf16[2,2,1,2,64,1024]{5,4,3,2,1,0:T(8,128)(2,1)} collective-permute-done((bf16[2,2,1,2,64,1024]{5,4,3,2,1,0:T(8,128)(2,1)}, bf16[2,2,1,2,64,1024]{5,4,3,2,1,0:T(8,128)(2,1)}, u32[]{:S(2)}, u32[]{:S(2)}) %collective-permute-start.22) | collective-permute-done | bytes 1048608 | tf_op jit(solution)/shard_map/ppermute | solution.py:18
  281.9 3.2 constant_dynamic-update-slice_fusion.3
  285.1 11.6 %shard_map.73 = bf16[2,64,1024]{2,1,0:T(8,128)(2,1)} custom-call(s32[32]{0:T(128)} %q_ref.1, bf16[2,32,64,512]{3,2,1,0:T(8,128)(2,1)} %bitcast.53.perm_ref, bf16[2,512,1024]{2,1,0:T(8,128)(2,1)} %bitcast.257), custom_call_target="tpu_custom_call" | custom-call | flops 4294967296 | bytes 6553600 | tf_op jit(solution)/shard_map/pallas_call | solution.py:136
  301.5 4.5 %collective-permute-start.27 = (f32[4,32,128]{2,1,0:T(8,128)S(1)}, f32[4,32,128]{2,1,0:T(8,128)S(1)}, u32[]{:S(2)}, u32[]{:S(2)}) collective-permute-start(f32[4,32,128]{2,1,0:T(8,128)S(1)} %get-tuple-element.16), channel_id=1, source_target_pairs={{0,5},{1,4},{2,7},{3,6},{4,1},{5,0},{6,3},{7,2},{8,13},{9,12},{10,... | collective-permute-start | bytes 196616 | tf_op jit(solution)/shard_map/ppermute | solution.py:18
  309.4 3.3 collective-permute-start.23
  315.3 3.4 %collective-permute-start.30 = (f32[4,32,128]{2,1,0:T(8,128)S(1)}, f32[4,32,128]{2,1,0:T(8,128)S(1)}, u32[]{:S(2)}, u32[]{:S(2)}) collective-permute-start(f32[4,32,128]{2,1,0:T(8,128)S(1)} %get-tuple-element.6), channel_id=1, source_target_pairs={{0,1},{1,0},{2,3},{3,2},{4,5},{5,4},{6,7},{7,6},{8,9},{9,8},{10,11... | collective-permute-start | bytes 196616 | tf_op jit(solution)/shard_map/ppermute | solution.py:18
  323.0 3.6 %collective-permute-start.34 = (f32[4,32,128]{2,1,0:T(8,128)S(1)}, f32[4,32,128]{2,1,0:T(8,128)S(1)}, u32[]{:S(2)}, u32[]{:S(2)}) collective-permute-start(f32[4,32,128]{2,1,0:T(8,128)S(1)} %get-tuple-element.6), channel_id=1, source_target_pairs={{0,5},{1,4},{2,7},{3,6},{4,1},{5,0},{6,3},{7,2},{8,13},{9,12},{10,... | collective-permute-start | bytes 196616 | tf_op jit(solution)/shard_map/ppermute | solution.py:18
  332.2 5.3 %collective-permute-done.36 = f32[4,32,128]{2,1,0:T(8,128)S(1)} collective-permute-done((f32[4,32,128]{2,1,0:T(8,128)S(1)}, f32[4,32,128]{2,1,0:T(8,128)S(1)}, u32[]{:S(2)}, u32[]{:S(2)}) %collective-permute-start.36) | collective-permute-done | bytes 65568 | tf_op jit(solution)/shard_map/ppermute | solution.py:18
  (160 shorter events, 85.9 us)
Async XLA Ops:
  1.0 10.1 %collective-permute-start.5 = (s32[2,2,2,2,1,1,512]{6,4,3,2,1,0,5:T(1,128)S(1)}, s32[2,2,2,2,1,1,512]{6,4,3,2,1,0,5:T(1,128)S(1)}, u32[]{:S(2)}, u32[]{:S(2)}) collective-permute-start(s32[2,2,2,2,1,1,512]{6,4,3,2,1,0,5:T(1,128)S(1)} %constant_dynamic-slice_fusion.12), channel_id=1, source_target_pairs={{0,8},{8,0},{16,40},{24,32},{32,24},{40,16},{48,56},{56,48},{64,72... | collective-permute-start | bytes 98312 | tf_op jit(solution)/shard_map/ppermute | solution.py:38
  15.3 25.4 %collective-permute-start = (bf16[2,2,2,2,1,1,64,512]{7,6,4,3,2,1,0,5:T(8,128)(2,1)}, bf16[2,2,2,2,1,1,64,512]{7,6,4,3,2,1,0,5:T(8,128)(2,1)}, u32[]{:S(2)}, u32[]{:S(2)}) collective-permute-start(bf16[2,2,2,2,1,1,64,512]{7,6,4,3,2,1,0,5:T(8,128)(2,1)} %constant_dynamic-slice_fusion.15), channel_id=1, source_target_pairs={{0,8},{8,0},{16,40},{24,32},{32,24},{40,16},{48,56},{56,48},{64,72... | collective-permute-start | bytes 3145736 | tf_op jit(solution)/shard_map/ppermute | solution.py:38
  16.2 24.4 %collective-permute-start.7 = (s32[2,2,2,1,1,1,1,512]{7,5,6,4,3,2,1,0:T(1,128)S(1)}, s32[2,2,2,1,1,1,1,512]{7,5,6,4,3,2,1,0:T(1,128)S(1)}, u32[]{:S(2)}, u32[]{:S(2)}) collective-permute-start(s32[2,2,2,1,1,1,1,512]{7,5,6,4,3,2,1,0:T(1,128)S(1)} %pad_add_fusion.1), channel_id=1, source_target_pairs={{0,32},{8,24},{16,48},{24,8},{32,0},{40,56},{48,16},{56,40},{64,96... | collective-permute-start | bytes 49160 | tf_op jit(solution)/shard_map/ppermute | solution.py:38
  44.9 15.1 %collective-permute-start.1 = (bf16[2,2,2,2,1,1,1,64,512]{8,7,1,3,2,6,5,4,0:T(8,128)(2,1)}, bf16[2,2,2,2,1,1,1,64,512]{8,7,1,3,2,6,5,4,0:T(8,128)(2,1)}, u32[]{:S(2)}, u32[]{:S(2)}) collective-permute-start(bf16[2,2,2,2,1,1,1,64,512]{8,7,1,3,2,6,5,4,0:T(8,128)(2,1)} %pad_maximum_fusion.3), channel_id=1, source_target_pairs={{0,16},{8,40},{16,0},{24,56},{32,48},{40,8},{48,32},{56,24},{64,80... | collective-permute-start | bytes 3145736 | tf_op jit(solution)/shard_map/ppermute | solution.py:38
  50.0 19.7 %collective-permute-start.9 = (s32[2,1,1,1,1,1,1,512]{7,6,5,4,3,2,1,0:T(1,128)S(1)}, s32[2,1,1,1,1,1,1,512]{7,6,5,4,3,2,1,0:T(1,128)S(1)}, u32[]{:S(2)}, u32[]{:S(2)}) collective-permute-start(s32[2,1,1,1,1,1,1,512]{7,6,5,4,3,2,1,0:T(1,128)S(1)} %pad_add_fusion.3), channel_id=1, source_target_pairs={{0,128},{8,136},{16,144},{24,152},{32,160},{40,168},{48,176},{56,1... | collective-permute-start | bytes 12296 | tf_op jit(solution)/shard_map/ppermute | solution.py:38
  63.3 9.4 %collective-permute-start.2 = (bf16[2,2,2,1,1,1,1,64,512]{8,7,1,2,6,5,4,3,0:T(8,128)(2,1)}, bf16[2,2,2,1,1,1,1,64,512]{8,7,1,2,6,5,4,3,0:T(8,128)(2,1)S(1)}, u32[]{:S(2)}, u32[]{:S(2)}) collective-permute-start(bf16[2,2,2,1,1,1,1,64,512]{8,7,1,2,6,5,4,3,0:T(8,128)(2,1)} %pad_maximum_fusion.6), channel_id=1, source_target_pairs={{0,32},{8,24},{16,48},{24,8},{32,0},{40,56},{48,16},{56,40},{64,96... | collective-permute-start | bytes 1572872 | tf_op jit(solution)/shard_map/ppermute | solution.py:38
  65.7 9.6 %collective-permute-start.15 = (bf16[32,32,64]{2,1,0:T(8,128)(2,1)S(1)}, bf16[32,32,64]{2,1,0:T(8,128)(2,1)S(1)}, u32[]{:S(2)}, u32[]{:S(2)}) collective-permute-start(bf16[32,32,64]{2,1,0:T(8,128)(2,1)S(1)} %convolution_convert_fusion), channel_id=1, source_target_pairs={{0,8},{8,16},{16,24},{24,32},{32,40},{40,48},{48,56},{56,64},{64,7... | collective-permute-start | bytes 393224 | tf_op jit(solution)/shard_map/ppermute | solution.py:13
  75.4 27.8 %collective-permute-start.16 = (bf16[2,32,32,64]{3,2,1,0:T(8,128)(2,1)S(1)}, bf16[2,32,32,64]{3,2,1,0:T(8,128)(2,1)S(1)}, u32[]{:S(2)}, u32[]{:S(2)}) collective-permute-start(bf16[2,32,32,64]{3,2,1,0:T(8,128)(2,1)S(1)} %pad_maximum_fusion.8), channel_id=1, source_target_pairs={{0,16},{8,248},{16,32},{24,8},{32,48},{40,24},{48,64},{56,40},{64,... | collective-permute-start | bytes 786440 | tf_op jit(solution)/shard_map/ppermute | solution.py:209
  82.2 21.3 %collective-permute-start.4 = (bf16[2,1,1,1,1,1,1,64,512]{8,7,6,5,4,3,2,1,0:T(8,128)(2,1)S(1)}, bf16[2,1,1,1,1,1,1,64,512]{8,7,6,5,4,3,2,1,0:T(8,128)(2,1)S(1)}, u32[]{:S(2)}, u32[]{:S(2)}) collective-permute-start(bf16[2,1,1,1,1,1,1,64,512]{8,7,6,5,4,3,2,1,0:T(8,128)(2,1)S(1)} %pad_maximum_fusion.14), channel_id=1, source_target_pairs={{0,128},{8,136},{16,144},{24,152},{32,160},{40,168},{48,176},{56,1... | collective-permute-start | bytes 393224 | tf_op jit(solution)/shard_map/ppermute | solution.py:38
  103.4 17.5 %collective-permute-start.17 = (bf16[2,32,32,64]{3,2,1,0:T(8,128)(2,1)S(1)}, bf16[2,32,32,64]{3,2,1,0:T(8,128)(2,1)S(1)}, u32[]{:S(2)}, u32[]{:S(2)}) collective-permute-start(bf16[2,32,32,64]{3,2,1,0:T(8,128)(2,1)S(1)} %pad_maximum_fusion.9), channel_id=1, source_target_pairs={{0,32},{8,232},{16,48},{24,248},{32,64},{40,8},{48,80},{56,24},{64... | collective-permute-start | bytes 786440 | tf_op jit(solution)/shard_map/ppermute | solution.py:209
  104.3 13.7 %collective-permute-start.10 = (bf16[2,1,1,1,1,1,1,64,512]{8,7,6,5,4,3,2,1,0:T(8,128)(2,1)S(1)}, bf16[2,1,1,1,1,1,1,64,512]{8,7,6,5,4,3,2,1,0:T(8,128)(2,1)S(1)}, u32[]{:S(2)}, u32[]{:S(2)}) collective-permute-start(bf16[2,1,1,1,1,1,1,64,512]{8,7,6,5,4,3,2,1,0:T(8,128)(2,1)S(1)} %pad_maximum_fusion.15), channel_id=1, source_target_pairs={{0,128},{8,136},{16,144},{24,152},{32,160},{40,168},{48,176},{56,1... | collective-permute-start | bytes 393224 | tf_op jit(solution)/shard_map/ppermute | solution.py:38
  121.9 15.4 %collective-permute-start.18 = (bf16[2,32,32,64]{3,2,1,0:T(8,128)(2,1)}, bf16[2,32,32,64]{3,2,1,0:T(8,128)(2,1)S(1)}, u32[]{:S(2)}, u32[]{:S(2)}) collective-permute-start(bf16[2,32,32,64]{3,2,1,0:T(8,128)(2,1)} %pad_maximum_fusion.10), channel_id=1, source_target_pairs={{0,64},{8,200},{16,80},{24,216},{32,96},{40,232},{48,112},{56,248}... | collective-permute-start | bytes 786440 | tf_op jit(solution)/shard_map/ppermute | solution.py:209
  125.5 21.7 %collective-permute-start.12 = (bf16[2,2,2,1,1,1,1,64,512]{8,7,6,5,4,3,2,1,0:T(8,128)(2,1)S(1)}, bf16[2,2,2,1,1,1,1,64,512]{8,7,6,5,4,3,2,1,0:T(8,128)(2,1)}, u32[]{:S(2)}, u32[]{:S(2)}) collective-permute-start(bf16[2,2,2,1,1,1,1,64,512]{8,7,6,5,4,3,2,1,0:T(8,128)(2,1)S(1)} %constant_dynamic-update-slice_fus, ...), channel_id=1, source_target_pairs={{0,32},{8,24},{16,48},{24,8},{32,0},{40,56},{48,16},{56,40},{64,96... | collective-permute-start | bytes 1572872 | tf_op jit(solution)/shard_map/ppermute | solution.py:38
  149.1 35.1 %collective-permute-start.13 = (bf16[2,2,2,2,1,1,1,64,512]{8,7,6,5,4,3,2,1,0:T(8,128)(2,1)}, bf16[2,2,2,2,1,1,1,64,512]{8,7,6,5,4,3,2,1,0:T(8,128)(2,1)}, u32[]{:S(2)}, u32[]{:S(2)}) collective-permute-start(bf16[2,2,2,2,1,1,1,64,512]{8,7,6,5,4,3,2,1,0:T(8,128)(2,1)} %constant_dynamic-update-slice_fusion.5), channel_id=1, source_target_pairs={{0,16},{8,40},{16,0},{24,56},{32,48},{40,8},{48,32},{56,24},{64,80... | collective-permute-start | bytes 3145736 | tf_op jit(solution)/shard_map/ppermute | solution.py:38
  149.7 30.1 %collective-permute-start.19 = (bf16[2,32,32,64]{3,2,1,0:T(8,128)(2,1)S(1)}, bf16[2,32,32,64]{3,2,1,0:T(8,128)(2,1)S(1)}, u32[]{:S(2)}, u32[]{:S(2)}) collective-permute-start(bf16[2,32,32,64]{3,2,1,0:T(8,128)(2,1)S(1)} %pad_maximum_fusion.11), channel_id=1, source_target_pairs={{0,128},{8,136},{16,144},{24,152},{32,160},{40,168},{48,176},{56,1... | collective-permute-start | bytes 786440 | tf_op jit(solution)/shard_map/ppermute | solution.py:209
  180.1 55.5 %collective-permute-start.20 = (bf16[2,1,1,1,64,1024]{5,4,3,2,1,0:T(8,128)(2,1)S(1)}, bf16[2,1,1,1,64,1024]{5,4,3,2,1,0:T(8,128)(2,1)S(1)}, u32[]{:S(2)}, u32[]{:S(2)}) collective-permute-start(bf16[2,1,1,1,64,1024]{5,4,3,2,1,0:T(8,128)(2,1)S(1)} %maximum_bitcast_fusion), channel_id=1, source_target_pairs={{0,1},{1,0},{2,3},{3,2},{4,5},{5,4},{6,7},{7,6},{8,9},{9,8},{10,11... | collective-permute-start | bytes 786440 | tf_op jit(solution)/shard_map/ppermute | solution.py:18
  185.6 96.3 %collective-permute-start.14 = (bf16[2,2,2,2,2,1,1,64,512]{8,7,6,5,4,3,2,1,0:T(8,128)(2,1)S(1)}, bf16[2,2,2,2,2,1,1,64,512]{8,7,6,5,4,3,2,1,0:T(8,128)(2,1)}, u32[]{:S(2)}, u32[]{:S(2)}) collective-permute-start(bf16[2,2,2,2,2,1,1,64,512]{8,7,6,5,4,3,2,1,0:T(8,128)(2,1)S(1)} %constant_dynamic-update-slice_fus, ...), channel_id=1, source_target_pairs={{0,8},{8,0},{16,40},{24,32},{32,24},{40,16},{48,56},{56,48},{64,72... | collective-permute-start | bytes 6291464 | tf_op jit(solution)/shard_map/ppermute | solution.py:38
  235.7 15.6 %collective-permute-start.21 = (bf16[2,1,1,2,64,1024]{5,4,3,2,1,0:T(8,128)(2,1)S(1)}, bf16[2,1,1,2,64,1024]{5,4,3,2,1,0:T(8,128)(2,1)}, u32[]{:S(2)}, u32[]{:S(2)}) collective-permute-start(bf16[2,1,1,2,64,1024]{5,4,3,2,1,0:T(8,128)(2,1)S(1)} %constant_dynamic-update-slice_fusion.2), channel_id=1, source_target_pairs={{0,4},{1,5},{2,6},{3,7},{4,0},{5,1},{6,2},{7,3},{8,12},{9,13},{10,... | collective-permute-start | bytes 1572872 | tf_op jit(solution)/shard_map/ppermute | solution.py:18
  253.2 24.7 %collective-permute-start.22 = (bf16[2,2,1,2,64,1024]{5,4,3,2,1,0:T(8,128)(2,1)}, bf16[2,2,1,2,64,1024]{5,4,3,2,1,0:T(8,128)(2,1)}, u32[]{:S(2)}, u32[]{:S(2)}) collective-permute-start(bf16[2,2,1,2,64,1024]{5,4,3,2,1,0:T(8,128)(2,1)} %constant_dynamic-update-slice_fusion.1), channel_id=1, source_target_pairs={{0,2},{1,3},{2,0},{3,1},{4,6},{5,7},{6,4},{7,5},{8,10},{9,11},{10,... | collective-permute-start | bytes 3145736 | tf_op jit(solution)/shard_map/ppermute | solution.py:18
  298.5 10.0 %collective-permute-start.29 = (f32[4,32,128]{2,1,0:T(8,128)S(1)}, f32[4,32,128]{2,1,0:T(8,128)S(1)}, u32[]{:S(2)}, u32[]{:S(2)}) collective-permute-start(f32[4,32,128]{2,1,0:T(8,128)S(1)} %get-tuple-element.14), channel_id=1, source_target_pairs={{0,7},{1,6},{2,5},{3,4},{4,3},{5,2},{6,1},{7,0},{8,15},{9,14},{10,... | collective-permute-start | bytes 196616 | tf_op jit(solution)/shard_map/ppermute | solution.py:18
  301.5 11.3 %collective-permute-start.27 = (f32[4,32,128]{2,1,0:T(8,128)S(1)}, f32[4,32,128]{2,1,0:T(8,128)S(1)}, u32[]{:S(2)}, u32[]{:S(2)}) collective-permute-start(f32[4,32,128]{2,1,0:T(8,128)S(1)} %get-tuple-element.16), channel_id=1, source_target_pairs={{0,5},{1,4},{2,7},{3,6},{4,1},{5,0},{6,3},{7,2},{8,13},{9,12},{10,... | collective-permute-start | bytes 196616 | tf_op jit(solution)/shard_map/ppermute | solution.py:18
  315.3 11.4 %collective-permute-start.30 = (f32[4,32,128]{2,1,0:T(8,128)S(1)}, f32[4,32,128]{2,1,0:T(8,128)S(1)}, u32[]{:S(2)}, u32[]{:S(2)}) collective-permute-start(f32[4,32,128]{2,1,0:T(8,128)S(1)} %get-tuple-element.6), channel_id=1, source_target_pairs={{0,1},{1,0},{2,3},{3,2},{4,5},{5,4},{6,7},{7,6},{8,9},{9,8},{10,11... | collective-permute-start | bytes 196616 | tf_op jit(solution)/shard_map/ppermute | solution.py:18
  318.7 10.8 %collective-permute-start.31 = (f32[4,32,128]{2,1,0:T(8,128)S(1)}, f32[4,32,128]{2,1,0:T(8,128)S(1)}, u32[]{:S(2)}, u32[]{:S(2)}) collective-permute-start(f32[4,32,128]{2,1,0:T(8,128)S(1)} %get-tuple-element.6), channel_id=1, source_target_pairs={{0,2},{1,3},{2,0},{3,1},{4,6},{5,7},{6,4},{7,5},{8,10},{9,11},{10,... | collective-permute-start | bytes 196616 | tf_op jit(solution)/shard_map/ppermute | solution.py:18
  319.0 10.7 %collective-permute-start.32 = (f32[4,32,128]{2,1,0:T(8,128)S(1)}, f32[4,32,128]{2,1,0:T(8,128)S(1)}, u32[]{:S(2)}, u32[]{:S(2)}) collective-permute-start(f32[4,32,128]{2,1,0:T(8,128)S(1)} %get-tuple-element.6), channel_id=1, source_target_pairs={{0,3},{1,2},{2,1},{3,0},{4,7},{5,6},{6,5},{7,4},{8,11},{9,10},{10,... | collective-permute-start | bytes 196616 | tf_op jit(solution)/shard_map/ppermute | solution.py:18
  (20 other events, 219.4 us)

commit v10 on v4

--- a/solution.py
+++ b/solution.py
@@ -135,7 +135,7 @@
     steps, slots, local, waves = permuted.shape
     cols = moving.shape[2]
     return pl.pallas_call(
-        functools.partial(contract_kernel, block, 8 if slots % 8 == 0 else 1),
+        functools.partial(contract_kernel, block, 16 if slots % 16 == 0 else 1),
         out_shape=jax.ShapeDtypeStruct((steps, local, cols), jnp.bfloat16),
         grid_spec=pltpu.PrefetchScalarGridSpec(
             num_scalar_prefetch=1,

time: 288 us -> 318 us (1.10)
  the two profiles are of different devices: /device:TPU:32 before, /device:TPU:128 now
where the time goes in v10:
time: 318 us; the launch traced here: 317 us
  waiting for transfers between devices  159 us (50%)
  starting transfers between devices  101 us (32%)
  other arithmetic  27.2 us (9%)
  Pallas kernels  11.1 us (3%)
  between operations  8.44 us (3%)
  local copies, waits for them, and re-layouts  8.32 us (3%)
    ppermute x15, waiting for transfers between devices, swap_relabelled(): return lax.ppermute(value, axis, pairs)  93.2 us
    ppermute x17, starting transfers between devices, swap(): return lax.ppermute(value, axis, [(i, i ^ bit) for i in range(count)])  82.1 us
    ppermute x17, waiting for transfers between devices, swap(): return lax.ppermute(value, axis, [(i, i ^ bit) for i in range(count)])  37.2 us
    ppermute x4, waiting for transfers between devices, body(): hopped = lax.ppermute(jnp.stack(moving), 'ka', pairs)  28.9 us
    ppermute x15, starting transfers between devices, swap_relabelled(): return lax.ppermute(value, axis, pairs)  13.1 us
    pallas_call x1, Pallas kernels, contract(): pl.pallas_call(functools.partial(contract_kernel, block, 16 if slots % 16...  11.1 us
    concatenate x8, other arithmetic, join(): return jnp.concatenate([low, high], axis=axis_at)  9.5 us
    select_n x8, other arithmetic, join(): low = jnp.where(mine == 0, h, g)  7.12 us
  transfers between devices with their start and end apart: 37, of which 20 were waited for; matrix products, arithmetic and copies ran while one was open for 9% of the time, Pallas kernels for 0%

profile of v10, /device:TPU:128, one launch (start us, length us, event | category | flops | bytes accessed | tf_op | source)
XLA Modules:
  0.0 317.0 jit_solution(4238296829891427305)
XLA Ops:
  12.6 3.8 %collective-permute-start.6 = (s32[2,2,2,2,1,1,1,512]{7,5,6,4,3,2,1,0:T(1,128)S(1)}, s32[2,2,2,2,1,1,1,512]{7,5,6,4,3,2,1,0:T(1,128)S(1)}, u32[]{:S(2)}, u32[]{:S(2)}) collective-permute-start(s32[2,2,2,2,1,1,1,512]{7,5,6,4,3,2,1,0:T(1,128)S(1)} %pad_add_fusion), channel_id=1, source_target_pairs={{0,16},{8,40},{16,0},{24,56},{32,48},{40,8},{48,32},{56,24},{64,80... | collective-permute-start | bytes 98312 | tf_op jit(solution)/shard_map/ppermute | solution.py:38
  16.4 14.3 %collective-permute-done.6 = s32[2,2,2,2,1,1,1,512]{7,5,6,4,3,2,1,0:T(1,128)S(1)} collective-permute-done((s32[2,2,2,2,1,1,1,512]{7,5,6,4,3,2,1,0:T(1,128)S(1)}, s32[2,2,2,2,1,1,1,512]{7,5,6,4,3,2,1,0:T(1,128)S(1)}, u32[]{:S(2)}, u32[]{:S(2)}) %collective-permute-start.6) | collective-permute-done | bytes 32800 | tf_op jit(solution)/shard_map/ppermute | solution.py:38
  30.8 3.3 %collective-permute-start.7 = (s32[2,2,2,1,1,1,1,512]{7,5,6,4,3,2,1,0:T(1,128)S(1)}, s32[2,2,2,1,1,1,1,512]{7,5,6,4,3,2,1,0:T(1,128)S(1)}, u32[]{:S(2)}, u32[]{:S(2)}) collective-permute-start(s32[2,2,2,1,1,1,1,512]{7,5,6,4,3,2,1,0:T(1,128)S(1)} %pad_add_fusion.1), channel_id=1, source_target_pairs={{0,32},{8,24},{16,48},{24,8},{32,0},{40,56},{48,16},{56,40},{64,96... | collective-permute-start | bytes 49160 | tf_op jit(solution)/shard_map/ppermute | solution.py:38
  43.2 13.1 %collective-permute-done.1 = bf16[2,2,2,2,1,1,1,64,512]{8,7,1,3,2,6,5,4,0:T(8,128)(2,1)} collective-permute-done((bf16[2,2,2,2,1,1,1,64,512]{8,7,1,3,2,6,5,4,0:T(8,128)(2,1)}, bf16[2,2,2,2,1,1,1,64,512]{8,7,1,3,2,6,5,4,0:T(8,128)(2,1)}, u32[]{:S(2)}, u32[]{:S(2)}) %collective-permute-start.1) | collective-permute-done | bytes 1048608 | tf_op jit(solution)/shard_map/ppermute | solution.py:38
  59.0 11.9 %collective-permute-done.2 = bf16[2,2,2,1,1,1,1,64,512]{8,7,1,2,6,5,4,3,0:T(8,128)(2,1)S(1)} collective-permute-done((bf16[2,2,2,1,1,1,1,64,512]{8,7,1,2,6,5,4,3,0:T(8,128)(2,1)S(1)}, bf16[2,2,2,1,1,1,1,64,512]{8,7,1,2,6,5,4,3,0:T(8,128)(2,1)S(1)}, u32[]{:S(2)}, u32[]{:S(2)}) %collective-permute-start.2) | collective-permute-done | bytes 524320 | tf_op jit(solution)/shard_map/ppermute | solution.py:38
  71.5 14.6 %collective-permute-done.3 = bf16[2,2,1,1,1,1,1,64,512]{8,7,1,6,5,4,3,2,0:T(8,128)(2,1)S(1)} collective-permute-done((bf16[2,2,1,1,1,1,1,64,512]{8,7,1,6,5,4,3,2,0:T(8,128)(2,1)S(1)}, bf16[2,2,1,1,1,1,1,64,512]{8,7,1,6,5,4,3,2,0:T(8,128)(2,1)S(1)}, u32[]{:S(2)}, u32[]{:S(2)}) %collective-permute-start.3) | collective-permute-done | bytes 262176 | tf_op jit(solution)/shard_map/ppermute | solution.py:38
  86.6 9.4 %collective-permute-done.4 = bf16[2,1,1,1,1,1,1,64,512]{8,7,6,5,4,3,2,1,0:T(8,128)(2,1)S(1)} collective-permute-done((bf16[2,1,1,1,1,1,1,64,512]{8,7,6,5,4,3,2,1,0:T(8,128)(2,1)S(1)}, bf16[2,1,1,1,1,1,1,64,512]{8,7,6,5,4,3,2,1,0:T(8,128)(2,1)S(1)}, u32[]{:S(2)}, u32[]{:S(2)}) %collective-permute-start.4) | collective-permute-done | bytes 131104 | tf_op jit(solution)/shard_map/ppermute | solution.py:38
  98.3 7.5 %collective-permute-done.10 = bf16[2,1,1,1,1,1,1,64,512]{8,7,6,5,4,3,2,1,0:T(8,128)(2,1)S(1)} collective-permute-done((bf16[2,1,1,1,1,1,1,64,512]{8,7,6,5,4,3,2,1,0:T(8,128)(2,1)S(1)}, bf16[2,1,1,1,1,1,1,64,512]{8,7,6,5,4,3,2,1,0:T(8,128)(2,1)S(1)}, u32[]{:S(2)}, u32[]{:S(2)}) %collective-permute-start.10) | collective-permute-done | bytes 131104 | tf_op jit(solution)/shard_map/ppermute | solution.py:38
  105.9 4.2 %collective-permute-done.17 = bf16[2,32,32,64]{3,2,1,0:T(8,128)(2,1)S(1)} collective-permute-done((bf16[2,32,32,64]{3,2,1,0:T(8,128)(2,1)S(1)}, bf16[2,32,32,64]{3,2,1,0:T(8,128)(2,1)S(1)}, u32[]{:S(2)}, u32[]{:S(2)}) %collective-permute-start.17) | collective-permute-done | bytes 262176 | tf_op jit(solution)/shard_map/ppermute | solution.py:210
  111.1 4.8 %collective-permute-start.18 = (bf16[2,32,32,64]{3,2,1,0:T(8,128)(2,1)}, bf16[2,32,32,64]{3,2,1,0:T(8,128)(2,1)S(1)}, u32[]{:S(2)}, u32[]{:S(2)}) collective-permute-start(bf16[2,32,32,64]{3,2,1,0:T(8,128)(2,1)} %pad_maximum_fusion.10), channel_id=1, source_target_pairs={{0,64},{8,200},{16,80},{24,216},{32,96},{40,232},{48,112},{56,248}... | collective-permute-start | bytes 786440 | tf_op jit(solution)/shard_map/ppermute | solution.py:210
  115.9 9.6 %collective-permute-done.11 = bf16[2,2,1,1,1,1,1,64,512]{8,7,6,5,4,3,2,1,0:T(8,128)(2,1)S(1)} collective-permute-done((bf16[2,2,1,1,1,1,1,64,512]{8,7,6,5,4,3,2,1,0:T(8,128)(2,1)S(1)}, bf16[2,2,1,1,1,1,1,64,512]{8,7,6,5,4,3,2,1,0:T(8,128)(2,1)S(1)}, u32[]{:S(2)}, u32[]{:S(2)}) %collective-permute-start.11) | collective-permute-done | bytes 262176 | tf_op jit(solution)/shard_map/ppermute | solution.py:38
  126.5 6.6 %collective-permute-done.18 = bf16[2,32,32,64]{3,2,1,0:T(8,128)(2,1)S(1)} collective-permute-done((bf16[2,32,32,64]{3,2,1,0:T(8,128)(2,1)}, bf16[2,32,32,64]{3,2,1,0:T(8,128)(2,1)S(1)}, u32[]{:S(2)}, u32[]{:S(2)}) %collective-permute-start.18) | collective-permute-done | bytes 262176 | tf_op jit(solution)/shard_map/ppermute | solution.py:210
  134.0 11.6 %collective-permute-done.12 = bf16[2,2,2,1,1,1,1,64,512]{8,7,6,5,4,3,2,1,0:T(8,128)(2,1)} collective-permute-done((bf16[2,2,2,1,1,1,1,64,512]{8,7,6,5,4,3,2,1,0:T(8,128)(2,1)}, bf16[2,2,2,1,1,1,1,64,512]{8,7,6,5,4,3,2,1,0:T(8,128)(2,1)}, u32[]{:S(2)}, u32[]{:S(2)}) %collective-permute-start.12) | collective-permute-done | bytes 524320 | tf_op jit(solution)/shard_map/ppermute | solution.py:38
  150.8 17.1 %collective-permute-done.19 = bf16[2,32,32,64]{3,2,1,0:T(8,128)(2,1)} collective-permute-done((bf16[2,32,32,64]{3,2,1,0:T(8,128)(2,1)S(1)}, bf16[2,32,32,64]{3,2,1,0:T(8,128)(2,1)}, u32[]{:S(2)}, u32[]{:S(2)}) %collective-permute-start.19) | collective-permute-done | bytes 262176 | tf_op jit(solution)/shard_map/ppermute | solution.py:210
  169.3 4.0 %collective-permute-start.20 = (bf16[2,1,1,1,64,1024]{5,4,3,2,1,0:T(8,128)(2,1)S(1)}, bf16[2,1,1,1,64,1024]{5,4,3,2,1,0:T(8,128)(2,1)S(1)}, u32[]{:S(2)}, u32[]{:S(2)}) collective-permute-start(bf16[2,1,1,1,64,1024]{5,4,3,2,1,0:T(8,128)(2,1)S(1)} %maximum_bitcast_fusion), channel_id=1, source_target_pairs={{0,1},{1,0},{2,3},{3,2},{4,5},{5,4},{6,7},{7,6},{8,9},{9,8},{10,11... | collective-permute-start | bytes 786440 | tf_op jit(solution)/shard_map/ppermute | solution.py:18
  173.3 4.3 %collective-permute-done.20 = bf16[2,1,1,1,64,1024]{5,4,3,2,1,0:T(8,128)(2,1)S(1)} collective-permute-done((bf16[2,1,1,1,64,1024]{5,4,3,2,1,0:T(8,128)(2,1)S(1)}, bf16[2,1,1,1,64,1024]{5,4,3,2,1,0:T(8,128)(2,1)S(1)}, u32[]{:S(2)}, u32[]{:S(2)}) %collective-permute-start.20) | collective-permute-done | bytes 262176 | tf_op jit(solution)/shard_map/ppermute | solution.py:18
  184.6 5.0 %collective-permute-done.21 = bf16[2,1,1,2,64,1024]{5,4,3,2,1,0:T(8,128)(2,1)} collective-permute-done((bf16[2,1,1,2,64,1024]{5,4,3,2,1,0:T(8,128)(2,1)}, bf16[2,1,1,2,64,1024]{5,4,3,2,1,0:T(8,128)(2,1)}, u32[]{:S(2)}, u32[]{:S(2)}) %collective-permute-start.21) | collective-permute-done | bytes 524320 | tf_op jit(solution)/shard_map/ppermute | solution.py:18
  194.2 19.4 %collective-permute-done.22 = bf16[2,2,1,2,64,1024]{5,4,3,2,1,0:T(8,128)(2,1)} collective-permute-done((bf16[2,2,1,2,64,1024]{5,4,3,2,1,0:T(8,128)(2,1)}, bf16[2,2,1,2,64,1024]{5,4,3,2,1,0:T(8,128)(2,1)}, u32[]{:S(2)}, u32[]{:S(2)}) %collective-permute-start.22) | collective-permute-done | bytes 1048608 | tf_op jit(solution)/shard_map/ppermute | solution.py:18
  220.8 11.1 %shard_map.73 = bf16[2,64,1024]{2,1,0:T(8,128)(2,1)} custom-call(s32[32]{0:T(128)} %q_ref.1, bf16[2,32,64,512]{3,2,1,0:T(8,128)(2,1)} %bitcast.256, bf16[2,512,1024]{2,1,0:T(8,128)(2,1)} %bitcast.262), custom_call_target="tpu_custom_call" | custom-call | flops 4294967296 | bytes 6553600 | tf_op jit(solution)/shard_map/pallas_call | solution.py:137
  233.8 46.8 %collective-permute-start.29 = (f32[4,32,128]{2,1,0:T(8,128)S(1)}, f32[4,32,128]{2,1,0:T(8,128)S(1)}, u32[]{:S(2)}, u32[]{:S(2)}) collective-permute-start(f32[4,32,128]{2,1,0:T(8,128)S(1)} %get-tuple-element.24), channel_id=1, source_target_pairs={{0,7},{1,6},{2,5},{3,4},{4,3},{5,2},{6,1},{7,0},{8,15},{9,14},{10,... | collective-permute-start | bytes 196616 | tf_op jit(solution)/shard_map/ppermute | solution.py:18
  280.6 4.4 %collective-permute-start.28 = (f32[4,32,128]{2,1,0:T(8,128)S(1)}, f32[4,32,128]{2,1,0:T(8,128)S(1)}, u32[]{:S(2)}, u32[]{:S(2)}) collective-permute-start(f32[4,32,128]{2,1,0:T(8,128)S(1)} %get-tuple-element.25), channel_id=1, source_target_pairs={{0,6},{1,7},{2,4},{3,5},{4,2},{5,3},{6,0},{7,1},{8,14},{9,15},{10,... | collective-permute-start | bytes 196616 | tf_op jit(solution)/shard_map/ppermute | solution.py:18
  285.8 4.3 %collective-permute-start.25 = (f32[4,32,128]{2,1,0:T(8,128)S(1)}, f32[4,32,128]{2,1,0:T(8,128)S(1)}, u32[]{:S(2)}, u32[]{:S(2)}) collective-permute-start(f32[4,32,128]{2,1,0:T(8,128)S(1)} %get-tuple-element.28), channel_id=1, source_target_pairs={{0,3},{1,2},{2,1},{3,0},{4,7},{5,6},{6,5},{7,4},{8,11},{9,10},{10,... | collective-permute-start | bytes 196616 | tf_op jit(solution)/shard_map/ppermute | solution.py:18
  299.5 4.4 %collective-permute-start.32 = (f32[4,32,128]{2,1,0:T(8,128)S(1)}, f32[4,32,128]{2,1,0:T(8,128)S(1)}, u32[]{:S(2)}, u32[]{:S(2)}) collective-permute-start(f32[4,32,128]{2,1,0:T(8,128)S(1)} %get-tuple-element.6), channel_id=1, source_target_pairs={{0,3},{1,2},{2,1},{3,0},{4,7},{5,6},{6,5},{7,4},{8,11},{9,10},{10,... | collective-permute-start | bytes 196616 | tf_op jit(solution)/shard_map/ppermute | solution.py:18
  307.6 5.6 %collective-permute-start.36 = (f32[4,32,128]{2,1,0:T(8,128)S(1)}, f32[4,32,128]{2,1,0:T(8,128)S(1)}, u32[]{:S(2)}, u32[]{:S(2)}) collective-permute-start(f32[4,32,128]{2,1,0:T(8,128)S(1)} %get-tuple-element.6), channel_id=1, source_target_pairs={{0,7},{1,6},{2,5},{3,4},{4,3},{5,2},{6,1},{7,0},{8,15},{9,14},{10,... | collective-permute-start | bytes 196616 | tf_op jit(solution)/shard_map/ppermute | solution.py:18
  (168 shorter events, 67.5 us)
Async XLA Ops:
  1.0 11.4 %collective-permute-start.5 = (s32[2,2,2,2,1,1,512]{6,4,3,2,1,0,5:T(1,128)S(1)}, s32[2,2,2,2,1,1,512]{6,4,3,2,1,0,5:T(1,128)S(1)}, u32[]{:S(2)}, u32[]{:S(2)}) collective-permute-start(s32[2,2,2,2,1,1,512]{6,4,3,2,1,0,5:T(1,128)S(1)} %constant_dynamic-slice_fusion.12), channel_id=1, source_target_pairs={{0,8},{8,0},{16,40},{24,32},{32,24},{40,16},{48,56},{56,48},{64,72... | collective-permute-start | bytes 98312 | tf_op jit(solution)/shard_map/ppermute | solution.py:38
  5.0 29.0 %collective-permute-start = (bf16[2,2,2,2,1,1,64,512]{7,6,4,3,2,1,0,5:T(8,128)(2,1)}, bf16[2,2,2,2,1,1,64,512]{7,6,4,3,2,1,0,5:T(8,128)(2,1)}, u32[]{:S(2)}, u32[]{:S(2)}) collective-permute-start(bf16[2,2,2,2,1,1,64,512]{7,6,4,3,2,1,0,5:T(8,128)(2,1)} %constant_dynamic-slice_fusion.15), channel_id=1, source_target_pairs={{0,8},{8,0},{16,40},{24,32},{32,24},{40,16},{48,56},{56,48},{64,72... | collective-permute-start | bytes 3145736 | tf_op jit(solution)/shard_map/ppermute | solution.py:38
  12.6 18.1 %collective-permute-start.6 = (s32[2,2,2,2,1,1,1,512]{7,5,6,4,3,2,1,0:T(1,128)S(1)}, s32[2,2,2,2,1,1,1,512]{7,5,6,4,3,2,1,0:T(1,128)S(1)}, u32[]{:S(2)}, u32[]{:S(2)}) collective-permute-start(s32[2,2,2,2,1,1,1,512]{7,5,6,4,3,2,1,0:T(1,128)S(1)} %pad_add_fusion), channel_id=1, source_target_pairs={{0,16},{8,40},{16,0},{24,56},{32,48},{40,8},{48,32},{56,24},{64,80... | collective-permute-start | bytes 98312 | tf_op jit(solution)/shard_map/ppermute | solution.py:38
  38.3 17.9 %collective-permute-start.1 = (bf16[2,2,2,2,1,1,1,64,512]{8,7,1,3,2,6,5,4,0:T(8,128)(2,1)}, bf16[2,2,2,2,1,1,1,64,512]{8,7,1,3,2,6,5,4,0:T(8,128)(2,1)}, u32[]{:S(2)}, u32[]{:S(2)}) collective-permute-start(bf16[2,2,2,2,1,1,1,64,512]{8,7,1,3,2,6,5,4,0:T(8,128)(2,1)} %pad_maximum_fusion.3), channel_id=1, source_target_pairs={{0,16},{8,40},{16,0},{24,56},{32,48},{40,8},{48,32},{56,24},{64,80... | collective-permute-start | bytes 3145736 | tf_op jit(solution)/shard_map/ppermute | solution.py:38
  40.4 45.9 %collective-permute-start.15 = (bf16[32,32,64]{2,1,0:T(8,128)(2,1)S(1)}, bf16[32,32,64]{2,1,0:T(8,128)(2,1)S(1)}, u32[]{:S(2)}, u32[]{:S(2)}) collective-permute-start(bf16[32,32,64]{2,1,0:T(8,128)(2,1)S(1)} %convolution_convert_fusion), channel_id=1, source_target_pairs={{0,8},{8,16},{16,24},{24,32},{32,40},{40,48},{48,56},{56,64},{64,7... | collective-permute-start | bytes 393224 | tf_op jit(solution)/shard_map/ppermute | solution.py:13
  58.7 12.1 %collective-permute-start.2 = (bf16[2,2,2,1,1,1,1,64,512]{8,7,1,2,6,5,4,3,0:T(8,128)(2,1)S(1)}, bf16[2,2,2,1,1,1,1,64,512]{8,7,1,2,6,5,4,3,0:T(8,128)(2,1)S(1)}, u32[]{:S(2)}, u32[]{:S(2)}) collective-permute-start(bf16[2,2,2,1,1,1,1,64,512]{8,7,1,2,6,5,4,3,0:T(8,128)(2,1)S(1)} %pad_maximum_fusion.6), channel_id=1, source_target_pairs={{0,32},{8,24},{16,48},{24,8},{32,0},{40,56},{48,16},{56,40},{64,96... | collective-permute-start | bytes 1572872 | tf_op jit(solution)/shard_map/ppermute | solution.py:38
  58.9 12.7 %collective-permute-start.9 = (s32[2,1,1,1,1,1,1,512]{7,6,5,4,3,2,1,0:T(1,128)S(1)}, s32[2,1,1,1,1,1,1,512]{7,6,5,4,3,2,1,0:T(1,128)S(1)}, u32[]{:S(2)}, u32[]{:S(2)}) collective-permute-start(s32[2,1,1,1,1,1,1,512]{7,6,5,4,3,2,1,0:T(1,128)S(1)} %pad_add_fusion.3), channel_id=1, source_target_pairs={{0,128},{8,136},{16,144},{24,152},{32,160},{40,168},{48,176},{56,1... | collective-permute-start | bytes 12296 | tf_op jit(solution)/shard_map/ppermute | solution.py:38
  71.0 15.1 %collective-permute-start.3 = (bf16[2,2,1,1,1,1,1,64,512]{8,7,1,6,5,4,3,2,0:T(8,128)(2,1)S(1)}, bf16[2,2,1,1,1,1,1,64,512]{8,7,1,6,5,4,3,2,0:T(8,128)(2,1)S(1)}, u32[]{:S(2)}, u32[]{:S(2)}) collective-permute-start(bf16[2,2,1,1,1,1,1,64,512]{8,7,1,6,5,4,3,2,0:T(8,128)(2,1)S(1)} %pad_maximum_fusion.13), channel_id=1, source_target_pairs={{0,64},{8,72},{16,80},{24,88},{32,96},{40,104},{48,112},{56,120},{... | collective-permute-start | bytes 786440 | tf_op jit(solution)/shard_map/ppermute | solution.py:38
  86.2 9.7 %collective-permute-start.4 = (bf16[2,1,1,1,1,1,1,64,512]{8,7,6,5,4,3,2,1,0:T(8,128)(2,1)S(1)}, bf16[2,1,1,1,1,1,1,64,512]{8,7,6,5,4,3,2,1,0:T(8,128)(2,1)S(1)}, u32[]{:S(2)}, u32[]{:S(2)}) collective-permute-start(bf16[2,1,1,1,1,1,1,64,512]{8,7,6,5,4,3,2,1,0:T(8,128)(2,1)S(1)} %pad_maximum_fusion.15), channel_id=1, source_target_pairs={{0,128},{8,136},{16,144},{24,152},{32,160},{40,168},{48,176},{56,1... | collective-permute-start | bytes 393224 | tf_op jit(solution)/shard_map/ppermute | solution.py:38
  86.5 11.4 %collective-permute-start.16 = (bf16[2,32,32,64]{3,2,1,0:T(8,128)(2,1)S(1)}, bf16[2,32,32,64]{3,2,1,0:T(8,128)(2,1)S(1)}, u32[]{:S(2)}, u32[]{:S(2)}) collective-permute-start(bf16[2,32,32,64]{3,2,1,0:T(8,128)(2,1)S(1)} %pad_maximum_fusion.8), channel_id=1, source_target_pairs={{0,16},{8,248},{16,32},{24,8},{32,48},{40,24},{48,64},{56,40},{64,... | collective-permute-start | bytes 786440 | tf_op jit(solution)/shard_map/ppermute | solution.py:210
  96.7 9.1 %collective-permute-start.10 = (bf16[2,1,1,1,1,1,1,64,512]{8,7,6,5,4,3,2,1,0:T(8,128)(2,1)S(1)}, bf16[2,1,1,1,1,1,1,64,512]{8,7,6,5,4,3,2,1,0:T(8,128)(2,1)S(1)}, u32[]{:S(2)}, u32[]{:S(2)}) collective-permute-start(bf16[2,1,1,1,1,1,1,64,512]{8,7,6,5,4,3,2,1,0:T(8,128)(2,1)S(1)} %pad_maximum_fusion.16), channel_id=1, source_target_pairs={{0,128},{8,136},{16,144},{24,152},{32,160},{40,168},{48,176},{56,1... | collective-permute-start | bytes 393224 | tf_op jit(solution)/shard_map/ppermute | solution.py:38
  98.0 12.1 %collective-permute-start.17 = (bf16[2,32,32,64]{3,2,1,0:T(8,128)(2,1)S(1)}, bf16[2,32,32,64]{3,2,1,0:T(8,128)(2,1)S(1)}, u32[]{:S(2)}, u32[]{:S(2)}) collective-permute-start(bf16[2,32,32,64]{3,2,1,0:T(8,128)(2,1)S(1)} %pad_maximum_fusion.9), channel_id=1, source_target_pairs={{0,32},{8,232},{16,48},{24,248},{32,64},{40,8},{48,80},{56,24},{64... | collective-permute-start | bytes 786440 | tf_op jit(solution)/shard_map/ppermute | solution.py:210
  105.8 19.7 %collective-permute-start.11 = (bf16[2,2,1,1,1,1,1,64,512]{8,7,6,5,4,3,2,1,0:T(8,128)(2,1)S(1)}, bf16[2,2,1,1,1,1,1,64,512]{8,7,6,5,4,3,2,1,0:T(8,128)(2,1)S(1)}, u32[]{:S(2)}, u32[]{:S(2)}) collective-permute-start(bf16[2,2,1,1,1,1,1,64,512]{8,7,6,5,4,3,2,1,0:T(8,128)(2,1)S(1)} %pad_maximum_fusion.14), channel_id=1, source_target_pairs={{0,64},{8,72},{16,80},{24,88},{32,96},{40,104},{48,112},{56,120},{... | collective-permute-start | bytes 786440 | tf_op jit(solution)/shard_map/ppermute | solution.py:38
  111.1 22.0 %collective-permute-start.18 = (bf16[2,32,32,64]{3,2,1,0:T(8,128)(2,1)}, bf16[2,32,32,64]{3,2,1,0:T(8,128)(2,1)S(1)}, u32[]{:S(2)}, u32[]{:S(2)}) collective-permute-start(bf16[2,32,32,64]{3,2,1,0:T(8,128)(2,1)} %pad_maximum_fusion.10), channel_id=1, source_target_pairs={{0,64},{8,200},{16,80},{24,216},{32,96},{40,232},{48,112},{56,248}... | collective-permute-start | bytes 786440 | tf_op jit(solution)/shard_map/ppermute | solution.py:210
  126.5 19.1 %collective-permute-start.12 = (bf16[2,2,2,1,1,1,1,64,512]{8,7,6,5,4,3,2,1,0:T(8,128)(2,1)}, bf16[2,2,2,1,1,1,1,64,512]{8,7,6,5,4,3,2,1,0:T(8,128)(2,1)}, u32[]{:S(2)}, u32[]{:S(2)}) collective-permute-start(bf16[2,2,2,1,1,1,1,64,512]{8,7,6,5,4,3,2,1,0:T(8,128)(2,1)} %pad_maximum_fusion.7), channel_id=1, source_target_pairs={{0,32},{8,24},{16,48},{24,8},{32,0},{40,56},{48,16},{56,40},{64,96... | collective-permute-start | bytes 1572872 | tf_op jit(solution)/shard_map/ppermute | solution.py:38
  133.3 34.7 %collective-permute-start.19 = (bf16[2,32,32,64]{3,2,1,0:T(8,128)(2,1)S(1)}, bf16[2,32,32,64]{3,2,1,0:T(8,128)(2,1)}, u32[]{:S(2)}, u32[]{:S(2)}) collective-permute-start(bf16[2,32,32,64]{3,2,1,0:T(8,128)(2,1)S(1)} %pad_maximum_fusion.11), channel_id=1, source_target_pairs={{0,128},{8,136},{16,144},{24,152},{32,160},{40,168},{48,176},{56,1... | collective-permute-start | bytes 786440 | tf_op jit(solution)/shard_map/ppermute | solution.py:210
  147.9 33.7 %collective-permute-start.13 = (bf16[2,2,2,2,1,1,1,64,512]{8,7,6,5,4,3,2,1,0:T(8,128)(2,1)}, bf16[2,2,2,2,1,1,1,64,512]{8,7,6,5,4,3,2,1,0:T(8,128)(2,1)}, u32[]{:S(2)}, u32[]{:S(2)}) collective-permute-start(bf16[2,2,2,2,1,1,1,64,512]{8,7,6,5,4,3,2,1,0:T(8,128)(2,1)} %pad_maximum_fusion.4), channel_id=1, source_target_pairs={{0,16},{8,40},{16,0},{24,56},{32,48},{40,8},{48,32},{56,24},{64,80... | collective-permute-start | bytes 3145736 | tf_op jit(solution)/shard_map/ppermute | solution.py:38
  178.6 11.0 %collective-permute-start.21 = (bf16[2,1,1,2,64,1024]{5,4,3,2,1,0:T(8,128)(2,1)}, bf16[2,1,1,2,64,1024]{5,4,3,2,1,0:T(8,128)(2,1)}, u32[]{:S(2)}, u32[]{:S(2)}) collective-permute-start(bf16[2,1,1,2,64,1024]{5,4,3,2,1,0:T(8,128)(2,1)} %pad_maximum_fusion.12), channel_id=1, source_target_pairs={{0,4},{1,5},{2,6},{3,7},{4,0},{5,1},{6,2},{7,3},{8,12},{9,13},{10,... | collective-permute-start | bytes 1572872 | tf_op jit(solution)/shard_map/ppermute | solution.py:18
  184.6 32.0 %collective-permute-start.14 = (bf16[2,2,2,2,2,1,1,64,512]{8,7,6,5,4,3,2,1,0:T(8,128)(2,1)}, bf16[2,2,2,2,2,1,1,64,512]{8,7,6,5,4,3,2,1,0:T(8,128)(2,1)}, u32[]{:S(2)}, u32[]{:S(2)}) collective-permute-start(bf16[2,2,2,2,2,1,1,64,512]{8,7,6,5,4,3,2,1,0:T(8,128)(2,1)} %pad_maximum_fusion.1), channel_id=1, source_target_pairs={{0,8},{8,0},{16,40},{24,32},{32,24},{40,16},{48,56},{56,48},{64,72... | collective-permute-start | bytes 6291464 | tf_op jit(solution)/shard_map/ppermute | solution.py:38
  192.7 20.8 %collective-permute-start.22 = (bf16[2,2,1,2,64,1024]{5,4,3,2,1,0:T(8,128)(2,1)}, bf16[2,2,1,2,64,1024]{5,4,3,2,1,0:T(8,128)(2,1)}, u32[]{:S(2)}, u32[]{:S(2)}) collective-permute-start(bf16[2,2,1,2,64,1024]{5,4,3,2,1,0:T(8,128)(2,1)} %pad_maximum_fusion.5), channel_id=1, source_target_pairs={{0,2},{1,3},{2,0},{3,1},{4,6},{5,7},{6,4},{7,5},{8,10},{9,11},{10,... | collective-permute-start | bytes 3145736 | tf_op jit(solution)/shard_map/ppermute | solution.py:18
  233.8 56.2 %collective-permute-start.29 = (f32[4,32,128]{2,1,0:T(8,128)S(1)}, f32[4,32,128]{2,1,0:T(8,128)S(1)}, u32[]{:S(2)}, u32[]{:S(2)}) collective-permute-start(f32[4,32,128]{2,1,0:T(8,128)S(1)} %get-tuple-element.24), channel_id=1, source_target_pairs={{0,7},{1,6},{2,5},{3,4},{4,3},{5,2},{6,1},{7,0},{8,15},{9,14},{10,... | collective-permute-start | bytes 196616 | tf_op jit(solution)/shard_map/ppermute | solution.py:18
  280.6 12.4 %collective-permute-start.28 = (f32[4,32,128]{2,1,0:T(8,128)S(1)}, f32[4,32,128]{2,1,0:T(8,128)S(1)}, u32[]{:S(2)}, u32[]{:S(2)}) collective-permute-start(f32[4,32,128]{2,1,0:T(8,128)S(1)} %get-tuple-element.25), channel_id=1, source_target_pairs={{0,6},{1,7},{2,4},{3,5},{4,2},{5,3},{6,0},{7,1},{8,14},{9,15},{10,... | collective-permute-start | bytes 196616 | tf_op jit(solution)/shard_map/ppermute | solution.py:18
  299.5 13.7 %collective-permute-start.32 = (f32[4,32,128]{2,1,0:T(8,128)S(1)}, f32[4,32,128]{2,1,0:T(8,128)S(1)}, u32[]{:S(2)}, u32[]{:S(2)}) collective-permute-start(f32[4,32,128]{2,1,0:T(8,128)S(1)} %get-tuple-element.6), channel_id=1, source_target_pairs={{0,3},{1,2},{2,1},{3,0},{4,7},{5,6},{6,5},{7,4},{8,11},{9,10},{10,... | collective-permute-start | bytes 196616 | tf_op jit(solution)/shard_map/ppermute | solution.py:18
  304.0 9.3 %collective-permute-start.33 = (f32[4,32,128]{2,1,0:T(8,128)S(1)}, f32[4,32,128]{2,1,0:T(8,128)S(1)}, u32[]{:S(2)}, u32[]{:S(2)}) collective-permute-start(f32[4,32,128]{2,1,0:T(8,128)S(1)} %get-tuple-element.6), channel_id=1, source_target_pairs={{0,4},{1,5},{2,6},{3,7},{4,0},{5,1},{6,2},{7,3},{8,12},{9,13},{10,... | collective-permute-start | bytes 196616 | tf_op jit(solution)/shard_map/ppermute | solution.py:18
  (24 other events, 364.0 us)

commit v11 on v10

--- a/solution.py
+++ b/solution.py
@@ -135,7 +135,7 @@
     steps, slots, local, waves = permuted.shape
     cols = moving.shape[2]
     return pl.pallas_call(
-        functools.partial(contract_kernel, block, 16 if slots % 16 == 0 else 1),
+        functools.partial(contract_kernel, block, 32 if slots % 32 == 0 else 1),
         out_shape=jax.ShapeDtypeStruct((steps, local, cols), jnp.bfloat16),
         grid_spec=pltpu.PrefetchScalarGridSpec(
             num_scalar_prefetch=1,

time: 318 us -> 288 us (0.906)
  the two profiles are of different devices: /device:TPU:128 before, /device:TPU:32 now
where the time goes in v11:
time: 288 us; the launch traced here: 285 us
  waiting for transfers between devices  148 us (51%)
  starting transfers between devices  80.8 us (28%)
  other arithmetic  27.2 us (9%)
  Pallas kernels  11 us (4%)
  between operations  8.42 us (3%)
  local copies, waits for them, and re-layouts  8.32 us (3%)
    ppermute x15, waiting for transfers between devices, swap_relabelled(): return lax.ppermute(value, axis, pairs)  74.6 us
    ppermute x17, waiting for transfers between devices, swap(): return lax.ppermute(value, axis, [(i, i ^ bit) for i in range(count)])  42.2 us
    ppermute x17, starting transfers between devices, swap(): return lax.ppermute(value, axis, [(i, i ^ bit) for i in range(count)])  35.9 us
    ppermute x15, starting transfers between devices, swap_relabelled(): return lax.ppermute(value, axis, pairs)  35.7 us
    ppermute x4, waiting for transfers between devices, body(): hopped = lax.ppermute(jnp.stack(moving), 'ka', pairs)  31.3 us
    pallas_call x1, Pallas kernels, contract(): pl.pallas_call(functools.partial(contract_kernel, block, 32 if slots % 32...  11 us
    concatenate x8, other arithmetic, join(): return jnp.concatenate([low, high], axis=axis_at)  9.5 us
    ppermute x4, starting transfers between devices, body(): hopped = lax.ppermute(jnp.stack(moving), 'ka', pairs)  9.06 us
  transfers between devices with their start and end apart: 37, of which 20 were waited for; matrix products, arithmetic and copies ran while one was open for 10% of the time, Pallas kernels for 0%

profile of v11, /device:TPU:32, one launch (start us, length us, event | category | flops | bytes accessed | tf_op | source)
XLA Modules:
  0.0 285.3 jit_solution(12226853028374306927)
XLA Ops:
  14.9 17.1 %collective-permute-done.6 = s32[2,2,2,2,1,1,1,512]{7,5,6,4,3,2,1,0:T(1,128)S(1)} collective-permute-done((s32[2,2,2,2,1,1,1,512]{7,5,6,4,3,2,1,0:T(1,128)S(1)}, s32[2,2,2,2,1,1,1,512]{7,5,6,4,3,2,1,0:T(1,128)S(1)}, u32[]{:S(2)}, u32[]{:S(2)}) %collective-permute-start.6) | collective-permute-done | bytes 32800 | tf_op jit(solution)/shard_map/ppermute | solution.py:38
  38.9 3.4 %collective-permute-start.8 = (s32[2,2,1,1,1,1,1,512]{7,5,6,4,3,2,1,0:T(1,128)S(1)}, s32[2,2,1,1,1,1,1,512]{7,5,6,4,3,2,1,0:T(1,128)S(1)}, u32[]{:S(2)}, u32[]{:S(2)}) collective-permute-start(s32[2,2,1,1,1,1,1,512]{7,5,6,4,3,2,1,0:T(1,128)S(1)} %pad_add_fusion.2), channel_id=1, source_target_pairs={{0,64},{8,72},{16,80},{24,88},{32,96},{40,104},{48,112},{56,120},{... | collective-permute-start | bytes 24584 | tf_op jit(solution)/shard_map/ppermute | solution.py:38
  44.1 10.6 %collective-permute-done.1 = bf16[2,2,2,2,1,1,1,64,512]{8,7,1,3,2,6,5,4,0:T(8,128)(2,1)} collective-permute-done((bf16[2,2,2,2,1,1,1,64,512]{8,7,1,3,2,6,5,4,0:T(8,128)(2,1)}, bf16[2,2,2,2,1,1,1,64,512]{8,7,1,3,2,6,5,4,0:T(8,128)(2,1)}, u32[]{:S(2)}, u32[]{:S(2)}) %collective-permute-start.1) | collective-permute-done | bytes 1048608 | tf_op jit(solution)/shard_map/ppermute | solution.py:38
  58.9 7.3 %collective-permute-start.9 = (s32[2,1,1,1,1,1,1,512]{7,6,5,4,3,2,1,0:T(1,128)S(1)}, s32[2,1,1,1,1,1,1,512]{7,6,5,4,3,2,1,0:T(1,128)S(1)}, u32[]{:S(2)}, u32[]{:S(2)}) collective-permute-start(s32[2,1,1,1,1,1,1,512]{7,6,5,4,3,2,1,0:T(1,128)S(1)} %pad_add_fusion.3), channel_id=1, source_target_pairs={{0,128},{8,136},{16,144},{24,152},{32,160},{40,168},{48,176},{56,1... | collective-permute-start | bytes 12296 | tf_op jit(solution)/shard_map/ppermute | solution.py:38
  71.1 5.1 %collective-permute-done.9 = s32[2,1,1,1,1,1,1,512]{7,6,5,4,3,2,1,0:T(1,128)S(1)} collective-permute-done((s32[2,1,1,1,1,1,1,512]{7,6,5,4,3,2,1,0:T(1,128)S(1)}, s32[2,1,1,1,1,1,1,512]{7,6,5,4,3,2,1,0:T(1,128)S(1)}, u32[]{:S(2)}, u32[]{:S(2)}) %collective-permute-start.9) | collective-permute-done | bytes 4128 | tf_op jit(solution)/shard_map/ppermute | solution.py:38
  76.2 4.4 %collective-permute-done.3 = bf16[2,2,1,1,1,1,1,64,512]{8,7,1,6,5,4,3,2,0:T(8,128)(2,1)S(1)} collective-permute-done((bf16[2,2,1,1,1,1,1,64,512]{8,7,1,6,5,4,3,2,0:T(8,128)(2,1)S(1)}, bf16[2,2,1,1,1,1,1,64,512]{8,7,1,6,5,4,3,2,0:T(8,128)(2,1)S(1)}, u32[]{:S(2)}, u32[]{:S(2)}) %collective-permute-start.3) | collective-permute-done | bytes 262176 | tf_op jit(solution)/shard_map/ppermute | solution.py:38
  80.7 6.4 %collective-permute-start.4 = (bf16[2,1,1,1,1,1,1,64,512]{8,7,6,5,4,3,2,1,0:T(8,128)(2,1)S(1)}, bf16[2,1,1,1,1,1,1,64,512]{8,7,6,5,4,3,2,1,0:T(8,128)(2,1)S(1)}, u32[]{:S(2)}, u32[]{:S(2)}) collective-permute-start(bf16[2,1,1,1,1,1,1,64,512]{8,7,6,5,4,3,2,1,0:T(8,128)(2,1)S(1)} %pad_maximum_fusion.15), channel_id=1, source_target_pairs={{0,128},{8,136},{16,144},{24,152},{32,160},{40,168},{48,176},{56,1... | collective-permute-start | bytes 393224 | tf_op jit(solution)/shard_map/ppermute | solution.py:38
  87.6 7.4 %collective-permute-done.4 = bf16[2,1,1,1,1,1,1,64,512]{8,7,6,5,4,3,2,1,0:T(8,128)(2,1)S(1)} collective-permute-done((bf16[2,1,1,1,1,1,1,64,512]{8,7,6,5,4,3,2,1,0:T(8,128)(2,1)S(1)}, bf16[2,1,1,1,1,1,1,64,512]{8,7,6,5,4,3,2,1,0:T(8,128)(2,1)S(1)}, u32[]{:S(2)}, u32[]{:S(2)}) %collective-permute-start.4) | collective-permute-done | bytes 131104 | tf_op jit(solution)/shard_map/ppermute | solution.py:38
  95.8 4.8 %collective-permute-start.10 = (bf16[2,1,1,1,1,1,1,64,512]{8,7,6,5,4,3,2,1,0:T(8,128)(2,1)S(1)}, bf16[2,1,1,1,1,1,1,64,512]{8,7,6,5,4,3,2,1,0:T(8,128)(2,1)S(1)}, u32[]{:S(2)}, u32[]{:S(2)}) collective-permute-start(bf16[2,1,1,1,1,1,1,64,512]{8,7,6,5,4,3,2,1,0:T(8,128)(2,1)S(1)} %pad_maximum_fusion.16), channel_id=1, source_target_pairs={{0,128},{8,136},{16,144},{24,152},{32,160},{40,168},{48,176},{56,1... | collective-permute-start | bytes 393224 | tf_op jit(solution)/shard_map/ppermute | solution.py:38
  100.8 8.7 %collective-permute-start.17 = (bf16[2,32,32,64]{3,2,1,0:T(8,128)(2,1)S(1)}, bf16[2,32,32,64]{3,2,1,0:T(8,128)(2,1)S(1)}, u32[]{:S(2)}, u32[]{:S(2)}) collective-permute-start(bf16[2,32,32,64]{3,2,1,0:T(8,128)(2,1)S(1)} %pad_maximum_fusion.9), channel_id=1, source_target_pairs={{0,32},{8,232},{16,48},{24,248},{32,64},{40,8},{48,80},{56,24},{64... | collective-permute-start | bytes 786440 | tf_op jit(solution)/shard_map/ppermute | solution.py:210
  110.4 8.7 %collective-permute-done.17 = bf16[2,32,32,64]{3,2,1,0:T(8,128)(2,1)S(1)} collective-permute-done((bf16[2,32,32,64]{3,2,1,0:T(8,128)(2,1)S(1)}, bf16[2,32,32,64]{3,2,1,0:T(8,128)(2,1)S(1)}, u32[]{:S(2)}, u32[]{:S(2)}) %collective-permute-start.17) | collective-permute-done | bytes 262176 | tf_op jit(solution)/shard_map/ppermute | solution.py:210
  122.7 3.7 %collective-permute-start.12 = (bf16[2,2,2,1,1,1,1,64,512]{8,7,6,5,4,3,2,1,0:T(8,128)(2,1)}, bf16[2,2,2,1,1,1,1,64,512]{8,7,6,5,4,3,2,1,0:T(8,128)(2,1)}, u32[]{:S(2)}, u32[]{:S(2)}) collective-permute-start(bf16[2,2,2,1,1,1,1,64,512]{8,7,6,5,4,3,2,1,0:T(8,128)(2,1)} %pad_maximum_fusion.7), channel_id=1, source_target_pairs={{0,32},{8,24},{16,48},{24,8},{32,0},{40,56},{48,16},{56,40},{64,96... | collective-permute-start | bytes 1572872 | tf_op jit(solution)/shard_map/ppermute | solution.py:38
  126.4 10.8 %collective-permute-done.18 = bf16[2,32,32,64]{3,2,1,0:T(8,128)(2,1)S(1)} collective-permute-done((bf16[2,32,32,64]{3,2,1,0:T(8,128)(2,1)}, bf16[2,32,32,64]{3,2,1,0:T(8,128)(2,1)S(1)}, u32[]{:S(2)}, u32[]{:S(2)}) %collective-permute-start.18) | collective-permute-done | bytes 262176 | tf_op jit(solution)/shard_map/ppermute | solution.py:210
  137.5 14.4 %collective-permute-done.12 = bf16[2,2,2,1,1,1,1,64,512]{8,7,6,5,4,3,2,1,0:T(8,128)(2,1)} collective-permute-done((bf16[2,2,2,1,1,1,1,64,512]{8,7,6,5,4,3,2,1,0:T(8,128)(2,1)}, bf16[2,2,2,1,1,1,1,64,512]{8,7,6,5,4,3,2,1,0:T(8,128)(2,1)}, u32[]{:S(2)}, u32[]{:S(2)}) %collective-permute-start.12) | collective-permute-done | bytes 524320 | tf_op jit(solution)/shard_map/ppermute | solution.py:38
  154.2 11.8 %collective-permute-done.19 = bf16[2,32,32,64]{3,2,1,0:T(8,128)(2,1)} collective-permute-done((bf16[2,32,32,64]{3,2,1,0:T(8,128)(2,1)S(1)}, bf16[2,32,32,64]{3,2,1,0:T(8,128)(2,1)}, u32[]{:S(2)}, u32[]{:S(2)}) %collective-permute-start.19) | collective-permute-done | bytes 262176 | tf_op jit(solution)/shard_map/ppermute | solution.py:210
  170.3 5.6 %collective-permute-done.20 = bf16[2,1,1,1,64,1024]{5,4,3,2,1,0:T(8,128)(2,1)S(1)} collective-permute-done((bf16[2,1,1,1,64,1024]{5,4,3,2,1,0:T(8,128)(2,1)S(1)}, bf16[2,1,1,1,64,1024]{5,4,3,2,1,0:T(8,128)(2,1)S(1)}, u32[]{:S(2)}, u32[]{:S(2)}) %collective-permute-start.20) | collective-permute-done | bytes 262176 | tf_op jit(solution)/shard_map/ppermute | solution.py:18
  182.9 5.0 %collective-permute-done.21 = bf16[2,1,1,2,64,1024]{5,4,3,2,1,0:T(8,128)(2,1)} collective-permute-done((bf16[2,1,1,2,64,1024]{5,4,3,2,1,0:T(8,128)(2,1)}, bf16[2,1,1,2,64,1024]{5,4,3,2,1,0:T(8,128)(2,1)}, u32[]{:S(2)}, u32[]{:S(2)}) %collective-permute-start.21) | collective-permute-done | bytes 524320 | tf_op jit(solution)/shard_map/ppermute | solution.py:18
  192.4 23.2 %collective-permute-done.22 = bf16[2,2,1,2,64,1024]{5,4,3,2,1,0:T(8,128)(2,1)} collective-permute-done((bf16[2,2,1,2,64,1024]{5,4,3,2,1,0:T(8,128)(2,1)}, bf16[2,2,1,2,64,1024]{5,4,3,2,1,0:T(8,128)(2,1)}, u32[]{:S(2)}, u32[]{:S(2)}) %collective-permute-start.22) | collective-permute-done | bytes 1048608 | tf_op jit(solution)/shard_map/ppermute | solution.py:18
  218.7 11.4 %collective-permute-done.14 = bf16[2,2,2,2,2,1,1,64,512]{8,7,6,5,4,3,2,1,0:T(8,128)(2,1)} collective-permute-done((bf16[2,2,2,2,2,1,1,64,512]{8,7,6,5,4,3,2,1,0:T(8,128)(2,1)}, bf16[2,2,2,2,2,1,1,64,512]{8,7,6,5,4,3,2,1,0:T(8,128)(2,1)}, u32[]{:S(2)}, u32[]{:S(2)}) %collective-permute-start.14) | collective-permute-done | bytes 2097184 | tf_op jit(solution)/shard_map/ppermute | solution.py:38
  234.3 11.0 %shard_map.73 = bf16[2,64,1024]{2,1,0:T(8,128)(2,1)} custom-call(s32[32]{0:T(128)} %q_ref.1, bf16[2,32,64,512]{3,2,1,0:T(8,128)(2,1)} %bitcast.256, bf16[2,512,1024]{2,1,0:T(8,128)(2,1)} %bitcast.262), custom_call_target="tpu_custom_call" | custom-call | flops 4294967296 | bytes 6553600 | tf_op jit(solution)/shard_map/pallas_call | solution.py:137
  252.3 4.1 %collective-permute-start.26 = (f32[4,32,128]{2,1,0:T(8,128)S(1)}, f32[4,32,128]{2,1,0:T(8,128)S(1)}, u32[]{:S(2)}, u32[]{:S(2)}) collective-permute-start(f32[4,32,128]{2,1,0:T(8,128)S(1)} %get-tuple-element.27), channel_id=1, source_target_pairs={{0,4},{1,5},{2,6},{3,7},{4,0},{5,1},{6,2},{7,3},{8,12},{9,13},{10,... | collective-permute-start | bytes 196616 | tf_op jit(solution)/shard_map/ppermute | solution.py:18
  267.6 3.3 %collective-permute-start.32 = (f32[4,32,128]{2,1,0:T(8,128)S(1)}, f32[4,32,128]{2,1,0:T(8,128)S(1)}, u32[]{:S(2)}, u32[]{:S(2)}) collective-permute-start(f32[4,32,128]{2,1,0:T(8,128)S(1)} %get-tuple-element.6), channel_id=1, source_target_pairs={{0,3},{1,2},{2,1},{3,0},{4,7},{5,6},{6,5},{7,4},{8,11},{9,10},{10,... | collective-permute-start | bytes 196616 | tf_op jit(solution)/shard_map/ppermute | solution.py:18
  271.8 3.5 %collective-permute-start.34 = (f32[4,32,128]{2,1,0:T(8,128)S(1)}, f32[4,32,128]{2,1,0:T(8,128)S(1)}, u32[]{:S(2)}, u32[]{:S(2)}) collective-permute-start(f32[4,32,128]{2,1,0:T(8,128)S(1)} %get-tuple-element.6), channel_id=1, source_target_pairs={{0,5},{1,4},{2,7},{3,6},{4,1},{5,0},{6,3},{7,2},{8,13},{9,12},{10,... | collective-permute-start | bytes 196616 | tf_op jit(solution)/shard_map/ppermute | solution.py:18
  276.4 3.7 %collective-permute-start.36 = (f32[4,32,128]{2,1,0:T(8,128)S(1)}, f32[4,32,128]{2,1,0:T(8,128)S(1)}, u32[]{:S(2)}, u32[]{:S(2)}) collective-permute-start(f32[4,32,128]{2,1,0:T(8,128)S(1)} %get-tuple-element.6), channel_id=1, source_target_pairs={{0,7},{1,6},{2,5},{3,4},{4,3},{5,2},{6,1},{7,0},{8,15},{9,14},{10,... | collective-permute-start | bytes 196616 | tf_op jit(solution)/shard_map/ppermute | solution.py:18
  (168 shorter events, 81.2 us)
Async XLA Ops:
  1.0 13.6 %collective-permute-start.5 = (s32[2,2,2,2,1,1,512]{6,4,3,2,1,0,5:T(1,128)S(1)}, s32[2,2,2,2,1,1,512]{6,4,3,2,1,0,5:T(1,128)S(1)}, u32[]{:S(2)}, u32[]{:S(2)}) collective-permute-start(s32[2,2,2,2,1,1,512]{6,4,3,2,1,0,5:T(1,128)S(1)} %constant_dynamic-slice_fusion.12), channel_id=1, source_target_pairs={{0,8},{8,0},{16,40},{24,32},{32,24},{40,16},{48,56},{56,48},{64,72... | collective-permute-start | bytes 98312 | tf_op jit(solution)/shard_map/ppermute | solution.py:38
  5.6 26.6 %collective-permute-start = (bf16[2,2,2,2,1,1,64,512]{7,6,4,3,2,1,0,5:T(8,128)(2,1)}, bf16[2,2,2,2,1,1,64,512]{7,6,4,3,2,1,0,5:T(8,128)(2,1)}, u32[]{:S(2)}, u32[]{:S(2)}) collective-permute-start(bf16[2,2,2,2,1,1,64,512]{7,6,4,3,2,1,0,5:T(8,128)(2,1)} %constant_dynamic-slice_fusion.15), channel_id=1, source_target_pairs={{0,8},{8,0},{16,40},{24,32},{32,24},{40,16},{48,56},{56,48},{64,72... | collective-permute-start | bytes 3145736 | tf_op jit(solution)/shard_map/ppermute | solution.py:38
  14.7 17.2 %collective-permute-start.6 = (s32[2,2,2,2,1,1,1,512]{7,5,6,4,3,2,1,0:T(1,128)S(1)}, s32[2,2,2,2,1,1,1,512]{7,5,6,4,3,2,1,0:T(1,128)S(1)}, u32[]{:S(2)}, u32[]{:S(2)}) collective-permute-start(s32[2,2,2,2,1,1,1,512]{7,5,6,4,3,2,1,0:T(1,128)S(1)} %pad_add_fusion), channel_id=1, source_target_pairs={{0,16},{8,40},{16,0},{24,56},{32,48},{40,8},{48,32},{56,24},{64,80... | collective-permute-start | bytes 98312 | tf_op jit(solution)/shard_map/ppermute | solution.py:38
  36.5 18.2 %collective-permute-start.1 = (bf16[2,2,2,2,1,1,1,64,512]{8,7,1,3,2,6,5,4,0:T(8,128)(2,1)}, bf16[2,2,2,2,1,1,1,64,512]{8,7,1,3,2,6,5,4,0:T(8,128)(2,1)}, u32[]{:S(2)}, u32[]{:S(2)}) collective-permute-start(bf16[2,2,2,2,1,1,1,64,512]{8,7,1,3,2,6,5,4,0:T(8,128)(2,1)} %pad_maximum_fusion.3), channel_id=1, source_target_pairs={{0,16},{8,40},{16,0},{24,56},{32,48},{40,8},{48,32},{56,24},{64,80... | collective-permute-start | bytes 3145736 | tf_op jit(solution)/shard_map/ppermute | solution.py:38
  42.6 44.6 %collective-permute-start.15 = (bf16[32,32,64]{2,1,0:T(8,128)(2,1)S(1)}, bf16[32,32,64]{2,1,0:T(8,128)(2,1)S(1)}, u32[]{:S(2)}, u32[]{:S(2)}) collective-permute-start(bf16[32,32,64]{2,1,0:T(8,128)(2,1)S(1)} %convolution_convert_fusion), channel_id=1, source_target_pairs={{0,8},{8,16},{16,24},{24,32},{32,40},{40,48},{48,56},{56,64},{64,7... | collective-permute-start | bytes 393224 | tf_op jit(solution)/shard_map/ppermute | solution.py:13
  57.1 11.4 %collective-permute-start.2 = (bf16[2,2,2,1,1,1,1,64,512]{8,7,1,2,6,5,4,3,0:T(8,128)(2,1)S(1)}, bf16[2,2,2,1,1,1,1,64,512]{8,7,1,2,6,5,4,3,0:T(8,128)(2,1)S(1)}, u32[]{:S(2)}, u32[]{:S(2)}) collective-permute-start(bf16[2,2,2,1,1,1,1,64,512]{8,7,1,2,6,5,4,3,0:T(8,128)(2,1)S(1)} %pad_maximum_fusion.6), channel_id=1, source_target_pairs={{0,32},{8,24},{16,48},{24,8},{32,0},{40,56},{48,16},{56,40},{64,96... | collective-permute-start | bytes 1572872 | tf_op jit(solution)/shard_map/ppermute | solution.py:38
  58.9 17.3 %collective-permute-start.9 = (s32[2,1,1,1,1,1,1,512]{7,6,5,4,3,2,1,0:T(1,128)S(1)}, s32[2,1,1,1,1,1,1,512]{7,6,5,4,3,2,1,0:T(1,128)S(1)}, u32[]{:S(2)}, u32[]{:S(2)}) collective-permute-start(s32[2,1,1,1,1,1,1,512]{7,6,5,4,3,2,1,0:T(1,128)S(1)} %pad_add_fusion.3), channel_id=1, source_target_pairs={{0,128},{8,136},{16,144},{24,152},{32,160},{40,168},{48,176},{56,1... | collective-permute-start | bytes 12296 | tf_op jit(solution)/shard_map/ppermute | solution.py:38
  68.7 11.9 %collective-permute-start.3 = (bf16[2,2,1,1,1,1,1,64,512]{8,7,1,6,5,4,3,2,0:T(8,128)(2,1)S(1)}, bf16[2,2,1,1,1,1,1,64,512]{8,7,1,6,5,4,3,2,0:T(8,128)(2,1)S(1)}, u32[]{:S(2)}, u32[]{:S(2)}) collective-permute-start(bf16[2,2,1,1,1,1,1,64,512]{8,7,1,6,5,4,3,2,0:T(8,128)(2,1)S(1)} %pad_maximum_fusion.13), channel_id=1, source_target_pairs={{0,64},{8,72},{16,80},{24,88},{32,96},{40,104},{48,112},{56,120},{... | collective-permute-start | bytes 786440 | tf_op jit(solution)/shard_map/ppermute | solution.py:38
  80.7 14.3 %collective-permute-start.4 = (bf16[2,1,1,1,1,1,1,64,512]{8,7,6,5,4,3,2,1,0:T(8,128)(2,1)S(1)}, bf16[2,1,1,1,1,1,1,64,512]{8,7,6,5,4,3,2,1,0:T(8,128)(2,1)S(1)}, u32[]{:S(2)}, u32[]{:S(2)}) collective-permute-start(bf16[2,1,1,1,1,1,1,64,512]{8,7,6,5,4,3,2,1,0:T(8,128)(2,1)S(1)} %pad_maximum_fusion.15), channel_id=1, source_target_pairs={{0,128},{8,136},{16,144},{24,152},{32,160},{40,168},{48,176},{56,1... | collective-permute-start | bytes 393224 | tf_op jit(solution)/shard_map/ppermute | solution.py:38
  87.3 13.3 %collective-permute-start.16 = (bf16[2,32,32,64]{3,2,1,0:T(8,128)(2,1)S(1)}, bf16[2,32,32,64]{3,2,1,0:T(8,128)(2,1)S(1)}, u32[]{:S(2)}, u32[]{:S(2)}) collective-permute-start(bf16[2,32,32,64]{3,2,1,0:T(8,128)(2,1)S(1)} %pad_maximum_fusion.8), channel_id=1, source_target_pairs={{0,16},{8,248},{16,32},{24,8},{32,48},{40,24},{48,64},{56,40},{64,... | collective-permute-start | bytes 786440 | tf_op jit(solution)/shard_map/ppermute | solution.py:210
  95.8 13.7 %collective-permute-start.10 = (bf16[2,1,1,1,1,1,1,64,512]{8,7,6,5,4,3,2,1,0:T(8,128)(2,1)S(1)}, bf16[2,1,1,1,1,1,1,64,512]{8,7,6,5,4,3,2,1,0:T(8,128)(2,1)S(1)}, u32[]{:S(2)}, u32[]{:S(2)}) collective-permute-start(bf16[2,1,1,1,1,1,1,64,512]{8,7,6,5,4,3,2,1,0:T(8,128)(2,1)S(1)} %pad_maximum_fusion.16), channel_id=1, source_target_pairs={{0,128},{8,136},{16,144},{24,152},{32,160},{40,168},{48,176},{56,1... | collective-permute-start | bytes 393224 | tf_op jit(solution)/shard_map/ppermute | solution.py:38
  100.8 18.2 %collective-permute-start.17 = (bf16[2,32,32,64]{3,2,1,0:T(8,128)(2,1)S(1)}, bf16[2,32,32,64]{3,2,1,0:T(8,128)(2,1)S(1)}, u32[]{:S(2)}, u32[]{:S(2)}) collective-permute-start(bf16[2,32,32,64]{3,2,1,0:T(8,128)(2,1)S(1)} %pad_maximum_fusion.9), channel_id=1, source_target_pairs={{0,32},{8,232},{16,48},{24,248},{32,64},{40,8},{48,80},{56,24},{64... | collective-permute-start | bytes 786440 | tf_op jit(solution)/shard_map/ppermute | solution.py:210
  109.6 12.3 %collective-permute-start.11 = (bf16[2,2,1,1,1,1,1,64,512]{8,7,6,5,4,3,2,1,0:T(8,128)(2,1)S(1)}, bf16[2,2,1,1,1,1,1,64,512]{8,7,6,5,4,3,2,1,0:T(8,128)(2,1)S(1)}, u32[]{:S(2)}, u32[]{:S(2)}) collective-permute-start(bf16[2,2,1,1,1,1,1,64,512]{8,7,6,5,4,3,2,1,0:T(8,128)(2,1)S(1)} %pad_maximum_fusion.14), channel_id=1, source_target_pairs={{0,64},{8,72},{16,80},{24,88},{32,96},{40,104},{48,112},{56,120},{... | collective-permute-start | bytes 786440 | tf_op jit(solution)/shard_map/ppermute | solution.py:38
  120.0 17.2 %collective-permute-start.18 = (bf16[2,32,32,64]{3,2,1,0:T(8,128)(2,1)}, bf16[2,32,32,64]{3,2,1,0:T(8,128)(2,1)S(1)}, u32[]{:S(2)}, u32[]{:S(2)}) collective-permute-start(bf16[2,32,32,64]{3,2,1,0:T(8,128)(2,1)} %pad_maximum_fusion.10), channel_id=1, source_target_pairs={{0,64},{8,200},{16,80},{24,216},{32,96},{40,232},{48,112},{56,248}... | collective-permute-start | bytes 786440 | tf_op jit(solution)/shard_map/ppermute | solution.py:210
  122.7 29.2 %collective-permute-start.12 = (bf16[2,2,2,1,1,1,1,64,512]{8,7,6,5,4,3,2,1,0:T(8,128)(2,1)}, bf16[2,2,2,1,1,1,1,64,512]{8,7,6,5,4,3,2,1,0:T(8,128)(2,1)}, u32[]{:S(2)}, u32[]{:S(2)}) collective-permute-start(bf16[2,2,2,1,1,1,1,64,512]{8,7,6,5,4,3,2,1,0:T(8,128)(2,1)} %pad_maximum_fusion.7), channel_id=1, source_target_pairs={{0,32},{8,24},{16,48},{24,8},{32,0},{40,56},{48,16},{56,40},{64,96... | collective-permute-start | bytes 1572872 | tf_op jit(solution)/shard_map/ppermute | solution.py:38
  137.4 28.7 %collective-permute-start.19 = (bf16[2,32,32,64]{3,2,1,0:T(8,128)(2,1)S(1)}, bf16[2,32,32,64]{3,2,1,0:T(8,128)(2,1)}, u32[]{:S(2)}, u32[]{:S(2)}) collective-permute-start(bf16[2,32,32,64]{3,2,1,0:T(8,128)(2,1)S(1)} %pad_maximum_fusion.11), channel_id=1, source_target_pairs={{0,128},{8,136},{16,144},{24,152},{32,160},{40,168},{48,176},{56,1... | collective-permute-start | bytes 786440 | tf_op jit(solution)/shard_map/ppermute | solution.py:210
  154.2 25.7 %collective-permute-start.13 = (bf16[2,2,2,2,1,1,1,64,512]{8,7,6,5,4,3,2,1,0:T(8,128)(2,1)}, bf16[2,2,2,2,1,1,1,64,512]{8,7,6,5,4,3,2,1,0:T(8,128)(2,1)}, u32[]{:S(2)}, u32[]{:S(2)}) collective-permute-start(bf16[2,2,2,2,1,1,1,64,512]{8,7,6,5,4,3,2,1,0:T(8,128)(2,1)} %pad_maximum_fusion.4), channel_id=1, source_target_pairs={{0,16},{8,40},{16,0},{24,56},{32,48},{40,8},{48,32},{56,24},{64,80... | collective-permute-start | bytes 3145736 | tf_op jit(solution)/shard_map/ppermute | solution.py:38
  176.9 11.0 %collective-permute-start.21 = (bf16[2,1,1,2,64,1024]{5,4,3,2,1,0:T(8,128)(2,1)}, bf16[2,1,1,2,64,1024]{5,4,3,2,1,0:T(8,128)(2,1)}, u32[]{:S(2)}, u32[]{:S(2)}) collective-permute-start(bf16[2,1,1,2,64,1024]{5,4,3,2,1,0:T(8,128)(2,1)} %pad_maximum_fusion.12), channel_id=1, source_target_pairs={{0,4},{1,5},{2,6},{3,7},{4,0},{5,1},{6,2},{7,3},{8,12},{9,13},{10,... | collective-permute-start | bytes 1572872 | tf_op jit(solution)/shard_map/ppermute | solution.py:18
  182.9 47.2 %collective-permute-start.14 = (bf16[2,2,2,2,2,1,1,64,512]{8,7,6,5,4,3,2,1,0:T(8,128)(2,1)}, bf16[2,2,2,2,2,1,1,64,512]{8,7,6,5,4,3,2,1,0:T(8,128)(2,1)}, u32[]{:S(2)}, u32[]{:S(2)}) collective-permute-start(bf16[2,2,2,2,2,1,1,64,512]{8,7,6,5,4,3,2,1,0:T(8,128)(2,1)} %pad_maximum_fusion.1), channel_id=1, source_target_pairs={{0,8},{8,0},{16,40},{24,32},{32,24},{40,16},{48,56},{56,48},{64,72... | collective-permute-start | bytes 6291464 | tf_op jit(solution)/shard_map/ppermute | solution.py:38
  191.0 24.6 %collective-permute-start.22 = (bf16[2,2,1,2,64,1024]{5,4,3,2,1,0:T(8,128)(2,1)}, bf16[2,2,1,2,64,1024]{5,4,3,2,1,0:T(8,128)(2,1)}, u32[]{:S(2)}, u32[]{:S(2)}) collective-permute-start(bf16[2,2,1,2,64,1024]{5,4,3,2,1,0:T(8,128)(2,1)} %pad_maximum_fusion.5), channel_id=1, source_target_pairs={{0,2},{1,3},{2,0},{3,1},{4,6},{5,7},{6,4},{7,5},{8,10},{9,11},{10,... | collective-permute-start | bytes 3145736 | tf_op jit(solution)/shard_map/ppermute | solution.py:18
  247.2 10.1 %collective-permute-start.29 = (f32[4,32,128]{2,1,0:T(8,128)S(1)}, f32[4,32,128]{2,1,0:T(8,128)S(1)}, u32[]{:S(2)}, u32[]{:S(2)}) collective-permute-start(f32[4,32,128]{2,1,0:T(8,128)S(1)} %get-tuple-element.24), channel_id=1, source_target_pairs={{0,7},{1,6},{2,5},{3,4},{4,3},{5,2},{6,1},{7,0},{8,15},{9,14},{10,... | collective-permute-start | bytes 196616 | tf_op jit(solution)/shard_map/ppermute | solution.py:18
  249.8 10.0 %collective-permute-start.28 = (f32[4,32,128]{2,1,0:T(8,128)S(1)}, f32[4,32,128]{2,1,0:T(8,128)S(1)}, u32[]{:S(2)}, u32[]{:S(2)}) collective-permute-start(f32[4,32,128]{2,1,0:T(8,128)S(1)} %get-tuple-element.25), channel_id=1, source_target_pairs={{0,6},{1,7},{2,4},{3,5},{4,2},{5,3},{6,0},{7,1},{8,14},{9,15},{10,... | collective-permute-start | bytes 196616 | tf_op jit(solution)/shard_map/ppermute | solution.py:18
  265.8 9.6 %collective-permute-start.30 = (f32[4,32,128]{2,1,0:T(8,128)S(1)}, f32[4,32,128]{2,1,0:T(8,128)S(1)}, u32[]{:S(2)}, u32[]{:S(2)}) collective-permute-start(f32[4,32,128]{2,1,0:T(8,128)S(1)} %get-tuple-element.6), channel_id=1, source_target_pairs={{0,1},{1,0},{2,3},{3,2},{4,5},{5,4},{6,7},{7,6},{8,9},{9,8},{10,11... | collective-permute-start | bytes 196616 | tf_op jit(solution)/shard_map/ppermute | solution.py:18
  267.6 12.6 %collective-permute-start.32 = (f32[4,32,128]{2,1,0:T(8,128)S(1)}, f32[4,32,128]{2,1,0:T(8,128)S(1)}, u32[]{:S(2)}, u32[]{:S(2)}) collective-permute-start(f32[4,32,128]{2,1,0:T(8,128)S(1)} %get-tuple-element.6), channel_id=1, source_target_pairs={{0,3},{1,2},{2,1},{3,0},{4,7},{5,6},{6,5},{7,4},{8,11},{9,10},{10,... | collective-permute-start | bytes 196616 | tf_op jit(solution)/shard_map/ppermute | solution.py:18
  (24 other events, 276.5 us)
